TPU v7x, 32 devices: a whole 2x2x4 slice. The times are simulated.
32 devices in a mesh: req: 16 (over z, y, x), unit: 2 (over core).
Axes of the slice: x: 2, y: 2, z: 4, core: 2. Of those that a mesh axis runs over, the one named last changes fastest.
Arguments:
- queries: bfloat16 [4096, 1536], P(('req', 'unit')), as said below
- kv_new: bfloat16 [4096, 512], P(('req', 'unit')), as said below
- kv_pool: bfloat16 [416, 128, 512], P(('req', 'unit')), may hold values from -6 to 6
- page_table: int32 [32, 13], P(('req', 'unit')), may hold values from 0 to 12, as said below
- ctx_pages: int32 [32], P(('req', 'unit')), may hold values from 4 to 12
- ssm_x: bfloat16 [4096, 3072], P(('req', 'unit')), may hold values from -6 to 6
- ssm_z: bfloat16 [4096, 3072], P(('req', 'unit')), may hold values from -6 to 6
- ssm_bc: bfloat16 [4096, 512], P(('req', 'unit')), may hold values from -1.5 to 1.5
- dt_raw: float32 [4096, 24], P(('req', 'unit'))
- dt_bias: float32 [24], replicated, may hold values from -1 to 0.5
- decay_rate: float32 [24], replicated, may hold values from 0.002 to 0.06
- skip_gain: float32 [24], replicated, may hold values from 0.5 to 1.5
- ssm_state: float32 [32, 24, 128, 256], P(('req', 'unit')), may hold values from -6 to 6
- ssm_norm_gain: float32 [3072], replicated, may hold values from 0.25 to 1.75
- resid: bfloat16 [4096, 3072], P(('req', 'unit')), as said below
- out_weight: bfloat16 [4608, 3072], P('unit'), may hold values from -0.09375 to 0.09375
- ffn_hidden: bfloat16 [4096, 6144], P(('req', 'unit')), may hold values from -6 to 6
- down_weight: bfloat16 [6144, 3072], P(('req', 'unit')), may hold values from -0.078125 to 0.078125
- page_owner: int32 [32, 13, 1], P(('req', 'unit')), may hold values from 0 to 1; in each aligned block of 13 rows (0 to 12, 13 to 25, ..., all dimensions but the last counted through in order) at most 7 rows name the same one
Outputs:
- layer_out: bfloat16 [4096, 3072], P(('req', 'unit'))
- decode_kv: bfloat16 [448, 128, 512], P(('req', 'unit'))
- decode_state: float32 [32, 24, 128, 256], P('req', 'unit')
Inputs may be any that keep to these rules, and one draw needn't show every extreme that they name: queries of the block. `kv_new`: keys and values of the block. `page_table`: each device's 1 * 13 entries name each of its 13 pool slots once. `resid`: residual stream. `page_owner`: among the 13 pages of one device at most 7 name the same owner.
All inputs are finite; a program needn't handle non-finite values.
Results may differ from a plain program's by a relative error of at most 0.007.
Values may be sent and summed in bfloat16 or wider, within the bound.
No kernel may reach another device: no remote copies, remote signals or barrier semaphores. Data moves between devices by JAX's collectives and lax.ppermute only.
A program may use at most 192 MiB of HBM per device.

v0:
```python
import math

import jax
import jax.numpy as jnp
from jax import lax
from jax.sharding import PartitionSpec as P

QUERY_HEADS = 12
KEY_VALUE_HEADS = 2
HEAD_WIDTH = 128
MIXER_HEADS = 24
PM = 128
NS = 256


norm_eps = 1e-05


def attend(query_block, pages_now, live_count):
    request_pages = pages_now.shape[0]
    block_length = pages_now.shape[1]
    kv_width = pages_now.shape[2]
    pages_flattened = pages_now.reshape(request_pages * block_length, kv_width)
    key_block_rows = pages_flattened[:, : KEY_VALUE_HEADS * HEAD_WIDTH].reshape(
        request_pages * block_length, KEY_VALUE_HEADS, HEAD_WIDTH
    )
    value_block_rows = pages_flattened[:, KEY_VALUE_HEADS * HEAD_WIDTH :].reshape(
        request_pages * block_length, KEY_VALUE_HEADS, HEAD_WIDTH
    )
    heads_per_group = QUERY_HEADS // KEY_VALUE_HEADS
    query_head_rows = query_block.reshape(
        block_length, KEY_VALUE_HEADS, heads_per_group, HEAD_WIDTH
    )
    scores = jnp.einsum(
        "tkgd,skd->kgts", query_head_rows, key_block_rows, preferred_element_type=jnp.float32
    )
    scores = scores * (1.0 / math.sqrt(HEAD_WIDTH))
    key_pos = jnp.arange(request_pages * block_length, dtype=jnp.int32)
    q_limit = live_count * block_length + jnp.arange(block_length, dtype=jnp.int32)
    visible = key_pos[None, :] <= q_limit[:, None]
    scores = jnp.where(visible[None, None], scores, -1e30)
    row_max = jnp.max(scores, axis=-1, keepdims=True)
    exponent = jnp.exp(scores - row_max)
    weights = (exponent / jnp.sum(exponent, axis=-1, keepdims=True)).astype(jnp.bfloat16)
    attended = jnp.einsum(
        "kgts,skd->tkgd", weights, value_block_rows, preferred_element_type=jnp.float32
    )
    return attended.reshape(block_length, QUERY_HEADS * HEAD_WIDTH).astype(jnp.bfloat16)


def ssm_block(
    ssm_in, gate_in, bc_rows, dt_rows, dt_bias, decay_rate, skip_gain, prior_state, norm_gain
):
    block_length = ssm_in.shape[0]
    step_size = jax.nn.softplus(dt_rows + dt_bias[None, :])
    cum = jnp.cumsum(-step_size * decay_rate[None, :], axis=0)
    b_rows = bc_rows[:, :NS]
    c_rows = bc_rows[:, NS:]
    cb_dots = jnp.dot(c_rows, b_rows.T, preferred_element_type=jnp.float32)
    cum_heads = cum.T
    log_gap = cum_heads[:, :, None] - cum_heads[:, None, :]
    causal = jnp.arange(block_length)[:, None] >= jnp.arange(block_length)[None, :]
    decay = jnp.exp(jnp.where(causal[None], log_gap, -1e30))
    mixing = (cb_dots[None] * decay * step_size.T[:, None, :]).astype(jnp.bfloat16)
    x_heads = ssm_in.reshape(block_length, MIXER_HEADS, PM)
    within = jnp.einsum("hts,shp->thp", mixing, x_heads, preferred_element_type=jnp.float32)
    carried = jnp.einsum(
        "tn,hpn->thp", c_rows.astype(jnp.float32), prior_state, precision=lax.Precision.HIGHEST
    )
    carried = carried * jnp.exp(cum)[:, :, None]
    x_float = x_heads.astype(jnp.float32)
    ssm_y = within + carried + skip_gain[None, :, None] * x_float
    total_decay = cum[block_length - 1]
    tail_weight = jnp.exp(total_decay[None, :] - cum) * step_size
    x_weighted = x_float * tail_weight[:, :, None]
    new_state = jnp.exp(total_decay)[:, None, None] * prior_state + jnp.einsum(
        "shp,sn->hpn", x_weighted, b_rows.astype(jnp.float32), precision=lax.Precision.HIGHEST
    )
    gated = ssm_y.reshape(block_length, MIXER_HEADS * PM) * jax.nn.silu(gate_in.astype(jnp.float32))
    gated = (
        gated
        * lax.rsqrt(jnp.mean(gated * gated, axis=-1, keepdims=True) + norm_eps)
        * norm_gain[None, :]
    )
    return (gated.astype(jnp.bfloat16), new_state)


def on_device(
    queries,
    kv_new,
    kv_pool,
    page_table,
    ctx_pages,
    ssm_x,
    ssm_z,
    ssm_bc,
    dt_raw,
    dt_bias,
    decay_rate,
    skip_gain,
    ssm_state,
    ssm_norm_gain,
    resid,
    out_weight,
    ffn_hidden,
    down_weight,
    page_owner,
):
    tok_rows = queries.shape[0]
    block_length = kv_pool.shape[1]
    kv_width = kv_pool.shape[2]
    req_count = page_table.shape[0]
    request_pages = page_table.shape[1]
    unit_count = lax.axis_size("unit")
    block_rows = down_weight.shape[0]
    width = down_weight.shape[1]

    def per_request(inputs):
        (
            query_block,
            fresh_kv,
            slot_row,
            live_count,
            ssm_in,
            gate_in,
            bc_rows,
            dt_rows,
            prior_state,
        ) = inputs
        stored = kv_pool[slot_row]
        pages_now = lax.dynamic_update_slice(
            stored, fresh_kv[None], (live_count, jnp.int32(0), jnp.int32(0))
        )
        attn_out = attend(query_block, pages_now, live_count)
        live = jnp.arange(request_pages, dtype=jnp.int32) <= live_count
        kept_pages = jnp.where(live[:, None, None], pages_now, jnp.zeros_like(pages_now))
        ssm_out, new_state = ssm_block(
            ssm_in,
            gate_in,
            bc_rows,
            dt_rows,
            dt_bias,
            decay_rate,
            skip_gain,
            prior_state,
            ssm_norm_gain,
        )
        return (jnp.concatenate([attn_out, ssm_out], axis=1), kept_pages, new_state)

    mixed_rows, kept_pages, new_state = lax.map(
        per_request,
        (
            queries.reshape(req_count, block_length, -1),
            kv_new.reshape(req_count, block_length, kv_width),
            page_table,
            ctx_pages,
            ssm_x.reshape(req_count, block_length, -1),
            ssm_z.reshape(req_count, block_length, -1),
            ssm_bc.reshape(req_count, block_length, -1),
            dt_raw.reshape(req_count, block_length, -1),
            ssm_state,
        ),
    )
    mixed_rows = mixed_rows.reshape(tok_rows, -1)
    exchanged = lax.all_to_all(mixed_rows, "unit", split_axis=1, concat_axis=0, tiled=True)
    mixer_sum = lax.psum_scatter(
        jnp.dot(exchanged, out_weight, preferred_element_type=jnp.float32).astype(jnp.bfloat16),
        "unit",
        scatter_dimension=0,
        tiled=True,
    ).astype(jnp.float32)
    after_mixers = resid.astype(jnp.float32) + mixer_sum
    w_piece = lax.all_gather(down_weight, ("req", "unit"), axis=0, tiled=True)
    count = w_piece.shape[0]
    group_of = jnp.arange(count, dtype=jnp.int32) // block_rows % unit_count
    updated = []
    for fold_unit_idx in range(unit_count):
        masked = jnp.where(
            (group_of == fold_unit_idx)[None, :], ffn_hidden, jnp.zeros_like(ffn_hidden)
        )
        updated.append(jnp.dot(masked, w_piece, preferred_element_type=jnp.float32))
    group_sums = tuple(updated)
    ffn_sum = jnp.zeros((tok_rows, width), jnp.float32)
    for unit_idx in range(unit_count):
        ffn_sum = ffn_sum + lax.optimization_barrier(
            group_sums[unit_idx].astype(jnp.bfloat16)
        ).astype(jnp.float32)
    layer_out = (after_mixers + ffn_sum).astype(jnp.bfloat16)
    slot_cap = max(2, (req_count * request_pages + unit_count - 1) // unit_count)
    owners = page_owner.reshape(req_count * request_pages)
    onehot = (owners[:, None] == jnp.arange(unit_count, dtype=jnp.int32)[None, :]).astype(jnp.int32)
    before = jnp.cumsum(onehot, axis=0) - onehot
    page_rank = jnp.sum(before * onehot, axis=1)
    dest_slot = owners * slot_cap + page_rank
    outgoing = jnp.zeros((unit_count * slot_cap, block_length, kv_width), jnp.bfloat16)
    outgoing = outgoing.at[dest_slot].set(kept_pages.reshape(-1, block_length, kv_width))
    arrived = lax.all_to_all(
        outgoing.reshape(unit_count, slot_cap, block_length, kv_width),
        "unit",
        split_axis=0,
        concat_axis=0,
        tiled=True,
    )
    decode_kv = arrived.reshape(unit_count * slot_cap, block_length, kv_width)
    decode_state = lax.all_to_all(
        new_state.astype(jnp.bfloat16), "unit", split_axis=1, concat_axis=0, tiled=True
    ).astype(new_state.dtype)
    return (layer_out, decode_kv, decode_state)


def solution(mesh):
    return jax.shard_map(
        on_device,
        mesh=mesh,
        in_specs=(
            P(("req", "unit"), None),
            P(("req", "unit"), None),
            P(("req", "unit"), None, None),
            P(("req", "unit"), None),
            P(("req", "unit")),
            P(("req", "unit"), None),
            P(("req", "unit"), None),
            P(("req", "unit"), None),
            P(("req", "unit"), None),
            P(),
            P(),
            P(),
            P(("req", "unit"), None, None, None),
            P(),
            P(("req", "unit"), None),
            P("unit", None),
            P(("req", "unit"), None),
            P(("req", "unit"), None),
            P(("req", "unit"), None, None),
        ),
        out_specs=(
            P(("req", "unit"), None),
            P(("req", "unit"), None, None),
            P("req", "unit", None, None),
        ),
        check_vma=False,
    )
```

profile of v0, /device:TPU:0, one launch (start us, length us, event | category | flops | bytes accessed | tf_op | source)
XLA Modules:
  0.0 272.1 jit_solution(12929461177080693311)
XLA Ops:
  11.2 1.2 copy.108
  14.8 1.4 copy.97
  16.2 1.4 copy.98
  17.5 2.0 copy.99
  21.6 1.4 copy-done.6
  23.0 3.0 %multiply_reduce_fusion = (f32[128]{0:T(128)S(1)}, f32[128,24,128]{0,2,1:T(8,128)}) fusion(bf16[128,24,128]{0,2,1:T(8,128)(2,1)S(1)} %bitcast.116, f32[24]{0:T(128)S(1)} %copy-done.19, f32[128,24]{0,1:T(8,128)S(1)} %copy.107, f32[1,24,128,256]{3,2,1,0:T(8,128)S(1)} %copy-done.6, bf16[128,512]{1,0:T(8,128)(2,1)S(1)} %copy-done.12, ...), kind=kOutput, calls=%fused_computation.31 | convolution fusion | flops 1213071232 | bytes 7943168 | tf_op jit(solution)/shard_map/while/body/eval_jaxpr/tn,hpn->thp/dot_general | solution.py:67
  26.1 8.7 %fusion.56 = (f32[2,6,128]{2,1,0:T(8,128)S(1)}, f32[2,6,128,1664]{2,3,1,0:T(8,128)}) fusion(pred[128,1664]{0,1:T(8,128)(4,1)S(1)} %iota_compare_fusion, bf16[1664,2,128,1]{0,2,3,1:T(8,128)(2,1)} %bitcast.122, bf16[128,2,6,128]{0,3,2,1:T(8,128)(2,1)} %bitcast.124), kind=kOutput, calls=%fused_computation.96 | convolution fusion | flops 664536704 | bytes 11687936 | tf_op jit(solution)/shard_map/while/body/eval_jaxpr/sub | solution.py:43
  34.8 2.1 fusion.13
  36.9 4.9 %fusion.21 = bf16[2,128,6,128]{3,1,2,0:T(8,128)(2,1)S(1)} fusion(bf16[1664,2,128,1]{0,2,3,1:T(8,128)(2,1)S(1)} %bitcast.121, f32[2,6,128,1664]{2,3,1,0:T(8,128)} %get-tuple-element.46, f32[2,6,128]{2,1,0:T(8,128)S(1)} %get-tuple-element.45), kind=kOutput, calls=%fused_computation.36 | convolution fusion | flops 659619840 | bytes 11474944 | tf_op jit(solution)/shard_map/while/body/eval_jaxpr/kgts,skd->tkgd/dot_general | solution.py:45
  42.8 4.6 %all-to-all-start = ((bf16[128,2,2304]{0,2,1:T(8,128)(2,1)}), bf16[128,2,2304]{0,2,1:T(8,128)(2,1)}, u32[]{:S(2)}, u32[]{:S(2)}) async-start(bf16[128,2,2304]{0,2,1:T(8,128)(2,1)} %bitcast.22), calls=%async_computation | async-start | bytes 2359296 | tf_op jit(solution)/shard_map/all_to_all | solution.py:165
  47.9 1.4 broadcast_in_dim.126
  49.3 5.0 %scatter_fusion = bf16[14,128,512]{2,1,0:T(8,128)(2,1)} fusion(bf16[14,128,512]{2,1,0:T(8,128)(2,1)} %broadcast_in_dim.126, s32[13]{0:T(128)S(1)} %fusion.47, bf16[13,128,512]{2,1,0:T(8,128)(2,1)S(1)} %broadcast_select_fusion), kind=kCustom, calls=%fused_computation.1 | custom fusion | bytes 5111860 | tf_op jit(solution)/shard_map/scatter | solution.py:196
  54.3 3.7 %all-to-all-start.1 = ((bf16[2,7,128,512]{3,2,1,0:T(8,128)(2,1)}), bf16[2,7,128,512]{3,2,1,0:T(8,128)(2,1)S(1)}, u32[]{:S(2)}, u32[]{:S(2)}) async-start(bf16[2,7,128,512]{3,2,1,0:T(8,128)(2,1)} %bitcast.29), calls=%async_computation.2 | async-start | bytes 3670016 | tf_op jit(solution)/shard_map/all_to_all | solution.py:197
  58.3 1.7 copy.109
  60.0 10.0 %convolution_convert_fusion = bf16[256,3072]{1,0:T(8,128)(2,1)} fusion(bf16[256,2304]{1,0:T(8,128)(2,1)S(1)} %bitcast.119, bf16[2304,3072]{1,0:T(8,128)(2,1)} %param.34), kind=kOutput, calls=%fused_computation.11 | convolution fusion | flops 3624665088 | bytes 16908288 | tf_op jit(solution)/shard_map/dot_general | solution.py:167
  71.1 4.4 %fusion.20 = bf16[1,24,128,256]{3,2,0,1:T(8,128)(2,1)} fusion(bf16[128,24,128]{0,2,1:T(8,128)(2,1)S(1)} %bitcast.117, f32[1,24,128,256]{3,2,1,0:T(8,128)} %param.31, f32[24]{0:T(128)S(1)} %fusion.53, f32[128,24]{0,1:T(8,128)S(1)} %get-tuple-element.41, bf16[128,512]{1,0:T(8,128)(2,1)S(1)} %copy-done.13), kind=kOutput, calls=%fused_computation.35 | convolution fusion | flops 1211105280 | bytes 5583360 | tf_op jit(solution)/shard_map/while/body/eval_jaxpr/shp,sn->hpn/dot_general | solution.py:76
  75.5 3.7 %all-to-all-start.2 = ((bf16[1,24,128,256]{3,2,0,1:T(8,128)(2,1)}), bf16[1,24,128,256]{3,2,0,1:T(8,128)(2,1)S(1)}, u32[]{:S(2)}, u32[]{:S(2)}) async-start(bf16[1,24,128,256]{3,2,0,1:T(8,128)(2,1)} %fusion.20), calls=%async_computation.3 | async-start | bytes 3145728 | tf_op jit(solution)/shard_map/all_to_all | solution.py:205
  79.2 2.6 all-to-all-done.2
  82.9 3.6 %convert.2 = f32[2,12,128,256]{3,2,1,0:T(8,128)} convert(bf16[2,12,128,256]{3,2,1,0:T(8,128)(2,1)} %bitcast.114) | non-fusion elementwise | flops 786432 | bytes 4718592 | tf_op jit(solution)/shard_map/convert_element_type | solution.py:207
  86.5 143.0 %all-gather.2.cloned.1.call-done = bf16[6144,3072]{1,0:T(8,128)(2,1)} async-done(((bf16[192,3072]{1,0:T(8,128)(2,1)}), bf16[6144,3072]{1,0:T(8,128)(2,1)}) %all-gather.2.cloned.1.call-update) | async-done | bytes 37748752 | tf_op jit(solution)/shard_map/all_gather | solution.py:173
  229.5 15.3 %convolution_convert_fusion.1 = bf16[128,3072]{1,0:T(8,128)(2,1)} fusion(bf16[6144,3072]{1,0:T(8,128)(2,1)} %all-gather.2.cloned.1.call-done, bf16[128,6144]{1,0:T(8,128)(2,1)S(1)} %copy-done.2, pred[6144]{0:T(1024)(128)(4,1)S(1)} %broadcast_compare_fusion.1), kind=kOutput, calls=%fused_computation.12 | convolution fusion | flops 4833017856 | bytes 40114176 | tf_op jit(solution)/shard_map/dot_general | solution.py:181
  244.8 15.3 %convolution_convert_fusion.2 = bf16[128,3072]{1,0:T(8,128)(2,1)} fusion(bf16[6144,3072]{1,0:T(8,128)(2,1)} %all-gather.2.cloned.1.call-done, bf16[128,6144]{1,0:T(8,128)(2,1)S(1)} %copy-done.2, pred[6144]{0:T(1024)(128)(4,1)S(1)} %broadcast_compare_fusion), kind=kOutput, calls=%fused_computation.13 | convolution fusion | flops 4833017856 | bytes 40114176 | tf_op jit(solution)/shard_map/dot_general | solution.py:181
  260.1 3.3 %add_convert_fusion = bf16[128,3072]{1,0:T(8,128)(2,1)} fusion(bf16[128,3072]{1,0:T(8,128)(2,1)} %convolution_convert_fusion.1, bf16[128,3072]{1,0:T(8,128)(2,1)} %convolution_convert_fusion.2, bf16[128,3072]{1,0:T(8,128)(2,1)} %reduce-scatter.2.cloned.1.call-done, bf16[128,3072]{1,0:T(8,128)(2,1)} %param.33), kind=kLoop, calls=%fused_computation.28 | loop fusion | flops 3145728 | bytes 3932160 | tf_op jit(solution)/shard_map/convert_element_type | solution.py:188
  263.5 1.2 copy.122
  (77 shorter events, 11.0 us)
Async XLA Ops:
  8.0 5.1 %copy-start = (bf16[13,128,512]{2,1,0:T(8,128)(2,1)S(1)}, bf16[13,128,512]{2,1,0:T(8,128)(2,1)}, u32[]{:S(2)}) copy-start(bf16[13,128,512]{2,1,0:T(8,128)(2,1)} %param.21) | copy-start | bytes 5111812
  8.0 1.9 copy-start.10
  8.0 3.2 %copy-start.11 = (bf16[128,3072]{1,0:T(8,128)(2,1)S(1)}, bf16[128,3072]{1,0:T(8,128)(2,1)}, u32[]{:S(2)}) copy-start(bf16[128,3072]{1,0:T(8,128)(2,1)} %param.25) | copy-start | bytes 2359300
  8.0 221.4 %all-gather.2.cloned.1.call-start = ((), (), s32[]{:S(2)}) async-start(), calls=%async_computation.5 | async-start | bytes 38928384 | tf_op jit(solution)/shard_map/all_gather | solution.py:173
  9.8 9.7 %copy-start.8 = (f32[128,24]{1,0:T(8,128)}, f32[128,24]{1,0:T(8,128)S(1)}, u32[]{:S(2)}) copy-start(f32[128,24]{1,0:T(8,128)S(1)} %reduce_window_sum.23) | copy-start | bytes 36868
  9.9 3.1 %copy-start.18 = (s32[1,13]{1,0:T(1,128)S(1)}, s32[1,13]{1,0:T(1,128)}, u32[]{:S(2)}) copy-start(s32[1,13]{1,0:T(1,128)} %param.22) | copy-start | bytes 160
  16.2 3.4 %copy-start.14 = (f32[128,24]{0,1:T(8,128)S(1)}, f32[128,24]{0,1:T(8,128)}, u32[]{:S(2)}) copy-start(f32[128,24]{0,1:T(8,128)} %param.27) | copy-start | bytes 36868
  16.2 3.4 %copy-start.16 = (f32[24]{0:T(128)S(1)}, f32[24]{0:T(128)}, u32[]{:S(2)}) copy-start(f32[24]{0:T(128)} %param.28) | copy-start | bytes 292
  16.2 4.6 %copy-start.4 = (bf16[128,3072]{0,1:T(8,128)(2,1)S(1)}, bf16[128,3072]{0,1:T(8,128)(2,1)}, u32[]{:S(2)}) copy-start(bf16[128,3072]{0,1:T(8,128)(2,1)} %copy.106) | copy-start | bytes 2359300
  17.5 4.0 %copy-start.7 = (bf16[128,3072]{0,1:T(8,128)(2,1)S(1)}, bf16[128,3072]{0,1:T(8,128)(2,1)}, u32[]{:S(2)}) copy-start(bf16[128,3072]{0,1:T(8,128)(2,1)} %copy.108) | copy-start | bytes 2359300
  19.7 1.9 copy-start.12
  20.8 2.2 copy-start.6
  20.8 2.2 copy-start.19
  26.1 8.7 %copy-start.15 = (f32[3072]{0:T(1024)S(1)}, f32[3072]{0:T(1024)}, u32[]{:S(2)}) copy-start(f32[3072]{0:T(1024)} %param.32) | copy-start | bytes 36868
  34.8 2.1 copy-start.9
  42.8 4.6 %copy-start.17 = (s32[1,13,1]{1,2,0:T(1,128)S(1)}, s32[1,13,1]{1,2,0:T(1,128)}, u32[]{:S(2)}) copy-start(s32[1,13,1]{1,2,0:T(1,128)} %param.37) | copy-start | bytes 160
  42.8 11.4 %all-to-all-start = ((bf16[128,2,2304]{0,2,1:T(8,128)(2,1)}), bf16[128,2,2304]{0,2,1:T(8,128)(2,1)}, u32[]{:S(2)}, u32[]{:S(2)}) async-start(bf16[128,2,2304]{0,2,1:T(8,128)(2,1)} %bitcast.22), calls=%async_computation | async-start | bytes 2359296 | tf_op jit(solution)/shard_map/all_to_all | solution.py:165
  54.3 21.2 %all-to-all-start.1 = ((bf16[2,7,128,512]{3,2,1,0:T(8,128)(2,1)}), bf16[2,7,128,512]{3,2,1,0:T(8,128)(2,1)S(1)}, u32[]{:S(2)}, u32[]{:S(2)}) async-start(bf16[2,7,128,512]{3,2,1,0:T(8,128)(2,1)} %bitcast.29), calls=%async_computation.2 | async-start | bytes 3670016 | tf_op jit(solution)/shard_map/all_to_all | solution.py:197
  58.0 202.1 %reduce-scatter.2.cloned.1.call-start = ((), (), s32[]{:S(2)}) async-start(), calls=%async_computation.4 | async-start | bytes 2359296 | tf_op jit(solution)/shard_map/reduce_scatter | solution.py:166
  69.9 1.1 copy-start.5
  69.9 1.2 copy-start.13
  75.5 6.3 %all-to-all-start.2 = ((bf16[1,24,128,256]{3,2,0,1:T(8,128)(2,1)}), bf16[1,24,128,256]{3,2,0,1:T(8,128)(2,1)S(1)}, u32[]{:S(2)}, u32[]{:S(2)}) async-start(bf16[1,24,128,256]{3,2,0,1:T(8,128)(2,1)} %fusion.20), calls=%async_computation.3 | async-start | bytes 3145728 | tf_op jit(solution)/shard_map/all_to_all | solution.py:205
  82.9 146.6 %copy-start.2 = (bf16[128,6144]{1,0:T(8,128)(2,1)S(1)}, bf16[128,6144]{1,0:T(8,128)(2,1)}, u32[]{:S(2)}) copy-start(bf16[128,6144]{1,0:T(8,128)(2,1)} %param.35) | copy-start | bytes 4718596
  260.1 4.6 %copy-start.1 = (bf16[13,128,512]{2,1,0:T(8,128)(2,1)S(1)}, bf16[13,128,512]{2,1,0:T(8,128)(2,1)}, u32[]{:S(2)}) copy-start(bf16[13,128,512]{2,1,0:T(8,128)(2,1)} %param.21) | copy-start | bytes 5111812
  (1 other events, 1.1 us)
Sparse Core Ops, SparseCore 0:
  11.8 217.6 all-gather.1
Sparse Core Ops, SparseCore 1:
  70.0 12.2 reduce-scatter.1
where the time goes:
time: 273 us; the launch traced here: 272 us
  waiting for transfers between devices  146 us (53%)
  matrix products  63.3 us (23%)
  local copies, waits for them, and re-layouts  22.1 us (8%)
  between operations  16.5 us (6%)
  starting transfers between devices  12.2 us (4%)
  other arithmetic  11.7 us (4%)
    all_gather x1, waiting for transfers between devices, on_device(): w_piece = lax.all_gather(down_weight, ('req', 'unit'), axis=0, tiled=True)  143 us
    dot_general x2, matrix products, on_device(): updated.append(jnp.dot(masked, w_piece, preferred_element_type=jnp.float32))  30.7 us
    dot_general x1, matrix products, on_device(): jnp.dot(exchanged, out_weight, preferred_element_type=jnp.float32)  9.95 us
    sub x1, matrix products, attend(): exponent = jnp.exp(scores - row_max)  8.71 us
    unnamed x44, local copies, waits for them, and re-layouts  8.5 us
  transfers between devices with their start and end apart: 5, of which 2 were waited for; matrix products, arithmetic and copies ran while one was open for 33% of the time, Pallas kernels for 0%

commit v1 on v0

v1 whole, which is shorter than its diff:
```python
import math

import jax
import jax.numpy as jnp
from jax import lax
from jax.sharding import PartitionSpec as P

QUERY_HEADS = 12
KEY_VALUE_HEADS = 2
HEAD_WIDTH = 128
MIXER_HEADS = 24
PM = 128
NS = 256

PLANE = 4

norm_eps = 1e-05


def attend(query_block, pages_now, live_count):
    request_pages = pages_now.shape[0]
    block_length = pages_now.shape[1]
    kv_width = pages_now.shape[2]
    pages_flattened = pages_now.reshape(request_pages * block_length, kv_width)
    key_block_rows = pages_flattened[:, : KEY_VALUE_HEADS * HEAD_WIDTH].reshape(
        request_pages * block_length, KEY_VALUE_HEADS, HEAD_WIDTH
    )
    value_block_rows = pages_flattened[:, KEY_VALUE_HEADS * HEAD_WIDTH :].reshape(
        request_pages * block_length, KEY_VALUE_HEADS, HEAD_WIDTH
    )
    heads_per_group = QUERY_HEADS // KEY_VALUE_HEADS
    query_head_rows = query_block.reshape(
        block_length, KEY_VALUE_HEADS, heads_per_group, HEAD_WIDTH
    )
    scores = jnp.einsum(
        "tkgd,skd->kgts", query_head_rows, key_block_rows, preferred_element_type=jnp.float32
    )
    scores = scores * (1.0 / math.sqrt(HEAD_WIDTH))
    key_pos = jnp.arange(request_pages * block_length, dtype=jnp.int32)
    q_limit = live_count * block_length + jnp.arange(block_length, dtype=jnp.int32)
    visible = key_pos[None, :] <= q_limit[:, None]
    scores = jnp.where(visible[None, None], scores, -1e30)
    row_max = jnp.max(scores, axis=-1, keepdims=True)
    exponent = jnp.exp(scores - row_max)
    weights = (exponent / jnp.sum(exponent, axis=-1, keepdims=True)).astype(jnp.bfloat16)
    attended = jnp.einsum(
        "kgts,skd->tkgd", weights, value_block_rows, preferred_element_type=jnp.float32
    )
    return attended.reshape(block_length, QUERY_HEADS * HEAD_WIDTH).astype(jnp.bfloat16)


def ssm_block(
    ssm_in, gate_in, bc_rows, dt_rows, dt_bias, decay_rate, skip_gain, prior_state, norm_gain
):
    block_length = ssm_in.shape[0]
    causal = jnp.arange(block_length)[:, None] >= jnp.arange(block_length)[None, :]
    step_size = jax.nn.softplus(dt_rows + dt_bias[None, :])
    cum = jnp.dot(
        causal.astype(jnp.float32),
        -step_size * decay_rate[None, :],
        precision=lax.Precision.HIGHEST,
    )
    b_rows = bc_rows[:, :NS]
    c_rows = bc_rows[:, NS:]
    cb_dots = jnp.dot(c_rows, b_rows.T, preferred_element_type=jnp.float32)
    cum_heads = cum.T
    log_gap = cum_heads[:, :, None] - cum_heads[:, None, :]
    decay = jnp.exp(jnp.where(causal[None], log_gap, -1e30))
    mixing = (cb_dots[None] * decay * step_size.T[:, None, :]).astype(jnp.bfloat16)
    x_heads = ssm_in.reshape(block_length, MIXER_HEADS, PM)
    within = jnp.einsum("hts,shp->thp", mixing, x_heads, preferred_element_type=jnp.float32)
    carried = jnp.einsum(
        "tn,hpn->thp", c_rows.astype(jnp.float32), prior_state, precision=lax.Precision.HIGHEST
    )
    carried = carried * jnp.exp(cum)[:, :, None]
    x_float = x_heads.astype(jnp.float32)
    ssm_y = within + carried + skip_gain[None, :, None] * x_float
    total_decay = cum[block_length - 1]
    tail_weight = jnp.exp(total_decay[None, :] - cum) * step_size
    x_weighted = x_float * tail_weight[:, :, None]
    new_state = jnp.exp(total_decay)[:, None, None] * prior_state + jnp.einsum(
        "shp,sn->hpn", x_weighted, b_rows.astype(jnp.float32), precision=lax.Precision.HIGHEST
    )
    gated = ssm_y.reshape(block_length, MIXER_HEADS * PM) * jax.nn.silu(gate_in.astype(jnp.float32))
    gated = (
        gated
        * lax.rsqrt(jnp.mean(gated * gated, axis=-1, keepdims=True) + norm_eps)
        * norm_gain[None, :]
    )
    return (gated.astype(jnp.bfloat16), new_state)


def swap_units(x):
    return lax.ppermute(x, "unit", [(0, 1), (1, 0)])


def folded_ring(length):
    return [0] + list(range(1, length, 2)) + list(range(2, length, 2))[::-1]


def chunk_widths(width):
    third = width // 3 // 128 * 128
    return [third, third, width - 2 * third] if third else [width]


def on_device(
    queries,
    kv_new,
    kv_pool,
    page_table,
    ctx_pages,
    ssm_x,
    ssm_z,
    ssm_bc,
    dt_raw,
    dt_bias,
    decay_rate,
    skip_gain,
    ssm_state,
    ssm_norm_gain,
    resid,
    out_weight,
    ffn_hidden,
    down_weight,
    page_owner,
):
    tok_rows = queries.shape[0]
    block_length = kv_pool.shape[1]
    kv_width = kv_pool.shape[2]
    request_pages = page_table.shape[1]
    n_req = lax.axis_size("req")
    block_rows, width = down_weight.shape
    u = lax.axis_index("unit")
    req = lax.axis_index("req")
    layers = n_req // PLANE
    layer, place = req // PLANE, req % PLANE
    half = width // 2
    first = u == 0

    mine = lax.dynamic_slice(down_weight, (0, u * half), (block_rows, half))
    other = lax.dynamic_slice(down_weight, (0, (1 - u) * half), (block_rows, half))
    widths = chunk_widths(half)
    edges = [sum(widths[:i]) for i in range(len(widths) + 1)]
    ring = folded_ring(layers)
    ring_pairs = [
        (ring[i] * PLANE + p, ring[(i + 1) % layers] * PLANE + p)
        for i in range(layers)
        for p in range(PLANE)
    ]
    ring_place = jnp.asarray([ring.index(i) for i in range(layers)], jnp.int32)[layer]
    ring_table = jnp.asarray(ring, jnp.int32)
    pieces = []
    for lo, hi in zip(edges[:-1], edges[1:]):
        got = swap_units(other[:, lo:hi])
        kept = mine[:, lo:hi]
        pieces.append(
            [jnp.concatenate([jnp.where(first, kept, got), jnp.where(first, got, kept)], axis=0)]
        )
    for _ in range(layers - 1):
        for piece in pieces:
            piece.append(lax.ppermute(piece[-1], "req", ring_pairs))

    chip_rows = block_rows * 2
    by_place = ffn_hidden.reshape(tok_rows, layers, PLANE, chip_rows).transpose(2, 1, 0, 3)

    def plane_pairs(d):
        return [(r, r - r % PLANE + ((r % PLANE) ^ d)) for r in range(n_req)]

    def to_plane(x, d):
        block = lax.dynamic_index_in_dim(x, place ^ d, 0, keepdims=False)
        return lax.ppermute(block, "req", plane_pairs(d)) if d else block

    hidden = jnp.stack([to_plane(by_place, d) for d in range(PLANE)])
    hidden_other = swap_units(hidden)
    hidden = jnp.stack([hidden, hidden_other], axis=1)
    hidden = jnp.transpose(hidden, (2, 0, 1, 3, 4)).reshape(layers, PLANE * 2 * tok_rows, chip_rows)
    order = ring_table[(ring_place - jnp.arange(layers, dtype=jnp.int32)) % layers]
    hidden = jnp.concatenate(
        [lax.dynamic_index_in_dim(hidden, order[k], 0, keepdims=False) for k in range(layers)], axis=1
    )

    slot_row = page_table[0]
    live_count = ctx_pages[0]
    stored = jnp.stack(
        [
            lax.dynamic_index_in_dim(kv_pool, slot_row[j], 0, keepdims=False)
            for j in range(request_pages)
        ]
    )
    pages_now = lax.dynamic_update_slice(
        stored, kv_new[None], (live_count, jnp.int32(0), jnp.int32(0))
    )
    attn_out = attend(queries, pages_now, live_count)
    live = jnp.arange(request_pages, dtype=jnp.int32) <= live_count
    ssm_out, new_state = ssm_block(
        ssm_x,
        ssm_z,
        ssm_bc,
        dt_raw,
        dt_bias,
        decay_rate,
        skip_gain,
        ssm_state[0],
        ssm_norm_gain,
    )
    mixed_rows = jnp.concatenate([attn_out, ssm_out], axis=1)
    mix_width = mixed_rows.shape[1] // 2
    stay = lax.dynamic_slice(mixed_rows, (0, u * mix_width), (tok_rows, mix_width))
    leave = lax.dynamic_slice(mixed_rows, (0, (1 - u) * mix_width), (tok_rows, mix_width))
    exchanged = jnp.concatenate([stay, swap_units(leave)], axis=0)
    mixed = jnp.dot(exchanged, out_weight, preferred_element_type=jnp.float32).astype(jnp.bfloat16)
    mixer_sum = mixed[:tok_rows].astype(jnp.float32) + swap_units(mixed[tok_rows:]).astype(
        jnp.float32
    )
    after_mixers = resid.astype(jnp.float32) + mixer_sum

    slot_cap = max(2, (request_pages + 1) // 2)
    owners = page_owner.reshape(request_pages)
    earlier = jnp.arange(request_pages)[:, None] > jnp.arange(request_pages)[None, :]
    same = owners[:, None] == owners[None, :]
    page_rank = jnp.sum((earlier & same).astype(jnp.int32), axis=1)
    dest_slot = owners * slot_cap + page_rank

    def slots_of(owner):
        blocks = []
        for k in range(slot_cap):
            hit = dest_slot == owner * slot_cap + k
            page = jnp.sum(jnp.where(hit, jnp.arange(request_pages, dtype=jnp.int32), 0))
            block = lax.dynamic_index_in_dim(pages_now, page, 0, keepdims=False)
            blocks.append(jnp.where(jnp.any(hit & live), block, jnp.zeros_like(block)))
        return jnp.stack(blocks)

    keep = slots_of(u)
    came = swap_units(slots_of(1 - u))
    decode_kv = jnp.concatenate([jnp.where(first, keep, came), jnp.where(first, came, keep)], axis=0)
    heads = MIXER_HEADS // 2
    keep = lax.dynamic_slice(new_state, (u * heads, 0, 0), (heads, PM, NS))
    send = lax.dynamic_slice(new_state, ((1 - u) * heads, 0, 0), (heads, PM, NS))
    came = swap_units(send.astype(jnp.bfloat16)).astype(jnp.float32)
    decode_state = jnp.stack([jnp.where(first, keep, came), jnp.where(first, came, keep)])

    own_cols, other_cols = [], []
    for piece in pieces:
        weight = jnp.concatenate(piece, axis=0)
        part = jnp.dot(hidden, weight, preferred_element_type=jnp.float32).astype(jnp.bfloat16)
        part = part.reshape(PLANE, 2 * tok_rows, -1)
        total = part[0].astype(jnp.float32)
        for d in range(1, PLANE):
            total = total + lax.ppermute(part[d], "req", plane_pairs(d)).astype(jnp.float32)
        own_cols.append(total[:tok_rows])
        other_cols.append(swap_units(total[tok_rows:].astype(jnp.bfloat16)).astype(jnp.float32))
    own_cols = jnp.concatenate(own_cols, axis=1)
    other_cols = jnp.concatenate(other_cols, axis=1)
    ffn_sum = jnp.concatenate(
        [jnp.where(first, own_cols, other_cols), jnp.where(first, other_cols, own_cols)], axis=1
    )
    layer_out = (after_mixers + ffn_sum).astype(jnp.bfloat16)
    return (layer_out, decode_kv, decode_state)


def solution(mesh):
    return jax.shard_map(
        on_device,
        mesh=mesh,
        in_specs=(
            P(("req", "unit"), None),
            P(("req", "unit"), None),
            P(("req", "unit"), None, None),
            P(("req", "unit"), None),
            P(("req", "unit")),
            P(("req", "unit"), None),
            P(("req", "unit"), None),
            P(("req", "unit"), None),
            P(("req", "unit"), None),
            P(),
            P(),
            P(),
            P(("req", "unit"), None, None, None),
            P(),
            P(("req", "unit"), None),
            P("unit", None),
            P(("req", "unit"), None),
            P(("req", "unit"), None),
            P(("req", "unit"), None, None),
        ),
        out_specs=(
            P(("req", "unit"), None),
            P(("req", "unit"), None, None),
            P("req", "unit", None, None),
        ),
        check_vma=False,
    )
```

time: 273 us -> 283 us (1.037)
  waiting for transfers between devices: 146 us -> 73.3 us
  between operations: 16.5 us -> 61 us
  starting transfers between devices: 12.2 us -> 42.8 us
  matrix products: 63.3 us -> 33.2 us
  other arithmetic: 11.7 us -> 38.9 us
  local copies, waits for them, and re-layouts: 22.1 us -> 31.9 us
    all_gather x1 -> x0, waiting for transfers between devices: 143 us -> none  [on_device(): w_piece = lax.all_gather(down_weight, ('req', 'unit'), axis=0, tiled=True)]
    ppermute x0 -> x32, waiting for transfers between devices: none -> 73.3 us  [the longest x9 43.8 us: on_device(): piece.append(lax.ppermute(piece[-1], 'req', ring_pairs))]
    ppermute x0 -> x32, starting transfers between devices: none -> 42.8 us  [the longest x9 19.3 us: on_device(): lax.ppermute(part[d], 'req', plane_pairs(d)).astype(jnp.float32)]
    dot_general x2 -> x4, matrix products: 30.7 us -> 6.12 us  [the longest x3 5.91 us: on_device(): jnp.dot(hidden, weight, preferred_element_type=jnp.float32)]
    unnamed x0 -> x9, other arithmetic: none -> 15.3 us
    all_to_all x3 -> x0, starting transfers between devices: 12 us -> none  [the longest x1 4.59 us: on_device(): lax.all_to_all(mixed_rows, 'unit', split_axis=1, concat_axis=0, tiled=True)]
    slice x0 -> x14, local copies, waits for them, and re-layouts: none -> 5.6 us  [the longest x1 1.82 us: on_device(): slot_row[j]]
    another operation x2 -> x4, other arithmetic: 0.36 us -> 5.63 us  [the longest x2 2.42 us: on_device(): jnp.stack([jnp.where(first, keep, came), jnp.where(first, came, keep)])]
  transfers between devices with their start and end apart: 5 -> 32, of which waited for: 2 -> 15; matrix products, arithmetic and copies ran while one was open for 33% -> 25% of each run, Pallas kernels for 0% -> 0%
where the time goes in v1:
time: 283 us; the launch traced here: 281 us
  waiting for transfers between devices  73.3 us (26%)
  between operations  61 us (22%)
  starting transfers between devices  42.8 us (15%)
  other arithmetic  38.9 us (14%)
  matrix products  33.2 us (12%)
  local copies, waits for them, and re-layouts  31.9 us (11%)
    ppermute x9, waiting for transfers between devices, on_device(): piece.append(lax.ppermute(piece[-1], 'req', ring_pairs))  43.8 us
    ppermute x9, starting transfers between devices, on_device(): lax.ppermute(part[d], 'req', plane_pairs(d)).astype(jnp.float32)  19.3 us
    ppermute x9, starting transfers between devices, on_device(): piece.append(lax.ppermute(piece[-1], 'req', ring_pairs))  17.6 us
    ppermute x3, waiting for transfers between devices, to_plane(): return lax.ppermute(block, 'req', plane_pairs(d)) if d else block  17 us
    unnamed x9, other arithmetic  15.3 us
    unnamed x87, local copies, waits for them, and re-layouts  13.7 us
    ppermute x9, waiting for transfers between devices, on_device(): lax.ppermute(part[d], 'req', plane_pairs(d)).astype(jnp.float32)  12.5 us
    dot_general x1, matrix products, on_device(): jnp.dot(exchanged, out_weight, preferred_element_type=jnp.float32)  9.32 us
  transfers between devices with their start and end apart: 32, of which 15 were waited for; matrix products, arithmetic and copies ran while one was open for 25% of the time, Pallas kernels for 0%

profile of v1, /device:TPU:0, one launch (start us, length us, event | category | flops | bytes accessed | tf_op | source)
XLA Modules:
  0.0 281.0 jit_solution(511103319318269431)
XLA Ops:
  80.3 6.1 %fusion.75 = (f32[2,6,128]{2,1,0:T(8,128)S(1)}, f32[2,6,128,1664]{2,3,1,0:T(8,128)}) fusion(pred[128,1664]{0,1:T(8,128)(4,1)S(1)} %iota_compare_fusion, bf16[1664,2,128,1]{0,2,3,1:T(8,128)(2,1)S(1)} %bitcast.138, bf16[128,2,6,128]{0,3,2,1:T(8,128)(2,1)S(1)} %bitcast.142), kind=kOutput, calls=%fused_computation.221 | convolution fusion | flops 664536704 | bytes 11687936 | tf_op jit(solution)/shard_map/sub | solution.py:44
  86.4 4.9 %fusion.19 = bf16[2,128,6,128]{3,1,2,0:T(8,128)(2,1)S(1)} fusion(bf16[1664,2,128,1]{0,2,3,1:T(8,128)(2,1)S(1)} %bitcast.139, f32[2,6,128,1664]{2,3,1,0:T(8,128)} %get-tuple-element.116, f32[2,6,128]{2,1,0:T(8,128)S(1)} %get-tuple-element.115), kind=kOutput, calls=%fused_computation.45 | convolution fusion | flops 659619840 | bytes 11474944 | tf_op jit(solution)/shard_map/kgts,skd->tkgd/dot_general | solution.py:46
  104.3 2.6 dynamic-slice_bitcast_fusion.7
  106.8 2.5 collective-permute-start.2
  111.1 4.3 %fusion.8 = f32[24,128,256]{2,1,0:T(8,128)} fusion(f32[1,24,128,256]{3,2,1,0:T(8,128)S(1)} %copy-done.2, bf16[128,24,128]{0,2,1:T(8,128)(2,1)} %bitcast.134, f32[24]{0:T(128)} %exp.32, f32[128,24]{0,1:T(8,128)S(1)} %get-tuple-element.95, bf16[128,512]{1,0:T(8,128)(2,1)} %param.28), kind=kOutput, calls=%fused_computation.17 | convolution fusion | flops 1210318848 | bytes 7156224 | tf_op jit(solution)/shard_map/shp,sn->hpn/dot_general | solution.py:81
  132.5 17.0 %collective-permute-done.3 = bf16[4,128,384]{1,2,0:T(8,128)(2,1)S(1)} collective-permute-done((bf16[4,128,384]{1,2,0:T(8,128)(2,1)}, bf16[4,128,384]{1,2,0:T(8,128)(2,1)S(1)}, u32[]{:S(2)}, u32[]{:S(2)}) %collective-permute-start.3) | collective-permute-done | bytes 393248 | tf_op jit(solution)/shard_map/ppermute | solution.py:171
  152.5 2.6 collective-permute-start.14
  155.2 9.3 %convolution_convert_fusion = bf16[256,3072]{1,0:T(8,128)(2,1)S(1)} fusion(bf16[2304,3072]{1,0:T(8,128)(2,1)} %param.36, bf16[128,2304]{1,0:T(8,128)(2,1)} %collective-permute-done, bf16[128,2304]{1,0:T(8,128)(2,1)S(1)} %copy-done.15), kind=kOutput, calls=%fused_computation.10 | convolution fusion | flops 3627024384 | bytes 16908288 | tf_op jit(solution)/shard_map/dot_general | solution.py:211
  166.9 2.5 collective-permute-done.14
  173.7 4.7 %collective-permute-done.21 = bf16[384,512]{1,0:T(8,128)(2,1)S(1)} collective-permute-done((bf16[384,512]{1,0:T(8,128)(2,1)S(1)}, bf16[384,512]{1,0:T(8,128)(2,1)S(1)}, u32[]{:S(2)}, u32[]{:S(2)}) %collective-permute-start.21) | collective-permute-done | bytes 393248 | tf_op jit(solution)/shard_map/ppermute | solution.py:161
  180.1 3.4 %collective-permute-start.22 = (bf16[384,512]{1,0:T(8,128)(2,1)S(1)}, bf16[384,512]{1,0:T(8,128)(2,1)S(1)}, u32[]{:S(2)}, u32[]{:S(2)}) collective-permute-start(bf16[384,512]{1,0:T(8,128)(2,1)S(1)} %collective-permute-done.21), channel_id=1, source_target_pairs={{0,8},{2,10},{4,12},{6,14},{8,24},{10,26},{12,28},{14,30},{24,16},... | collective-permute-start | bytes 1179656 | tf_op jit(solution)/shard_map/ppermute | solution.py:161
  183.6 3.2 %collective-permute-done.8 = bf16[384,512]{1,0:T(8,128)(2,1)S(1)} collective-permute-done((bf16[384,512]{1,0:T(8,128)(2,1)S(1)}, bf16[384,512]{1,0:T(8,128)(2,1)S(1)}, u32[]{:S(2)}, u32[]{:S(2)}) %collective-permute-start.8) | collective-permute-done | bytes 393248 | tf_op jit(solution)/shard_map/ppermute | solution.py:161
  188.5 2.8 %broadcast_select_fusion.1 = (bf16[7,128,512]{2,1,0:T(8,128)(2,1)}, bf16[7,128,512]{2,1,0:T(8,128)(2,1)}) fusion(bf16[7,128,512]{2,1,0:T(8,128)(2,1)} %get-tuple-element.52, bf16[7,128,512]{2,1,0:T(8,128)(2,1)} %collective-permute-done.30, pred[]{:T(512)S(6)} %eq.104), kind=kLoop, calls=%fused_computation.55 | loop fusion | flops 917504 | bytes 3670017 | tf_op jit(solution)/shard_map/jit(_where)/select_n | solution.py:235
  191.3 3.9 %collective-permute-done.15 = bf16[384,512]{1,0:T(8,128)(2,1)S(1)} collective-permute-done((bf16[384,512]{1,0:T(8,128)(2,1)S(1)}, bf16[384,512]{1,0:T(8,128)(2,1)S(1)}, u32[]{:S(2)}, u32[]{:S(2)}) %collective-permute-start.15) | collective-permute-done | bytes 393248 | tf_op jit(solution)/shard_map/ppermute | solution.py:161
  197.0 6.7 %collective-permute-done.22 = bf16[384,512]{1,0:T(8,128)(2,1)S(1)} collective-permute-done((bf16[384,512]{1,0:T(8,128)(2,1)S(1)}, bf16[384,512]{1,0:T(8,128)(2,1)S(1)}, u32[]{:S(2)}, u32[]{:S(2)}) %collective-permute-start.22) | collective-permute-done | bytes 393248 | tf_op jit(solution)/shard_map/ppermute | solution.py:161
  205.4 6.6 %collective-permute-done.9 = bf16[384,512]{1,0:T(8,128)(2,1)S(1)} collective-permute-done((bf16[384,512]{1,0:T(8,128)(2,1)S(1)}, bf16[384,512]{1,0:T(8,128)(2,1)S(1)}, u32[]{:S(2)}, u32[]{:S(2)}) %collective-permute-start.9) | collective-permute-done | bytes 393248 | tf_op jit(solution)/shard_map/ppermute | solution.py:161
  212.1 8.4 %collective-permute-done.16 = bf16[384,512]{1,0:T(8,128)(2,1)S(1)} collective-permute-done((bf16[384,512]{1,0:T(8,128)(2,1)S(1)}, bf16[384,512]{1,0:T(8,128)(2,1)S(1)}, u32[]{:S(2)}, u32[]{:S(2)}) %collective-permute-start.16) | collective-permute-done | bytes 393248 | tf_op jit(solution)/shard_map/ppermute | solution.py:161
  220.5 7.8 %collective-permute-done.23 = bf16[384,512]{1,0:T(8,128)(2,1)S(1)} collective-permute-done((bf16[384,512]{1,0:T(8,128)(2,1)S(1)}, bf16[384,512]{1,0:T(8,128)(2,1)S(1)}, u32[]{:S(2)}, u32[]{:S(2)}) %collective-permute-start.23) | collective-permute-done | bytes 393248 | tf_op jit(solution)/shard_map/ppermute | solution.py:161
  231.4 3.4 %copy.80 = bf16[4,4,2,128,384]{4,3,2,1,0:T(8,128)(2,1)S(1)} copy(bf16[4,4,2,128,384]{3,4,0,1,2:T(8,128)(2,1)} %maximum_bitcast_fusion) | data formatting | bytes 6291456 | tf_op jit(solution)/shard_map/transpose | solution.py:176
  249.7 5.8 %collective-permute-start.19 = (bf16[256,512]{1,0:T(8,128)(2,1)S(1)}, bf16[256,512]{1,0:T(8,128)(2,1)S(1)}, u32[]{:S(2)}, u32[]{:S(2)}) collective-permute-start(bf16[256,512]{1,0:T(8,128)(2,1)S(1)} %get-tuple-element.90), channel_id=1, source_target_pairs={{0,6},{2,4},{4,2},{6,0},{8,14},{10,12},{12,10},{14,8},{16,22},{18,... | collective-permute-start | bytes 786440 | tf_op jit(solution)/shard_map/ppermute | solution.py:249
  255.6 3.3 %collective-permute-done.17 = bf16[256,512]{1,0:T(8,128)(2,1)S(1)} collective-permute-done((bf16[256,512]{1,0:T(8,128)(2,1)S(1)}, bf16[256,512]{1,0:T(8,128)(2,1)S(1)}, u32[]{:S(2)}, u32[]{:S(2)}) %collective-permute-start.17) | collective-permute-done | bytes 262176 | tf_op jit(solution)/shard_map/ppermute | solution.py:249
  260.4 6.3 %collective-permute-start.26 = (bf16[256,512]{1,0:T(8,128)(2,1)S(1)}, bf16[256,512]{1,0:T(8,128)(2,1)S(1)}, u32[]{:S(2)}, u32[]{:S(2)}) collective-permute-start(bf16[256,512]{1,0:T(8,128)(2,1)S(1)} %get-tuple-element.93), channel_id=1, source_target_pairs={{0,6},{2,4},{4,2},{6,0},{8,14},{10,12},{12,10},{14,8},{16,22},{18,... | collective-permute-start | bytes 786440 | tf_op jit(solution)/shard_map/ppermute | solution.py:249
  266.9 3.3 %collective-permute-done.24 = bf16[256,512]{1,0:T(8,128)(2,1)S(1)} collective-permute-done((bf16[256,512]{1,0:T(8,128)(2,1)S(1)}, bf16[256,512]{1,0:T(8,128)(2,1)S(1)}, u32[]{:S(2)}, u32[]{:S(2)}) %collective-permute-start.24) | collective-permute-done | bytes 262176 | tf_op jit(solution)/shard_map/ppermute | solution.py:249
  270.9 4.3 %collective-permute-done.26 = bf16[256,512]{1,0:T(8,128)(2,1)S(1)} collective-permute-done((bf16[256,512]{1,0:T(8,128)(2,1)S(1)}, bf16[256,512]{1,0:T(8,128)(2,1)S(1)}, u32[]{:S(2)}, u32[]{:S(2)}) %collective-permute-start.26) | collective-permute-done | bytes 262176 | tf_op jit(solution)/shard_map/ppermute | solution.py:249
  (206 shorter events, 94.4 us)
Async XLA Ops:
  77.2 103.0 %collective-permute-start.30 = (bf16[7,128,512]{2,1,0:T(8,128)(2,1)}, bf16[7,128,512]{2,1,0:T(8,128)(2,1)}, u32[]{:S(2)}, u32[]{:S(2)}) collective-permute-start(bf16[7,128,512]{2,1,0:T(8,128)(2,1)} %get-tuple-element.53), channel_id=1, source_target_pairs={{0,1},{1,0},{2,3},{3,2},{4,5},{5,4},{6,7},{7,6},{8,9},{9,8},{10,11... | collective-permute-start | bytes 2752520 | tf_op jit(solution)/shard_map/ppermute | solution.py:94
  100.6 51.9 %collective-permute-start = (bf16[128,2304]{1,0:T(8,128)(2,1)}, bf16[128,2304]{1,0:T(8,128)(2,1)}, u32[]{:S(2)}, u32[]{:S(2)}) collective-permute-start(bf16[128,2304]{1,0:T(8,128)(2,1)} %get-tuple-element.75), channel_id=1, source_target_pairs={{0,1},{1,0},{2,3},{3,2},{4,5},{5,4},{6,7},{7,6},{8,9},{9,8},{10,11... | collective-permute-start | bytes 1769480 | tf_op jit(solution)/shard_map/ppermute | solution.py:94
  102.3 14.5 %collective-permute-start.6 = (bf16[192,512]{1,0:T(8,128)(2,1)}, bf16[192,512]{1,0:T(8,128)(2,1)}, u32[]{:S(2)}, u32[]{:S(2)}) collective-permute-start(bf16[192,512]{1,0:T(8,128)(2,1)} %constant_dynamic-slice_fusion), channel_id=1, source_target_pairs={{0,1},{1,0},{2,3},{3,2},{4,5},{5,4},{6,7},{7,6},{8,9},{9,8},{10,11... | collective-permute-start | bytes 589832 | tf_op jit(solution)/shard_map/ppermute | solution.py:94
  106.8 25.6 %collective-permute-start.2 = (bf16[4,128,384]{1,2,0:T(8,128)(2,1)}, bf16[4,128,384]{1,2,0:T(8,128)(2,1)}, u32[]{:S(2)}, u32[]{:S(2)}) collective-permute-start(bf16[4,128,384]{1,2,0:T(8,128)(2,1)} %get-tuple-element.73), channel_id=1, source_target_pairs={{0,2},{2,0},{4,6},{6,4},{8,10},{10,8},{12,14},{14,12},{16,18},{18,... | collective-permute-start | bytes 1179656 | tf_op jit(solution)/shard_map/ppermute | solution.py:171
  129.5 20.0 %collective-permute-start.3 = (bf16[4,128,384]{1,2,0:T(8,128)(2,1)}, bf16[4,128,384]{1,2,0:T(8,128)(2,1)S(1)}, u32[]{:S(2)}, u32[]{:S(2)}) collective-permute-start(bf16[4,128,384]{1,2,0:T(8,128)(2,1)} %get-tuple-element.71), channel_id=1, source_target_pairs={{0,4},{2,6},{4,0},{6,2},{8,12},{10,14},{12,8},{14,10},{16,20},{18,... | collective-permute-start | bytes 1179656 | tf_op jit(solution)/shard_map/ppermute | solution.py:171
  131.1 20.0 %collective-permute-start.4 = (bf16[4,128,384]{1,2,0:T(8,128)(2,1)}, bf16[4,128,384]{1,2,0:T(8,128)(2,1)S(1)}, u32[]{:S(2)}, u32[]{:S(2)}) collective-permute-start(bf16[4,128,384]{1,2,0:T(8,128)(2,1)} %get-tuple-element.72), channel_id=1, source_target_pairs={{0,6},{2,4},{4,2},{6,0},{8,14},{10,12},{12,10},{14,8},{16,22},{18,... | collective-permute-start | bytes 1179656 | tf_op jit(solution)/shard_map/ppermute | solution.py:171
  132.5 33.0 %collective-permute-start.31 = (bf16[12,128,256]{2,1,0:T(8,128)(2,1)S(1)}, bf16[12,128,256]{2,1,0:T(8,128)(2,1)S(1)}, u32[]{:S(2)}, u32[]{:S(2)}) collective-permute-start(bf16[12,128,256]{2,1,0:T(8,128)(2,1)S(1)} %dynamic-slice_convert_fusion), channel_id=1, source_target_pairs={{0,1},{1,0},{2,3},{3,2},{4,5},{5,4},{6,7},{7,6},{8,9},{9,8},{10,11... | collective-permute-start | bytes 2359304 | tf_op jit(solution)/shard_map/ppermute | solution.py:94
  149.5 17.3 %collective-permute-start.7 = (bf16[384,512]{1,0:T(8,128)(2,1)S(1)}, bf16[384,512]{1,0:T(8,128)(2,1)S(1)}, u32[]{:S(2)}, u32[]{:S(2)}) collective-permute-start(bf16[384,512]{1,0:T(8,128)(2,1)S(1)} %pad_maximum_fusion.5), channel_id=1, source_target_pairs={{0,8},{2,10},{4,12},{6,14},{8,24},{10,26},{12,28},{14,30},{24,16},... | collective-permute-start | bytes 1179656 | tf_op jit(solution)/shard_map/ppermute | solution.py:161
  152.4 76.0 %collective-permute-start.5 = (bf16[4,4,128,384]{2,3,1,0:T(8,128)(2,1)S(1)}, bf16[4,4,128,384]{2,3,1,0:T(8,128)(2,1)S(1)}, u32[]{:S(2)}, u32[]{:S(2)}) collective-permute-start(bf16[4,4,128,384]{2,3,1,0:T(8,128)(2,1)S(1)} %get-tuple-element.69), channel_id=1, source_target_pairs={{0,1},{1,0},{2,3},{3,2},{4,5},{5,4},{6,7},{7,6},{8,9},{9,8},{10,11... | collective-permute-start | bytes 4718600 | tf_op jit(solution)/shard_map/ppermute | solution.py:94
  152.5 16.9 %collective-permute-start.14 = (bf16[384,512]{1,0:T(8,128)(2,1)S(1)}, bf16[384,512]{1,0:T(8,128)(2,1)S(1)}, u32[]{:S(2)}, u32[]{:S(2)}) collective-permute-start(bf16[384,512]{1,0:T(8,128)(2,1)S(1)} %pad_maximum_fusion.6), channel_id=1, source_target_pairs={{0,8},{2,10},{4,12},{6,14},{8,24},{10,26},{12,28},{14,30},{24,16},... | collective-permute-start | bytes 1179656 | tf_op jit(solution)/shard_map/ppermute | solution.py:161
  165.5 12.8 %collective-permute-start.21 = (bf16[384,512]{1,0:T(8,128)(2,1)S(1)}, bf16[384,512]{1,0:T(8,128)(2,1)S(1)}, u32[]{:S(2)}, u32[]{:S(2)}) collective-permute-start(bf16[384,512]{1,0:T(8,128)(2,1)S(1)} %pad_maximum_fusion.7), channel_id=1, source_target_pairs={{0,8},{2,10},{4,12},{6,14},{8,24},{10,26},{12,28},{14,30},{24,16},... | collective-permute-start | bytes 1179656 | tf_op jit(solution)/shard_map/ppermute | solution.py:161
  166.8 110.4 %collective-permute-start.1 = (bf16[128,3072]{1,0:T(8,128)(2,1)}, bf16[128,3072]{1,0:T(8,128)(2,1)}, u32[]{:S(2)}, u32[]{:S(2)}) collective-permute-start(bf16[128,3072]{1,0:T(8,128)(2,1)} %slice.225), channel_id=1, source_target_pairs={{0,1},{1,0},{2,3},{3,2},{4,5},{5,4},{6,7},{7,6},{8,9},{9,8},{10,11... | collective-permute-start | bytes 2359304 | tf_op jit(solution)/shard_map/ppermute | solution.py:94
  169.5 17.3 %collective-permute-start.8 = (bf16[384,512]{1,0:T(8,128)(2,1)S(1)}, bf16[384,512]{1,0:T(8,128)(2,1)S(1)}, u32[]{:S(2)}, u32[]{:S(2)}) collective-permute-start(bf16[384,512]{1,0:T(8,128)(2,1)S(1)} %collective-permute-done.7), channel_id=1, source_target_pairs={{0,8},{2,10},{4,12},{6,14},{8,24},{10,26},{12,28},{14,30},{24,16},... | collective-permute-start | bytes 1179656 | tf_op jit(solution)/shard_map/ppermute | solution.py:161
  178.4 16.9 %collective-permute-start.15 = (bf16[384,512]{1,0:T(8,128)(2,1)S(1)}, bf16[384,512]{1,0:T(8,128)(2,1)S(1)}, u32[]{:S(2)}, u32[]{:S(2)}) collective-permute-start(bf16[384,512]{1,0:T(8,128)(2,1)S(1)} %collective-permute-done.14), channel_id=1, source_target_pairs={{0,8},{2,10},{4,12},{6,14},{8,24},{10,26},{12,28},{14,30},{24,16},... | collective-permute-start | bytes 1179656 | tf_op jit(solution)/shard_map/ppermute | solution.py:161
  180.1 23.5 %collective-permute-start.22 = (bf16[384,512]{1,0:T(8,128)(2,1)S(1)}, bf16[384,512]{1,0:T(8,128)(2,1)S(1)}, u32[]{:S(2)}, u32[]{:S(2)}) collective-permute-start(bf16[384,512]{1,0:T(8,128)(2,1)S(1)} %collective-permute-done.21), channel_id=1, source_target_pairs={{0,8},{2,10},{4,12},{6,14},{8,24},{10,26},{12,28},{14,30},{24,16},... | collective-permute-start | bytes 1179656 | tf_op jit(solution)/shard_map/ppermute | solution.py:161
  186.8 25.3 %collective-permute-start.9 = (bf16[384,512]{1,0:T(8,128)(2,1)S(1)}, bf16[384,512]{1,0:T(8,128)(2,1)S(1)}, u32[]{:S(2)}, u32[]{:S(2)}) collective-permute-start(bf16[384,512]{1,0:T(8,128)(2,1)S(1)} %collective-permute-done.8), channel_id=1, source_target_pairs={{0,8},{2,10},{4,12},{6,14},{8,24},{10,26},{12,28},{14,30},{24,16},... | collective-permute-start | bytes 1179656 | tf_op jit(solution)/shard_map/ppermute | solution.py:161
  195.2 25.3 %collective-permute-start.16 = (bf16[384,512]{1,0:T(8,128)(2,1)S(1)}, bf16[384,512]{1,0:T(8,128)(2,1)S(1)}, u32[]{:S(2)}, u32[]{:S(2)}) collective-permute-start(bf16[384,512]{1,0:T(8,128)(2,1)S(1)} %collective-permute-done.15), channel_id=1, source_target_pairs={{0,8},{2,10},{4,12},{6,14},{8,24},{10,26},{12,28},{14,30},{24,16},... | collective-permute-start | bytes 1179656 | tf_op jit(solution)/shard_map/ppermute | solution.py:161
  203.6 24.7 %collective-permute-start.23 = (bf16[384,512]{1,0:T(8,128)(2,1)S(1)}, bf16[384,512]{1,0:T(8,128)(2,1)S(1)}, u32[]{:S(2)}, u32[]{:S(2)}) collective-permute-start(bf16[384,512]{1,0:T(8,128)(2,1)S(1)} %collective-permute-done.22), channel_id=1, source_target_pairs={{0,8},{2,10},{4,12},{6,14},{8,24},{10,26},{12,28},{14,30},{24,16},... | collective-permute-start | bytes 1179656 | tf_op jit(solution)/shard_map/ppermute | solution.py:161
  240.4 15.0 %collective-permute-start.12 = (bf16[256,512]{1,0:T(8,128)(2,1)S(1)}, bf16[256,512]{1,0:T(8,128)(2,1)S(1)}, u32[]{:S(2)}, u32[]{:S(2)}) collective-permute-start(bf16[256,512]{1,0:T(8,128)(2,1)S(1)} %get-tuple-element.87), channel_id=1, source_target_pairs={{0,6},{2,4},{4,2},{6,0},{8,14},{10,12},{12,10},{14,8},{16,22},{18,... | collective-permute-start | bytes 786440 | tf_op jit(solution)/shard_map/ppermute | solution.py:249
  243.9 15.0 %collective-permute-start.17 = (bf16[256,512]{1,0:T(8,128)(2,1)S(1)}, bf16[256,512]{1,0:T(8,128)(2,1)S(1)}, u32[]{:S(2)}, u32[]{:S(2)}) collective-permute-start(bf16[256,512]{1,0:T(8,128)(2,1)S(1)} %get-tuple-element.89), channel_id=1, source_target_pairs={{0,2},{2,0},{4,6},{6,4},{8,10},{10,8},{12,14},{14,12},{16,18},{18,... | collective-permute-start | bytes 786440 | tf_op jit(solution)/shard_map/ppermute | solution.py:249
  247.6 12.8 %collective-permute-start.18 = (bf16[256,512]{1,0:T(8,128)(2,1)S(1)}, bf16[256,512]{1,0:T(8,128)(2,1)S(1)}, u32[]{:S(2)}, u32[]{:S(2)}) collective-permute-start(bf16[256,512]{1,0:T(8,128)(2,1)S(1)} %get-tuple-element.91), channel_id=1, source_target_pairs={{0,4},{2,6},{4,0},{6,2},{8,12},{10,14},{12,8},{14,10},{16,20},{18,... | collective-permute-start | bytes 786440 | tf_op jit(solution)/shard_map/ppermute | solution.py:249
  249.7 17.0 %collective-permute-start.19 = (bf16[256,512]{1,0:T(8,128)(2,1)S(1)}, bf16[256,512]{1,0:T(8,128)(2,1)S(1)}, u32[]{:S(2)}, u32[]{:S(2)}) collective-permute-start(bf16[256,512]{1,0:T(8,128)(2,1)S(1)} %get-tuple-element.90), channel_id=1, source_target_pairs={{0,6},{2,4},{4,2},{6,0},{8,14},{10,12},{12,10},{14,8},{16,22},{18,... | collective-permute-start | bytes 786440 | tf_op jit(solution)/shard_map/ppermute | solution.py:249
  255.5 14.7 %collective-permute-start.24 = (bf16[256,512]{1,0:T(8,128)(2,1)S(1)}, bf16[256,512]{1,0:T(8,128)(2,1)S(1)}, u32[]{:S(2)}, u32[]{:S(2)}) collective-permute-start(bf16[256,512]{1,0:T(8,128)(2,1)S(1)} %get-tuple-element.92), channel_id=1, source_target_pairs={{0,2},{2,0},{4,6},{6,4},{8,10},{10,8},{12,14},{14,12},{16,18},{18,... | collective-permute-start | bytes 786440 | tf_op jit(solution)/shard_map/ppermute | solution.py:249
  260.4 14.8 %collective-permute-start.26 = (bf16[256,512]{1,0:T(8,128)(2,1)S(1)}, bf16[256,512]{1,0:T(8,128)(2,1)S(1)}, u32[]{:S(2)}, u32[]{:S(2)}) collective-permute-start(bf16[256,512]{1,0:T(8,128)(2,1)S(1)} %get-tuple-element.93), channel_id=1, source_target_pairs={{0,6},{2,4},{4,2},{6,0},{8,14},{10,12},{12,10},{14,8},{16,22},{18,... | collective-permute-start | bytes 786440 | tf_op jit(solution)/shard_map/ppermute | solution.py:249
  (41 other events, 294.4 us)

commit v2 on v1

v2 whole, which is shorter than its diff:
```python
import functools
import math

import jax
import jax.numpy as jnp
from jax import lax
from jax.experimental import pallas as pl
from jax.experimental.pallas import tpu as pltpu
from jax.sharding import PartitionSpec as P

QUERY_HEADS = 12
KEY_VALUE_HEADS = 2
HEAD_WIDTH = 128
MIXER_HEADS = 24
PM = 128
NS = 256

PLANE = 4

norm_eps = 1e-05

F32, BF16 = jnp.float32, jnp.bfloat16
VMEM = pl.BlockSpec(memory_space=pltpu.VMEM)
SMEM = pl.BlockSpec(memory_space=pltpu.SMEM)
ANY = pl.BlockSpec(memory_space=pl.ANY)
PARAMS = pltpu.CompilerParams(vmem_limit_bytes=48 * 1024 * 1024)


def cost(flops, moved, exps=0):
    return pl.CostEstimate(flops=flops, bytes_accessed=moved, transcendentals=exps)


def contract_last(a, b):
    return lax.dot_general(a, b, (((1,), (1,)), ((), ())), preferred_element_type=F32)


def two_terms(x):
    high = x.astype(BF16)
    return high, (x - high.astype(F32)).astype(BF16)


def attend_kernel(
    table, ctx, owner, unit, q_ref, new_ref, pool, out_ref, held, leave, pages, zero, sems, osems
):
    count, length, _ = pages.shape
    slots = leave.shape[0]
    live = ctx[0]
    u = unit[0]
    for j in range(count):

        @pl.when(j == live)
        def _():
            pltpu.make_async_copy(new_ref, pages.at[j], sems.at[j]).start()

        @pl.when(j != live)
        def _():
            pltpu.make_async_copy(pool.at[table[0, j]], pages.at[j], sems.at[j]).start()

    zero[...] = jnp.zeros_like(zero)
    for j in range(count):
        pltpu.make_async_copy(new_ref, pages.at[j], sems.at[j]).wait()

    named = [jnp.int32(0), jnp.int32(0)]
    for j in range(count):
        own = owner[0, j] == u
        rank = jnp.where(own, named[0], named[1])
        named = [named[0] + own.astype(jnp.int32), named[1] + 1 - own.astype(jnp.int32)]
        for source, when in ((pages.at[j], j <= live), (zero, j > live)):

            @pl.when(when & own)
            def _():
                pltpu.make_async_copy(source, held.at[u * slots + rank], osems.at[j]).start()

            @pl.when(when & jnp.logical_not(own))
            def _():
                pltpu.make_async_copy(source, leave.at[rank], osems.at[j]).start()

    for k in range(slots):

        @pl.when(k >= named[0])
        def _():
            pltpu.make_async_copy(zero, held.at[u * slots + k], osems.at[count + k]).start()

        @pl.when(k >= named[1])
        def _():
            pltpu.make_async_copy(zero, leave.at[k], osems.at[count + slots + k]).start()

    group = QUERY_HEADS // KEY_VALUE_HEADS
    heads = 3
    rows, keys = heads * length, count * length
    limit = live * length + lax.broadcasted_iota(jnp.int32, (rows, 1), 0) % length
    visible = lax.broadcasted_iota(jnp.int32, (rows, keys), 1) <= limit
    scale = 1.0 / math.sqrt(HEAD_WIDTH)
    for k in range(KEY_VALUE_HEADS):
        key_rows = pages[:, :, k * HEAD_WIDTH : (k + 1) * HEAD_WIDTH].reshape(keys, HEAD_WIDTH)
        lo = (KEY_VALUE_HEADS + k) * HEAD_WIDTH
        value_rows = pages[:, :, lo : lo + HEAD_WIDTH].reshape(keys, HEAD_WIDTH)
        for first in range(k * group, (k + 1) * group, heads):
            spans = [
                slice(h * HEAD_WIDTH, (h + 1) * HEAD_WIDTH) for h in range(first, first + heads)
            ]
            q = jnp.concatenate([q_ref[:, span] for span in spans], axis=0)
            scores = jnp.where(visible, contract_last(q, key_rows), -1e30)
            top = jnp.max(scores, axis=1, keepdims=True)
            exponent = jnp.exp((scores - top) * scale)
            weights = (exponent * (1.0 / jnp.sum(exponent, axis=1, keepdims=True))).astype(BF16)
            attended = jnp.dot(weights, value_rows, preferred_element_type=F32).astype(BF16)
            for i, span in enumerate(spans):
                out_ref[:, span] = attended[i * length : (i + 1) * length]

    for j in range(count):
        pltpu.make_async_copy(zero, leave.at[0], osems.at[j]).wait()
    for k in range(slots):

        @pl.when(k >= named[0])
        def _():
            pltpu.make_async_copy(zero, leave.at[0], osems.at[count + k]).wait()

        @pl.when(k >= named[1])
        def _():
            pltpu.make_async_copy(zero, leave.at[0], osems.at[count + slots + k]).wait()


def attend(table, ctx, owner, unit, queries, kv_new, pool):
    count, length, width = pool.shape
    slots = max(2, (count + 1) // 2)
    pairs = QUERY_HEADS * length * count * length
    return pl.pallas_call(
        attend_kernel,
        out_shape=(
            jax.ShapeDtypeStruct(queries.shape, BF16),
            jax.ShapeDtypeStruct((2 * slots, length, width), BF16),
            jax.ShapeDtypeStruct((slots, length, width), BF16),
        ),
        in_specs=[SMEM, SMEM, SMEM, SMEM, VMEM, VMEM, ANY],
        out_specs=(VMEM, ANY, ANY),
        scratch_shapes=[
            pltpu.VMEM((count, length, width), BF16),
            pltpu.VMEM((length, width), BF16),
            pltpu.SemaphoreType.DMA((count,)),
            pltpu.SemaphoreType.DMA((count + 2 * slots,)),
        ],
        compiler_params=PARAMS,
        cost_estimate=cost(4 * pairs * HEAD_WIDTH * 4, 6 << 20, pairs),
        name="attend",
    )(table, ctx, owner, unit, queries, kv_new, pool)


def state_kernel(
    unit,
    skip,
    attn_ref,
    x_ref,
    z_ref,
    bc_ref,
    dt_ref,
    bias_ref,
    rate_ref,
    gain_ref,
    state_ref,
    stay_ref,
    leave_ref,
    held,
    send_ref,
    gated,
    fresh,
    sems,
):
    length = x_ref.shape[0]
    heads, share = MIXER_HEADS, MIXER_HEADS // 2
    u = unit[0]
    rows = lax.broadcasted_iota(jnp.int32, (length, length), 0)
    cols = lax.broadcasted_iota(jnp.int32, (length, length), 1)
    causal = rows >= cols
    raw = dt_ref[...] + bias_ref[...]
    step = jnp.maximum(raw, 0.0) + jnp.log1p(jnp.exp(-jnp.abs(raw)))
    cum = jnp.dot(
        causal.astype(F32),
        -step * rate_ref[...],
        precision=lax.Precision.HIGHEST,
        preferred_element_type=F32,
    )
    blank = jnp.zeros((length, length - heads), F32)
    cum_rows = jnp.transpose(jnp.concatenate([cum, blank], axis=1))
    step_rows = jnp.transpose(jnp.concatenate([step, blank], axis=1))
    last = cum[length - 1 : length, :]
    b_rows, c_rows = bc_ref[:, :NS], bc_ref[:, NS:]
    dots = contract_last(c_rows, b_rows)
    square = jnp.zeros((length, PM), F32)
    for h in range(heads):
        span = slice(h * PM, (h + 1) * PM)
        cum_t, cum_s = cum[:, h : h + 1], cum_rows[h : h + 1, :]
        step_s, end = step_rows[h : h + 1, :], last[:, h : h + 1]
        decay = jnp.exp(jnp.where(causal, cum_t - cum_s, -1e30))
        mixing = (dots * decay * step_s).astype(BF16)
        x = x_ref[:, span]
        x_float = x.astype(F32)
        prior = state_ref[0, h]
        high, low = two_terms(prior)
        carried = contract_last(c_rows, high) + contract_last(c_rows, low)
        y = jnp.dot(mixing, x, preferred_element_type=F32)
        y = y + carried * jnp.exp(cum_t) + skip[h] * x_float
        z = z_ref[:, span].astype(F32)
        g = y * (z / (1.0 + jnp.exp(-z)))
        gated[:, span] = g
        square = square + g * g
        weighted = jnp.transpose(x_float) * (jnp.exp(end - cum_s) * step_s)
        high, low = two_terms(weighted)
        new = jnp.exp(end) * prior + (
            jnp.dot(high, b_rows, preferred_element_type=F32)
            + jnp.dot(low, b_rows, preferred_element_type=F32)
        )
        place = h % share

        @pl.when(u == h // share)
        def _():
            fresh[place] = new
            pltpu.make_async_copy(fresh.at[place], held.at[u, place], sems.at[place]).start()

        @pl.when(u != h // share)
        def _():
            send_ref[place] = new.astype(BF16)

    mean = jnp.sum(square, axis=1, keepdims=True) * (1.0 / (heads * PM))
    out = (gated[...] * lax.rsqrt(mean + norm_eps) * gain_ref[...]).astype(BF16)
    attn_width = attn_ref.shape[1]
    cut = stay_ref.shape[1] - attn_width
    for which, low_ref, high_ref in ((0, stay_ref, leave_ref), (1, leave_ref, stay_ref)):

        @pl.when(u == which)
        def _():
            low_ref[:, :attn_width] = attn_ref[...]
            low_ref[:, attn_width:] = out[:, :cut]
            high_ref[...] = out[:, cut:]

    for place in range(share):
        pltpu.make_async_copy(fresh.at[place], held.at[0, place], sems.at[place]).wait()


def state_space(unit, skip, attn, x, z, bc, dt, bias, rate, gain, state):
    length, width = x.shape
    share = MIXER_HEADS // 2
    half = (attn.shape[1] + width) // 2
    return pl.pallas_call(
        state_kernel,
        out_shape=(
            jax.ShapeDtypeStruct((length, half), BF16),
            jax.ShapeDtypeStruct((length, half), BF16),
            jax.ShapeDtypeStruct((2, share, PM, NS), F32),
            jax.ShapeDtypeStruct((share, PM, NS), BF16),
        ),
        in_specs=[SMEM, SMEM] + [VMEM] * 9,
        out_specs=(VMEM, VMEM, ANY, VMEM),
        scratch_shapes=[
            pltpu.VMEM((length, width), F32),
            pltpu.VMEM((share, PM, NS), F32),
            pltpu.SemaphoreType.DMA((share,)),
        ],
        compiler_params=PARAMS,
        cost_estimate=cost(4 << 30, 10 << 20, MIXER_HEADS * length * length * 2),
        name="state_space",
    )(unit, skip, attn, x, z, bc, dt, bias, rate, gain, state)


def settle_kernel(unit, pages, state, pages_in, state_in, pages_out, state_out, wide, sem):
    slots = pages.shape[0]
    u = unit[0]
    copy = pltpu.make_async_copy(pages, pages_out.at[pl.ds((1 - u) * slots, slots)], sem.at[0])
    copy.start()
    wide[...] = state[...].astype(F32)
    other = pltpu.make_async_copy(wide, state_out.at[1 - u], sem.at[1])
    other.start()
    copy.wait()
    other.wait()


def settle(unit, pages, state, pages_held, state_held):
    return pl.pallas_call(
        settle_kernel,
        out_shape=(
            jax.ShapeDtypeStruct(pages_held.shape, pages_held.dtype),
            jax.ShapeDtypeStruct(state_held.shape, state_held.dtype),
        ),
        in_specs=[SMEM, ANY, VMEM, ANY, ANY],
        out_specs=(ANY, ANY),
        scratch_shapes=[pltpu.VMEM(state.shape, F32), pltpu.SemaphoreType.DMA((2,))],
        input_output_aliases={3: 0, 4: 1},
        compiler_params=PARAMS,
        cost_estimate=cost(0, 5 << 20),
        name="settle",
    )(unit, pages, state, pages_held, state_held)


def spread_kernel(where, *refs):
    *sources, mine_ref, other_ref = refs
    half = sources[0].shape[1] // 2
    first = [s[:, :half] for s in sources]
    second = [s[:, half:] for s in sources]
    for which, low_ref, high_ref in ((0, mine_ref, other_ref), (1, other_ref, mine_ref)):

        @pl.when(where[1] == which)
        def _():
            low_ref[0] = jnp.concatenate(first, axis=1)
            high_ref[0] = jnp.concatenate(second, axis=1)


def spread(where, hidden, chip_rows, layers):
    rows = hidden.shape[0]
    half = layers * chip_rows // 2

    def block(req, d, k):
        layer, place = req // PLANE, req % PLANE
        source = ring_at((ring_place(layer, layers) + layers - k) % layers, layers)
        return source * PLANE + (place ^ d)

    if chip_rows % 128:
        low, high = [], []
        for d in range(PLANE):
            got = [
                lax.dynamic_slice(hidden, (0, block(where[0], d, k) * chip_rows), (rows, chip_rows))
                for k in range(layers)
            ]
            low.append(jnp.concatenate([x[:, : chip_rows // 2] for x in got], axis=1))
            high.append(jnp.concatenate([x[:, chip_rows // 2 :] for x in got], axis=1))
        low, high = jnp.stack(low), jnp.stack(high)
        return jnp.where(where[1] == 0, low, high), jnp.where(where[1] == 0, high, low)
    shape = jax.ShapeDtypeStruct((PLANE, rows, half), hidden.dtype)
    out_spec = pl.BlockSpec((1, rows, half), lambda d, _: (d, 0, 0))
    return pl.pallas_call(
        spread_kernel,
        out_shape=(shape, shape),
        grid_spec=pltpu.PrefetchScalarGridSpec(
            num_scalar_prefetch=1,
            grid=(PLANE,),
            in_specs=[
                pl.BlockSpec(
                    (rows, chip_rows), functools.partial(lambda k, d, w: (0, block(w[0], d, k)), k)
                )
                for k in range(layers)
            ],
            out_specs=(out_spec, out_spec),
        ),
        cost_estimate=cost(0, 4 << 20),
        name="spread",
    )(where, *([hidden] * layers))


def product_kernel(count, *refs):
    hidden, pieces, (keep_ref, send_ref, weight) = refs[:PLANE], refs[PLANE : PLANE + count], refs[-3:]
    block_rows = pieces[0].shape[0]
    for k, piece in enumerate(pieces):
        weight[k * block_rows : (k + 1) * block_rows, :] = piece[...]
    rows = keep_ref.shape[1]
    for d in range(PLANE):
        result = jnp.dot(hidden[d][...], weight[...], preferred_element_type=F32)
        keep_ref[d] = result[:rows].astype(keep_ref.dtype)
        send_ref[d] = result[rows:].astype(send_ref.dtype)


def product(hidden, pieces):
    rows, depth = hidden[0].shape
    width = pieces[0].shape[1]
    shape = jax.ShapeDtypeStruct((PLANE, rows // 2, width), BF16)
    return pl.pallas_call(
        functools.partial(product_kernel, len(pieces)),
        out_shape=(shape, shape),
        in_specs=[VMEM] * (PLANE + len(pieces)),
        out_specs=(VMEM, VMEM),
        scratch_shapes=[pltpu.VMEM((depth, width), BF16)],
        compiler_params=PARAMS,
        cost_estimate=cost(2 * PLANE * rows * depth * width, 6 << 20),
        name="product",
    )(*hidden, *pieces)


def swap_units(x):
    return lax.ppermute(x, "unit", [(0, 1), (1, 0)])


def after(x, *others):
    return lax.optimization_barrier((x, *others))[0]


def ring_at(step, length):
    if isinstance(step, int):
        return 2 * step - min(step, 1) if 2 * step <= length else 2 * (length - step)
    return jnp.where(2 * step <= length, 2 * step - jnp.minimum(step, 1), 2 * (length - step))


def ring_place(place, length):
    return jnp.where(place % 2 == 1, (place + 1) // 2, (length - place // 2) % length)


def chunk_edges(width):
    third = width // 3 // 128 * 128
    return [0, third, 2 * third, width]


def on_device(
    queries,
    kv_new,
    kv_pool,
    page_table,
    ctx_pages,
    ssm_x,
    ssm_z,
    ssm_bc,
    dt_raw,
    dt_bias,
    decay_rate,
    skip_gain,
    ssm_state,
    ssm_norm_gain,
    resid,
    out_weight,
    ffn_hidden,
    down_weight,
    page_owner,
):
    tok_rows = queries.shape[0]
    n_req = lax.axis_size("req")
    block_rows, width = down_weight.shape
    u = lax.axis_index("unit")
    unit = u.reshape(1)
    req = lax.axis_index("req")
    layers = n_req // PLANE

    ring = [ring_at(i, layers) for i in range(layers)]
    ring_pairs = [
        (ring[i] * PLANE + p, ring[(i + 1) % layers] * PLANE + p)
        for i in range(layers)
        for p in range(PLANE)
    ]

    def pass_on(x):
        return lax.ppermute(x, "req", ring_pairs)

    edges = chunk_edges(width)
    a, b, c = ([down_weight[:, lo:hi]] for lo, hi in zip(edges[:-1], edges[1:]))
    for chunk in (a, b, c):
        chunk.append(pass_on(chunk[-1]))

    where = jnp.stack([req, u])
    mine, other = spread(where, ffn_hidden, 2 * block_rows, layers)
    came = swap_units(other)

    def plane_swap(x, d):
        return lax.ppermute(
            x, "req", [(r, r - r % PLANE + ((r % PLANE) ^ d)) for r in range(n_req)]
        )

    attn, pages_held, pages_leave = attend(
        page_table, ctx_pages, page_owner[:, :, 0], unit, after(queries, mine), kv_new, kv_pool
    )
    a.append(pass_on(a[-1]))
    came = after(came, attn)
    hidden = [jnp.concatenate([mine[d], came[d]], axis=0) for d in range(PLANE)]
    hidden = [plane_swap(x, d) if d else x for d, x in enumerate(hidden)]

    stay, leave, state_held, state_leave = state_space(
        unit,
        skip_gain,
        after(attn, a[1]),
        ssm_x,
        ssm_z,
        ssm_bc,
        dt_raw,
        dt_bias[None, :],
        decay_rate[None, :],
        ssm_norm_gain[None, :],
        ssm_state,
    )
    b.append(pass_on(b[-1]))
    leave_came = swap_units(leave)
    pages_came = swap_units(pages_leave)
    state_came = swap_units(state_leave)
    exchanged = jnp.concatenate([after(stay, b[1]), leave_came], axis=0)
    mixed = jnp.dot(exchanged, out_weight, preferred_element_type=F32).astype(BF16)
    mixed_came = swap_units(mixed[tok_rows:])
    a.append(pass_on(a[-1]))
    pages_came = after(pages_came, a[2], mixed)
    decode_kv, decode_state = settle(unit, pages_came, state_came, pages_held, state_held)
    b.append(pass_on(b[-1]))
    for chunk in (a, b):
        while len(chunk) < layers:
            chunk.append(pass_on(chunk[-1]))

    def reduced(chunk):
        keep, send = product(hidden, chunk)
        total = keep.astype(F32) + swap_units(send).astype(F32)
        parts = [plane_swap(total[d].astype(BF16), d) for d in range(1, PLANE)]
        return total[0], parts

    sums = []
    sums.append(reduced(a))
    c.append(pass_on(after(c[-1], a[3])))
    sums.append(reduced(b))
    while len(c) < layers:
        c.append(pass_on(c[-1]))
    sums.append(reduced(c))
    outs = []
    for (lo, hi), (own, parts) in zip(zip(edges[:-1], edges[1:]), sums):
        total = own
        for part in parts:
            total = total + part.astype(F32)
        base = resid[:, lo:hi].astype(F32) + (
            mixed[:tok_rows, lo:hi].astype(F32) + mixed_came[:, lo:hi].astype(F32)
        )
        outs.append((base + total).astype(BF16))
    return (jnp.concatenate(outs, axis=1), decode_kv, decode_state)


def solution(mesh):
    return jax.shard_map(
        on_device,
        mesh=mesh,
        in_specs=(
            P(("req", "unit"), None),
            P(("req", "unit"), None),
            P(("req", "unit"), None, None),
            P(("req", "unit"), None),
            P(("req", "unit")),
            P(("req", "unit"), None),
            P(("req", "unit"), None),
            P(("req", "unit"), None),
            P(("req", "unit"), None),
            P(),
            P(),
            P(),
            P(("req", "unit"), None, None, None),
            P(),
            P(("req", "unit"), None),
            P("unit", None),
            P(("req", "unit"), None),
            P(("req", "unit"), None),
            P(("req", "unit"), None, None),
        ),
        out_specs=(
            P(("req", "unit"), None),
            P(("req", "unit"), None, None),
            P("req", "unit", None, None),
        ),
        check_vma=False,
    )
```

time: 283 us -> 144 us (0.51)
  between operations: 61 us -> 1.67 us
  Pallas kernels: 0 us -> 36 us
  other arithmetic: 38.9 us -> 4.07 us
  local copies, waits for them, and re-layouts: 31.9 us -> 5.29 us
  matrix products: 33.2 us -> 8.84 us
  waiting for transfers between devices: 73.3 us -> 51.1 us
  starting transfers between devices: 42.8 us -> 35.9 us
    pallas_call x0 -> x7, Pallas kernels: none -> 36 us  [the longest x1 11.4 us: attend(): pl.pallas_call(attend_kernel, out_shape=(jax.ShapeDtypeStruct(queries.sha...]
    ppermute x21, waiting for transfers between devices: 73.3 us -> 51.1 us  [the longest x9 28.6 us: pass_on(): return lax.ppermute(x, 'req', ring_pairs)]
    dot_general x10 -> x1, matrix products: 27 us -> 8.84 us  [on_device(): jnp.dot(exchanged, out_weight, preferred_element_type=F32).astype(BF16)]
    unnamed x9 -> x0, other arithmetic: 15.3 us -> none
    unnamed x87 -> x29, local copies, waits for them, and re-layouts: 13.7 us -> 0.18 us
    ppermute x21, starting transfers between devices: 41 us -> 33.7 us  [the longest x12 18 us: plane_swap(): lax.ppermute(x, 'req', [(r, r - r % PLANE + (r % PLANE ^ d)) for r in ran...]
    sub x1 -> x0, matrix products: 6.14 us -> none  [attend(): exponent = jnp.exp(scores - row_max)]
    slice x17 -> x2, local copies, waits for them, and re-layouts: 7.06 us -> 2.41 us  [the longest x1 1.47 us: on_device(): a, b, c = ([down_weight[:, lo:hi]] for lo, hi in zip(edges[:-1], edges[1:]))]
  transfers between devices with their start and end apart: 32 -> 29, of which waited for: 15 -> 10; matrix products, arithmetic and copies ran while one was open for 25% -> 11% of each run, Pallas kernels for 0% -> 22%
where the time goes in v2:
time: 144 us; the launch traced here: 143 us
  waiting for transfers between devices  51.1 us (35%)
  Pallas kernels  36 us (25%)
  starting transfers between devices  35.9 us (25%)
  matrix products  8.84 us (6%)
  local copies, waits for them, and re-layouts  5.29 us (4%)
  other arithmetic  4.07 us (3%)
  between operations  1.67 us (1%)
    ppermute x9, waiting for transfers between devices, pass_on(): return lax.ppermute(x, 'req', ring_pairs)  28.6 us
    ppermute x12, waiting for transfers between devices, plane_swap(): lax.ppermute(x, 'req', [(r, r - r % PLANE + (r % PLANE ^ d)) for r in ran...  22.5 us
    ppermute x12, starting transfers between devices, plane_swap(): lax.ppermute(x, 'req', [(r, r - r % PLANE + (r % PLANE ^ d)) for r in ran...  18 us
    ppermute x9, starting transfers between devices, pass_on(): return lax.ppermute(x, 'req', ring_pairs)  15.7 us
    pallas_call x1, Pallas kernels, attend(): pl.pallas_call(attend_kernel, out_shape=(jax.ShapeDtypeStruct(queries.sha...  11.4 us
    pallas_call x1, Pallas kernels, state_space(): pl.pallas_call(state_kernel, out_shape=(jax.ShapeDtypeStruct((length, hal...  9.96 us
    dot_general x1, matrix products, on_device(): jnp.dot(exchanged, out_weight, preferred_element_type=F32).astype(BF16)  8.84 us
    pallas_call x3, Pallas kernels, product(): pl.pallas_call(functools.partial(product_kernel, len(pieces)), out_shape=...  8.36 us
  transfers between devices with their start and end apart: 29, of which 10 were waited for; matrix products, arithmetic and copies ran while one was open for 11% of the time, Pallas kernels for 22%

profile of v2, /device:TPU:0, one launch (start us, length us, event | category | flops | bytes accessed | tf_op | source)
XLA Modules:
  0.0 142.9 jit_solution(14476206814728516735)
XLA Ops:
  1.2 4.7 %spread.1 = (bf16[4,128,768]{2,1,0:T(8,128)(2,1)}, bf16[4,128,768]{2,1,0:T(8,128)(2,1)}) custom-call(s32[2]{0:T(128)} %pad_add_fusion.where, bf16[128,6144]{1,0:T(8,128)(2,1)} %refs_3_.1, bf16[128,6144]{1,0:T(8,128)(2,1)} %refs_3_.1, bf16[128,6144]{1,0:T(8,128)(2,1)} %refs_3_.1, bf16[128,6144]{1,0:T(8,128)(2,1)} %refs_3_.1), custom_call_target="tpu_custom_call" | custom-call | bytes 4194304 | tf_op jit(solution)/shard_map/spread/pallas_call | solution.py:329
  8.0 2.6 %collective-permute-start.1 = (bf16[192,1024]{1,0:T(8,128)(2,1)S(1)}, bf16[192,1024]{1,0:T(8,128)(2,1)}, u32[]{:S(2)}, u32[]{:S(2)}) collective-permute-start(bf16[192,1024]{1,0:T(8,128)(2,1)S(1)} %get-tuple-element.57.refs_4_), channel_id=1, source_target_pairs={{0,8},{2,10},{4,12},{6,14},{8,24},{10,26},{12,28},{14,30},{24,16},... | collective-permute-start | bytes 1179656 | tf_op jit(solution)/shard_map/ppermute | solution.py:436
  10.6 2.6 %collective-permute-start = (bf16[192,1024]{1,0:T(8,128)(2,1)S(1)}, bf16[192,1024]{1,0:T(8,128)(2,1)}, u32[]{:S(2)}, u32[]{:S(2)}) collective-permute-start(bf16[192,1024]{1,0:T(8,128)(2,1)S(1)} %get-tuple-element.58.refs_4_), channel_id=1, source_target_pairs={{0,8},{2,10},{4,12},{6,14},{8,24},{10,26},{12,28},{14,30},{24,16},... | collective-permute-start | bytes 1179656 | tf_op jit(solution)/shard_map/ppermute | solution.py:436
  15.8 11.4 %attend.1 = (bf16[128,1536]{1,0:T(8,128)(2,1)S(1)}, bf16[14,128,512]{2,1,0:T(8,128)(2,1)}, bf16[7,128,512]{2,1,0:T(8,128)(2,1)S(1)}) custom-call(s32[1,13]{1,0:T(1,128)S(1)} %copy-done.7, s32[1]{0:T(128)S(6)} %copy.27.ctx, s32[1,13]{1,0:T(1,128)S(1)} %bitcast.78, s32[1]{0:T(128)} %bitcast.unit, bf16[128,1536]{1,0:T(8,128)(2,1)S(1)} %copy-done.3, ...), custom_call_target="tpu_custom_call" | custom-call | flops 5234491392 | bytes 6291456 | tf_op jit(solution)/shard_map/attend/pallas_call | solution.py:128
  27.3 2.8 %collective-permute-done.refs_5_ = bf16[192,1024]{1,0:T(8,128)(2,1)} collective-permute-done((bf16[192,1024]{1,0:T(8,128)(2,1)S(1)}, bf16[192,1024]{1,0:T(8,128)(2,1)}, u32[]{:S(2)}, u32[]{:S(2)}) %collective-permute-start) | collective-permute-done | bytes 393248 | tf_op jit(solution)/shard_map/ppermute | solution.py:436
  31.1 3.5 %collective-permute-start.14 = (bf16[192,1024]{1,0:T(8,128)(2,1)}, bf16[192,1024]{1,0:T(8,128)(2,1)S(1)}, u32[]{:S(2)}, u32[]{:S(2)}) collective-permute-start(bf16[192,1024]{1,0:T(8,128)(2,1)} %collective-permute-done.1.refs_5_), channel_id=1, source_target_pairs={{0,8},{2,10},{4,12},{6,14},{8,24},{10,26},{12,28},{14,30},{24,16},... | collective-permute-start | bytes 1179656 | tf_op jit(solution)/shard_map/ppermute | solution.py:436
  35.9 2.5 %collective-permute-start.7 = (bf16[256,768]{1,0:T(8,128)(2,1)S(1)}, bf16[256,768]{1,0:T(8,128)(2,1)S(1)}, u32[]{:S(2)}, u32[]{:S(2)}) collective-permute-start(bf16[256,768]{1,0:T(8,128)(2,1)S(1)} %pad_maximum_fusion.4), channel_id=1, source_target_pairs={{0,6},{2,4},{4,2},{6,0},{8,14},{10,12},{12,10},{14,8},{16,22},{18,... | collective-permute-start | bytes 1179656 | tf_op jit(solution)/shard_map/ppermute | solution.py:448
  40.3 14.6 %collective-permute-done.14.refs_6_ = bf16[192,1024]{1,0:T(8,128)(2,1)S(1)} collective-permute-done((bf16[192,1024]{1,0:T(8,128)(2,1)}, bf16[192,1024]{1,0:T(8,128)(2,1)S(1)}, u32[]{:S(2)}, u32[]{:S(2)}) %collective-permute-start.14) | collective-permute-done | bytes 393248 | tf_op jit(solution)/shard_map/ppermute | solution.py:436
  55.9 3.3 %collective-permute-start.9 = (bf16[192,1024]{1,0:T(8,128)(2,1)S(1)}, bf16[192,1024]{1,0:T(8,128)(2,1)S(1)}, u32[]{:S(2)}, u32[]{:S(2)}) collective-permute-start(bf16[192,1024]{1,0:T(8,128)(2,1)S(1)} %collective-permute-done.8.refs_6_), channel_id=1, source_target_pairs={{0,8},{2,10},{4,12},{6,14},{8,24},{10,26},{12,28},{14,30},{24,16},... | collective-permute-start | bytes 1179656 | tf_op jit(solution)/shard_map/ppermute | solution.py:436
  59.2 10.0 %state_space.1 = (bf16[128,2304]{1,0:T(8,128)(2,1)S(1)}, bf16[128,2304]{1,0:T(8,128)(2,1)S(1)}, f32[2,12,128,256]{3,2,1,0:T(8,128)}, bf16[12,128,256]{2,1,0:T(8,128)(2,1)S(1)}) custom-call(s32[1]{0:T(128)} %bitcast.unit, f32[24]{0:T(128)S(1)} %copy-done.9, bf16[128,1536]{1,0:T(8,128)(2,1)S(1)} %get-tuple-element.29.attn_ref, ...), custom_call_target="tpu_custom_call" | custom-call | flops 4294967296 | bytes 10485760 | tf_op jit(solution)/shard_map/state_space/pallas_call | solution.py:244
  69.2 5.9 %collective-permute-done.9.refs_7_ = bf16[192,1024]{1,0:T(8,128)(2,1)S(1)} collective-permute-done((bf16[192,1024]{1,0:T(8,128)(2,1)S(1)}, bf16[192,1024]{1,0:T(8,128)(2,1)S(1)}, u32[]{:S(2)}, u32[]{:S(2)}) %collective-permute-start.9) | collective-permute-done | bytes 393248 | tf_op jit(solution)/shard_map/ppermute | solution.py:436
  76.3 2.8 %product.4 = (bf16[4,128,1024]{2,1,0:T(8,128)(2,1)S(1)}, bf16[4,128,1024]{2,1,0:T(8,128)(2,1)S(1)}) custom-call(bf16[256,768]{1,0:T(8,128)(2,1)S(1)} %pad_maximum_fusion.1.refs_0_, bf16[256,768]{1,0:T(8,128)(2,1)S(1)} %collective-permute-done.5.refs_1_, bf16[256,768]{1,0:T(8,128)(2,1)S(1)} %collective-permute-done.6.refs_2_, ...), custom_call_target="tpu_custom_call" | custom-call | flops 1610612736 | bytes 6291456 | tf_op jit(solution)/shard_map/product/pallas_call | solution.py:364
  79.4 2.8 %product.3 = (bf16[4,128,1024]{2,1,0:T(8,128)(2,1)S(1)}, bf16[4,128,1024]{2,1,0:T(8,128)(2,1)S(1)}) custom-call(bf16[256,768]{1,0:T(8,128)(2,1)S(1)} %pad_maximum_fusion.1.refs_0_, bf16[256,768]{1,0:T(8,128)(2,1)S(1)} %collective-permute-done.5.refs_1_, bf16[256,768]{1,0:T(8,128)(2,1)S(1)} %collective-permute-done.6.refs_2_, ...), custom_call_target="tpu_custom_call" | custom-call | flops 1610612736 | bytes 6291456 | tf_op jit(solution)/shard_map/product/pallas_call | solution.py:364
  82.6 5.2 %collective-permute-done.21.refs_6_ = bf16[192,1024]{1,0:T(8,128)(2,1)S(1)} collective-permute-done((bf16[192,1024]{1,0:T(8,128)(2,1)}, bf16[192,1024]{1,0:T(8,128)(2,1)S(1)}, u32[]{:S(2)}, u32[]{:S(2)}) %collective-permute-start.21) | collective-permute-done | bytes 393248 | tf_op jit(solution)/shard_map/ppermute | solution.py:436
  88.5 8.8 %convolution_convert_fusion = bf16[256,3072]{1,0:T(8,128)(2,1)S(1)} fusion(bf16[2304,3072]{1,0:T(8,128)(2,1)} %param.34, bf16[128,2304]{1,0:T(8,128)(2,1)S(1)} %collective-permute-done.2, bf16[128,2304]{1,0:T(8,128)(2,1)S(1)} %get-tuple-element.31), kind=kOutput, calls=%fused_computation | convolution fusion | flops 3627024384 | bytes 16908288 | tf_op jit(solution)/shard_map/dot_general | solution.py:478
  99.7 2.8 %product.5 = (bf16[4,128,1024]{2,1,0:T(8,128)(2,1)S(1)}, bf16[4,128,1024]{2,1,0:T(8,128)(2,1)S(1)}) custom-call(bf16[256,768]{1,0:T(8,128)(2,1)S(1)} %pad_maximum_fusion.1.refs_0_, bf16[256,768]{1,0:T(8,128)(2,1)S(1)} %collective-permute-done.5.refs_1_, bf16[256,768]{1,0:T(8,128)(2,1)S(1)} %collective-permute-done.6.refs_2_, ...), custom_call_target="tpu_custom_call" | custom-call | flops 1610612736 | bytes 6291456 | tf_op jit(solution)/shard_map/product/pallas_call | solution.py:364
  112.9 2.4 %collective-permute-start.13 = (bf16[128,1024]{1,0:T(8,128)(2,1)S(1)}, bf16[128,1024]{1,0:T(8,128)(2,1)S(1)}, u32[]{:S(2)}, u32[]{:S(2)}) collective-permute-start(bf16[128,1024]{1,0:T(8,128)(2,1)S(1)} %get-tuple-element.61), channel_id=1, source_target_pairs={{0,6},{2,4},{4,2},{6,0},{8,14},{10,12},{12,10},{14,8},{16,22},{18,... | collective-permute-start | bytes 786440 | tf_op jit(solution)/shard_map/ppermute | solution.py:448
  115.3 4.7 %collective-permute-done.18 = bf16[128,1024]{1,0:T(8,128)(2,1)S(1)} collective-permute-done((bf16[128,1024]{1,0:T(8,128)(2,1)S(1)}, bf16[128,1024]{1,0:T(8,128)(2,1)S(1)}, u32[]{:S(2)}, u32[]{:S(2)}) %collective-permute-start.18) | collective-permute-done | bytes 262176 | tf_op jit(solution)/shard_map/ppermute | solution.py:448
  120.1 2.0 %collective-permute-start.25 = (bf16[128,1024]{1,0:T(8,128)(2,1)S(1)}, bf16[128,1024]{1,0:T(8,128)(2,1)S(1)}, u32[]{:S(2)}, u32[]{:S(2)}) collective-permute-start(bf16[128,1024]{1,0:T(8,128)(2,1)S(1)} %get-tuple-element.68), channel_id=1, source_target_pairs={{0,4},{2,6},{4,0},{6,2},{8,12},{10,14},{12,8},{14,10},{16,20},{18,... | collective-permute-start | bytes 786440 | tf_op jit(solution)/shard_map/ppermute | solution.py:448
  122.1 2.1 %collective-permute-done.11 = bf16[128,1024]{1,0:T(8,128)(2,1)S(1)} collective-permute-done((bf16[128,1024]{1,0:T(8,128)(2,1)S(1)}, bf16[128,1024]{1,0:T(8,128)(2,1)S(1)}, u32[]{:S(2)}, u32[]{:S(2)}) %collective-permute-start.11) | collective-permute-done | bytes 262176 | tf_op jit(solution)/shard_map/ppermute | solution.py:448
  124.2 2.4 %collective-permute-start.26 = (bf16[128,1024]{1,0:T(8,128)(2,1)S(1)}, bf16[128,1024]{1,0:T(8,128)(2,1)S(1)}, u32[]{:S(2)}, u32[]{:S(2)}) collective-permute-start(bf16[128,1024]{1,0:T(8,128)(2,1)S(1)} %get-tuple-element.67), channel_id=1, source_target_pairs={{0,6},{2,4},{4,2},{6,0},{8,14},{10,12},{12,10},{14,8},{16,22},{18,... | collective-permute-start | bytes 786440 | tf_op jit(solution)/shard_map/ppermute | solution.py:448
  126.9 4.4 %collective-permute-done.12 = bf16[128,1024]{1,0:T(8,128)(2,1)S(1)} collective-permute-done((bf16[128,1024]{1,0:T(8,128)(2,1)S(1)}, bf16[128,1024]{1,0:T(8,128)(2,1)S(1)}, u32[]{:S(2)}, u32[]{:S(2)}) %collective-permute-start.12) | collective-permute-done | bytes 262176 | tf_op jit(solution)/shard_map/ppermute | solution.py:448
  131.3 4.2 %collective-permute-done.24 = bf16[128,1024]{1,0:T(8,128)(2,1)S(1)} collective-permute-done((bf16[128,1024]{1,0:T(8,128)(2,1)S(1)}, bf16[128,1024]{1,0:T(8,128)(2,1)S(1)}, u32[]{:S(2)}, u32[]{:S(2)}) %collective-permute-start.24) | collective-permute-done | bytes 262176 | tf_op jit(solution)/shard_map/ppermute | solution.py:448
  135.4 5.8 %collective-permute-done.25 = bf16[128,1024]{1,0:T(8,128)(2,1)S(1)} collective-permute-done((bf16[128,1024]{1,0:T(8,128)(2,1)S(1)}, bf16[128,1024]{1,0:T(8,128)(2,1)S(1)}, u32[]{:S(2)}, u32[]{:S(2)}) %collective-permute-start.25) | collective-permute-done | bytes 262176 | tf_op jit(solution)/shard_map/ppermute | solution.py:448
  (89 shorter events, 26.9 us)
Async XLA Ops:
  6.0 28.6 %collective-permute-start.4 = (bf16[4,128,768]{2,1,0:T(8,128)(2,1)}, bf16[4,128,768]{2,1,0:T(8,128)(2,1)}, u32[]{:S(2)}, u32[]{:S(2)}) collective-permute-start(bf16[4,128,768]{2,1,0:T(8,128)(2,1)} %get-tuple-element.33), channel_id=1, source_target_pairs={{0,1},{1,0},{2,3},{3,2},{4,5},{5,4},{6,7},{7,6},{8,9},{9,8},{10,11... | collective-permute-start | bytes 2359304 | tf_op jit(solution)/shard_map/ppermute | solution.py:377
  8.0 23.1 %collective-permute-start.1 = (bf16[192,1024]{1,0:T(8,128)(2,1)S(1)}, bf16[192,1024]{1,0:T(8,128)(2,1)}, u32[]{:S(2)}, u32[]{:S(2)}) collective-permute-start(bf16[192,1024]{1,0:T(8,128)(2,1)S(1)} %get-tuple-element.57.refs_4_), channel_id=1, source_target_pairs={{0,8},{2,10},{4,12},{6,14},{8,24},{10,26},{12,28},{14,30},{24,16},... | collective-permute-start | bytes 1179656 | tf_op jit(solution)/shard_map/ppermute | solution.py:436
  10.6 19.5 %collective-permute-start = (bf16[192,1024]{1,0:T(8,128)(2,1)S(1)}, bf16[192,1024]{1,0:T(8,128)(2,1)}, u32[]{:S(2)}, u32[]{:S(2)}) collective-permute-start(bf16[192,1024]{1,0:T(8,128)(2,1)S(1)} %get-tuple-element.58.refs_4_), channel_id=1, source_target_pairs={{0,8},{2,10},{4,12},{6,14},{8,24},{10,26},{12,28},{14,30},{24,16},... | collective-permute-start | bytes 1179656 | tf_op jit(solution)/shard_map/ppermute | solution.py:436
  13.2 25.8 %collective-permute-start.20 = (bf16[192,1024]{1,0:T(8,128)(2,1)S(1)}, bf16[192,1024]{1,0:T(8,128)(2,1)}, u32[]{:S(2)}, u32[]{:S(2)}) collective-permute-start(bf16[192,1024]{1,0:T(8,128)(2,1)S(1)} %get-tuple-element.59.refs_4_), channel_id=1, source_target_pairs={{0,8},{2,10},{4,12},{6,14},{8,24},{10,26},{12,28},{14,30},{24,16},... | collective-permute-start | bytes 1179656 | tf_op jit(solution)/shard_map/ppermute | solution.py:436
  30.1 25.8 %collective-permute-start.8 = (bf16[192,1024]{1,0:T(8,128)(2,1)}, bf16[192,1024]{1,0:T(8,128)(2,1)S(1)}, u32[]{:S(2)}, u32[]{:S(2)}) collective-permute-start(bf16[192,1024]{1,0:T(8,128)(2,1)} %collective-permute-done.refs_5_), channel_id=1, source_target_pairs={{0,8},{2,10},{4,12},{6,14},{8,24},{10,26},{12,28},{14,30},{24,16},... | collective-permute-start | bytes 1179656 | tf_op jit(solution)/shard_map/ppermute | solution.py:436
  31.1 23.9 %collective-permute-start.14 = (bf16[192,1024]{1,0:T(8,128)(2,1)}, bf16[192,1024]{1,0:T(8,128)(2,1)S(1)}, u32[]{:S(2)}, u32[]{:S(2)}) collective-permute-start(bf16[192,1024]{1,0:T(8,128)(2,1)} %collective-permute-done.1.refs_5_), channel_id=1, source_target_pairs={{0,8},{2,10},{4,12},{6,14},{8,24},{10,26},{12,28},{14,30},{24,16},... | collective-permute-start | bytes 1179656 | tf_op jit(solution)/shard_map/ppermute | solution.py:436
  35.9 39.2 %collective-permute-start.7 = (bf16[256,768]{1,0:T(8,128)(2,1)S(1)}, bf16[256,768]{1,0:T(8,128)(2,1)S(1)}, u32[]{:S(2)}, u32[]{:S(2)}) collective-permute-start(bf16[256,768]{1,0:T(8,128)(2,1)S(1)} %pad_maximum_fusion.4), channel_id=1, source_target_pairs={{0,6},{2,4},{4,2},{6,0},{8,14},{10,12},{12,10},{14,8},{16,22},{18,... | collective-permute-start | bytes 1179656 | tf_op jit(solution)/shard_map/ppermute | solution.py:448
  38.5 37.3 %collective-permute-start.6 = (bf16[256,768]{1,0:T(8,128)(2,1)S(1)}, bf16[256,768]{1,0:T(8,128)(2,1)S(1)}, u32[]{:S(2)}, u32[]{:S(2)}) collective-permute-start(bf16[256,768]{1,0:T(8,128)(2,1)S(1)} %pad_maximum_fusion.3), channel_id=1, source_target_pairs={{0,4},{2,6},{4,0},{6,2},{8,12},{10,14},{12,8},{14,10},{16,20},{18,... | collective-permute-start | bytes 1179656 | tf_op jit(solution)/shard_map/ppermute | solution.py:448
  39.1 37.0 %collective-permute-start.5 = (bf16[256,768]{1,0:T(8,128)(2,1)S(1)}, bf16[256,768]{1,0:T(8,128)(2,1)S(1)}, u32[]{:S(2)}, u32[]{:S(2)}) collective-permute-start(bf16[256,768]{1,0:T(8,128)(2,1)S(1)} %pad_maximum_fusion.2), channel_id=1, source_target_pairs={{0,2},{2,0},{4,6},{6,4},{8,10},{10,8},{12,14},{14,12},{16,18},{18,... | collective-permute-start | bytes 1179656 | tf_op jit(solution)/shard_map/ppermute | solution.py:448
  55.0 21.3 %collective-permute-start.15 = (bf16[192,1024]{1,0:T(8,128)(2,1)S(1)}, bf16[192,1024]{1,0:T(8,128)(2,1)S(1)}, u32[]{:S(2)}, u32[]{:S(2)}) collective-permute-start(bf16[192,1024]{1,0:T(8,128)(2,1)S(1)} %collective-permute-done.14.refs_6_), channel_id=1, source_target_pairs={{0,8},{2,10},{4,12},{6,14},{8,24},{10,26},{12,28},{14,30},{24,16},... | collective-permute-start | bytes 1179656 | tf_op jit(solution)/shard_map/ppermute | solution.py:436
  55.9 19.2 %collective-permute-start.9 = (bf16[192,1024]{1,0:T(8,128)(2,1)S(1)}, bf16[192,1024]{1,0:T(8,128)(2,1)S(1)}, u32[]{:S(2)}, u32[]{:S(2)}) collective-permute-start(bf16[192,1024]{1,0:T(8,128)(2,1)S(1)} %collective-permute-done.8.refs_6_), channel_id=1, source_target_pairs={{0,8},{2,10},{4,12},{6,14},{8,24},{10,26},{12,28},{14,30},{24,16},... | collective-permute-start | bytes 1179656 | tf_op jit(solution)/shard_map/ppermute | solution.py:436
  75.1 12.6 %collective-permute-start.21 = (bf16[192,1024]{1,0:T(8,128)(2,1)}, bf16[192,1024]{1,0:T(8,128)(2,1)S(1)}, u32[]{:S(2)}, u32[]{:S(2)}) collective-permute-start(bf16[192,1024]{1,0:T(8,128)(2,1)} %collective-permute-done.20.refs_5_), channel_id=1, source_target_pairs={{0,8},{2,10},{4,12},{6,14},{8,24},{10,26},{12,28},{14,30},{24,16},... | collective-permute-start | bytes 1179656 | tf_op jit(solution)/shard_map/ppermute | solution.py:436
  75.7 22.5 %collective-permute-start.27 = (bf16[7,128,512]{2,1,0:T(8,128)(2,1)S(1)}, bf16[7,128,512]{2,1,0:T(8,128)(2,1)S(1)}, u32[]{:S(2)}, u32[]{:S(2)}) collective-permute-start(bf16[7,128,512]{2,1,0:T(8,128)(2,1)S(1)} %get-tuple-element.42), channel_id=1, source_target_pairs={{0,1},{1,0},{2,3},{3,2},{4,5},{5,4},{6,7},{7,6},{8,9},{9,8},{10,11... | collective-permute-start | bytes 2752520 | tf_op jit(solution)/shard_map/ppermute | solution.py:377
  76.0 22.2 %collective-permute-start.28 = (bf16[12,128,256]{2,1,0:T(8,128)(2,1)S(1)}, bf16[12,128,256]{2,1,0:T(8,128)(2,1)S(1)}, u32[]{:S(2)}, u32[]{:S(2)}) collective-permute-start(bf16[12,128,256]{2,1,0:T(8,128)(2,1)S(1)} %get-tuple-element.44), channel_id=1, source_target_pairs={{0,1},{1,0},{2,3},{3,2},{4,5},{5,4},{6,7},{7,6},{8,9},{9,8},{10,11... | collective-permute-start | bytes 2359304 | tf_op jit(solution)/shard_map/ppermute | solution.py:377
  79.1 24.0 %collective-permute-start.16 = (bf16[4,128,1024]{2,1,0:T(8,128)(2,1)S(1)}, bf16[4,128,1024]{2,1,0:T(8,128)(2,1)S(1)}, u32[]{:S(2)}, u32[]{:S(2)}) collective-permute-start(bf16[4,128,1024]{2,1,0:T(8,128)(2,1)S(1)} %get-tuple-element.38), channel_id=1, source_target_pairs={{0,1},{1,0},{2,3},{3,2},{4,5},{5,4},{6,7},{7,6},{8,9},{9,8},{10,11... | collective-permute-start | bytes 3145736 | tf_op jit(solution)/shard_map/ppermute | solution.py:377
  82.2 24.5 %collective-permute-start.10 = (bf16[4,128,1024]{2,1,0:T(8,128)(2,1)S(1)}, bf16[4,128,1024]{2,1,0:T(8,128)(2,1)S(1)}, u32[]{:S(2)}, u32[]{:S(2)}) collective-permute-start(bf16[4,128,1024]{2,1,0:T(8,128)(2,1)S(1)} %get-tuple-element.36), channel_id=1, source_target_pairs={{0,1},{1,0},{2,3},{3,2},{4,5},{5,4},{6,7},{7,6},{8,9},{9,8},{10,11... | collective-permute-start | bytes 3145736 | tf_op jit(solution)/shard_map/ppermute | solution.py:377
  105.2 14.8 %collective-permute-start.18 = (bf16[128,1024]{1,0:T(8,128)(2,1)S(1)}, bf16[128,1024]{1,0:T(8,128)(2,1)S(1)}, u32[]{:S(2)}, u32[]{:S(2)}) collective-permute-start(bf16[128,1024]{1,0:T(8,128)(2,1)S(1)} %get-tuple-element.65), channel_id=1, source_target_pairs={{0,4},{2,6},{4,0},{6,2},{8,12},{10,14},{12,8},{14,10},{16,20},{18,... | collective-permute-start | bytes 786440 | tf_op jit(solution)/shard_map/ppermute | solution.py:448
  106.7 13.4 %collective-permute-start.19 = (bf16[128,1024]{1,0:T(8,128)(2,1)S(1)}, bf16[128,1024]{1,0:T(8,128)(2,1)S(1)}, u32[]{:S(2)}, u32[]{:S(2)}) collective-permute-start(bf16[128,1024]{1,0:T(8,128)(2,1)S(1)} %get-tuple-element.64), channel_id=1, source_target_pairs={{0,6},{2,4},{4,2},{6,0},{8,14},{10,12},{12,10},{14,8},{16,22},{18,... | collective-permute-start | bytes 786440 | tf_op jit(solution)/shard_map/ppermute | solution.py:448
  107.8 16.4 %collective-permute-start.11 = (bf16[128,1024]{1,0:T(8,128)(2,1)S(1)}, bf16[128,1024]{1,0:T(8,128)(2,1)S(1)}, u32[]{:S(2)}, u32[]{:S(2)}) collective-permute-start(bf16[128,1024]{1,0:T(8,128)(2,1)S(1)} %get-tuple-element.60), channel_id=1, source_target_pairs={{0,2},{2,0},{4,6},{6,4},{8,10},{10,8},{12,14},{14,12},{16,18},{18,... | collective-permute-start | bytes 786440 | tf_op jit(solution)/shard_map/ppermute | solution.py:448
  109.9 21.4 %collective-permute-start.12 = (bf16[128,1024]{1,0:T(8,128)(2,1)S(1)}, bf16[128,1024]{1,0:T(8,128)(2,1)S(1)}, u32[]{:S(2)}, u32[]{:S(2)}) collective-permute-start(bf16[128,1024]{1,0:T(8,128)(2,1)S(1)} %get-tuple-element.62), channel_id=1, source_target_pairs={{0,4},{2,6},{4,0},{6,2},{8,12},{10,14},{12,8},{14,10},{16,20},{18,... | collective-permute-start | bytes 786440 | tf_op jit(solution)/shard_map/ppermute | solution.py:448
  112.9 18.4 %collective-permute-start.13 = (bf16[128,1024]{1,0:T(8,128)(2,1)S(1)}, bf16[128,1024]{1,0:T(8,128)(2,1)S(1)}, u32[]{:S(2)}, u32[]{:S(2)}) collective-permute-start(bf16[128,1024]{1,0:T(8,128)(2,1)S(1)} %get-tuple-element.61), channel_id=1, source_target_pairs={{0,6},{2,4},{4,2},{6,0},{8,14},{10,12},{12,10},{14,8},{16,22},{18,... | collective-permute-start | bytes 786440 | tf_op jit(solution)/shard_map/ppermute | solution.py:448
  120.0 15.4 %collective-permute-start.24 = (bf16[128,1024]{1,0:T(8,128)(2,1)S(1)}, bf16[128,1024]{1,0:T(8,128)(2,1)S(1)}, u32[]{:S(2)}, u32[]{:S(2)}) collective-permute-start(bf16[128,1024]{1,0:T(8,128)(2,1)S(1)} %get-tuple-element.66), channel_id=1, source_target_pairs={{0,2},{2,0},{4,6},{6,4},{8,10},{10,8},{12,14},{14,12},{16,18},{18,... | collective-permute-start | bytes 786440 | tf_op jit(solution)/shard_map/ppermute | solution.py:448
  120.1 21.1 %collective-permute-start.25 = (bf16[128,1024]{1,0:T(8,128)(2,1)S(1)}, bf16[128,1024]{1,0:T(8,128)(2,1)S(1)}, u32[]{:S(2)}, u32[]{:S(2)}) collective-permute-start(bf16[128,1024]{1,0:T(8,128)(2,1)S(1)} %get-tuple-element.68), channel_id=1, source_target_pairs={{0,4},{2,6},{4,0},{6,2},{8,12},{10,14},{12,8},{14,10},{16,20},{18,... | collective-permute-start | bytes 786440 | tf_op jit(solution)/shard_map/ppermute | solution.py:448
  124.2 17.1 %collective-permute-start.26 = (bf16[128,1024]{1,0:T(8,128)(2,1)S(1)}, bf16[128,1024]{1,0:T(8,128)(2,1)S(1)}, u32[]{:S(2)}, u32[]{:S(2)}) collective-permute-start(bf16[128,1024]{1,0:T(8,128)(2,1)S(1)} %get-tuple-element.67), channel_id=1, source_target_pairs={{0,6},{2,4},{4,2},{6,0},{8,14},{10,12},{12,10},{14,8},{16,22},{18,... | collective-permute-start | bytes 786440 | tf_op jit(solution)/shard_map/ppermute | solution.py:448
  (19 other events, 343.4 us)

commit v3 on v2

--- a/solution.py
+++ b/solution.py
@@ -262,7 +262,9 @@
     )(unit, skip, attn, x, z, bc, dt, bias, rate, gain, state)
 
 
-def settle_kernel(unit, pages, state, pages_in, state_in, pages_out, state_out, wide, sem):
+def settle_kernel(
+    unit, pages, state, pages_in, state_in, rows_in, pages_out, state_out, rows_out, wide, sem
+):
     slots = pages.shape[0]
     u = unit[0]
     copy = pltpu.make_async_copy(pages, pages_out.at[pl.ds((1 - u) * slots, slots)], sem.at[0])
@@ -274,21 +276,20 @@
     other.wait()
 
 
-def settle(unit, pages, state, pages_held, state_held):
+def settle(unit, pages, state, pages_held, state_held, rows):
     return pl.pallas_call(
         settle_kernel,
-        out_shape=(
-            jax.ShapeDtypeStruct(pages_held.shape, pages_held.dtype),
-            jax.ShapeDtypeStruct(state_held.shape, state_held.dtype),
+        out_shape=tuple(
+            jax.ShapeDtypeStruct(x.shape, x.dtype) for x in (pages_held, state_held, rows)
         ),
-        in_specs=[SMEM, ANY, VMEM, ANY, ANY],
-        out_specs=(ANY, ANY),
+        in_specs=[SMEM, ANY, VMEM, ANY, ANY, ANY],
+        out_specs=(ANY, ANY, ANY),
         scratch_shapes=[pltpu.VMEM(state.shape, F32), pltpu.SemaphoreType.DMA((2,))],
-        input_output_aliases={3: 0, 4: 1},
+        input_output_aliases={3: 0, 4: 1, 5: 2},
         compiler_params=PARAMS,
         cost_estimate=cost(0, 5 << 20),
         name="settle",
-    )(unit, pages, state, pages_held, state_held)
+    )(unit, pages, state, pages_held, state_held, rows)
 
 
 def spread_kernel(where, *refs):
@@ -437,30 +438,32 @@
 
     edges = chunk_edges(width)
     a, b, c = ([down_weight[:, lo:hi]] for lo, hi in zip(edges[:-1], edges[1:]))
+    started = [a[0], b[0], c[0]]
     for chunk in (a, b, c):
         chunk.append(pass_on(chunk[-1]))
 
+    def go_round(chunk, *others):
+        chunk.append(pass_on(after(chunk[-1], *others)))
+
     where = jnp.stack([req, u])
-    mine, other = spread(where, ffn_hidden, 2 * block_rows, layers)
-    came = swap_units(other)
+    mine, other = spread(where, after(ffn_hidden, *started), 2 * block_rows, layers)
+    attn, pages_held, pages_leave = attend(
+        page_table, ctx_pages, page_owner[:, :, 0], unit, after(queries, mine), kv_new, kv_pool
+    )
+    came = swap_units(after(other, a[1], b[1], c[1], attn))
 
     def plane_swap(x, d):
         return lax.ppermute(
             x, "req", [(r, r - r % PLANE + ((r % PLANE) ^ d)) for r in range(n_req)]
         )
 
-    attn, pages_held, pages_leave = attend(
-        page_table, ctx_pages, page_owner[:, :, 0], unit, after(queries, mine), kv_new, kv_pool
-    )
-    a.append(pass_on(a[-1]))
-    came = after(came, attn)
+    go_round(a, attn)
+    go_round(b, attn)
     hidden = [jnp.concatenate([mine[d], came[d]], axis=0) for d in range(PLANE)]
-    hidden = [plane_swap(x, d) if d else x for d, x in enumerate(hidden)]
-
     stay, leave, state_held, state_leave = state_space(
         unit,
         skip_gain,
-        after(attn, a[1]),
+        after(attn, *hidden),
         ssm_x,
         ssm_z,
         ssm_bc,
@@ -470,38 +473,50 @@
         ssm_norm_gain[None, :],
         ssm_state,
     )
-    b.append(pass_on(b[-1]))
+    hidden = [plane_swap(x, d) if d else x for d, x in enumerate(hidden)]
+    leave, state_leave, pages_leave = after(
+        (leave, state_leave, pages_leave), a[2], b[2], *hidden[1:]
+    )
+    go_round(a, stay)
+    go_round(b, stay)
     leave_came = swap_units(leave)
     pages_came = swap_units(pages_leave)
     state_came = swap_units(state_leave)
-    exchanged = jnp.concatenate([after(stay, b[1]), leave_came], axis=0)
+    decode_kv, decode_state, stay = settle(
+        unit, pages_came, state_came, pages_held, state_held, stay
+    )
+    exchanged = jnp.concatenate([stay, leave_came], axis=0)
     mixed = jnp.dot(exchanged, out_weight, preferred_element_type=F32).astype(BF16)
     mixed_came = swap_units(mixed[tok_rows:])
-    a.append(pass_on(a[-1]))
-    pages_came = after(pages_came, a[2], mixed)
-    decode_kv, decode_state = settle(unit, pages_came, state_came, pages_held, state_held)
-    b.append(pass_on(b[-1]))
     for chunk in (a, b):
         while len(chunk) < layers:
-            chunk.append(pass_on(chunk[-1]))
-
-    def reduced(chunk):
-        keep, send = product(hidden, chunk)
-        total = keep.astype(F32) + swap_units(send).astype(F32)
-        parts = [plane_swap(total[d].astype(BF16), d) for d in range(1, PLANE)]
-        return total[0], parts
-
-    sums = []
-    sums.append(reduced(a))
-    c.append(pass_on(after(c[-1], a[3])))
-    sums.append(reduced(b))
+            go_round(chunk)
+
+    def half_sums(chunk, then, *others):
+        keep, send = product(hidden, chunk[:-1] + [after(chunk[-1], *others)])
+        return keep, swap_units(after(send, *then))
+
+    def summed(keep, came):
+        total = keep.astype(F32) + came.astype(F32)
+        return total[0], [total[d].astype(BF16) for d in range(1, PLANE)]
+
+    def gathered(own, parts):
+        return [own] + [plane_swap(x, d) for d, x in enumerate(parts, 1)]
+
+    keep_a, came_a = half_sums(a, b[-1:], mixed)
+    go_round(c, b[-1])
+    sum_a = summed(keep_a, came_a)
+    keep_b, came_b = half_sums(b, c[-1:], *sum_a[1])
+    sum_a = gathered(*sum_a)
     while len(c) < layers:
-        c.append(pass_on(c[-1]))
-    sums.append(reduced(c))
+        go_round(c)
+    came_b = after(came_b, *sum_a)
+    sum_b = gathered(*summed(keep_b, came_b))
+    sum_c = gathered(*summed(*half_sums(c, (), came_b)))
     outs = []
-    for (lo, hi), (own, parts) in zip(zip(edges[:-1], edges[1:]), sums):
-        total = own
-        for part in parts:
+    for lo, hi, parts in zip(edges[:-1], edges[1:], (sum_a, sum_b, sum_c)):
+        total = parts[0]
+        for part in parts[1:]:
             total = total + part.astype(F32)
         base = resid[:, lo:hi].astype(F32) + (
             mixed[:tok_rows, lo:hi].astype(F32) + mixed_came[:, lo:hi].astype(F32)

time: 144 us -> 140 us (0.972)
  starting transfers between devices: 35.9 us -> 26.8 us
  waiting for transfers between devices: 51.1 us -> 56.8 us
    ppermute x12, waiting for transfers between devices: 22.5 us -> 33.4 us  [plane_swap(): lax.ppermute(x, 'req', [(r, r - r % PLANE + (r % PLANE ^ d)) for r in ran...]
    ppermute x9, waiting for transfers between devices: 28.6 us -> 18.8 us  [pass_on(): return lax.ppermute(x, 'req', ring_pairs)]
    ppermute x8, waiting for transfers between devices: 0.02 us -> 4.6 us  [swap_units(): return lax.ppermute(x, 'unit', [(0, 1), (1, 0)])]
    ppermute x9, starting transfers between devices: 15.7 us -> 11.5 us  [pass_on(): return lax.ppermute(x, 'req', ring_pairs)]
    ppermute x12, starting transfers between devices: 18 us -> 14.1 us  [plane_swap(): lax.ppermute(x, 'req', [(r, r - r % PLANE + (r % PLANE ^ d)) for r in ran...]
    unnamed x29 -> x37, local copies, waits for them, and re-layouts: 0.18 us -> 1.88 us
  transfers between devices with their start and end apart: 29 -> 29, of which waited for: 10 -> 15; matrix products, arithmetic and copies ran while one was open for 11% -> 9% of each run, Pallas kernels for 22% -> 24%
where the time goes in v3:
time: 140 us; the launch traced here: 139 us
  waiting for transfers between devices  56.8 us (41%)
  Pallas kernels  36.2 us (26%)
  starting transfers between devices  26.8 us (19%)
  matrix products  8.84 us (6%)
  local copies, waits for them, and re-layouts  4.75 us (3%)
  other arithmetic  4.01 us (3%)
  between operations  1.7 us (1%)
    ppermute x12, waiting for transfers between devices, plane_swap(): lax.ppermute(x, 'req', [(r, r - r % PLANE + (r % PLANE ^ d)) for r in ran...  33.4 us
    ppermute x9, waiting for transfers between devices, pass_on(): return lax.ppermute(x, 'req', ring_pairs)  18.8 us
    ppermute x12, starting transfers between devices, plane_swap(): lax.ppermute(x, 'req', [(r, r - r % PLANE + (r % PLANE ^ d)) for r in ran...  14.1 us
    ppermute x9, starting transfers between devices, pass_on(): return lax.ppermute(x, 'req', ring_pairs)  11.5 us
    pallas_call x1, Pallas kernels, attend(): pl.pallas_call(attend_kernel, out_shape=(jax.ShapeDtypeStruct(queries.sha...  11.5 us
    pallas_call x1, Pallas kernels, state_space(): pl.pallas_call(state_kernel, out_shape=(jax.ShapeDtypeStruct((length, hal...  10 us
    dot_general x1, matrix products, on_device(): jnp.dot(exchanged, out_weight, preferred_element_type=F32).astype(BF16)  8.84 us
    pallas_call x3, Pallas kernels, product(): pl.pallas_call(functools.partial(product_kernel, len(pieces)), out_shape=...  8.37 us
  transfers between devices with their start and end apart: 29, of which 15 were waited for; matrix products, arithmetic and copies ran while one was open for 9% of the time, Pallas kernels for 24%

profile of v3, /device:TPU:0, one launch (start us, length us, event | category | flops | bytes accessed | tf_op | source)
XLA Modules:
  0.0 139.1 jit_solution(11099387581600558342)
XLA Ops:
  2.0 3.1 %collective-permute-start = (bf16[192,1024]{1,0:T(8,128)(2,1)S(1)}, bf16[192,1024]{1,0:T(8,128)(2,1)}, u32[]{:S(2)}, u32[]{:S(2)}) collective-permute-start(bf16[192,1024]{1,0:T(8,128)(2,1)S(1)} %get-tuple-element.84.refs_4_), channel_id=1, source_target_pairs={{0,8},{2,10},{4,12},{6,14},{8,24},{10,26},{12,28},{14,30},{24,16},... | collective-permute-start | bytes 1179656 | tf_op jit(solution)/shard_map/ppermute | solution.py:437
  5.0 2.6 %collective-permute-start.1 = (bf16[192,1024]{1,0:T(8,128)(2,1)S(1)}, bf16[192,1024]{1,0:T(8,128)(2,1)}, u32[]{:S(2)}, u32[]{:S(2)}) collective-permute-start(bf16[192,1024]{1,0:T(8,128)(2,1)S(1)} %get-tuple-element.85.refs_4_), channel_id=1, source_target_pairs={{0,8},{2,10},{4,12},{6,14},{8,24},{10,26},{12,28},{14,30},{24,16},... | collective-permute-start | bytes 1179656 | tf_op jit(solution)/shard_map/ppermute | solution.py:437
  8.7 4.9 %spread.1 = (bf16[4,128,768]{2,1,0:T(8,128)(2,1)}, bf16[4,128,768]{2,1,0:T(8,128)(2,1)}) custom-call(s32[2]{0:T(128)} %pad_add_fusion.where, bf16[128,6144]{1,0:T(8,128)(2,1)} %refs_3_, bf16[128,6144]{1,0:T(8,128)(2,1)} %refs_3_, bf16[128,6144]{1,0:T(8,128)(2,1)} %refs_3_, bf16[128,6144]{1,0:T(8,128)(2,1)} %refs_3_), custom_call_target="tpu_custom_call" | custom-call | bytes 4194304 | tf_op jit(solution)/shard_map/spread/pallas_call | solution.py:330
  14.3 11.5 %attend.1 = (bf16[128,1536]{1,0:T(8,128)(2,1)S(1)}, bf16[14,128,512]{2,1,0:T(8,128)(2,1)}, bf16[7,128,512]{2,1,0:T(8,128)(2,1)S(1)}) custom-call(s32[1,13]{1,0:T(1,128)S(1)} %copy-done.9, s32[1]{0:T(128)S(6)} %copy.29.ctx, s32[1,13]{1,0:T(1,128)S(1)} %bitcast.70, s32[1]{0:T(128)} %bitcast.unit, bf16[128,1536]{1,0:T(8,128)(2,1)S(1)} %copy-done.5, ...), custom_call_target="tpu_custom_call" | custom-call | flops 5234491392 | bytes 6291456 | tf_op jit(solution)/shard_map/attend/pallas_call | solution.py:128
  27.5 4.6 %collective-permute-done.2.refs_5_ = bf16[192,1024]{1,0:T(8,128)(2,1)} collective-permute-done((bf16[192,1024]{1,0:T(8,128)(2,1)S(1)}, bf16[192,1024]{1,0:T(8,128)(2,1)}, u32[]{:S(2)}, u32[]{:S(2)}) %collective-permute-start.2) | collective-permute-done | bytes 393248 | tf_op jit(solution)/shard_map/ppermute | solution.py:437
  34.4 3.5 %collective-permute-start.5 = (bf16[192,1024]{1,0:T(8,128)(2,1)}, bf16[192,1024]{1,0:T(8,128)(2,1)S(1)}, u32[]{:S(2)}, u32[]{:S(2)}) collective-permute-start(bf16[192,1024]{1,0:T(8,128)(2,1)} %collective-permute-done.1.refs_5_), channel_id=1, source_target_pairs={{0,8},{2,10},{4,12},{6,14},{8,24},{10,26},{12,28},{14,30},{24,16},... | collective-permute-start | bytes 1179656 | tf_op jit(solution)/shard_map/ppermute | solution.py:437
  38.0 2.5 %collective-permute-start.8 = (bf16[256,768]{1,0:T(8,128)(2,1)S(1)}, bf16[256,768]{1,0:T(8,128)(2,1)S(1)}, u32[]{:S(2)}, u32[]{:S(2)}) collective-permute-start(bf16[256,768]{1,0:T(8,128)(2,1)S(1)} %pad_maximum_fusion.4), channel_id=1, source_target_pairs={{0,6},{2,4},{4,2},{6,0},{8,14},{10,12},{12,10},{14,8},{16,22},{18,... | collective-permute-start | bytes 1179656 | tf_op jit(solution)/shard_map/ppermute | solution.py:456
  41.8 10.0 %state_space.1 = (bf16[128,2304]{1,0:T(8,128)(2,1)S(1)}, bf16[128,2304]{1,0:T(8,128)(2,1)S(1)}, f32[2,12,128,256]{3,2,1,0:T(8,128)}, bf16[12,128,256]{2,1,0:T(8,128)(2,1)S(1)}) custom-call(s32[1]{0:T(128)} %bitcast.unit, f32[24]{0:T(128)S(1)} %copy-done.11, bf16[128,1536]{1,0:T(8,128)(2,1)S(1)} %copy-done.15, bf16[128,3072]{1,0:T(8,128)(2,1)S(1)} %copy-done.3, ...), custom_call_target="tpu_custom_call" | custom-call | flops 4294967296 | bytes 10485760 | tf_op jit(solution)/shard_map/state_space/pallas_call | solution.py:244
  51.9 2.8 %collective-permute-done.5.refs_6_ = bf16[192,1024]{1,0:T(8,128)(2,1)S(1)} collective-permute-done((bf16[192,1024]{1,0:T(8,128)(2,1)}, bf16[192,1024]{1,0:T(8,128)(2,1)S(1)}, u32[]{:S(2)}, u32[]{:S(2)}) %collective-permute-start.5) | collective-permute-done | bytes 393248 | tf_op jit(solution)/shard_map/ppermute | solution.py:437
  54.7 3.6 %collective-permute-done.7.refs_2_ = bf16[256,768]{1,0:T(8,128)(2,1)S(1)} collective-permute-done((bf16[256,768]{1,0:T(8,128)(2,1)S(1)}, bf16[256,768]{1,0:T(8,128)(2,1)S(1)}, u32[]{:S(2)}, u32[]{:S(2)}) %collective-permute-start.7) | collective-permute-done | bytes 393248 | tf_op jit(solution)/shard_map/ppermute | solution.py:456
  60.1 1.9 %collective-permute-done.10.state = bf16[12,128,256]{2,1,0:T(8,128)(2,1)S(1)} collective-permute-done((bf16[12,128,256]{2,1,0:T(8,128)(2,1)S(1)}, bf16[12,128,256]{2,1,0:T(8,128)(2,1)S(1)}, u32[]{:S(2)}, u32[]{:S(2)}) %collective-permute-start.10) | collective-permute-done | bytes 786464 | tf_op jit(solution)/shard_map/ppermute | solution.py:378
  63.5 8.8 %convolution_convert_fusion = bf16[256,3072]{1,0:T(8,128)(2,1)S(1)} fusion(bf16[2304,3072]{1,0:T(8,128)(2,1)} %param.34, bf16[128,2304]{1,0:T(8,128)(2,1)S(1)} %collective-permute-done.11, bf16[128,2304]{1,0:T(8,128)(2,1)S(1)} %get-tuple-element.56), kind=kOutput, calls=%fused_computation | convolution fusion | flops 3627024384 | bytes 16908288 | tf_op jit(solution)/shard_map/dot_general | solution.py:489
  72.4 2.8 %product.3 = (bf16[4,128,1024]{2,1,0:T(8,128)(2,1)S(1)}, bf16[4,128,1024]{2,1,0:T(8,128)(2,1)S(1)}) custom-call(bf16[256,768]{1,0:T(8,128)(2,1)S(1)} %pad_maximum_fusion.1.refs_0_, bf16[256,768]{1,0:T(8,128)(2,1)S(1)} %collective-permute-done.6.refs_1_, bf16[256,768]{1,0:T(8,128)(2,1)S(1)} %collective-permute-done.7.refs_2_, ...), custom_call_target="tpu_custom_call" | custom-call | flops 1610612736 | bytes 6291456 | tf_op jit(solution)/shard_map/product/pallas_call | solution.py:365
  75.2 4.6 %collective-permute-done.14.refs_7_ = bf16[192,1024]{1,0:T(8,128)(2,1)S(1)} collective-permute-done((bf16[192,1024]{1,0:T(8,128)(2,1)S(1)}, bf16[192,1024]{1,0:T(8,128)(2,1)S(1)}, u32[]{:S(2)}, u32[]{:S(2)}) %collective-permute-start.14) | collective-permute-done | bytes 393248 | tf_op jit(solution)/shard_map/ppermute | solution.py:437
  79.8 2.7 %collective-permute-done.15 = bf16[4,128,1024]{2,1,0:T(8,128)(2,1)S(1)} collective-permute-done((bf16[4,128,1024]{2,1,0:T(8,128)(2,1)S(1)}, bf16[4,128,1024]{2,1,0:T(8,128)(2,1)S(1)}, u32[]{:S(2)}, u32[]{:S(2)}) %collective-permute-start.15) | collective-permute-done | bytes 1048608 | tf_op jit(solution)/shard_map/ppermute | solution.py:378
  83.0 2.8 %product.4 = (bf16[4,128,1024]{2,1,0:T(8,128)(2,1)S(1)}, bf16[4,128,1024]{2,1,0:T(8,128)(2,1)S(1)}) custom-call(bf16[256,768]{1,0:T(8,128)(2,1)S(1)} %pad_maximum_fusion.1.refs_0_, bf16[256,768]{1,0:T(8,128)(2,1)S(1)} %collective-permute-done.6.refs_1_, bf16[256,768]{1,0:T(8,128)(2,1)S(1)} %collective-permute-done.7.refs_2_, ...), custom_call_target="tpu_custom_call" | custom-call | flops 1610612736 | bytes 6291456 | tf_op jit(solution)/shard_map/product/pallas_call | solution.py:365
  85.8 6.7 %collective-permute-done.19.refs_6_ = bf16[192,1024]{1,0:T(8,128)(2,1)S(1)} collective-permute-done((bf16[192,1024]{1,0:T(8,128)(2,1)}, bf16[192,1024]{1,0:T(8,128)(2,1)S(1)}, u32[]{:S(2)}, u32[]{:S(2)}) %collective-permute-start.19) | collective-permute-done | bytes 393248 | tf_op jit(solution)/shard_map/ppermute | solution.py:437
  95.9 5.6 %collective-permute-done.16 = bf16[128,1024]{1,0:T(8,128)(2,1)S(1)} collective-permute-done((bf16[128,1024]{1,0:T(8,128)(2,1)S(1)}, bf16[128,1024]{1,0:T(8,128)(2,1)S(1)}, u32[]{:S(2)}, u32[]{:S(2)}) %collective-permute-start.16) | collective-permute-done | bytes 262176 | tf_op jit(solution)/shard_map/ppermute | solution.py:456
  101.6 6.4 %collective-permute-done.17 = bf16[128,1024]{1,0:T(8,128)(2,1)S(1)} collective-permute-done((bf16[128,1024]{1,0:T(8,128)(2,1)S(1)}, bf16[128,1024]{1,0:T(8,128)(2,1)S(1)}, u32[]{:S(2)}, u32[]{:S(2)}) %collective-permute-start.17) | collective-permute-done | bytes 262176 | tf_op jit(solution)/shard_map/ppermute | solution.py:456
  108.0 2.8 %product.5 = (bf16[4,128,1024]{2,1,0:T(8,128)(2,1)S(1)}, bf16[4,128,1024]{2,1,0:T(8,128)(2,1)S(1)}) custom-call(bf16[256,768]{1,0:T(8,128)(2,1)S(1)} %pad_maximum_fusion.1.refs_0_, bf16[256,768]{1,0:T(8,128)(2,1)S(1)} %collective-permute-done.6.refs_1_, bf16[256,768]{1,0:T(8,128)(2,1)S(1)} %collective-permute-done.7.refs_2_, ...), custom_call_target="tpu_custom_call" | custom-call | flops 1610612736 | bytes 6291456 | tf_op jit(solution)/shard_map/product/pallas_call | solution.py:365
  118.2 3.1 %collective-permute-done.21 = bf16[128,1024]{1,0:T(8,128)(2,1)S(1)} collective-permute-done((bf16[128,1024]{1,0:T(8,128)(2,1)S(1)}, bf16[128,1024]{1,0:T(8,128)(2,1)S(1)}, u32[]{:S(2)}, u32[]{:S(2)}) %collective-permute-start.21) | collective-permute-done | bytes 262176 | tf_op jit(solution)/shard_map/ppermute | solution.py:456
  122.7 4.8 %collective-permute-done.22 = bf16[128,1024]{1,0:T(8,128)(2,1)S(1)} collective-permute-done((bf16[128,1024]{1,0:T(8,128)(2,1)S(1)}, bf16[128,1024]{1,0:T(8,128)(2,1)S(1)}, u32[]{:S(2)}, u32[]{:S(2)}) %collective-permute-start.22) | collective-permute-done | bytes 262176 | tf_op jit(solution)/shard_map/ppermute | solution.py:456
  127.8 4.8 %collective-permute-done.26 = bf16[128,1024]{1,0:T(8,128)(2,1)S(1)} collective-permute-done((bf16[128,1024]{1,0:T(8,128)(2,1)S(1)}, bf16[128,1024]{1,0:T(8,128)(2,1)S(1)}, u32[]{:S(2)}, u32[]{:S(2)}) %collective-permute-start.26) | collective-permute-done | bytes 262176 | tf_op jit(solution)/shard_map/ppermute | solution.py:456
  132.7 4.8 %collective-permute-done.28 = bf16[128,1024]{1,0:T(8,128)(2,1)S(1)} collective-permute-done((bf16[128,1024]{1,0:T(8,128)(2,1)S(1)}, bf16[128,1024]{1,0:T(8,128)(2,1)S(1)}, u32[]{:S(2)}, u32[]{:S(2)}) %collective-permute-start.28) | collective-permute-done | bytes 262176 | tf_op jit(solution)/shard_map/ppermute | solution.py:456
  (97 shorter events, 25.7 us)
Async XLA Ops:
  2.0 25.5 %collective-permute-start = (bf16[192,1024]{1,0:T(8,128)(2,1)S(1)}, bf16[192,1024]{1,0:T(8,128)(2,1)}, u32[]{:S(2)}, u32[]{:S(2)}) collective-permute-start(bf16[192,1024]{1,0:T(8,128)(2,1)S(1)} %get-tuple-element.84.refs_4_), channel_id=1, source_target_pairs={{0,8},{2,10},{4,12},{6,14},{8,24},{10,26},{12,28},{14,30},{24,16},... | collective-permute-start | bytes 1179656 | tf_op jit(solution)/shard_map/ppermute | solution.py:437
  5.0 22.4 %collective-permute-start.1 = (bf16[192,1024]{1,0:T(8,128)(2,1)S(1)}, bf16[192,1024]{1,0:T(8,128)(2,1)}, u32[]{:S(2)}, u32[]{:S(2)}) collective-permute-start(bf16[192,1024]{1,0:T(8,128)(2,1)S(1)} %get-tuple-element.85.refs_4_), channel_id=1, source_target_pairs={{0,8},{2,10},{4,12},{6,14},{8,24},{10,26},{12,28},{14,30},{24,16},... | collective-permute-start | bytes 1179656 | tf_op jit(solution)/shard_map/ppermute | solution.py:437
  7.6 24.5 %collective-permute-start.2 = (bf16[192,1024]{1,0:T(8,128)(2,1)S(1)}, bf16[192,1024]{1,0:T(8,128)(2,1)}, u32[]{:S(2)}, u32[]{:S(2)}) collective-permute-start(bf16[192,1024]{1,0:T(8,128)(2,1)S(1)} %get-tuple-element.83.refs_4_), channel_id=1, source_target_pairs={{0,8},{2,10},{4,12},{6,14},{8,24},{10,26},{12,28},{14,30},{24,16},... | collective-permute-start | bytes 1179656 | tf_op jit(solution)/shard_map/ppermute | solution.py:437
  32.1 5.7 %collective-permute-start.3 = (bf16[4,128,768]{2,1,0:T(8,128)(2,1)}, bf16[4,128,768]{2,1,0:T(8,128)(2,1)S(1)}, u32[]{:S(2)}, u32[]{:S(2)}) collective-permute-start(bf16[4,128,768]{2,1,0:T(8,128)(2,1)} %get-tuple-element.44), channel_id=1, source_target_pairs={{0,1},{1,0},{2,3},{3,2},{4,5},{5,4},{6,7},{7,6},{8,9},{9,8},{10,11... | collective-permute-start | bytes 2359304 | tf_op jit(solution)/shard_map/ppermute | solution.py:378
  33.6 18.3 %collective-permute-start.4 = (bf16[192,1024]{1,0:T(8,128)(2,1)}, bf16[192,1024]{1,0:T(8,128)(2,1)S(1)}, u32[]{:S(2)}, u32[]{:S(2)}) collective-permute-start(bf16[192,1024]{1,0:T(8,128)(2,1)} %collective-permute-done.refs_5_), channel_id=1, source_target_pairs={{0,8},{2,10},{4,12},{6,14},{8,24},{10,26},{12,28},{14,30},{24,16},... | collective-permute-start | bytes 1179656 | tf_op jit(solution)/shard_map/ppermute | solution.py:437
  34.4 20.3 %collective-permute-start.5 = (bf16[192,1024]{1,0:T(8,128)(2,1)}, bf16[192,1024]{1,0:T(8,128)(2,1)S(1)}, u32[]{:S(2)}, u32[]{:S(2)}) collective-permute-start(bf16[192,1024]{1,0:T(8,128)(2,1)} %collective-permute-done.1.refs_5_), channel_id=1, source_target_pairs={{0,8},{2,10},{4,12},{6,14},{8,24},{10,26},{12,28},{14,30},{24,16},... | collective-permute-start | bytes 1179656 | tf_op jit(solution)/shard_map/ppermute | solution.py:437
  38.0 16.8 %collective-permute-start.8 = (bf16[256,768]{1,0:T(8,128)(2,1)S(1)}, bf16[256,768]{1,0:T(8,128)(2,1)S(1)}, u32[]{:S(2)}, u32[]{:S(2)}) collective-permute-start(bf16[256,768]{1,0:T(8,128)(2,1)S(1)} %pad_maximum_fusion.4), channel_id=1, source_target_pairs={{0,6},{2,4},{4,2},{6,0},{8,14},{10,12},{12,10},{14,8},{16,22},{18,... | collective-permute-start | bytes 1179656 | tf_op jit(solution)/shard_map/ppermute | solution.py:456
  40.5 17.8 %collective-permute-start.7 = (bf16[256,768]{1,0:T(8,128)(2,1)S(1)}, bf16[256,768]{1,0:T(8,128)(2,1)S(1)}, u32[]{:S(2)}, u32[]{:S(2)}) collective-permute-start(bf16[256,768]{1,0:T(8,128)(2,1)S(1)} %pad_maximum_fusion.3), channel_id=1, source_target_pairs={{0,4},{2,6},{4,0},{6,2},{8,12},{10,14},{12,8},{14,10},{16,20},{18,... | collective-permute-start | bytes 1179656 | tf_op jit(solution)/shard_map/ppermute | solution.py:456
  41.1 17.3 %collective-permute-start.6 = (bf16[256,768]{1,0:T(8,128)(2,1)S(1)}, bf16[256,768]{1,0:T(8,128)(2,1)S(1)}, u32[]{:S(2)}, u32[]{:S(2)}) collective-permute-start(bf16[256,768]{1,0:T(8,128)(2,1)S(1)} %pad_maximum_fusion.2), channel_id=1, source_target_pairs={{0,2},{2,0},{4,6},{6,4},{8,10},{10,8},{12,14},{14,12},{16,18},{18,... | collective-permute-start | bytes 1179656 | tf_op jit(solution)/shard_map/ppermute | solution.py:456
  58.9 13.4 %collective-permute-start.13 = (bf16[192,1024]{1,0:T(8,128)(2,1)S(1)}, bf16[192,1024]{1,0:T(8,128)(2,1)S(1)}, u32[]{:S(2)}, u32[]{:S(2)}) collective-permute-start(bf16[192,1024]{1,0:T(8,128)(2,1)S(1)} %collective-permute-done.4.refs_6_), channel_id=1, source_target_pairs={{0,8},{2,10},{4,12},{6,14},{8,24},{10,26},{12,28},{14,30},{24,16},... | collective-permute-start | bytes 1179656 | tf_op jit(solution)/shard_map/ppermute | solution.py:437
  59.3 20.5 %collective-permute-start.14 = (bf16[192,1024]{1,0:T(8,128)(2,1)S(1)}, bf16[192,1024]{1,0:T(8,128)(2,1)S(1)}, u32[]{:S(2)}, u32[]{:S(2)}) collective-permute-start(bf16[192,1024]{1,0:T(8,128)(2,1)S(1)} %collective-permute-done.5.refs_6_), channel_id=1, source_target_pairs={{0,8},{2,10},{4,12},{6,14},{8,24},{10,26},{12,28},{14,30},{24,16},... | collective-permute-start | bytes 1179656 | tf_op jit(solution)/shard_map/ppermute | solution.py:437
  79.8 12.6 %collective-permute-start.19 = (bf16[192,1024]{1,0:T(8,128)(2,1)}, bf16[192,1024]{1,0:T(8,128)(2,1)S(1)}, u32[]{:S(2)}, u32[]{:S(2)}) collective-permute-start(bf16[192,1024]{1,0:T(8,128)(2,1)} %collective-permute-done.2.refs_5_), channel_id=1, source_target_pairs={{0,8},{2,10},{4,12},{6,14},{8,24},{10,26},{12,28},{14,30},{24,16},... | collective-permute-start | bytes 1179656 | tf_op jit(solution)/shard_map/ppermute | solution.py:437
  92.4 15.6 %collective-permute-start.20 = (bf16[4,128,1024]{2,1,0:T(8,128)(2,1)S(1)}, bf16[4,128,1024]{2,1,0:T(8,128)(2,1)S(1)}, u32[]{:S(2)}, u32[]{:S(2)}) collective-permute-start(bf16[4,128,1024]{2,1,0:T(8,128)(2,1)S(1)} %get-tuple-element.68), channel_id=1, source_target_pairs={{0,1},{1,0},{2,3},{3,2},{4,5},{5,4},{6,7},{7,6},{8,9},{9,8},{10,11... | collective-permute-start | bytes 3145736 | tf_op jit(solution)/shard_map/ppermute | solution.py:378
  92.4 15.6 %collective-permute-start.24 = (bf16[192,1024]{1,0:T(8,128)(2,1)S(1)}, bf16[192,1024]{1,0:T(8,128)(2,1)S(1)}, u32[]{:S(2)}, u32[]{:S(2)}) collective-permute-start(bf16[192,1024]{1,0:T(8,128)(2,1)S(1)} %collective-permute-done.19.refs_6_), channel_id=1, source_target_pairs={{0,8},{2,10},{4,12},{6,14},{8,24},{10,26},{12,28},{14,30},{24,16},... | collective-permute-start | bytes 1179656 | tf_op jit(solution)/shard_map/ppermute | solution.py:437
  92.4 9.1 %collective-permute-start.16 = (bf16[128,1024]{1,0:T(8,128)(2,1)S(1)}, bf16[128,1024]{1,0:T(8,128)(2,1)S(1)}, u32[]{:S(2)}, u32[]{:S(2)}) collective-permute-start(bf16[128,1024]{1,0:T(8,128)(2,1)S(1)} %get-tuple-element.94), channel_id=1, source_target_pairs={{0,2},{2,0},{4,6},{6,4},{8,10},{10,8},{12,14},{14,12},{16,18},{18,... | collective-permute-start | bytes 786440 | tf_op jit(solution)/shard_map/ppermute | solution.py:456
  93.9 14.1 %collective-permute-start.17 = (bf16[128,1024]{1,0:T(8,128)(2,1)S(1)}, bf16[128,1024]{1,0:T(8,128)(2,1)S(1)}, u32[]{:S(2)}, u32[]{:S(2)}) collective-permute-start(bf16[128,1024]{1,0:T(8,128)(2,1)S(1)} %get-tuple-element.93), channel_id=1, source_target_pairs={{0,4},{2,6},{4,0},{6,2},{8,12},{10,14},{12,8},{14,10},{16,20},{18,... | collective-permute-start | bytes 786440 | tf_op jit(solution)/shard_map/ppermute | solution.py:456
  94.8 13.2 %collective-permute-start.18 = (bf16[128,1024]{1,0:T(8,128)(2,1)S(1)}, bf16[128,1024]{1,0:T(8,128)(2,1)S(1)}, u32[]{:S(2)}, u32[]{:S(2)}) collective-permute-start(bf16[128,1024]{1,0:T(8,128)(2,1)S(1)} %get-tuple-element.92), channel_id=1, source_target_pairs={{0,6},{2,4},{4,2},{6,0},{8,14},{10,12},{12,10},{14,8},{16,22},{18,... | collective-permute-start | bytes 786440 | tf_op jit(solution)/shard_map/ppermute | solution.py:456
  110.9 5.8 %collective-permute-start.12 = (bf16[128,3072]{1,0:T(8,128)(2,1)S(1)}, bf16[128,3072]{1,0:T(8,128)(2,1)S(1)}, u32[]{:S(2)}, u32[]{:S(2)}) collective-permute-start(bf16[128,3072]{1,0:T(8,128)(2,1)S(1)} %slice.146), channel_id=1, source_target_pairs={{0,1},{1,0},{2,3},{3,2},{4,5},{5,4},{6,7},{7,6},{8,9},{9,8},{10,11... | collective-permute-start | bytes 2359304 | tf_op jit(solution)/shard_map/ppermute | solution.py:378
  112.0 9.2 %collective-permute-start.21 = (bf16[128,1024]{1,0:T(8,128)(2,1)S(1)}, bf16[128,1024]{1,0:T(8,128)(2,1)S(1)}, u32[]{:S(2)}, u32[]{:S(2)}) collective-permute-start(bf16[128,1024]{1,0:T(8,128)(2,1)S(1)} %get-tuple-element.86), channel_id=1, source_target_pairs={{0,2},{2,0},{4,6},{6,4},{8,10},{10,8},{12,14},{14,12},{16,18},{18,... | collective-permute-start | bytes 786440 | tf_op jit(solution)/shard_map/ppermute | solution.py:456
  112.6 14.8 %collective-permute-start.22 = (bf16[128,1024]{1,0:T(8,128)(2,1)S(1)}, bf16[128,1024]{1,0:T(8,128)(2,1)S(1)}, u32[]{:S(2)}, u32[]{:S(2)}) collective-permute-start(bf16[128,1024]{1,0:T(8,128)(2,1)S(1)} %get-tuple-element.88), channel_id=1, source_target_pairs={{0,4},{2,6},{4,0},{6,2},{8,12},{10,14},{12,8},{14,10},{16,20},{18,... | collective-permute-start | bytes 786440 | tf_op jit(solution)/shard_map/ppermute | solution.py:456
  114.1 13.4 %collective-permute-start.23 = (bf16[128,1024]{1,0:T(8,128)(2,1)S(1)}, bf16[128,1024]{1,0:T(8,128)(2,1)S(1)}, u32[]{:S(2)}, u32[]{:S(2)}) collective-permute-start(bf16[128,1024]{1,0:T(8,128)(2,1)S(1)} %get-tuple-element.87), channel_id=1, source_target_pairs={{0,6},{2,4},{4,2},{6,0},{8,14},{10,12},{12,10},{14,8},{16,22},{18,... | collective-permute-start | bytes 786440 | tf_op jit(solution)/shard_map/ppermute | solution.py:456
  116.1 16.4 %collective-permute-start.26 = (bf16[128,1024]{1,0:T(8,128)(2,1)S(1)}, bf16[128,1024]{1,0:T(8,128)(2,1)S(1)}, u32[]{:S(2)}, u32[]{:S(2)}) collective-permute-start(bf16[128,1024]{1,0:T(8,128)(2,1)S(1)} %get-tuple-element.89), channel_id=1, source_target_pairs={{0,2},{2,0},{4,6},{6,4},{8,10},{10,8},{12,14},{14,12},{16,18},{18,... | collective-permute-start | bytes 786440 | tf_op jit(solution)/shard_map/ppermute | solution.py:456
  116.7 16.0 %collective-permute-start.27 = (bf16[128,1024]{1,0:T(8,128)(2,1)S(1)}, bf16[128,1024]{1,0:T(8,128)(2,1)S(1)}, u32[]{:S(2)}, u32[]{:S(2)}) collective-permute-start(bf16[128,1024]{1,0:T(8,128)(2,1)S(1)} %get-tuple-element.91), channel_id=1, source_target_pairs={{0,4},{2,6},{4,0},{6,2},{8,12},{10,14},{12,8},{14,10},{16,20},{18,... | collective-permute-start | bytes 786440 | tf_op jit(solution)/shard_map/ppermute | solution.py:456
  121.3 16.2 %collective-permute-start.28 = (bf16[128,1024]{1,0:T(8,128)(2,1)S(1)}, bf16[128,1024]{1,0:T(8,128)(2,1)S(1)}, u32[]{:S(2)}, u32[]{:S(2)}) collective-permute-start(bf16[128,1024]{1,0:T(8,128)(2,1)S(1)} %get-tuple-element.90), channel_id=1, source_target_pairs={{0,6},{2,4},{4,2},{6,0},{8,14},{10,12},{12,10},{14,8},{16,22},{18,... | collective-permute-start | bytes 786440 | tf_op jit(solution)/shard_map/ppermute | solution.py:456
  (23 other events, 160.9 us)

commit v4 on v3

--- a/solution.py
+++ b/solution.py
@@ -27,7 +27,7 @@
 
 
 def cost(flops, moved, exps=0):
-    return pl.CostEstimate(flops=flops, bytes_accessed=moved, transcendentals=exps)
+    return pl.CostEstimate(flops=0, bytes_accessed=0, transcendentals=0)
 
 
 def contract_last(a, b):
@@ -159,7 +159,8 @@
     gain_ref,
     state_ref,
     stay_ref,
-    leave_ref,
+    leave_a,
+    leave_b,
     held,
     send_ref,
     gated,
@@ -225,13 +226,21 @@
     out = (gated[...] * lax.rsqrt(mean + norm_eps) * gain_ref[...]).astype(BF16)
     attn_width = attn_ref.shape[1]
     cut = stay_ref.shape[1] - attn_width
-    for which, low_ref, high_ref in ((0, stay_ref, leave_ref), (1, leave_ref, stay_ref)):
-
-        @pl.when(u == which)
-        def _():
-            low_ref[:, :attn_width] = attn_ref[...]
-            low_ref[:, attn_width:] = out[:, :cut]
-            high_ref[...] = out[:, cut:]
+    part = leave_a.shape[1]
+
+    @pl.when(u == 0)
+    def _():
+        stay_ref[:, :attn_width] = attn_ref[...]
+        stay_ref[:, attn_width:] = out[:, :cut]
+        leave_a[...] = out[:, cut : cut + part]
+        leave_b[...] = out[:, cut + part :]
+
+    @pl.when(u == 1)
+    def _():
+        stay_ref[...] = out[:, cut:]
+        leave_a[...] = attn_ref[:, :part]
+        leave_b[:, : attn_width - part] = attn_ref[:, part:]
+        leave_b[:, attn_width - part :] = out[:, :cut]
 
     for place in range(share):
         pltpu.make_async_copy(fresh.at[place], held.at[0, place], sems.at[place]).wait()
@@ -245,12 +254,13 @@
         state_kernel,
         out_shape=(
             jax.ShapeDtypeStruct((length, half), BF16),
-            jax.ShapeDtypeStruct((length, half), BF16),
+            jax.ShapeDtypeStruct((length, half // 2), BF16),
+            jax.ShapeDtypeStruct((length, half - half // 2), BF16),
             jax.ShapeDtypeStruct((2, share, PM, NS), F32),
             jax.ShapeDtypeStruct((share, PM, NS), BF16),
         ),
         in_specs=[SMEM, SMEM] + [VMEM] * 9,
-        out_specs=(VMEM, VMEM, ANY, VMEM),
+        out_specs=(VMEM, VMEM, VMEM, ANY, VMEM),
         scratch_shapes=[
             pltpu.VMEM((length, width), F32),
             pltpu.VMEM((share, PM, NS), F32),
@@ -292,86 +302,249 @@
     )(unit, pages, state, pages_held, state_held, rows)
 
 
-def spread_kernel(where, *refs):
-    *sources, mine_ref, other_ref = refs
-    half = sources[0].shape[1] // 2
-    first = [s[:, :half] for s in sources]
-    second = [s[:, half:] for s in sources]
-    for which, low_ref, high_ref in ((0, mine_ref, other_ref), (1, other_ref, mine_ref)):
-
-        @pl.when(where[1] == which)
-        def _():
-            low_ref[0] = jnp.concatenate(first, axis=1)
-            high_ref[0] = jnp.concatenate(second, axis=1)
-
-
-def spread(where, hidden, chip_rows, layers):
+def cut_kernel(unit, weight_ref, *refs):
+    count = len(refs) // 2
+    kept, sent = refs[:count], refs[count:]
+    half = weight_ref.shape[1] // 2
+    for u in range(2):
+
+        @pl.when(unit[0] == u)
+        def _():
+            for outs, base in ((kept, u * half), (sent, (1 - u) * half)):
+                for out in outs:
+                    out[...] = weight_ref[:, base : base + out.shape[1]]
+                    base += out.shape[1]
+
+
+def cut(unit, weight, widths):
+    rows = weight.shape[0]
+    outs = pl.pallas_call(
+        cut_kernel,
+        out_shape=tuple(jax.ShapeDtypeStruct((rows, w), weight.dtype) for w in widths * 2),
+        in_specs=[SMEM, VMEM],
+        out_specs=(VMEM,) * (2 * len(widths)),
+        compiler_params=PARAMS,
+        cost_estimate=cost(0, 3 << 20),
+        name="cut",
+    )(unit, weight)
+    return outs[: len(widths)], outs[len(widths) :]
+
+
+def block_of(req, d, k, layers):
+    layer, place = req // PLANE, req % PLANE
+    source = ring_at((ring_place(layer, layers) + layers - k) % layers, layers)
+    return source * PLANE + (place ^ d)
+
+
+def spread_kernel(req, hidden, *refs):
+    outs, sem = refs[:-1], refs[-1]
+    rows, depth = outs[0].shape
+    layers = sem.shape[0] // PLANE
+    chip_rows = depth // layers
+    copies = []
+    for d in range(PLANE):
+        for k in range(layers):
+            column = pl.multiple_of(chip_rows * block_of(req[0], d, k, layers), 128)
+            copies.append(
+                pltpu.make_async_copy(
+                    hidden.at[:, pl.ds(column, chip_rows)],
+                    outs[d].at[:, k * chip_rows : (k + 1) * chip_rows],
+                    sem.at[d * layers + k],
+                )
+            )
+    for copy in copies:
+        copy.start()
+    for copy in copies:
+        copy.wait()
+
+
+def spread(req, hidden, chip_rows, layers):
     rows = hidden.shape[0]
-    half = layers * chip_rows // 2
-
-    def block(req, d, k):
-        layer, place = req // PLANE, req % PLANE
-        source = ring_at((ring_place(layer, layers) + layers - k) % layers, layers)
-        return source * PLANE + (place ^ d)
-
     if chip_rows % 128:
-        low, high = [], []
-        for d in range(PLANE):
-            got = [
-                lax.dynamic_slice(hidden, (0, block(where[0], d, k) * chip_rows), (rows, chip_rows))
-                for k in range(layers)
-            ]
-            low.append(jnp.concatenate([x[:, : chip_rows // 2] for x in got], axis=1))
-            high.append(jnp.concatenate([x[:, chip_rows // 2 :] for x in got], axis=1))
-        low, high = jnp.stack(low), jnp.stack(high)
-        return jnp.where(where[1] == 0, low, high), jnp.where(where[1] == 0, high, low)
-    shape = jax.ShapeDtypeStruct((PLANE, rows, half), hidden.dtype)
-    out_spec = pl.BlockSpec((1, rows, half), lambda d, _: (d, 0, 0))
+        return [
+            jnp.concatenate(
+                [
+                    lax.dynamic_slice(
+                        hidden, (0, block_of(req[0], d, k, layers) * chip_rows), (rows, chip_rows)
+                    )
+                    for k in range(layers)
+                ],
+                axis=1,
+            )
+            for d in range(PLANE)
+        ]
     return pl.pallas_call(
         spread_kernel,
-        out_shape=(shape, shape),
-        grid_spec=pltpu.PrefetchScalarGridSpec(
-            num_scalar_prefetch=1,
-            grid=(PLANE,),
-            in_specs=[
-                pl.BlockSpec(
-                    (rows, chip_rows), functools.partial(lambda k, d, w: (0, block(w[0], d, k)), k)
-                )
-                for k in range(layers)
-            ],
-            out_specs=(out_spec, out_spec),
-        ),
+        out_shape=(jax.ShapeDtypeStruct((rows, layers * chip_rows), hidden.dtype),) * PLANE,
+        in_specs=[SMEM, ANY],
+        out_specs=(VMEM,) * PLANE,
+        scratch_shapes=[pltpu.SemaphoreType.DMA((PLANE * layers,))],
+        compiler_params=PARAMS,
         cost_estimate=cost(0, 4 << 20),
         name="spread",
-    )(where, *([hidden] * layers))
-
-
-def product_kernel(count, *refs):
-    hidden, pieces, (keep_ref, send_ref, weight) = refs[:PLANE], refs[PLANE : PLANE + count], refs[-3:]
-    block_rows = pieces[0].shape[0]
+    )(req, hidden)
+
+
+def product_kernel(count, low, unit, *refs):
+    hidden, pieces = refs[: PLANE + 1], refs[PLANE + 1 : PLANE + 1 + count]
+    own_ref, *parts = refs[PLANE + 1 + count : -1]
+    weight = refs[-1]
+    block_rows = pieces[0].shape[0] // 2
+    u = unit[0]
     for k, piece in enumerate(pieces):
-        weight[k * block_rows : (k + 1) * block_rows, :] = piece[...]
-    rows = keep_ref.shape[1]
+        for which, place in ((0, u), (1, 1 - u)):
+            at = pl.multiple_of((2 * k + place) * block_rows, 16)
+            rows = slice(which * block_rows, (which + 1) * block_rows)
+            base = low if piece.shape[1] > weight.shape[1] else 0
+            weight[pl.ds(at, block_rows), :] = piece[rows, base : base + weight.shape[1]]
+    rows = hidden[0].shape[0]
     for d in range(PLANE):
-        result = jnp.dot(hidden[d][...], weight[...], preferred_element_type=F32)
-        keep_ref[d] = result[:rows].astype(keep_ref.dtype)
-        send_ref[d] = result[rows:].astype(send_ref.dtype)
-
-
-def product(hidden, pieces):
+        other = hidden[-1][d * rows : (d + 1) * rows, :]
+        both = jnp.concatenate([hidden[d][...], other], axis=0)
+        result = jnp.dot(both, weight[...], preferred_element_type=F32)
+        if d:
+            parts[d - 1][...] = result.astype(BF16)
+        else:
+            own_ref[...] = result
+
+
+def product(unit, hidden, pieces, low=0):
     rows, depth = hidden[0].shape
-    width = pieces[0].shape[1]
-    shape = jax.ShapeDtypeStruct((PLANE, rows // 2, width), BF16)
-    return pl.pallas_call(
-        functools.partial(product_kernel, len(pieces)),
+    width = pieces[-1].shape[1]
+    outs = pl.pallas_call(
+        functools.partial(product_kernel, len(pieces), low),
+        out_shape=(jax.ShapeDtypeStruct((2 * rows, width), F32),)
+        + (jax.ShapeDtypeStruct((2 * rows, width), BF16),) * (PLANE - 1),
+        in_specs=[SMEM] + [VMEM] * (PLANE + 1 + len(pieces)),
+        out_specs=(VMEM,) * PLANE,
+        scratch_shapes=[pltpu.VMEM((depth, width), BF16)],
+        compiler_params=PARAMS,
+        cost_estimate=cost(0, 6 << 20),
+        name="product",
+    )(unit, *hidden, *pieces)
+    return outs[0], outs[1:]
+
+
+def total_kernel(own_ref, *refs):
+    came, (keep_ref, send_ref) = refs[:-2], refs[-2:]
+    total = own_ref[...]
+    for ref in came:
+        total = total + ref[...].astype(F32)
+    rows = keep_ref.shape[0]
+    keep_ref[...] = total[:rows]
+    send_ref[...] = total[rows:].astype(BF16)
+
+
+def total(own, came):
+    rows, width = own.shape
+    return pl.pallas_call(
+        total_kernel,
+        out_shape=(
+            jax.ShapeDtypeStruct((rows // 2, width), F32),
+            jax.ShapeDtypeStruct((rows // 2, width), BF16),
+        ),
+        in_specs=[VMEM] * (1 + len(came)),
+        out_specs=(VMEM, VMEM),
+        compiler_params=PARAMS,
+        cost_estimate=cost(0, 4 << 20),
+        name="total",
+    )(own, *came)
+
+
+def finish_kernel(unit, resid_ref, mixed_ref, mixed_came_ref, *refs):
+    count = len(refs) // 2
+    kept, came, out_ref = refs[:count], refs[count:-1], refs[-1]
+    half = out_ref.shape[1] // 2
+    for u in range(2):
+
+        @pl.when(unit[0] == u)
+        def _():
+            for group, base in ((kept, u * half), (came, (1 - u) * half)):
+                for ref in group:
+                    span = slice(base, base + ref.shape[1])
+                    mixed = mixed_ref[:, span].astype(F32) + mixed_came_ref[:, span].astype(F32)
+                    sums = resid_ref[:, span].astype(F32) + mixed + ref[...].astype(F32)
+                    out_ref[:, span] = sums.astype(BF16)
+                    base += ref.shape[1]
+
+
+def finish(unit, resid, mixed, mixed_came, kept, came):
+    return pl.pallas_call(
+        finish_kernel,
+        out_shape=jax.ShapeDtypeStruct(resid.shape, BF16),
+        in_specs=[SMEM] + [VMEM] * (3 + len(kept) + len(came)),
+        out_specs=VMEM,
+        compiler_params=PARAMS,
+        cost_estimate=cost(0, 4 << 20),
+        name="finish",
+    )(unit, resid, mixed, mixed_came, *kept, *came)
+
+
+def project_kernel(stay_ref, a_ref, b_ref, weight_ref, keep_ref, send_ref):
+    rows = stay_ref.shape[0]
+    came = jnp.concatenate([a_ref[...], b_ref[...]], axis=1)
+    both = jnp.concatenate([stay_ref[...], came], axis=0)
+    result = jnp.dot(both, weight_ref[...], preferred_element_type=F32).astype(BF16)
+    keep_ref[...] = result[:rows]
+    send_ref[...] = result[rows:]
+
+
+def project(stay, came_a, came_b, weight):
+    rows, depth = stay.shape
+    width = weight.shape[1]
+    tile = 512 if width % 512 == 0 else width
+    fixed = [pl.BlockSpec(x.shape, lambda i: (0, 0)) for x in (stay, came_a, came_b)]
+    out_spec = pl.BlockSpec((rows, tile), lambda i: (0, i))
+    shape = jax.ShapeDtypeStruct((rows, width), BF16)
+    return pl.pallas_call(
+        project_kernel,
+        grid=(width // tile,),
         out_shape=(shape, shape),
-        in_specs=[VMEM] * (PLANE + len(pieces)),
-        out_specs=(VMEM, VMEM),
-        scratch_shapes=[pltpu.VMEM((depth, width), BF16)],
-        compiler_params=PARAMS,
-        cost_estimate=cost(2 * PLANE * rows * depth * width, 6 << 20),
-        name="product",
-    )(*hidden, *pieces)
+        in_specs=fixed + [pl.BlockSpec((depth, tile), lambda i: (0, i))],
+        out_specs=(out_spec, out_spec),
+        compiler_params=PARAMS,
+        cost_estimate=cost(0, 15 << 20),
+        name="project",
+    )(stay, came_a, came_b, weight)
+
+
+def split_kernel(x_ref, *outs):
+    base = 0
+    for out in outs:
+        out[...] = x_ref[:, base : base + out.shape[1]]
+        base += out.shape[1]
+
+
+def split_columns(x, widths):
+    return pl.pallas_call(
+        split_kernel,
+        out_shape=tuple(jax.ShapeDtypeStruct((x.shape[0], w), x.dtype) for w in widths),
+        in_specs=[VMEM],
+        out_specs=(VMEM,) * len(widths),
+        compiler_params=PARAMS,
+        cost_estimate=cost(0, 2 << 20),
+        name="split_columns",
+    )(x)
+
+
+def stack_kernel(*refs):
+    *parts, out = refs
+    rows = parts[0].shape[0]
+    for i, part in enumerate(parts):
+        out[i * rows : (i + 1) * rows, :] = part[...]
+
+
+def stack_rows(parts):
+    rows, width = parts[0].shape
+    return pl.pallas_call(
+        stack_kernel,
+        out_shape=jax.ShapeDtypeStruct((len(parts) * rows, width), parts[0].dtype),
+        in_specs=[VMEM] * len(parts),
+        out_specs=VMEM,
+        compiler_params=PARAMS,
+        cost_estimate=cost(0, 2 << 20),
+        name="stack_rows",
+    )(*parts)
 
 
 def swap_units(x):
@@ -392,9 +565,9 @@
     return jnp.where(place % 2 == 1, (place + 1) // 2, (length - place // 2) % length)
 
 
-def chunk_edges(width):
-    third = width // 3 // 128 * 128
-    return [0, third, 2 * third, width]
+def chunk_widths(width):
+    first = width * 5 // 12 // 128 * 128
+    return [first, width - first]
 
 
 def on_device(
@@ -436,34 +609,31 @@
     def pass_on(x):
         return lax.ppermute(x, "req", ring_pairs)
 
-    edges = chunk_edges(width)
-    a, b, c = ([down_weight[:, lo:hi]] for lo, hi in zip(edges[:-1], edges[1:]))
-    started = [a[0], b[0], c[0]]
-    for chunk in (a, b, c):
+    widths = chunk_widths(width // 2)
+    kept, sent = cut(unit, down_weight, widths)
+    a, b = ([stack_rows([k, swap_units(s)])] for k, s in zip(kept, sent))
+    started = [a[0], b[0]]
+    for chunk in (a, b):
         chunk.append(pass_on(chunk[-1]))
 
     def go_round(chunk, *others):
         chunk.append(pass_on(after(chunk[-1], *others)))
-
-    where = jnp.stack([req, u])
-    mine, other = spread(where, after(ffn_hidden, *started), 2 * block_rows, layers)
-    attn, pages_held, pages_leave = attend(
-        page_table, ctx_pages, page_owner[:, :, 0], unit, after(queries, mine), kv_new, kv_pool
-    )
-    came = swap_units(after(other, a[1], b[1], c[1], attn))
 
     def plane_swap(x, d):
         return lax.ppermute(
             x, "req", [(r, r - r % PLANE + ((r % PLANE) ^ d)) for r in range(n_req)]
         )
 
+    mine = spread(req.reshape(1), after(ffn_hidden, *started), 2 * block_rows, layers)
+    hidden = [plane_swap(x, d) if d else x for d, x in enumerate(mine)]
+    attn, pages_held, pages_leave = attend(
+        page_table, ctx_pages, page_owner[:, :, 0], unit, after(queries, mine[0]), kv_new, kv_pool
+    )
     go_round(a, attn)
-    go_round(b, attn)
-    hidden = [jnp.concatenate([mine[d], came[d]], axis=0) for d in range(PLANE)]
-    stay, leave, state_held, state_leave = state_space(
+    stay, leave_a, leave_b, state_held, state_leave = state_space(
         unit,
         skip_gain,
-        after(attn, *hidden),
+        after(attn, a[1]),
         ssm_x,
         ssm_z,
         ssm_bc,
@@ -473,56 +643,45 @@
         ssm_norm_gain[None, :],
         ssm_state,
     )
-    hidden = [plane_swap(x, d) if d else x for d, x in enumerate(hidden)]
-    leave, state_leave, pages_leave = after(
-        (leave, state_leave, pages_leave), a[2], b[2], *hidden[1:]
+    go_round(b, stay)
+    leave_came = [swap_units(x) for x in after((leave_a, leave_b), b[1], a[2 % len(a)])]
+    hidden = after(hidden, stay)
+    gathered = after(stack_rows(hidden), *leave_came)
+    hidden = list(hidden) + [swap_units(gathered)]
+    mixed, mixed_leave = project(stay, *leave_came, out_weight)
+    while len(a) < layers:
+        go_round(a, mixed)
+    mixed_leave, state_leave, pages_leave = after((mixed_leave, state_leave, pages_leave), mixed)
+    decode_kv, decode_state, mixed = settle(
+        unit,
+        swap_units(pages_leave),
+        swap_units(state_leave),
+        pages_held,
+        state_held,
+        after(mixed, hidden[-1]),
     )
-    go_round(a, stay)
-    go_round(b, stay)
-    leave_came = swap_units(leave)
-    pages_came = swap_units(pages_leave)
-    state_came = swap_units(state_leave)
-    decode_kv, decode_state, stay = settle(
-        unit, pages_came, state_came, pages_held, state_held, stay
-    )
-    exchanged = jnp.concatenate([stay, leave_came], axis=0)
-    mixed = jnp.dot(exchanged, out_weight, preferred_element_type=F32).astype(BF16)
-    mixed_came = swap_units(mixed[tok_rows:])
-    for chunk in (a, b):
-        while len(chunk) < layers:
-            go_round(chunk)
-
-    def half_sums(chunk, then, *others):
-        keep, send = product(hidden, chunk[:-1] + [after(chunk[-1], *others)])
-        return keep, swap_units(after(send, *then))
-
-    def summed(keep, came):
-        total = keep.astype(F32) + came.astype(F32)
-        return total[0], [total[d].astype(BF16) for d in range(1, PLANE)]
-
-    def gathered(own, parts):
-        return [own] + [plane_swap(x, d) for d, x in enumerate(parts, 1)]
-
-    keep_a, came_a = half_sums(a, b[-1:], mixed)
-    go_round(c, b[-1])
-    sum_a = summed(keep_a, came_a)
-    keep_b, came_b = half_sums(b, c[-1:], *sum_a[1])
-    sum_a = gathered(*sum_a)
-    while len(c) < layers:
-        go_round(c)
-    came_b = after(came_b, *sum_a)
-    sum_b = gathered(*summed(keep_b, came_b))
-    sum_c = gathered(*summed(*half_sums(c, (), came_b)))
-    outs = []
-    for lo, hi, parts in zip(edges[:-1], edges[1:], (sum_a, sum_b, sum_c)):
-        total = parts[0]
-        for part in parts[1:]:
-            total = total + part.astype(F32)
-        base = resid[:, lo:hi].astype(F32) + (
-            mixed[:tok_rows, lo:hi].astype(F32) + mixed_came[:, lo:hi].astype(F32)
-        )
-        outs.append((base + total).astype(BF16))
-    return (jnp.concatenate(outs, axis=1), decode_kv, decode_state)
+    mixed_came = swap_units(mixed_leave)
+    while len(b) < layers - 1:
+        go_round(b, mixed)
+    b_last = b[-1]
+    split = b_last.shape[1] // 256 * 128
+    ends = ((0, split), (split, b_last.shape[1]))
+    last = [pass_on(x) for x in split_columns(b_last, [hi - lo for lo, hi in ends])]
+
+    own, parts = product(unit, hidden, a[:-1] + [after(a[-1], mixed, mixed_came)])
+    sums, received = [], [plane_swap(x, d) for d, x in enumerate(parts, 1)]
+    sums.append(total(own, received))
+    order = parts
+    for (lo, hi), end in zip(ends, last):
+        own, parts = product(unit, hidden, b + [after(end, *order)], lo)
+        parts = after(parts, *received)
+        received = [plane_swap(x, d) for d, x in enumerate(parts, 1)]
+        order = sums[-1]
+        sums.append(total(own, after(received, *order)))
+    kept, leave = zip(*sums)
+    came = [swap_units(x) for x in leave]
+    layer_out = finish(unit, resid, mixed, mixed_came, kept, came)
+    return (layer_out, decode_kv, decode_state)
 
 
 def solution(mesh):

time: 140 us -> 134 us (0.957)
  Pallas kernels: 36.2 us -> 46 us
  matrix products: 8.84 us -> 0 us
  waiting for transfers between devices: 56.8 us -> 48.3 us
  local copies, waits for them, and re-layouts: 4.75 us -> 10.1 us
  other arithmetic: 4.01 us -> 0 us
    ppermute x12, waiting for transfers between devices: 33.4 us -> 12.3 us  [plane_swap(): lax.ppermute(x, 'req', [(r, r - r % PLANE + (r % PLANE ^ d)) for r in ran...]
    ppermute x9 -> x7, waiting for transfers between devices: 18.8 us -> 33.3 us  [pass_on(): return lax.ppermute(x, 'req', ring_pairs)]
    pallas_call x4 -> x14, Pallas kernels: 13.2 us -> 23.1 us  [the longest x3 11 us: product(): pl.pallas_call(functools.partial(product_kernel, len(pieces), low), out_s...]
    dot_general x1 -> x0, matrix products: 8.84 us -> none  [on_device(): jnp.dot(exchanged, out_weight, preferred_element_type=F32).astype(BF16)]
    unnamed x37 -> x43, local copies, waits for them, and re-layouts: 1.88 us -> 10.1 us
    ppermute x8 -> x11, waiting for transfers between devices: 4.6 us -> 2.64 us  [swap_units(): return lax.ppermute(x, 'unit', [(0, 1), (1, 0)])]
    ppermute x8 -> x11, starting transfers between devices: 1.15 us -> 2.8 us  [swap_units(): return lax.ppermute(x, 'unit', [(0, 1), (1, 0)])]
    another operation x3 -> x0, other arithmetic: 1.52 us -> none
  transfers between devices with their start and end apart: 29 -> 30, of which waited for: 15 -> 12; matrix products, arithmetic and copies ran while one was open for 9% -> 0% of each run, Pallas kernels for 24% -> 33%
where the time goes in v4:
time: 134 us; the launch traced here: 133 us
  waiting for transfers between devices  48.3 us (36%)
  Pallas kernels  46 us (34%)
  starting transfers between devices  27.3 us (20%)
  local copies, waits for them, and re-layouts  10.1 us (8%)
  between operations  1.66 us (1%)
    ppermute x7, waiting for transfers between devices, pass_on(): return lax.ppermute(x, 'req', ring_pairs)  33.3 us
    ppermute x12, starting transfers between devices, plane_swap(): lax.ppermute(x, 'req', [(r, r - r % PLANE + (r % PLANE ^ d)) for r in ran...  14.1 us
    ppermute x12, waiting for transfers between devices, plane_swap(): lax.ppermute(x, 'req', [(r, r - r % PLANE + (r % PLANE ^ d)) for r in ran...  12.3 us
    pallas_call x1, Pallas kernels, attend(): pl.pallas_call(attend_kernel, out_shape=(jax.ShapeDtypeStruct(queries.sha...  11.4 us
    pallas_call x3, Pallas kernels, product(): pl.pallas_call(functools.partial(product_kernel, len(pieces), low), out_s...  11 us
    ppermute x7, starting transfers between devices, pass_on(): return lax.ppermute(x, 'req', ring_pairs)  10.5 us
    unnamed x43, local copies, waits for them, and re-layouts  10.1 us
    pallas_call x1, Pallas kernels, state_space(): pl.pallas_call(state_kernel, out_shape=(jax.ShapeDtypeStruct((length, hal...  9.99 us
  transfers between devices with their start and end apart: 30, of which 12 were waited for; matrix products, arithmetic and copies ran while one was open for 0% of the time, Pallas kernels for 33%

profile of v4, /device:TPU:0, one launch (start us, length us, event | category | flops | bytes accessed | tf_op | source)
XLA Modules:
  0.0 133.4 jit_solution(11250797233204839662)
XLA Ops:
  3.7 3.0 %collective-permute-start.2 = (bf16[384,640]{1,0:T(8,128)(2,1)S(1)}, bf16[384,640]{1,0:T(8,128)(2,1)}, u32[]{:S(2)}, u32[]{:S(2)}) collective-permute-start(bf16[384,640]{1,0:T(8,128)(2,1)S(1)} %stack_rows.3.refs_5_), channel_id=1, source_target_pairs={{0,8},{2,10},{4,12},{6,14},{8,24},{10,26},{12,28},{14,30},{24,16},... | collective-permute-start | bytes 1474568 | tf_op jit(solution)/shard_map/ppermute | solution.py:610
  6.8 2.6 %collective-permute-start.3 = (bf16[384,896]{1,0:T(8,128)(2,1)S(1)}, bf16[384,896]{1,0:T(8,128)(2,1)S(1)}, u32[]{:S(2)}, u32[]{:S(2)}) collective-permute-start(bf16[384,896]{1,0:T(8,128)(2,1)S(1)} %stack_rows.4.refs_5_), channel_id=1, source_target_pairs={{0,8},{2,10},{4,12},{6,14},{8,24},{10,26},{12,28},{14,30},{24,16},... | collective-permute-start | bytes 2064392 | tf_op jit(solution)/shard_map/ppermute | solution.py:610
  11.5 1.5 %spread.1 = (bf16[128,1536]{1,0:T(8,128)(2,1)S(1)}, bf16[128,1536]{1,0:T(8,128)(2,1)}, bf16[128,1536]{1,0:T(8,128)(2,1)}, bf16[128,1536]{1,0:T(8,128)(2,1)}) custom-call(s32[1]{0:T(128)} %bitcast.2.req, bf16[128,6144]{1,0:T(8,128)(2,1)S(1)} %copy-done.1), custom_call_target="tpu_custom_call" | custom-call | tf_op jit(solution)/shard_map/spread/pallas_call | solution.py:376
  14.5 11.4 %attend.1 = (bf16[128,1536]{1,0:T(8,128)(2,1)S(1)}, bf16[14,128,512]{2,1,0:T(8,128)(2,1)}, bf16[7,128,512]{2,1,0:T(8,128)(2,1)S(1)}) custom-call(s32[1,13]{1,0:T(1,128)S(1)} %copy-done.12, s32[1]{0:T(128)S(6)} %copy.29.ctx, s32[1,13]{1,0:T(1,128)S(1)} %bitcast.7, s32[1]{0:T(128)} %bitcast.unit, bf16[128,1536]{1,0:T(8,128)(2,1)S(1)} %copy-done.6, ...), custom_call_target="tpu_custom_call" | custom-call | tf_op jit(solution)/shard_map/attend/pallas_call | solution.py:128
  28.1 1.5 %collective-permute-start.10 = (bf16[128,1536]{1,0:T(8,128)(2,1)}, bf16[128,1536]{1,0:T(8,128)(2,1)S(1)}, u32[]{:S(2)}, u32[]{:S(2)}) collective-permute-start(bf16[128,1536]{1,0:T(8,128)(2,1)} %get-tuple-element.100), channel_id=1, source_target_pairs={{0,4},{2,6},{4,0},{6,2},{8,12},{10,14},{12,8},{14,10},{16,20},{18,... | collective-permute-start | bytes 1179656 | tf_op jit(solution)/shard_map/ppermute | solution.py:623
  35.9 10.0 %state_space.1 = (bf16[128,2304]{1,0:T(8,128)(2,1)S(1)}, bf16[128,1152]{1,0:T(8,128)(2,1)S(1)}, bf16[128,1152]{1,0:T(8,128)(2,1)S(1)}, f32[2,12,128,256]{3,2,1,0:T(8,128)}, bf16[12,128,256]{2,1,0:T(8,128)(2,1)S(1)}) custom-call(s32[1]{0:T(128)} %bitcast.unit, f32[24]{0:T(128)S(1)} %copy-done.14, bf16[128,1536]{1,0:T(8,128)(2,1)S(1)} %copy-done.8, ...), custom_call_target="tpu_custom_call" | custom-call | tf_op jit(solution)/shard_map/state_space/pallas_call | solution.py:253
  48.7 8.6 %project.1 = (bf16[128,3072]{1,0:T(8,128)(2,1)S(1)}, bf16[128,3072]{1,0:T(8,128)(2,1)S(1)}) custom-call(bf16[128,2304]{1,0:T(8,128)(2,1)S(1)} %get-tuple-element.85.stay_ref, bf16[128,1152]{1,0:T(8,128)(2,1)S(1)} %collective-permute-done.5.a_ref, bf16[128,1152]{1,0:T(8,128)(2,1)S(1)} %collective-permute-done.6.b_ref, bf16[2304,3072]{1,0:T(8,128)(2,1)} %weight_ref.3), custom_call_target="tpu_custom_call" | custom-call | tf_op jit(solution)/shard_map/project/pallas_call | solution.py:499
  58.8 1.7 %collective-permute-start.14 = (bf16[384,640]{1,0:T(8,128)(2,1)}, bf16[384,640]{1,0:T(8,128)(2,1)S(1)}, u32[]{:S(2)}, u32[]{:S(2)}) collective-permute-start(bf16[384,640]{1,0:T(8,128)(2,1)} %collective-permute-done.4.refs_7_), channel_id=1, source_target_pairs={{0,8},{2,10},{4,12},{6,14},{8,24},{10,26},{12,28},{14,30},{24,16},... | collective-permute-start | bytes 1474568 | tf_op jit(solution)/shard_map/ppermute | solution.py:610
  61.1 1.5 %settle.1 = (bf16[14,128,512]{2,1,0:T(8,128)(2,1)}, f32[2,12,128,256]{3,2,1,0:T(8,128)}, bf16[128,3072]{1,0:T(8,128)(2,1)S(1)}) custom-call(s32[1]{0:T(128)} %bitcast.unit, bf16[7,128,512]{2,1,0:T(8,128)(2,1)S(1)} %collective-permute-done.7.pages, ...), custom_call_target="tpu_custom_call", output_to_operand_aliasing={{0}: (3, {}), {1}: (4, {}), {2}: (5, {})} | custom-call | tf_op jit(solution)/shard_map/settle/pallas_call | solution.py:290
  62.6 24.7 %collective-permute-done.14.refs_8_ = bf16[384,640]{1,0:T(8,128)(2,1)S(1)} collective-permute-done((bf16[384,640]{1,0:T(8,128)(2,1)}, bf16[384,640]{1,0:T(8,128)(2,1)S(1)}, u32[]{:S(2)}, u32[]{:S(2)}) %collective-permute-start.14) | collective-permute-done | bytes 491552 | tf_op jit(solution)/shard_map/ppermute | solution.py:610
  87.2 4.4 %product.3 = (f32[256,640]{1,0:T(8,128)S(1)}, bf16[256,640]{1,0:T(8,128)(2,1)S(1)}, bf16[256,640]{1,0:T(8,128)(2,1)S(1)}, bf16[256,640]{1,0:T(8,128)(2,1)S(1)}) custom-call(s32[1]{0:T(128)} %bitcast.unit, bf16[128,1536]{1,0:T(8,128)(2,1)S(1)} %get-tuple-element.102.refs_0_, bf16[128,1536]{1,0:T(8,128)(2,1)S(1)} %collective-permute-done.9.refs_1_, ...), custom_call_target="tpu_custom_call" | custom-call | tf_op jit(solution)/shard_map/product/pallas_call | solution.py:414
  91.6 1.6 %collective-permute-start.15 = (bf16[256,640]{1,0:T(8,128)(2,1)S(1)}, bf16[256,640]{1,0:T(8,128)(2,1)S(1)}, u32[]{:S(2)}, u32[]{:S(2)}) collective-permute-start(bf16[256,640]{1,0:T(8,128)(2,1)S(1)} %get-tuple-element.113), channel_id=1, source_target_pairs={{0,2},{2,0},{4,6},{6,4},{8,10},{10,8},{12,14},{14,12},{16,18},{18,... | collective-permute-start | bytes 983048 | tf_op jit(solution)/shard_map/ppermute | solution.py:623
  93.2 1.5 %collective-permute-start.16 = (bf16[256,640]{1,0:T(8,128)(2,1)S(1)}, bf16[256,640]{1,0:T(8,128)(2,1)S(1)}, u32[]{:S(2)}, u32[]{:S(2)}) collective-permute-start(bf16[256,640]{1,0:T(8,128)(2,1)S(1)} %get-tuple-element.114), channel_id=1, source_target_pairs={{0,4},{2,6},{4,0},{6,2},{8,12},{10,14},{12,8},{14,10},{16,20},{18,... | collective-permute-start | bytes 983048 | tf_op jit(solution)/shard_map/ppermute | solution.py:623
  95.3 2.2 %collective-permute-start.23 = (bf16[384,512]{1,0:T(8,128)(2,1)S(1)}, bf16[384,512]{1,0:T(8,128)(2,1)S(1)}, u32[]{:S(2)}, u32[]{:S(2)}) collective-permute-start(bf16[384,512]{1,0:T(8,128)(2,1)S(1)} %get-tuple-element.132), channel_id=1, source_target_pairs={{0,8},{2,10},{4,12},{6,14},{8,24},{10,26},{12,28},{14,30},{24,16},... | collective-permute-start | bytes 1179656 | tf_op jit(solution)/shard_map/ppermute | solution.py:610
  97.5 8.7 %collective-permute-done.19.refs_8_ = bf16[384,384]{1,0:T(8,128)(2,1)S(1)} collective-permute-done((bf16[384,384]{1,0:T(8,128)(2,1)S(1)}, bf16[384,384]{1,0:T(8,128)(2,1)S(1)}, u32[]{:S(2)}, u32[]{:S(2)}) %collective-permute-start.19) | collective-permute-done | bytes 294944 | tf_op jit(solution)/shard_map/ppermute | solution.py:610
  106.2 3.3 %product.4 = (f32[256,384]{1,0:T(8,128)S(1)}, bf16[256,384]{1,0:T(8,128)(2,1)S(1)}, bf16[256,384]{1,0:T(8,128)(2,1)S(1)}, bf16[256,384]{1,0:T(8,128)(2,1)S(1)}) custom-call(s32[1]{0:T(128)} %bitcast.unit, bf16[128,1536]{1,0:T(8,128)(2,1)S(1)} %get-tuple-element.102.refs_0_, bf16[128,1536]{1,0:T(8,128)(2,1)S(1)} %collective-permute-done.9.refs_1_, ...), custom_call_target="tpu_custom_call" | custom-call | tf_op jit(solution)/shard_map/product/pallas_call | solution.py:414
  109.5 1.6 %collective-permute-start.20 = (bf16[256,384]{1,0:T(8,128)(2,1)S(1)}, bf16[256,384]{1,0:T(8,128)(2,1)S(1)}, u32[]{:S(2)}, u32[]{:S(2)}) collective-permute-start(bf16[256,384]{1,0:T(8,128)(2,1)S(1)} %get-tuple-element.124), channel_id=1, source_target_pairs={{0,2},{2,0},{4,6},{6,4},{8,10},{10,8},{12,14},{14,12},{16,18},{18,... | collective-permute-start | bytes 589832 | tf_op jit(solution)/shard_map/ppermute | solution.py:623
  111.1 1.5 %collective-permute-start.21 = (bf16[256,384]{1,0:T(8,128)(2,1)S(1)}, bf16[256,384]{1,0:T(8,128)(2,1)S(1)}, u32[]{:S(2)}, u32[]{:S(2)}) collective-permute-start(bf16[256,384]{1,0:T(8,128)(2,1)S(1)} %get-tuple-element.125), channel_id=1, source_target_pairs={{0,4},{2,6},{4,0},{6,2},{8,12},{10,14},{12,8},{14,10},{16,20},{18,... | collective-permute-start | bytes 589832 | tf_op jit(solution)/shard_map/ppermute | solution.py:623
  113.2 3.3 %product.5 = (f32[256,512]{1,0:T(8,128)S(1)}, bf16[256,512]{1,0:T(8,128)(2,1)S(1)}, bf16[256,512]{1,0:T(8,128)(2,1)S(1)}, bf16[256,512]{1,0:T(8,128)(2,1)S(1)}) custom-call(s32[1]{0:T(128)} %bitcast.unit, bf16[128,1536]{1,0:T(8,128)(2,1)S(1)} %get-tuple-element.102.refs_0_, bf16[128,1536]{1,0:T(8,128)(2,1)S(1)} %collective-permute-done.9.refs_1_, ...), custom_call_target="tpu_custom_call" | custom-call | tf_op jit(solution)/shard_map/product/pallas_call | solution.py:414
  116.5 2.0 %collective-permute-done.21.refs_1_ = bf16[256,384]{1,0:T(8,128)(2,1)S(1)} collective-permute-done((bf16[256,384]{1,0:T(8,128)(2,1)S(1)}, bf16[256,384]{1,0:T(8,128)(2,1)S(1)}, u32[]{:S(2)}, u32[]{:S(2)}) %collective-permute-start.21) | collective-permute-done | bytes 196640 | tf_op jit(solution)/shard_map/ppermute | solution.py:623
  118.5 1.7 %collective-permute-done.22.refs_2_ = bf16[256,384]{1,0:T(8,128)(2,1)S(1)} collective-permute-done((bf16[256,384]{1,0:T(8,128)(2,1)S(1)}, bf16[256,384]{1,0:T(8,128)(2,1)S(1)}, u32[]{:S(2)}, u32[]{:S(2)}) %collective-permute-start.22) | collective-permute-done | bytes 196640 | tf_op jit(solution)/shard_map/ppermute | solution.py:623
  122.0 1.8 %collective-permute-start.26 = (bf16[256,512]{1,0:T(8,128)(2,1)S(1)}, bf16[256,512]{1,0:T(8,128)(2,1)S(1)}, u32[]{:S(2)}, u32[]{:S(2)}) collective-permute-start(bf16[256,512]{1,0:T(8,128)(2,1)S(1)} %get-tuple-element.140), channel_id=1, source_target_pairs={{0,6},{2,4},{4,2},{6,0},{8,14},{10,12},{12,10},{14,8},{16,22},{18,... | collective-permute-start | bytes 786440 | tf_op jit(solution)/shard_map/ppermute | solution.py:623
  123.8 2.9 %collective-permute-done.24.refs_0_ = bf16[256,512]{1,0:T(8,128)(2,1)S(1)} collective-permute-done((bf16[256,512]{1,0:T(8,128)(2,1)S(1)}, bf16[256,512]{1,0:T(8,128)(2,1)S(1)}, u32[]{:S(2)}, u32[]{:S(2)}) %collective-permute-start.24) | collective-permute-done | bytes 262176 | tf_op jit(solution)/shard_map/ppermute | solution.py:623
  126.7 2.5 %collective-permute-done.25.refs_1_ = bf16[256,512]{1,0:T(8,128)(2,1)S(1)} collective-permute-done((bf16[256,512]{1,0:T(8,128)(2,1)S(1)}, bf16[256,512]{1,0:T(8,128)(2,1)S(1)}, u32[]{:S(2)}, u32[]{:S(2)}) %collective-permute-start.25) | collective-permute-done | bytes 262176 | tf_op jit(solution)/shard_map/ppermute | solution.py:623
  (96 shorter events, 26.4 us)
Async XLA Ops:
  2.5 4.2 %collective-permute-start.1 = (bf16[192,896]{1,0:T(8,128)(2,1)S(1)}, bf16[192,896]{1,0:T(8,128)(2,1)S(1)}, u32[]{:S(2)}, u32[]{:S(2)}) collective-permute-start(bf16[192,896]{1,0:T(8,128)(2,1)S(1)} %get-tuple-element.79), channel_id=1, source_target_pairs={{0,1},{1,0},{2,3},{3,2},{4,5},{5,4},{6,7},{7,6},{8,9},{9,8},{10,11... | collective-permute-start | bytes 1032200 | tf_op jit(solution)/shard_map/ppermute | solution.py:551
  3.7 24.0 %collective-permute-start.2 = (bf16[384,640]{1,0:T(8,128)(2,1)S(1)}, bf16[384,640]{1,0:T(8,128)(2,1)}, u32[]{:S(2)}, u32[]{:S(2)}) collective-permute-start(bf16[384,640]{1,0:T(8,128)(2,1)S(1)} %stack_rows.3.refs_5_), channel_id=1, source_target_pairs={{0,8},{2,10},{4,12},{6,14},{8,24},{10,26},{12,28},{14,30},{24,16},... | collective-permute-start | bytes 1474568 | tf_op jit(solution)/shard_map/ppermute | solution.py:610
  6.8 39.1 %collective-permute-start.3 = (bf16[384,896]{1,0:T(8,128)(2,1)S(1)}, bf16[384,896]{1,0:T(8,128)(2,1)S(1)}, u32[]{:S(2)}, u32[]{:S(2)}) collective-permute-start(bf16[384,896]{1,0:T(8,128)(2,1)S(1)} %stack_rows.4.refs_5_), channel_id=1, source_target_pairs={{0,8},{2,10},{4,12},{6,14},{8,24},{10,26},{12,28},{14,30},{24,16},... | collective-permute-start | bytes 2064392 | tf_op jit(solution)/shard_map/ppermute | solution.py:610
  27.7 18.3 %collective-permute-start.4 = (bf16[384,640]{1,0:T(8,128)(2,1)}, bf16[384,640]{1,0:T(8,128)(2,1)}, u32[]{:S(2)}, u32[]{:S(2)}) collective-permute-start(bf16[384,640]{1,0:T(8,128)(2,1)} %collective-permute-done.2.refs_6_), channel_id=1, source_target_pairs={{0,8},{2,10},{4,12},{6,14},{8,24},{10,26},{12,28},{14,30},{24,16},... | collective-permute-start | bytes 1474568 | tf_op jit(solution)/shard_map/ppermute | solution.py:610
  28.1 19.2 %collective-permute-start.10 = (bf16[128,1536]{1,0:T(8,128)(2,1)}, bf16[128,1536]{1,0:T(8,128)(2,1)S(1)}, u32[]{:S(2)}, u32[]{:S(2)}) collective-permute-start(bf16[128,1536]{1,0:T(8,128)(2,1)} %get-tuple-element.100), channel_id=1, source_target_pairs={{0,4},{2,6},{4,0},{6,2},{8,12},{10,14},{12,8},{14,10},{16,20},{18,... | collective-permute-start | bytes 1179656 | tf_op jit(solution)/shard_map/ppermute | solution.py:623
  29.6 17.7 %collective-permute-start.11 = (bf16[128,1536]{1,0:T(8,128)(2,1)}, bf16[128,1536]{1,0:T(8,128)(2,1)S(1)}, u32[]{:S(2)}, u32[]{:S(2)}) collective-permute-start(bf16[128,1536]{1,0:T(8,128)(2,1)} %get-tuple-element.101), channel_id=1, source_target_pairs={{0,6},{2,4},{4,2},{6,0},{8,14},{10,12},{12,10},{14,8},{16,22},{18,... | collective-permute-start | bytes 1179656 | tf_op jit(solution)/shard_map/ppermute | solution.py:623
  31.1 17.5 %collective-permute-start.9 = (bf16[128,1536]{1,0:T(8,128)(2,1)}, bf16[128,1536]{1,0:T(8,128)(2,1)S(1)}, u32[]{:S(2)}, u32[]{:S(2)}) collective-permute-start(bf16[128,1536]{1,0:T(8,128)(2,1)} %get-tuple-element.99), channel_id=1, source_target_pairs={{0,2},{2,0},{4,6},{6,4},{8,10},{10,8},{12,14},{14,12},{16,18},{18,... | collective-permute-start | bytes 1179656 | tf_op jit(solution)/shard_map/ppermute | solution.py:623
  48.7 10.2 %collective-permute-start.12 = (bf16[512,1536]{1,0:T(8,128)(2,1)S(1)}, bf16[512,1536]{1,0:T(8,128)(2,1)S(1)}, u32[]{:S(2)}, u32[]{:S(2)}) collective-permute-start(bf16[512,1536]{1,0:T(8,128)(2,1)S(1)} %stack_rows.5), channel_id=1, source_target_pairs={{0,1},{1,0},{2,3},{3,2},{4,5},{5,4},{6,7},{7,6},{8,9},{9,8},{10,11... | collective-permute-start | bytes 4718600 | tf_op jit(solution)/shard_map/ppermute | solution.py:551
  57.4 3.7 %collective-permute-start.7 = (bf16[7,128,512]{2,1,0:T(8,128)(2,1)S(1)}, bf16[7,128,512]{2,1,0:T(8,128)(2,1)S(1)}, u32[]{:S(2)}, u32[]{:S(2)}) collective-permute-start(bf16[7,128,512]{2,1,0:T(8,128)(2,1)S(1)} %copy-done.18), channel_id=1, source_target_pairs={{0,1},{1,0},{2,3},{3,2},{4,5},{5,4},{6,7},{7,6},{8,9},{9,8},{10,11... | collective-permute-start | bytes 2752520 | tf_op jit(solution)/shard_map/ppermute | solution.py:551
  57.9 29.3 %collective-permute-start.13 = (bf16[128,3072]{1,0:T(8,128)(2,1)S(1)}, bf16[128,3072]{1,0:T(8,128)(2,1)S(1)}, u32[]{:S(2)}, u32[]{:S(2)}) collective-permute-start(bf16[128,3072]{1,0:T(8,128)(2,1)S(1)} %get-tuple-element.109), channel_id=1, source_target_pairs={{0,1},{1,0},{2,3},{3,2},{4,5},{5,4},{6,7},{7,6},{8,9},{9,8},{10,11... | collective-permute-start | bytes 2359304 | tf_op jit(solution)/shard_map/ppermute | solution.py:551
  58.4 36.8 %collective-permute-start.18 = (bf16[384,896]{1,0:T(8,128)(2,1)S(1)}, bf16[384,896]{1,0:T(8,128)(2,1)S(1)}, u32[]{:S(2)}, u32[]{:S(2)}) collective-permute-start(bf16[384,896]{1,0:T(8,128)(2,1)S(1)} %collective-permute-done.3.refs_6_), channel_id=1, source_target_pairs={{0,8},{2,10},{4,12},{6,14},{8,24},{10,26},{12,28},{14,30},{24,16},... | collective-permute-start | bytes 2064392 | tf_op jit(solution)/shard_map/ppermute | solution.py:610
  58.8 28.4 %collective-permute-start.14 = (bf16[384,640]{1,0:T(8,128)(2,1)}, bf16[384,640]{1,0:T(8,128)(2,1)S(1)}, u32[]{:S(2)}, u32[]{:S(2)}) collective-permute-start(bf16[384,640]{1,0:T(8,128)(2,1)} %collective-permute-done.4.refs_7_), channel_id=1, source_target_pairs={{0,8},{2,10},{4,12},{6,14},{8,24},{10,26},{12,28},{14,30},{24,16},... | collective-permute-start | bytes 1474568 | tf_op jit(solution)/shard_map/ppermute | solution.py:610
  91.6 17.8 %collective-permute-start.15 = (bf16[256,640]{1,0:T(8,128)(2,1)S(1)}, bf16[256,640]{1,0:T(8,128)(2,1)S(1)}, u32[]{:S(2)}, u32[]{:S(2)}) collective-permute-start(bf16[256,640]{1,0:T(8,128)(2,1)S(1)} %get-tuple-element.113), channel_id=1, source_target_pairs={{0,2},{2,0},{4,6},{6,4},{8,10},{10,8},{12,14},{14,12},{16,18},{18,... | collective-permute-start | bytes 983048 | tf_op jit(solution)/shard_map/ppermute | solution.py:623
  93.2 16.3 %collective-permute-start.16 = (bf16[256,640]{1,0:T(8,128)(2,1)S(1)}, bf16[256,640]{1,0:T(8,128)(2,1)S(1)}, u32[]{:S(2)}, u32[]{:S(2)}) collective-permute-start(bf16[256,640]{1,0:T(8,128)(2,1)S(1)} %get-tuple-element.114), channel_id=1, source_target_pairs={{0,4},{2,6},{4,0},{6,2},{8,12},{10,14},{12,8},{14,10},{16,20},{18,... | collective-permute-start | bytes 983048 | tf_op jit(solution)/shard_map/ppermute | solution.py:623
  94.7 14.8 %collective-permute-start.17 = (bf16[256,640]{1,0:T(8,128)(2,1)S(1)}, bf16[256,640]{1,0:T(8,128)(2,1)S(1)}, u32[]{:S(2)}, u32[]{:S(2)}) collective-permute-start(bf16[256,640]{1,0:T(8,128)(2,1)S(1)} %get-tuple-element.115), channel_id=1, source_target_pairs={{0,6},{2,4},{4,2},{6,0},{8,14},{10,12},{12,10},{14,8},{16,22},{18,... | collective-permute-start | bytes 983048 | tf_op jit(solution)/shard_map/ppermute | solution.py:623
  95.3 10.9 %collective-permute-start.19 = (bf16[384,384]{1,0:T(8,128)(2,1)S(1)}, bf16[384,384]{1,0:T(8,128)(2,1)S(1)}, u32[]{:S(2)}, u32[]{:S(2)}) collective-permute-start(bf16[384,384]{1,0:T(8,128)(2,1)S(1)} %get-tuple-element.118), channel_id=1, source_target_pairs={{0,8},{2,10},{4,12},{6,14},{8,24},{10,26},{12,28},{14,30},{24,16},... | collective-permute-start | bytes 884744 | tf_op jit(solution)/shard_map/ppermute | solution.py:610
  95.3 17.9 %collective-permute-start.23 = (bf16[384,512]{1,0:T(8,128)(2,1)S(1)}, bf16[384,512]{1,0:T(8,128)(2,1)S(1)}, u32[]{:S(2)}, u32[]{:S(2)}) collective-permute-start(bf16[384,512]{1,0:T(8,128)(2,1)S(1)} %get-tuple-element.132), channel_id=1, source_target_pairs={{0,8},{2,10},{4,12},{6,14},{8,24},{10,26},{12,28},{14,30},{24,16},... | collective-permute-start | bytes 1179656 | tf_op jit(solution)/shard_map/ppermute | solution.py:610
  109.5 7.0 %collective-permute-start.20 = (bf16[256,384]{1,0:T(8,128)(2,1)S(1)}, bf16[256,384]{1,0:T(8,128)(2,1)S(1)}, u32[]{:S(2)}, u32[]{:S(2)}) collective-permute-start(bf16[256,384]{1,0:T(8,128)(2,1)S(1)} %get-tuple-element.124), channel_id=1, source_target_pairs={{0,2},{2,0},{4,6},{6,4},{8,10},{10,8},{12,14},{14,12},{16,18},{18,... | collective-permute-start | bytes 589832 | tf_op jit(solution)/shard_map/ppermute | solution.py:623
  111.1 7.4 %collective-permute-start.21 = (bf16[256,384]{1,0:T(8,128)(2,1)S(1)}, bf16[256,384]{1,0:T(8,128)(2,1)S(1)}, u32[]{:S(2)}, u32[]{:S(2)}) collective-permute-start(bf16[256,384]{1,0:T(8,128)(2,1)S(1)} %get-tuple-element.125), channel_id=1, source_target_pairs={{0,4},{2,6},{4,0},{6,2},{8,12},{10,14},{12,8},{14,10},{16,20},{18,... | collective-permute-start | bytes 589832 | tf_op jit(solution)/shard_map/ppermute | solution.py:623
  112.6 7.6 %collective-permute-start.22 = (bf16[256,384]{1,0:T(8,128)(2,1)S(1)}, bf16[256,384]{1,0:T(8,128)(2,1)S(1)}, u32[]{:S(2)}, u32[]{:S(2)}) collective-permute-start(bf16[256,384]{1,0:T(8,128)(2,1)S(1)} %get-tuple-element.126), channel_id=1, source_target_pairs={{0,6},{2,4},{4,2},{6,0},{8,14},{10,12},{12,10},{14,8},{16,22},{18,... | collective-permute-start | bytes 589832 | tf_op jit(solution)/shard_map/ppermute | solution.py:623
  120.2 6.5 %collective-permute-start.24 = (bf16[256,512]{1,0:T(8,128)(2,1)S(1)}, bf16[256,512]{1,0:T(8,128)(2,1)S(1)}, u32[]{:S(2)}, u32[]{:S(2)}) collective-permute-start(bf16[256,512]{1,0:T(8,128)(2,1)S(1)} %get-tuple-element.138), channel_id=1, source_target_pairs={{0,2},{2,0},{4,6},{6,4},{8,10},{10,8},{12,14},{14,12},{16,18},{18,... | collective-permute-start | bytes 786440 | tf_op jit(solution)/shard_map/ppermute | solution.py:623
  120.6 8.6 %collective-permute-start.25 = (bf16[256,512]{1,0:T(8,128)(2,1)S(1)}, bf16[256,512]{1,0:T(8,128)(2,1)S(1)}, u32[]{:S(2)}, u32[]{:S(2)}) collective-permute-start(bf16[256,512]{1,0:T(8,128)(2,1)S(1)} %get-tuple-element.139), channel_id=1, source_target_pairs={{0,4},{2,6},{4,0},{6,2},{8,12},{10,14},{12,8},{14,10},{16,20},{18,... | collective-permute-start | bytes 786440 | tf_op jit(solution)/shard_map/ppermute | solution.py:623
  122.0 8.5 %collective-permute-start.26 = (bf16[256,512]{1,0:T(8,128)(2,1)S(1)}, bf16[256,512]{1,0:T(8,128)(2,1)S(1)}, u32[]{:S(2)}, u32[]{:S(2)}) collective-permute-start(bf16[256,512]{1,0:T(8,128)(2,1)S(1)} %get-tuple-element.140), channel_id=1, source_target_pairs={{0,6},{2,4},{4,2},{6,0},{8,14},{10,12},{12,10},{14,8},{16,22},{18,... | collective-permute-start | bytes 786440 | tf_op jit(solution)/shard_map/ppermute | solution.py:623
  123.7 7.4 %collective-permute-start.27 = (bf16[128,640]{1,0:T(8,128)(2,1)S(1)}, bf16[128,640]{1,0:T(8,128)(2,1)S(1)}, u32[]{:S(2)}, u32[]{:S(2)}) collective-permute-start(bf16[128,640]{1,0:T(8,128)(2,1)S(1)} %get-tuple-element.127), channel_id=1, source_target_pairs={{0,1},{1,0},{2,3},{3,2},{4,5},{5,4},{6,7},{7,6},{8,9},{9,8},{10,11... | collective-permute-start | bytes 491528 | tf_op jit(solution)/shard_map/ppermute | solution.py:551
  (27 other events, 189.9 us)

commit v5 on v4

--- a/solution.py
+++ b/solution.py
@@ -302,32 +302,28 @@
     )(unit, pages, state, pages_held, state_held, rows)
 
 
-def cut_kernel(unit, weight_ref, *refs):
-    count = len(refs) // 2
-    kept, sent = refs[:count], refs[count:]
+def cut_kernel(unit, weight_ref, kept, sent):
     half = weight_ref.shape[1] // 2
-    for u in range(2):
+    for u, low_ref, high_ref in ((0, kept, sent), (1, sent, kept)):
 
         @pl.when(unit[0] == u)
         def _():
-            for outs, base in ((kept, u * half), (sent, (1 - u) * half)):
-                for out in outs:
-                    out[...] = weight_ref[:, base : base + out.shape[1]]
-                    base += out.shape[1]
-
-
-def cut(unit, weight, widths):
-    rows = weight.shape[0]
-    outs = pl.pallas_call(
+            low_ref[...] = weight_ref[:, :half]
+            high_ref[...] = weight_ref[:, half:]
+
+
+def cut(unit, weight):
+    rows, width = weight.shape
+    shape = jax.ShapeDtypeStruct((rows, width // 2), weight.dtype)
+    return pl.pallas_call(
         cut_kernel,
-        out_shape=tuple(jax.ShapeDtypeStruct((rows, w), weight.dtype) for w in widths * 2),
+        out_shape=(shape, shape),
         in_specs=[SMEM, VMEM],
-        out_specs=(VMEM,) * (2 * len(widths)),
+        out_specs=(VMEM, VMEM),
         compiler_params=PARAMS,
         cost_estimate=cost(0, 3 << 20),
         name="cut",
     )(unit, weight)
-    return outs[: len(widths)], outs[len(widths) :]
 
 
 def block_of(req, d, k, layers):
@@ -385,9 +381,10 @@
     )(req, hidden)
 
 
-def product_kernel(count, low, unit, *refs):
-    hidden, pieces = refs[: PLANE + 1], refs[PLANE + 1 : PLANE + 1 + count]
-    own_ref, *parts = refs[PLANE + 1 + count : -1]
+def product_kernel(bases, unit, *refs):
+    count = len(bases)
+    hidden, pieces = refs[: PLANE + 2], refs[PLANE + 2 : PLANE + 2 + count]
+    own_ref, *parts = refs[PLANE + 2 + count : -1]
     weight = refs[-1]
     block_rows = pieces[0].shape[0] // 2
     u = unit[0]
@@ -395,11 +392,12 @@
         for which, place in ((0, u), (1, 1 - u)):
             at = pl.multiple_of((2 * k + place) * block_rows, 16)
             rows = slice(which * block_rows, (which + 1) * block_rows)
-            base = low if piece.shape[1] > weight.shape[1] else 0
+            base = bases[k]
             weight[pl.ds(at, block_rows), :] = piece[rows, base : base + weight.shape[1]]
     rows = hidden[0].shape[0]
     for d in range(PLANE):
-        other = hidden[-1][d * rows : (d + 1) * rows, :]
+        place = d % (PLANE // 2) * rows
+        other = hidden[PLANE + d // (PLANE // 2)][place : place + rows, :]
         both = jnp.concatenate([hidden[d][...], other], axis=0)
         result = jnp.dot(both, weight[...], preferred_element_type=F32)
         if d:
@@ -411,11 +409,12 @@
 def product(unit, hidden, pieces, low=0):
     rows, depth = hidden[0].shape
     width = pieces[-1].shape[1]
+    bases = [0 if x.shape[1] == width else low for x in pieces]
     outs = pl.pallas_call(
-        functools.partial(product_kernel, len(pieces), low),
+        functools.partial(product_kernel, tuple(bases)),
         out_shape=(jax.ShapeDtypeStruct((2 * rows, width), F32),)
         + (jax.ShapeDtypeStruct((2 * rows, width), BF16),) * (PLANE - 1),
-        in_specs=[SMEM] + [VMEM] * (PLANE + 1 + len(pieces)),
+        in_specs=[SMEM] + [VMEM] * (PLANE + 2 + len(pieces)),
         out_specs=(VMEM,) * PLANE,
         scratch_shapes=[pltpu.VMEM((depth, width), BF16)],
         compiler_params=PARAMS,
@@ -451,7 +450,7 @@
     )(own, *came)
 
 
-def finish_kernel(unit, resid_ref, mixed_ref, mixed_came_ref, *refs):
+def finish_kernel(unit, resid_ref, mixed_ref, low_ref, high_ref, *refs):
     count = len(refs) // 2
     kept, came, out_ref = refs[:count], refs[count:-1], refs[-1]
     half = out_ref.shape[1] // 2
@@ -459,10 +458,13 @@
 
         @pl.when(unit[0] == u)
         def _():
-            for group, base in ((kept, u * half), (came, (1 - u) * half)):
+            for group, which in ((kept, u), (came, 1 - u)):
+                base = 0
+                other_ref = high_ref if which else low_ref
                 for ref in group:
-                    span = slice(base, base + ref.shape[1])
-                    mixed = mixed_ref[:, span].astype(F32) + mixed_came_ref[:, span].astype(F32)
+                    span = slice(which * half + base, which * half + base + ref.shape[1])
+                    mixed = mixed_ref[:, span].astype(F32)
+                    mixed = mixed + other_ref[:, base : base + ref.shape[1]].astype(F32)
                     sums = resid_ref[:, span].astype(F32) + mixed + ref[...].astype(F32)
                     out_ref[:, span] = sums.astype(BF16)
                     base += ref.shape[1]
@@ -472,36 +474,51 @@
     return pl.pallas_call(
         finish_kernel,
         out_shape=jax.ShapeDtypeStruct(resid.shape, BF16),
-        in_specs=[SMEM] + [VMEM] * (3 + len(kept) + len(came)),
+        in_specs=[SMEM] + [VMEM] * (4 + len(kept) + len(came)),
         out_specs=VMEM,
         compiler_params=PARAMS,
         cost_estimate=cost(0, 4 << 20),
         name="finish",
-    )(unit, resid, mixed, mixed_came, *kept, *came)
-
-
-def project_kernel(stay_ref, a_ref, b_ref, weight_ref, keep_ref, send_ref):
+    )(unit, resid, mixed, *mixed_came, *kept, *came)
+
+
+def project_kernel(stay_ref, a_ref, b_ref, weight_ref, keep_ref, low_ref, high_ref):
     rows = stay_ref.shape[0]
+    half = pl.num_programs(0) // 2
     came = jnp.concatenate([a_ref[...], b_ref[...]], axis=1)
     both = jnp.concatenate([stay_ref[...], came], axis=0)
     result = jnp.dot(both, weight_ref[...], preferred_element_type=F32).astype(BF16)
     keep_ref[...] = result[:rows]
-    send_ref[...] = result[rows:]
+
+    @pl.when(pl.program_id(0) < half)
+    def _():
+        low_ref[...] = result[rows:]
+
+    @pl.when(pl.program_id(0) >= half)
+    def _():
+        high_ref[...] = result[rows:]
 
 
 def project(stay, came_a, came_b, weight):
     rows, depth = stay.shape
     width = weight.shape[1]
-    tile = 512 if width % 512 == 0 else width
+    tile = 512 if width % 1024 == 0 else width // 2
+    half = width // tile // 2
     fixed = [pl.BlockSpec(x.shape, lambda i: (0, 0)) for x in (stay, came_a, came_b)]
-    out_spec = pl.BlockSpec((rows, tile), lambda i: (0, i))
-    shape = jax.ShapeDtypeStruct((rows, width), BF16)
     return pl.pallas_call(
         project_kernel,
-        grid=(width // tile,),
-        out_shape=(shape, shape),
+        grid=(2 * half,),
+        out_shape=(
+            jax.ShapeDtypeStruct((rows, width), BF16),
+            jax.ShapeDtypeStruct((rows, width // 2), BF16),
+            jax.ShapeDtypeStruct((rows, width // 2), BF16),
+        ),
         in_specs=fixed + [pl.BlockSpec((depth, tile), lambda i: (0, i))],
-        out_specs=(out_spec, out_spec),
+        out_specs=(
+            pl.BlockSpec((rows, tile), lambda i: (0, i)),
+            pl.BlockSpec((rows, tile), lambda i: (0, jnp.minimum(i, half - 1))),
+            pl.BlockSpec((rows, tile), lambda i: (0, jnp.maximum(i - half, 0))),
+        ),
         compiler_params=PARAMS,
         cost_estimate=cost(0, 15 << 20),
         name="project",
@@ -566,8 +583,8 @@
 
 
 def chunk_widths(width):
-    first = width * 5 // 12 // 128 * 128
-    return [first, width - first]
+    first, last = width // 4 // 128 * 128, width // 3 // 128 * 128
+    return [first, width - first - last, last]
 
 
 def on_device(
@@ -609,31 +626,27 @@
     def pass_on(x):
         return lax.ppermute(x, "req", ring_pairs)
 
-    widths = chunk_widths(width // 2)
-    kept, sent = cut(unit, down_weight, widths)
-    a, b = ([stack_rows([k, swap_units(s)])] for k, s in zip(kept, sent))
-    started = [a[0], b[0]]
-    for chunk in (a, b):
-        chunk.append(pass_on(chunk[-1]))
-
-    def go_round(chunk, *others):
-        chunk.append(pass_on(after(chunk[-1], *others)))
+    kept, sent = cut(unit, down_weight)
+    hops = [stack_rows([kept, swap_units(sent)])]
+    if layers > 2:
+        hops.append(pass_on(hops[0]))
 
     def plane_swap(x, d):
         return lax.ppermute(
             x, "req", [(r, r - r % PLANE + ((r % PLANE) ^ d)) for r in range(n_req)]
         )
 
-    mine = spread(req.reshape(1), after(ffn_hidden, *started), 2 * block_rows, layers)
+    mine = spread(req.reshape(1), after(ffn_hidden, hops[0]), 2 * block_rows, layers)
     hidden = [plane_swap(x, d) if d else x for d, x in enumerate(mine)]
     attn, pages_held, pages_leave = attend(
         page_table, ctx_pages, page_owner[:, :, 0], unit, after(queries, mine[0]), kv_new, kv_pool
     )
-    go_round(a, attn)
+    while len(hops) < layers - 1:
+        hops.append(pass_on(after(hops[-1], attn)))
     stay, leave_a, leave_b, state_held, state_leave = state_space(
         unit,
         skip_gain,
-        after(attn, a[1]),
+        after(attn, *hops[1:2]),
         ssm_x,
         ssm_z,
         ssm_bc,
@@ -643,41 +656,33 @@
         ssm_norm_gain[None, :],
         ssm_state,
     )
-    go_round(b, stay)
-    leave_came = [swap_units(x) for x in after((leave_a, leave_b), b[1], a[2 % len(a)])]
     hidden = after(hidden, stay)
-    gathered = after(stack_rows(hidden), *leave_came)
-    hidden = list(hidden) + [swap_units(gathered)]
-    mixed, mixed_leave = project(stay, *leave_came, out_weight)
-    while len(a) < layers:
-        go_round(a, mixed)
-    mixed_leave, state_leave, pages_leave = after((mixed_leave, state_leave, pages_leave), mixed)
-    decode_kv, decode_state, mixed = settle(
-        unit,
-        swap_units(pages_leave),
-        swap_units(state_leave),
-        pages_held,
-        state_held,
-        after(mixed, hidden[-1]),
-    )
-    mixed_came = swap_units(mixed_leave)
-    while len(b) < layers - 1:
-        go_round(b, mixed)
-    b_last = b[-1]
-    split = b_last.shape[1] // 256 * 128
-    ends = ((0, split), (split, b_last.shape[1]))
-    last = [pass_on(x) for x in split_columns(b_last, [hi - lo for lo, hi in ends])]
-
-    own, parts = product(unit, hidden, a[:-1] + [after(a[-1], mixed, mixed_came)])
-    sums, received = [], [plane_swap(x, d) for d, x in enumerate(parts, 1)]
-    sums.append(total(own, received))
-    order = parts
-    for (lo, hi), end in zip(ends, last):
-        own, parts = product(unit, hidden, b + [after(end, *order)], lo)
-        parts = after(parts, *received)
+    leave_came = [swap_units(x) for x in after((leave_a, leave_b), *hidden)]
+    pair = PLANE // 2
+    gathered = [after(stack_rows(x), *leave_came) for x in (hidden[:pair], hidden[pair:])]
+    swapped = [swap_units(x) for x in gathered]
+    hidden = list(hidden) + swapped
+    mixed, *mixed_leave = project(stay, *leave_came, out_weight)
+    mixed_came = [swap_units(x) for x in after(mixed_leave, hops[-1], *swapped)]
+    widths = chunk_widths(width // 2)
+    ends = [pass_on(x) for x in split_columns(after(hops[-1], mixed), widths)]
+    sums, order, received, low = [], mixed_came, [], 0
+    for n, end in enumerate(ends):
+        own, parts = product(unit, hidden, hops + [after(end, *order)], low)
+        order, low = list(parts) + [x[0] for x in sums], low + widths[n]
+        if received:
+            parts = after(parts, *received)
+        if n == len(ends) - 1:
+            state_leave, pages_leave = after((state_leave, pages_leave), *parts)
+            state_came, pages_came = swap_units(state_leave), swap_units(pages_leave)
         received = [plane_swap(x, d) for d, x in enumerate(parts, 1)]
-        order = sums[-1]
-        sums.append(total(own, after(received, *order)))
+        token = sums[-1][0] if sums else own
+        if n == len(ends) - 1:
+            decode_kv, decode_state, token = settle(
+                unit, pages_came, state_came, pages_held, state_held, token
+            )
+            sums[-1] = (token, sums[-1][1])
+        sums.append(total(own, after(received, token)))
     kept, leave = zip(*sums)
     came = [swap_units(x) for x in leave]
     layer_out = finish(unit, resid, mixed, mixed_came, kept, came)

time: 134 us -> 127 us (0.948)
  waiting for transfers between devices: 48.3 us -> 35.4 us
  local copies, waits for them, and re-layouts: 10.1 us -> 13.6 us
  Pallas kernels: 46 us -> 48.3 us
    ppermute x7 -> x5, waiting for transfers between devices: 33.3 us -> 13.8 us  [pass_on(): return lax.ppermute(x, 'req', ring_pairs)]
    ppermute x12, waiting for transfers between devices: 12.3 us -> 18.6 us  [plane_swap(): lax.ppermute(x, 'req', [(r, r - r % PLANE + (r % PLANE ^ d)) for r in ran...]
    unnamed x43 -> x47, local copies, waits for them, and re-layouts: 10.1 us -> 13.6 us
    ppermute x7 -> x5, starting transfers between devices: 10.5 us -> 9.83 us  [pass_on(): return lax.ppermute(x, 'req', ring_pairs)]
    ppermute x11 -> x12, starting transfers between devices: 2.8 us -> 3.31 us  [swap_units(): return lax.ppermute(x, 'unit', [(0, 1), (1, 0)])]
    ppermute x11 -> x12, waiting for transfers between devices: 2.64 us -> 3.01 us  [swap_units(): return lax.ppermute(x, 'unit', [(0, 1), (1, 0)])]
  transfers between devices with their start and end apart: 30 -> 29, of which waited for: 12 -> 11; matrix products, arithmetic and copies ran while one was open for 0% -> 1% of each run, Pallas kernels for 33% -> 37%
where the time goes in v5:
time: 127 us; the launch traced here: 126 us
  Pallas kernels  48.3 us (38%)
  waiting for transfers between devices  35.4 us (28%)
  starting transfers between devices  27.3 us (21%)
  local copies, waits for them, and re-layouts  13.6 us (11%)
  between operations  1.65 us (1%)
    ppermute x12, waiting for transfers between devices, plane_swap(): lax.ppermute(x, 'req', [(r, r - r % PLANE + (r % PLANE ^ d)) for r in ran...  18.6 us
    ppermute x12, starting transfers between devices, plane_swap(): lax.ppermute(x, 'req', [(r, r - r % PLANE + (r % PLANE ^ d)) for r in ran...  14.1 us
    ppermute x5, waiting for transfers between devices, pass_on(): return lax.ppermute(x, 'req', ring_pairs)  13.8 us
    unnamed x47, local copies, waits for them, and re-layouts  13.6 us
    pallas_call x3, Pallas kernels, product(): pl.pallas_call(functools.partial(product_kernel, tuple(bases)), out_shape...  12.2 us
    pallas_call x1, Pallas kernels, attend(): pl.pallas_call(attend_kernel, out_shape=(jax.ShapeDtypeStruct(queries.sha...  11.4 us
    pallas_call x1, Pallas kernels, state_space(): pl.pallas_call(state_kernel, out_shape=(jax.ShapeDtypeStruct((length, hal...  9.99 us
    ppermute x5, starting transfers between devices, pass_on(): return lax.ppermute(x, 'req', ring_pairs)  9.83 us
  transfers between devices with their start and end apart: 29, of which 11 were waited for; matrix products, arithmetic and copies ran while one was open for 1% of the time, Pallas kernels for 37%

profile of v5, /device:TPU:0, one launch (start us, length us, event | category | flops | bytes accessed | tf_op | source)
XLA Modules:
  0.0 126.3 jit_solution(14789476004505121514)
XLA Ops:
  2.5 1.6 %collective-permute-done.refs_1_ = bf16[192,1536]{1,0:T(8,128)(2,1)S(1)} collective-permute-done((bf16[192,1536]{1,0:T(8,128)(2,1)S(1)}, bf16[192,1536]{1,0:T(8,128)(2,1)S(1)}, u32[]{:S(2)}, u32[]{:S(2)}) %collective-permute-start) | collective-permute-done | bytes 589856 | tf_op jit(solution)/shard_map/ppermute | solution.py:568
  4.2 3.0 %collective-permute-start.1 = (bf16[384,1536]{1,0:T(8,128)(2,1)S(1)}, bf16[384,1536]{1,0:T(8,128)(2,1)}, u32[]{:S(2)}, u32[]{:S(2)}) collective-permute-start(bf16[384,1536]{1,0:T(8,128)(2,1)S(1)} %stack_rows.3.refs_6_), channel_id=1, source_target_pairs={{0,8},{2,10},{4,12},{6,14},{8,24},{10,26},{12,28},{14,30},{24,16},... | collective-permute-start | bytes 3538952 | tf_op jit(solution)/shard_map/ppermute | solution.py:627
  10.1 1.6 %collective-permute-start.2 = (bf16[128,1536]{1,0:T(8,128)(2,1)}, bf16[128,1536]{1,0:T(8,128)(2,1)S(1)}, u32[]{:S(2)}, u32[]{:S(2)}) collective-permute-start(bf16[128,1536]{1,0:T(8,128)(2,1)} %get-tuple-element.89), channel_id=1, source_target_pairs={{0,2},{2,0},{4,6},{6,4},{8,10},{10,8},{12,14},{14,12},{16,18},{18,... | collective-permute-start | bytes 1179656 | tf_op jit(solution)/shard_map/ppermute | solution.py:635
  11.7 1.5 %collective-permute-start.3 = (bf16[128,1536]{1,0:T(8,128)(2,1)}, bf16[128,1536]{1,0:T(8,128)(2,1)S(1)}, u32[]{:S(2)}, u32[]{:S(2)}) collective-permute-start(bf16[128,1536]{1,0:T(8,128)(2,1)} %get-tuple-element.90), channel_id=1, source_target_pairs={{0,4},{2,6},{4,0},{6,2},{8,12},{10,14},{12,8},{14,10},{16,20},{18,... | collective-permute-start | bytes 1179656 | tf_op jit(solution)/shard_map/ppermute | solution.py:635
  15.8 11.4 %attend.1 = (bf16[128,1536]{1,0:T(8,128)(2,1)S(1)}, bf16[14,128,512]{2,1,0:T(8,128)(2,1)}, bf16[7,128,512]{2,1,0:T(8,128)(2,1)S(1)}) custom-call(s32[1,13]{1,0:T(1,128)S(1)} %copy-done.16, s32[1]{0:T(128)S(6)} %copy.29.ctx, s32[1,13]{1,0:T(1,128)S(1)} %bitcast.7, s32[1]{0:T(128)} %bitcast.unit, bf16[128,1536]{1,0:T(8,128)(2,1)S(1)} %copy-done.9, ...), custom_call_target="tpu_custom_call" | custom-call | tf_op jit(solution)/shard_map/attend/pallas_call | solution.py:128
  29.0 5.6 %collective-permute-done.1.refs_7_ = bf16[384,1536]{1,0:T(8,128)(2,1)} collective-permute-done((bf16[384,1536]{1,0:T(8,128)(2,1)S(1)}, bf16[384,1536]{1,0:T(8,128)(2,1)}, u32[]{:S(2)}, u32[]{:S(2)}) %collective-permute-start.1) | collective-permute-done | bytes 1179680 | tf_op jit(solution)/shard_map/ppermute | solution.py:627
  43.1 10.0 %state_space.1 = (bf16[128,2304]{1,0:T(8,128)(2,1)S(1)}, bf16[128,1152]{1,0:T(8,128)(2,1)S(1)}, bf16[128,1152]{1,0:T(8,128)(2,1)S(1)}, f32[2,12,128,256]{3,2,1,0:T(8,128)}, bf16[12,128,256]{2,1,0:T(8,128)(2,1)S(1)}) custom-call(s32[1]{0:T(128)} %bitcast.unit, f32[24]{0:T(128)S(1)} %copy-done.18, bf16[128,1536]{1,0:T(8,128)(2,1)S(1)} %copy-done.11, ...), custom_call_target="tpu_custom_call" | custom-call | tf_op jit(solution)/shard_map/state_space/pallas_call | solution.py:253
  55.7 8.7 %project.1 = (bf16[128,3072]{1,0:T(8,128)(2,1)S(1)}, bf16[128,1536]{1,0:T(8,128)(2,1)S(1)}, bf16[128,1536]{1,0:T(8,128)(2,1)S(1)}) custom-call(bf16[128,2304]{1,0:T(8,128)(2,1)S(1)} %get-tuple-element.86.stay_ref, bf16[128,1152]{1,0:T(8,128)(2,1)S(1)} %collective-permute-done.5.a_ref, bf16[128,1152]{1,0:T(8,128)(2,1)S(1)} %collective-permute-done.6.b_ref, ...), custom_call_target="tpu_custom_call" | custom-call | tf_op jit(solution)/shard_map/project/pallas_call | solution.py:508
  65.2 3.5 %collective-permute-start.12 = (bf16[384,384]{1,0:T(8,128)(2,1)S(1)}, bf16[384,384]{1,0:T(8,128)(2,1)S(1)}, u32[]{:S(2)}, u32[]{:S(2)}) collective-permute-start(bf16[384,384]{1,0:T(8,128)(2,1)S(1)} %get-tuple-element.107), channel_id=1, source_target_pairs={{0,8},{2,10},{4,12},{6,14},{8,24},{10,26},{12,28},{14,30},{24,16},... | collective-permute-start | bytes 884744 | tf_op jit(solution)/shard_map/ppermute | solution.py:627
  68.8 7.3 %collective-permute-done.12.refs_9_ = bf16[384,384]{1,0:T(8,128)(2,1)S(1)} collective-permute-done((bf16[384,384]{1,0:T(8,128)(2,1)S(1)}, bf16[384,384]{1,0:T(8,128)(2,1)S(1)}, u32[]{:S(2)}, u32[]{:S(2)}) %collective-permute-start.12) | collective-permute-done | bytes 294944 | tf_op jit(solution)/shard_map/ppermute | solution.py:627
  76.1 3.7 %product.3 = (f32[256,384]{1,0:T(8,128)S(1)}, bf16[256,384]{1,0:T(8,128)(2,1)S(1)}, bf16[256,384]{1,0:T(8,128)(2,1)S(1)}, bf16[256,384]{1,0:T(8,128)(2,1)S(1)}) custom-call(s32[1]{0:T(128)} %bitcast.unit, bf16[128,1536]{1,0:T(8,128)(2,1)S(1)} %get-tuple-element.92.refs_0_, bf16[128,1536]{1,0:T(8,128)(2,1)S(1)} %collective-permute-done.2.refs_1_, ...), custom_call_target="tpu_custom_call" | custom-call | tf_op jit(solution)/shard_map/product/pallas_call | solution.py:413
  79.8 1.6 %collective-permute-start.13 = (bf16[256,384]{1,0:T(8,128)(2,1)S(1)}, bf16[256,384]{1,0:T(8,128)(2,1)S(1)}, u32[]{:S(2)}, u32[]{:S(2)}) collective-permute-start(bf16[256,384]{1,0:T(8,128)(2,1)S(1)} %get-tuple-element.110), channel_id=1, source_target_pairs={{0,2},{2,0},{4,6},{6,4},{8,10},{10,8},{12,14},{14,12},{16,18},{18,... | collective-permute-start | bytes 589832 | tf_op jit(solution)/shard_map/ppermute | solution.py:635
  81.3 1.5 %collective-permute-start.14 = (bf16[256,384]{1,0:T(8,128)(2,1)S(1)}, bf16[256,384]{1,0:T(8,128)(2,1)S(1)}, u32[]{:S(2)}, u32[]{:S(2)}) collective-permute-start(bf16[256,384]{1,0:T(8,128)(2,1)S(1)} %get-tuple-element.111), channel_id=1, source_target_pairs={{0,4},{2,6},{4,0},{6,2},{8,12},{10,14},{12,8},{14,10},{16,20},{18,... | collective-permute-start | bytes 589832 | tf_op jit(solution)/shard_map/ppermute | solution.py:635
  83.3 2.5 %collective-permute-start.16 = (bf16[384,512]{1,0:T(8,128)(2,1)S(1)}, bf16[384,512]{1,0:T(8,128)(2,1)S(1)}, u32[]{:S(2)}, u32[]{:S(2)}) collective-permute-start(bf16[384,512]{1,0:T(8,128)(2,1)S(1)} %get-tuple-element.119), channel_id=1, source_target_pairs={{0,8},{2,10},{4,12},{6,14},{8,24},{10,26},{12,28},{14,30},{24,16},... | collective-permute-start | bytes 1179656 | tf_op jit(solution)/shard_map/ppermute | solution.py:627
  86.6 4.9 %product.4 = (f32[256,640]{1,0:T(8,128)S(1)}, bf16[256,640]{1,0:T(8,128)(2,1)S(1)}, bf16[256,640]{1,0:T(8,128)(2,1)S(1)}, bf16[256,640]{1,0:T(8,128)(2,1)S(1)}) custom-call(s32[1]{0:T(128)} %bitcast.unit, bf16[128,1536]{1,0:T(8,128)(2,1)S(1)} %get-tuple-element.92.refs_0_, bf16[128,1536]{1,0:T(8,128)(2,1)S(1)} %collective-permute-done.2.refs_1_, ...), custom_call_target="tpu_custom_call" | custom-call | tf_op jit(solution)/shard_map/product/pallas_call | solution.py:413
  91.5 1.6 %collective-permute-start.18 = (bf16[256,640]{1,0:T(8,128)(2,1)S(1)}, bf16[256,640]{1,0:T(8,128)(2,1)S(1)}, u32[]{:S(2)}, u32[]{:S(2)}) collective-permute-start(bf16[256,640]{1,0:T(8,128)(2,1)S(1)} %get-tuple-element.129), channel_id=1, source_target_pairs={{0,2},{2,0},{4,6},{6,4},{8,10},{10,8},{12,14},{14,12},{16,18},{18,... | collective-permute-start | bytes 983048 | tf_op jit(solution)/shard_map/ppermute | solution.py:635
  93.1 1.5 %collective-permute-start.19 = (bf16[256,640]{1,0:T(8,128)(2,1)S(1)}, bf16[256,640]{1,0:T(8,128)(2,1)S(1)}, u32[]{:S(2)}, u32[]{:S(2)}) collective-permute-start(bf16[256,640]{1,0:T(8,128)(2,1)S(1)} %get-tuple-element.130), channel_id=1, source_target_pairs={{0,4},{2,6},{4,0},{6,2},{8,12},{10,14},{12,8},{14,10},{16,20},{18,... | collective-permute-start | bytes 983048 | tf_op jit(solution)/shard_map/ppermute | solution.py:635
  95.2 3.7 %product.5 = (f32[256,512]{1,0:T(8,128)S(1)}, bf16[256,512]{1,0:T(8,128)(2,1)S(1)}, bf16[256,512]{1,0:T(8,128)(2,1)S(1)}, bf16[256,512]{1,0:T(8,128)(2,1)S(1)}) custom-call(s32[1]{0:T(128)} %bitcast.unit, bf16[128,1536]{1,0:T(8,128)(2,1)S(1)} %get-tuple-element.92.refs_0_, bf16[128,1536]{1,0:T(8,128)(2,1)S(1)} %collective-permute-done.2.refs_1_, ...), custom_call_target="tpu_custom_call" | custom-call | tf_op jit(solution)/shard_map/product/pallas_call | solution.py:413
  98.9 3.3 %collective-permute-done.18.refs_0_ = bf16[256,640]{1,0:T(8,128)(2,1)S(1)} collective-permute-done((bf16[256,640]{1,0:T(8,128)(2,1)S(1)}, bf16[256,640]{1,0:T(8,128)(2,1)S(1)}, u32[]{:S(2)}, u32[]{:S(2)}) %collective-permute-start.18) | collective-permute-done | bytes 327712 | tf_op jit(solution)/shard_map/ppermute | solution.py:635
  102.2 5.7 %collective-permute-done.19.refs_1_ = bf16[256,640]{1,0:T(8,128)(2,1)S(1)} collective-permute-done((bf16[256,640]{1,0:T(8,128)(2,1)S(1)}, bf16[256,640]{1,0:T(8,128)(2,1)S(1)}, u32[]{:S(2)}, u32[]{:S(2)}) %collective-permute-start.19) | collective-permute-done | bytes 327712 | tf_op jit(solution)/shard_map/ppermute | solution.py:635
  112.2 1.5 %settle.1 = (bf16[14,128,512]{2,1,0:T(8,128)(2,1)}, f32[2,12,128,256]{3,2,1,0:T(8,128)}, f32[128,640]{1,0:T(8,128)S(1)}) custom-call(s32[1]{0:T(128)} %bitcast.unit, bf16[7,128,512]{2,1,0:T(8,128)(2,1)S(1)} %collective-permute-done.21.pages, ...), custom_call_target="tpu_custom_call", output_to_operand_aliasing={{0}: (3, {}), {1}: (4, {}), {2}: (5, {})} | custom-call | tf_op jit(solution)/shard_map/settle/pallas_call | solution.py:290
  113.7 3.9 %collective-permute-done.23.refs_0_ = bf16[256,512]{1,0:T(8,128)(2,1)S(1)} collective-permute-done((bf16[256,512]{1,0:T(8,128)(2,1)S(1)}, bf16[256,512]{1,0:T(8,128)(2,1)S(1)}, u32[]{:S(2)}, u32[]{:S(2)}) %collective-permute-start.23) | collective-permute-done | bytes 262176 | tf_op jit(solution)/shard_map/ppermute | solution.py:635
  117.6 4.1 %collective-permute-done.24.refs_1_ = bf16[256,512]{1,0:T(8,128)(2,1)S(1)} collective-permute-done((bf16[256,512]{1,0:T(8,128)(2,1)S(1)}, bf16[256,512]{1,0:T(8,128)(2,1)S(1)}, u32[]{:S(2)}, u32[]{:S(2)}) %collective-permute-start.24) | collective-permute-done | bytes 262176 | tf_op jit(solution)/shard_map/ppermute | solution.py:635
  121.7 1.6 %collective-permute-done.25.refs_2_ = bf16[256,512]{1,0:T(8,128)(2,1)S(1)} collective-permute-done((bf16[256,512]{1,0:T(8,128)(2,1)S(1)}, bf16[256,512]{1,0:T(8,128)(2,1)S(1)}, u32[]{:S(2)}, u32[]{:S(2)}) %collective-permute-start.25) | collective-permute-done | bytes 262176 | tf_op jit(solution)/shard_map/ppermute | solution.py:635
  (98 shorter events, 29.3 us)
Async XLA Ops:
  4.2 30.4 %collective-permute-start.1 = (bf16[384,1536]{1,0:T(8,128)(2,1)S(1)}, bf16[384,1536]{1,0:T(8,128)(2,1)}, u32[]{:S(2)}, u32[]{:S(2)}) collective-permute-start(bf16[384,1536]{1,0:T(8,128)(2,1)S(1)} %stack_rows.3.refs_6_), channel_id=1, source_target_pairs={{0,8},{2,10},{4,12},{6,14},{8,24},{10,26},{12,28},{14,30},{24,16},... | collective-permute-start | bytes 3538952 | tf_op jit(solution)/shard_map/ppermute | solution.py:627
  10.1 43.0 %collective-permute-start.2 = (bf16[128,1536]{1,0:T(8,128)(2,1)}, bf16[128,1536]{1,0:T(8,128)(2,1)S(1)}, u32[]{:S(2)}, u32[]{:S(2)}) collective-permute-start(bf16[128,1536]{1,0:T(8,128)(2,1)} %get-tuple-element.89), channel_id=1, source_target_pairs={{0,2},{2,0},{4,6},{6,4},{8,10},{10,8},{12,14},{14,12},{16,18},{18,... | collective-permute-start | bytes 1179656 | tf_op jit(solution)/shard_map/ppermute | solution.py:635
  11.7 41.4 %collective-permute-start.3 = (bf16[128,1536]{1,0:T(8,128)(2,1)}, bf16[128,1536]{1,0:T(8,128)(2,1)S(1)}, u32[]{:S(2)}, u32[]{:S(2)}) collective-permute-start(bf16[128,1536]{1,0:T(8,128)(2,1)} %get-tuple-element.90), channel_id=1, source_target_pairs={{0,4},{2,6},{4,0},{6,2},{8,12},{10,14},{12,8},{14,10},{16,20},{18,... | collective-permute-start | bytes 1179656 | tf_op jit(solution)/shard_map/ppermute | solution.py:635
  13.2 39.9 %collective-permute-start.4 = (bf16[128,1536]{1,0:T(8,128)(2,1)}, bf16[128,1536]{1,0:T(8,128)(2,1)}, u32[]{:S(2)}, u32[]{:S(2)}) collective-permute-start(bf16[128,1536]{1,0:T(8,128)(2,1)} %get-tuple-element.91), channel_id=1, source_target_pairs={{0,6},{2,4},{4,2},{6,0},{8,14},{10,12},{12,10},{14,8},{16,22},{18,... | collective-permute-start | bytes 1179656 | tf_op jit(solution)/shard_map/ppermute | solution.py:635
  34.6 29.8 %collective-permute-start.7 = (bf16[384,1536]{1,0:T(8,128)(2,1)}, bf16[384,1536]{1,0:T(8,128)(2,1)S(1)}, u32[]{:S(2)}, u32[]{:S(2)}) collective-permute-start(bf16[384,1536]{1,0:T(8,128)(2,1)} %collective-permute-done.1.refs_7_), channel_id=1, source_target_pairs={{0,8},{2,10},{4,12},{6,14},{8,24},{10,26},{12,28},{14,30},{24,16},... | collective-permute-start | bytes 3538952 | tf_op jit(solution)/shard_map/ppermute | solution.py:627
  55.2 9.2 %collective-permute-start.9 = (bf16[256,1536]{1,0:T(8,128)(2,1)S(1)}, bf16[256,1536]{1,0:T(8,128)(2,1)S(1)}, u32[]{:S(2)}, u32[]{:S(2)}) collective-permute-start(bf16[256,1536]{1,0:T(8,128)(2,1)S(1)} %stack_rows.5), channel_id=1, source_target_pairs={{0,1},{1,0},{2,3},{3,2},{4,5},{5,4},{6,7},{7,6},{8,9},{9,8},{10,11... | collective-permute-start | bytes 2359304 | tf_op jit(solution)/shard_map/ppermute | solution.py:568
  55.4 9.1 %collective-permute-start.8 = (bf16[256,1536]{1,0:T(8,128)(2,1)S(1)}, bf16[256,1536]{1,0:T(8,128)(2,1)S(1)}, u32[]{:S(2)}, u32[]{:S(2)}) collective-permute-start(bf16[256,1536]{1,0:T(8,128)(2,1)S(1)} %stack_rows.4), channel_id=1, source_target_pairs={{0,1},{1,0},{2,3},{3,2},{4,5},{5,4},{6,7},{7,6},{8,9},{9,8},{10,11... | collective-permute-start | bytes 2359304 | tf_op jit(solution)/shard_map/ppermute | solution.py:568
  64.5 11.6 %collective-permute-start.10 = (bf16[128,1536]{1,0:T(8,128)(2,1)S(1)}, bf16[128,1536]{1,0:T(8,128)(2,1)S(1)}, u32[]{:S(2)}, u32[]{:S(2)}) collective-permute-start(bf16[128,1536]{1,0:T(8,128)(2,1)S(1)} %get-tuple-element.104), channel_id=1, source_target_pairs={{0,1},{1,0},{2,3},{3,2},{4,5},{5,4},{6,7},{7,6},{8,9},{9,8},{10,11... | collective-permute-start | bytes 1179656 | tf_op jit(solution)/shard_map/ppermute | solution.py:568
  64.7 11.4 %collective-permute-start.11 = (bf16[128,1536]{1,0:T(8,128)(2,1)S(1)}, bf16[128,1536]{1,0:T(8,128)(2,1)S(1)}, u32[]{:S(2)}, u32[]{:S(2)}) collective-permute-start(bf16[128,1536]{1,0:T(8,128)(2,1)S(1)} %get-tuple-element.105), channel_id=1, source_target_pairs={{0,1},{1,0},{2,3},{3,2},{4,5},{5,4},{6,7},{7,6},{8,9},{9,8},{10,11... | collective-permute-start | bytes 1179656 | tf_op jit(solution)/shard_map/ppermute | solution.py:568
  65.2 10.9 %collective-permute-start.12 = (bf16[384,384]{1,0:T(8,128)(2,1)S(1)}, bf16[384,384]{1,0:T(8,128)(2,1)S(1)}, u32[]{:S(2)}, u32[]{:S(2)}) collective-permute-start(bf16[384,384]{1,0:T(8,128)(2,1)S(1)} %get-tuple-element.107), channel_id=1, source_target_pairs={{0,8},{2,10},{4,12},{6,14},{8,24},{10,26},{12,28},{14,30},{24,16},... | collective-permute-start | bytes 884744 | tf_op jit(solution)/shard_map/ppermute | solution.py:627
  68.7 17.9 %collective-permute-start.17 = (bf16[384,640]{1,0:T(8,128)(2,1)S(1)}, bf16[384,640]{1,0:T(8,128)(2,1)S(1)}, u32[]{:S(2)}, u32[]{:S(2)}) collective-permute-start(bf16[384,640]{1,0:T(8,128)(2,1)S(1)} %get-tuple-element.120), channel_id=1, source_target_pairs={{0,8},{2,10},{4,12},{6,14},{8,24},{10,26},{12,28},{14,30},{24,16},... | collective-permute-start | bytes 1474568 | tf_op jit(solution)/shard_map/ppermute | solution.py:627
  79.8 11.7 %collective-permute-start.13 = (bf16[256,384]{1,0:T(8,128)(2,1)S(1)}, bf16[256,384]{1,0:T(8,128)(2,1)S(1)}, u32[]{:S(2)}, u32[]{:S(2)}) collective-permute-start(bf16[256,384]{1,0:T(8,128)(2,1)S(1)} %get-tuple-element.110), channel_id=1, source_target_pairs={{0,2},{2,0},{4,6},{6,4},{8,10},{10,8},{12,14},{14,12},{16,18},{18,... | collective-permute-start | bytes 589832 | tf_op jit(solution)/shard_map/ppermute | solution.py:635
  81.3 10.2 %collective-permute-start.14 = (bf16[256,384]{1,0:T(8,128)(2,1)S(1)}, bf16[256,384]{1,0:T(8,128)(2,1)S(1)}, u32[]{:S(2)}, u32[]{:S(2)}) collective-permute-start(bf16[256,384]{1,0:T(8,128)(2,1)S(1)} %get-tuple-element.111), channel_id=1, source_target_pairs={{0,4},{2,6},{4,0},{6,2},{8,12},{10,14},{12,8},{14,10},{16,20},{18,... | collective-permute-start | bytes 589832 | tf_op jit(solution)/shard_map/ppermute | solution.py:635
  82.8 8.7 %collective-permute-start.15 = (bf16[256,384]{1,0:T(8,128)(2,1)S(1)}, bf16[256,384]{1,0:T(8,128)(2,1)S(1)}, u32[]{:S(2)}, u32[]{:S(2)}) collective-permute-start(bf16[256,384]{1,0:T(8,128)(2,1)S(1)} %get-tuple-element.112), channel_id=1, source_target_pairs={{0,6},{2,4},{4,2},{6,0},{8,14},{10,12},{12,10},{14,8},{16,22},{18,... | collective-permute-start | bytes 589832 | tf_op jit(solution)/shard_map/ppermute | solution.py:635
  83.3 11.9 %collective-permute-start.16 = (bf16[384,512]{1,0:T(8,128)(2,1)S(1)}, bf16[384,512]{1,0:T(8,128)(2,1)S(1)}, u32[]{:S(2)}, u32[]{:S(2)}) collective-permute-start(bf16[384,512]{1,0:T(8,128)(2,1)S(1)} %get-tuple-element.119), channel_id=1, source_target_pairs={{0,8},{2,10},{4,12},{6,14},{8,24},{10,26},{12,28},{14,30},{24,16},... | collective-permute-start | bytes 1179656 | tf_op jit(solution)/shard_map/ppermute | solution.py:627
  91.5 10.7 %collective-permute-start.18 = (bf16[256,640]{1,0:T(8,128)(2,1)S(1)}, bf16[256,640]{1,0:T(8,128)(2,1)S(1)}, u32[]{:S(2)}, u32[]{:S(2)}) collective-permute-start(bf16[256,640]{1,0:T(8,128)(2,1)S(1)} %get-tuple-element.129), channel_id=1, source_target_pairs={{0,2},{2,0},{4,6},{6,4},{8,10},{10,8},{12,14},{14,12},{16,18},{18,... | collective-permute-start | bytes 983048 | tf_op jit(solution)/shard_map/ppermute | solution.py:635
  93.1 14.9 %collective-permute-start.19 = (bf16[256,640]{1,0:T(8,128)(2,1)S(1)}, bf16[256,640]{1,0:T(8,128)(2,1)S(1)}, u32[]{:S(2)}, u32[]{:S(2)}) collective-permute-start(bf16[256,640]{1,0:T(8,128)(2,1)S(1)} %get-tuple-element.130), channel_id=1, source_target_pairs={{0,4},{2,6},{4,0},{6,2},{8,12},{10,14},{12,8},{14,10},{16,20},{18,... | collective-permute-start | bytes 983048 | tf_op jit(solution)/shard_map/ppermute | solution.py:635
  94.6 13.3 %collective-permute-start.20 = (bf16[256,640]{1,0:T(8,128)(2,1)S(1)}, bf16[256,640]{1,0:T(8,128)(2,1)S(1)}, u32[]{:S(2)}, u32[]{:S(2)}) collective-permute-start(bf16[256,640]{1,0:T(8,128)(2,1)S(1)} %get-tuple-element.131), channel_id=1, source_target_pairs={{0,6},{2,4},{4,2},{6,0},{8,14},{10,12},{12,10},{14,8},{16,22},{18,... | collective-permute-start | bytes 983048 | tf_op jit(solution)/shard_map/ppermute | solution.py:635
  107.9 4.3 %collective-permute-start.21 = (bf16[7,128,512]{2,1,0:T(8,128)(2,1)S(1)}, bf16[7,128,512]{2,1,0:T(8,128)(2,1)S(1)}, u32[]{:S(2)}, u32[]{:S(2)}) collective-permute-start(bf16[7,128,512]{2,1,0:T(8,128)(2,1)S(1)} %copy-done.22), channel_id=1, source_target_pairs={{0,1},{1,0},{2,3},{3,2},{4,5},{5,4},{6,7},{7,6},{8,9},{9,8},{10,11... | collective-permute-start | bytes 2752520 | tf_op jit(solution)/shard_map/ppermute | solution.py:568
  107.9 4.2 %collective-permute-start.22 = (bf16[12,128,256]{2,1,0:T(8,128)(2,1)S(1)}, bf16[12,128,256]{2,1,0:T(8,128)(2,1)S(1)}, u32[]{:S(2)}, u32[]{:S(2)}) collective-permute-start(bf16[12,128,256]{2,1,0:T(8,128)(2,1)S(1)} %get-tuple-element.136), channel_id=1, source_target_pairs={{0,1},{1,0},{2,3},{3,2},{4,5},{5,4},{6,7},{7,6},{8,9},{9,8},{10,11... | collective-permute-start | bytes 2359304 | tf_op jit(solution)/shard_map/ppermute | solution.py:568
  108.4 9.2 %collective-permute-start.23 = (bf16[256,512]{1,0:T(8,128)(2,1)S(1)}, bf16[256,512]{1,0:T(8,128)(2,1)S(1)}, u32[]{:S(2)}, u32[]{:S(2)}) collective-permute-start(bf16[256,512]{1,0:T(8,128)(2,1)S(1)} %get-tuple-element.132), channel_id=1, source_target_pairs={{0,2},{2,0},{4,6},{6,4},{8,10},{10,8},{12,14},{14,12},{16,18},{18,... | collective-permute-start | bytes 786440 | tf_op jit(solution)/shard_map/ppermute | solution.py:635
  109.7 12.0 %collective-permute-start.24 = (bf16[256,512]{1,0:T(8,128)(2,1)S(1)}, bf16[256,512]{1,0:T(8,128)(2,1)S(1)}, u32[]{:S(2)}, u32[]{:S(2)}) collective-permute-start(bf16[256,512]{1,0:T(8,128)(2,1)S(1)} %get-tuple-element.133), channel_id=1, source_target_pairs={{0,4},{2,6},{4,0},{6,2},{8,12},{10,14},{12,8},{14,10},{16,20},{18,... | collective-permute-start | bytes 786440 | tf_op jit(solution)/shard_map/ppermute | solution.py:635
  110.5 12.8 %collective-permute-start.25 = (bf16[256,512]{1,0:T(8,128)(2,1)S(1)}, bf16[256,512]{1,0:T(8,128)(2,1)S(1)}, u32[]{:S(2)}, u32[]{:S(2)}) collective-permute-start(bf16[256,512]{1,0:T(8,128)(2,1)S(1)} %get-tuple-element.134), channel_id=1, source_target_pairs={{0,6},{2,4},{4,2},{6,0},{8,14},{10,12},{12,10},{14,8},{16,22},{18,... | collective-permute-start | bytes 786440 | tf_op jit(solution)/shard_map/ppermute | solution.py:635
  112.1 12.9 %collective-permute-start.27 = (bf16[128,640]{1,0:T(8,128)(2,1)S(1)}, bf16[128,640]{1,0:T(8,128)(2,1)S(1)}, u32[]{:S(2)}, u32[]{:S(2)}) collective-permute-start(bf16[128,640]{1,0:T(8,128)(2,1)S(1)} %get-tuple-element.151), channel_id=1, source_target_pairs={{0,1},{1,0},{2,3},{3,2},{4,5},{5,4},{6,7},{7,6},{8,9},{9,8},{10,11... | collective-permute-start | bytes 491528 | tf_op jit(solution)/shard_map/ppermute | solution.py:568
  (28 other events, 237.5 us)

commit v6 on v5

--- a/solution.py
+++ b/solution.py
@@ -381,46 +381,80 @@
     )(req, hidden)
 
 
-def product_kernel(bases, unit, *refs):
-    count = len(bases)
-    hidden, pieces = refs[: PLANE + 2], refs[PLANE + 2 : PLANE + 2 + count]
-    own_ref, *parts = refs[PLANE + 2 + count : -1]
-    weight = refs[-1]
+def place_rows(weight, pieces, unit):
     block_rows = pieces[0].shape[0] // 2
-    u = unit[0]
     for k, piece in enumerate(pieces):
-        for which, place in ((0, u), (1, 1 - u)):
+        for which, place in ((0, unit), (1, 1 - unit)):
             at = pl.multiple_of((2 * k + place) * block_rows, 16)
-            rows = slice(which * block_rows, (which + 1) * block_rows)
-            base = bases[k]
-            weight[pl.ds(at, block_rows), :] = piece[rows, base : base + weight.shape[1]]
+            weight[pl.ds(at, block_rows), :] = piece[which * block_rows : (which + 1) * block_rows, :]
+
+
+def begin_kernel(unit, *refs):
+    hidden, weight = refs[: PLANE + 2], refs[-1]
+    depth, width = weight.shape
+    count = depth // refs[PLANE + 2].shape[0]
+    pieces, (last_ref, *outs) = refs[PLANE + 2 : PLANE + 2 + count], refs[PLANE + 2 + count : -1]
+    place_rows(weight, pieces, unit[0])
     rows = hidden[0].shape[0]
     for d in range(PLANE):
         place = d % (PLANE // 2) * rows
         other = hidden[PLANE + d // (PLANE // 2)][place : place + rows, :]
         both = jnp.concatenate([hidden[d][...], other], axis=0)
-        result = jnp.dot(both, weight[...], preferred_element_type=F32)
+        span = slice(2 * d * rows, 2 * (d + 1) * rows)
+        last_ref[span, :] = both[:, depth:]
+        low = 0
+        for out in outs:
+            chunk = weight[:, low : low + out.shape[1]]
+            out[span, :] = jnp.dot(both[:, :depth], chunk, preferred_element_type=F32)
+            low += out.shape[1]
+
+
+def begin(unit, hidden, pieces, widths):
+    rows, depth = hidden[0].shape
+    done = len(pieces) * pieces[0].shape[0]
+    every = 2 * PLANE * rows
+    outs = pl.pallas_call(
+        begin_kernel,
+        out_shape=(jax.ShapeDtypeStruct((every, depth - done), BF16),)
+        + tuple(jax.ShapeDtypeStruct((every, w), F32) for w in widths),
+        in_specs=[SMEM] + [VMEM] * (PLANE + 2 + len(pieces)),
+        out_specs=(VMEM,) * (1 + len(widths)),
+        scratch_shapes=[pltpu.VMEM((done, pieces[0].shape[1]), BF16)],
+        compiler_params=PARAMS,
+        cost_estimate=cost(0, 12 << 20),
+        name="begin",
+    )(unit, *hidden, *pieces)
+    return outs[0], outs[1:]
+
+
+def product_kernel(unit, hidden, partial, piece, own_ref, *refs):
+    parts, weight = refs[:-1], refs[-1]
+    place_rows(weight, [piece], unit[0])
+    rows = own_ref.shape[0]
+    for d in range(PLANE):
+        span = slice(d * rows, (d + 1) * rows)
+        result = partial[span, :] + jnp.dot(
+            hidden[span, :], weight[...], preferred_element_type=F32
+        )
         if d:
             parts[d - 1][...] = result.astype(BF16)
         else:
             own_ref[...] = result
 
 
-def product(unit, hidden, pieces, low=0):
-    rows, depth = hidden[0].shape
-    width = pieces[-1].shape[1]
-    bases = [0 if x.shape[1] == width else low for x in pieces]
+def product(unit, hidden, partial, piece):
+    rows, width = partial.shape[0] // PLANE, partial.shape[1]
     outs = pl.pallas_call(
-        functools.partial(product_kernel, tuple(bases)),
-        out_shape=(jax.ShapeDtypeStruct((2 * rows, width), F32),)
-        + (jax.ShapeDtypeStruct((2 * rows, width), BF16),) * (PLANE - 1),
-        in_specs=[SMEM] + [VMEM] * (PLANE + 2 + len(pieces)),
+        product_kernel,
+        out_shape=(jax.ShapeDtypeStruct((rows, width), F32),)
+        + (jax.ShapeDtypeStruct((rows, width), BF16),) * (PLANE - 1),
+        in_specs=[SMEM] + [VMEM] * 3,
         out_specs=(VMEM,) * PLANE,
-        scratch_shapes=[pltpu.VMEM((depth, width), BF16)],
+        scratch_shapes=[pltpu.VMEM(piece.shape, BF16)],
         compiler_params=PARAMS,
         cost_estimate=cost(0, 6 << 20),
         name="product",
-    )(unit, *hidden, *pieces)
+    )(unit, hidden, partial, piece)
     return outs[0], outs[1:]
 
 
@@ -663,25 +697,25 @@
     swapped = [swap_units(x) for x in gathered]
     hidden = list(hidden) + swapped
     mixed, *mixed_leave = project(stay, *leave_came, out_weight)
-    mixed_came = [swap_units(x) for x in after(mixed_leave, hops[-1], *swapped)]
+    state_leave, pages_leave = after((state_leave, pages_leave), stay)
+    state_came, pages_came = swap_units(state_leave), swap_units(pages_leave)
+    mixed_came = [
+        swap_units(x) for x in after(mixed_leave, hops[-1], state_came, pages_came, *swapped)
+    ]
     widths = chunk_widths(width // 2)
     ends = [pass_on(x) for x in split_columns(after(hops[-1], mixed), widths)]
-    sums, order, received, low = [], mixed_came, [], 0
-    for n, end in enumerate(ends):
-        own, parts = product(unit, hidden, hops + [after(end, *order)], low)
-        order, low = list(parts) + [x[0] for x in sums], low + widths[n]
+    decode_kv, decode_state, mixed = settle(
+        unit, pages_came, state_came, pages_held, state_held, mixed
+    )
+    last_hidden, partial = begin(unit, hidden, hops, widths)
+    sums, order, received = [], [mixed, *mixed_came], []
+    for n, (piece, end) in enumerate(zip(partial, ends)):
+        own, parts = product(unit, last_hidden, piece, after(end, *order))
+        order = list(parts) + [x[0] for x in sums]
         if received:
-            parts = after(parts, *received)
-        if n == len(ends) - 1:
-            state_leave, pages_leave = after((state_leave, pages_leave), *parts)
-            state_came, pages_came = swap_units(state_leave), swap_units(pages_leave)
+            parts = after(parts, *(received if n < len(ends) - 1 else received[:1]))
         received = [plane_swap(x, d) for d, x in enumerate(parts, 1)]
         token = sums[-1][0] if sums else own
-        if n == len(ends) - 1:
-            decode_kv, decode_state, token = settle(
-                unit, pages_came, state_came, pages_held, state_held, token
-            )
-            sums[-1] = (token, sums[-1][1])
         sums.append(total(own, after(received, token)))
     kept, leave = zip(*sums)
     came = [swap_units(x) for x in leave]

time: 127 us -> 125 us (0.984)
  starting transfers between devices: 27.3 us -> 25.4 us
  Pallas kernels: 48.3 us -> 49.9 us
    ppermute x5, waiting for transfers between devices: 13.8 us -> 6.6 us  [pass_on(): return lax.ppermute(x, 'req', ring_pairs)]
    ppermute x12, waiting for transfers between devices: 18.6 us -> 25.3 us  [plane_swap(): lax.ppermute(x, 'req', [(r, r - r % PLANE + (r % PLANE ^ d)) for r in ran...]
    ppermute x5, starting transfers between devices: 9.83 us -> 7.96 us  [pass_on(): return lax.ppermute(x, 'req', ring_pairs)]
    pallas_call x3 -> x4, Pallas kernels: 12.2 us -> 11.8 us  [the longest x1 9.41 us: begin(): pl.pallas_call(begin_kernel, out_shape=(jax.ShapeDtypeStruct((every, dept...]
  transfers between devices with their start and end apart: 29 -> 29, of which waited for: 11 -> 10; matrix products, arithmetic and copies ran while one was open for 1% -> 1% of each run, Pallas kernels for 37% -> 39%
where the time goes in v6:
time: 125 us; the launch traced here: 124 us
  Pallas kernels  49.9 us (40%)
  waiting for transfers between devices  34.6 us (28%)
  starting transfers between devices  25.4 us (20%)
  local copies, waits for them, and re-layouts  12.9 us (10%)
  between operations  1.64 us (1%)
    ppermute x12, waiting for transfers between devices, plane_swap(): lax.ppermute(x, 'req', [(r, r - r % PLANE + (r % PLANE ^ d)) for r in ran...  25.3 us
    ppermute x12, starting transfers between devices, plane_swap(): lax.ppermute(x, 'req', [(r, r - r % PLANE + (r % PLANE ^ d)) for r in ran...  14.1 us
    unnamed x47, local copies, waits for them, and re-layouts  12.9 us
    pallas_call x1, Pallas kernels, attend(): pl.pallas_call(attend_kernel, out_shape=(jax.ShapeDtypeStruct(queries.sha...  11.5 us
    pallas_call x1, Pallas kernels, state_space(): pl.pallas_call(state_kernel, out_shape=(jax.ShapeDtypeStruct((length, hal...  10.1 us
    pallas_call x1, Pallas kernels, begin(): pl.pallas_call(begin_kernel, out_shape=(jax.ShapeDtypeStruct((every, dept...  9.41 us
    pallas_call x1, Pallas kernels, project(): pl.pallas_call(project_kernel, grid=(2 * half,), out_shape=(jax.ShapeDtyp...  8.7 us
    ppermute x5, starting transfers between devices, pass_on(): return lax.ppermute(x, 'req', ring_pairs)  7.96 us
  transfers between devices with their start and end apart: 29, of which 10 were waited for; matrix products, arithmetic and copies ran while one was open for 1% of the time, Pallas kernels for 39%

profile of v6, /device:TPU:0, one launch (start us, length us, event | category | flops | bytes accessed | tf_op | source)
XLA Modules:
  0.0 124.4 jit_solution(16274602976259528779)
XLA Ops:
  2.5 1.6 %collective-permute-done.refs_1_ = bf16[192,1536]{1,0:T(8,128)(2,1)S(1)} collective-permute-done((bf16[192,1536]{1,0:T(8,128)(2,1)S(1)}, bf16[192,1536]{1,0:T(8,128)(2,1)S(1)}, u32[]{:S(2)}, u32[]{:S(2)}) %collective-permute-start) | collective-permute-done | bytes 589856 | tf_op jit(solution)/shard_map/ppermute | solution.py:602
  4.2 3.0 %collective-permute-start.1 = (bf16[384,1536]{1,0:T(8,128)(2,1)S(1)}, bf16[384,1536]{1,0:T(8,128)(2,1)}, u32[]{:S(2)}, u32[]{:S(2)}) collective-permute-start(bf16[384,1536]{1,0:T(8,128)(2,1)S(1)} %stack_rows.3.refs_6_), channel_id=1, source_target_pairs={{0,8},{2,10},{4,12},{6,14},{8,24},{10,26},{12,28},{14,30},{24,16},... | collective-permute-start | bytes 3538952 | tf_op jit(solution)/shard_map/ppermute | solution.py:661
  7.2 1.4 %copy-done.4 = bf16[128,6144]{1,0:T(8,128)(2,1)S(1)} copy-done((bf16[128,6144]{1,0:T(8,128)(2,1)S(1)}, bf16[128,6144]{1,0:T(8,128)(2,1)}, u32[]{:S(2)}) %copy-start.4) | copy-done | bytes 1572888
  8.6 1.5 %spread.1 = (bf16[128,1536]{1,0:T(8,128)(2,1)S(1)}, bf16[128,1536]{1,0:T(8,128)(2,1)}, bf16[128,1536]{1,0:T(8,128)(2,1)}, bf16[128,1536]{1,0:T(8,128)(2,1)}) custom-call(s32[1]{0:T(128)} %bitcast.2.req, bf16[128,6144]{1,0:T(8,128)(2,1)S(1)} %copy-done.4), custom_call_target="tpu_custom_call" | custom-call | tf_op jit(solution)/shard_map/spread/pallas_call | solution.py:372
  10.1 1.6 %collective-permute-start.4 = (bf16[128,1536]{1,0:T(8,128)(2,1)}, bf16[128,1536]{1,0:T(8,128)(2,1)}, u32[]{:S(2)}, u32[]{:S(2)}) collective-permute-start(bf16[128,1536]{1,0:T(8,128)(2,1)} %get-tuple-element.99), channel_id=1, source_target_pairs={{0,2},{2,0},{4,6},{6,4},{8,10},{10,8},{12,14},{14,12},{16,18},{18,... | collective-permute-start | bytes 1179656 | tf_op jit(solution)/shard_map/ppermute | solution.py:669
  11.7 1.5 %collective-permute-start.5 = (bf16[128,1536]{1,0:T(8,128)(2,1)}, bf16[128,1536]{1,0:T(8,128)(2,1)}, u32[]{:S(2)}, u32[]{:S(2)}) collective-permute-start(bf16[128,1536]{1,0:T(8,128)(2,1)} %get-tuple-element.100), channel_id=1, source_target_pairs={{0,4},{2,6},{4,0},{6,2},{8,12},{10,14},{12,8},{14,10},{16,20},{18,... | collective-permute-start | bytes 1179656 | tf_op jit(solution)/shard_map/ppermute | solution.py:669
  16.0 11.5 %attend.1 = (bf16[128,1536]{1,0:T(8,128)(2,1)S(1)}, bf16[14,128,512]{2,1,0:T(8,128)(2,1)}, bf16[7,128,512]{2,1,0:T(8,128)(2,1)S(1)}) custom-call(s32[1,13]{1,0:T(1,128)S(1)} %copy-done.16, s32[1]{0:T(128)S(6)} %copy.29.ctx, s32[1,13]{1,0:T(1,128)S(1)} %bitcast.7, s32[1]{0:T(128)} %bitcast.unit, bf16[128,1536]{1,0:T(8,128)(2,1)S(1)} %copy-done.10, ...), custom_call_target="tpu_custom_call" | custom-call | tf_op jit(solution)/shard_map/attend/pallas_call | solution.py:128
  29.2 5.4 %collective-permute-done.1.refs_7_ = bf16[384,1536]{1,0:T(8,128)(2,1)} collective-permute-done((bf16[384,1536]{1,0:T(8,128)(2,1)S(1)}, bf16[384,1536]{1,0:T(8,128)(2,1)}, u32[]{:S(2)}, u32[]{:S(2)}) %collective-permute-start.1) | collective-permute-done | bytes 1179680 | tf_op jit(solution)/shard_map/ppermute | solution.py:661
  41.4 10.1 %state_space.1 = (bf16[128,2304]{1,0:T(8,128)(2,1)S(1)}, bf16[128,1152]{1,0:T(8,128)(2,1)S(1)}, bf16[128,1152]{1,0:T(8,128)(2,1)S(1)}, f32[2,12,128,256]{3,2,1,0:T(8,128)}, bf16[12,128,256]{2,1,0:T(8,128)(2,1)S(1)}) custom-call(s32[1]{0:T(128)} %bitcast.unit, f32[24]{0:T(128)S(1)} %copy-done.18, bf16[128,1536]{1,0:T(8,128)(2,1)S(1)} %copy-done.12, ...), custom_call_target="tpu_custom_call" | custom-call | tf_op jit(solution)/shard_map/state_space/pallas_call | solution.py:253
  55.4 8.7 %project.1 = (bf16[128,3072]{1,0:T(8,128)(2,1)S(1)}, bf16[128,1536]{1,0:T(8,128)(2,1)S(1)}, bf16[128,1536]{1,0:T(8,128)(2,1)S(1)}) custom-call(bf16[128,2304]{1,0:T(8,128)(2,1)S(1)} %get-tuple-element.92.stay_ref, bf16[128,1152]{1,0:T(8,128)(2,1)S(1)} %collective-permute-done.7.a_ref, bf16[128,1152]{1,0:T(8,128)(2,1)S(1)} %collective-permute-done.8.b_ref, ...), custom_call_target="tpu_custom_call" | custom-call | tf_op jit(solution)/shard_map/project/pallas_call | solution.py:542
  65.6 3.5 %collective-permute-start.14 = (bf16[384,384]{1,0:T(8,128)(2,1)S(1)}, bf16[384,384]{1,0:T(8,128)(2,1)S(1)}, u32[]{:S(2)}, u32[]{:S(2)}) collective-permute-start(bf16[384,384]{1,0:T(8,128)(2,1)S(1)} %get-tuple-element.120), channel_id=1, source_target_pairs={{0,8},{2,10},{4,12},{6,14},{8,24},{10,26},{12,28},{14,30},{24,16},... | collective-permute-start | bytes 884744 | tf_op jit(solution)/shard_map/ppermute | solution.py:661
  69.1 9.4 %begin.1 = (bf16[1024,384]{1,0:T(8,128)(2,1)S(1)}, f32[1024,384]{1,0:T(8,128)}, f32[1024,640]{1,0:T(8,128)}, f32[1024,512]{1,0:T(8,128)}) custom-call(s32[1]{0:T(128)} %bitcast.unit, bf16[128,1536]{1,0:T(8,128)(2,1)S(1)} %get-tuple-element.102.refs_0_, bf16[128,1536]{1,0:T(8,128)(2,1)} %collective-permute-done.4.refs_1_, ...), custom_call_target="tpu_custom_call" | custom-call | tf_op jit(solution)/shard_map/begin/pallas_call | solution.py:416
  78.5 1.5 %settle.1 = (bf16[14,128,512]{2,1,0:T(8,128)(2,1)}, f32[2,12,128,256]{3,2,1,0:T(8,128)}, bf16[128,3072]{1,0:T(8,128)(2,1)S(1)}) custom-call(s32[1]{0:T(128)} %bitcast.unit, bf16[7,128,512]{2,1,0:T(8,128)(2,1)S(1)} %collective-permute-done.2.pages, ...), custom_call_target="tpu_custom_call", output_to_operand_aliasing={{0}: (3, {}), {1}: (4, {}), {2}: (5, {})} | custom-call | tf_op jit(solution)/shard_map/settle/pallas_call | solution.py:290
  81.5 1.6 %collective-permute-start.15 = (bf16[256,384]{1,0:T(8,128)(2,1)S(1)}, bf16[256,384]{1,0:T(8,128)(2,1)S(1)}, u32[]{:S(2)}, u32[]{:S(2)}) collective-permute-start(bf16[256,384]{1,0:T(8,128)(2,1)S(1)} %get-tuple-element.123), channel_id=1, source_target_pairs={{0,2},{2,0},{4,6},{6,4},{8,10},{10,8},{12,14},{14,12},{16,18},{18,... | collective-permute-start | bytes 589832 | tf_op jit(solution)/shard_map/ppermute | solution.py:669
  83.1 1.5 %collective-permute-start.16 = (bf16[256,384]{1,0:T(8,128)(2,1)S(1)}, bf16[256,384]{1,0:T(8,128)(2,1)S(1)}, u32[]{:S(2)}, u32[]{:S(2)}) collective-permute-start(bf16[256,384]{1,0:T(8,128)(2,1)S(1)} %get-tuple-element.124), channel_id=1, source_target_pairs={{0,4},{2,6},{4,0},{6,2},{8,12},{10,14},{12,8},{14,10},{16,20},{18,... | collective-permute-start | bytes 589832 | tf_op jit(solution)/shard_map/ppermute | solution.py:669
  88.0 1.4 %collective-permute-done.15.refs_0_ = bf16[256,384]{1,0:T(8,128)(2,1)S(1)} collective-permute-done((bf16[256,384]{1,0:T(8,128)(2,1)S(1)}, bf16[256,384]{1,0:T(8,128)(2,1)S(1)}, u32[]{:S(2)}, u32[]{:S(2)}) %collective-permute-start.15) | collective-permute-done | bytes 196640 | tf_op jit(solution)/shard_map/ppermute | solution.py:669
  89.4 4.3 %collective-permute-done.16.refs_1_ = bf16[256,384]{1,0:T(8,128)(2,1)S(1)} collective-permute-done((bf16[256,384]{1,0:T(8,128)(2,1)S(1)}, bf16[256,384]{1,0:T(8,128)(2,1)S(1)}, u32[]{:S(2)}, u32[]{:S(2)}) %collective-permute-start.16) | collective-permute-done | bytes 196640 | tf_op jit(solution)/shard_map/ppermute | solution.py:669
  95.7 1.4 %collective-permute-start.21 = (bf16[256,640]{1,0:T(8,128)(2,1)S(1)}, bf16[256,640]{1,0:T(8,128)(2,1)S(1)}, u32[]{:S(2)}, u32[]{:S(2)}) collective-permute-start(bf16[256,640]{1,0:T(8,128)(2,1)S(1)} %get-tuple-element.139), channel_id=1, source_target_pairs={{0,6},{2,4},{4,2},{6,0},{8,14},{10,12},{12,10},{14,8},{16,22},{18,... | collective-permute-start | bytes 983048 | tf_op jit(solution)/shard_map/ppermute | solution.py:669
  98.0 6.3 %collective-permute-done.19.refs_0_ = bf16[256,640]{1,0:T(8,128)(2,1)S(1)} collective-permute-done((bf16[256,640]{1,0:T(8,128)(2,1)S(1)}, bf16[256,640]{1,0:T(8,128)(2,1)S(1)}, u32[]{:S(2)}, u32[]{:S(2)}) %collective-permute-start.19) | collective-permute-done | bytes 327712 | tf_op jit(solution)/shard_map/ppermute | solution.py:669
  106.3 1.4 %collective-permute-start.25 = (bf16[256,512]{1,0:T(8,128)(2,1)S(1)}, bf16[256,512]{1,0:T(8,128)(2,1)S(1)}, u32[]{:S(2)}, u32[]{:S(2)}) collective-permute-start(bf16[256,512]{1,0:T(8,128)(2,1)S(1)} %get-tuple-element.153), channel_id=1, source_target_pairs={{0,6},{2,4},{4,2},{6,0},{8,14},{10,12},{12,10},{14,8},{16,22},{18,... | collective-permute-start | bytes 786440 | tf_op jit(solution)/shard_map/ppermute | solution.py:669
  107.8 5.1 %collective-permute-done.20.refs_1_ = bf16[256,640]{1,0:T(8,128)(2,1)S(1)} collective-permute-done((bf16[256,640]{1,0:T(8,128)(2,1)S(1)}, bf16[256,640]{1,0:T(8,128)(2,1)S(1)}, u32[]{:S(2)}, u32[]{:S(2)}) %collective-permute-start.20) | collective-permute-done | bytes 327712 | tf_op jit(solution)/shard_map/ppermute | solution.py:669
  113.2 3.8 %collective-permute-done.23.refs_0_ = bf16[256,512]{1,0:T(8,128)(2,1)S(1)} collective-permute-done((bf16[256,512]{1,0:T(8,128)(2,1)S(1)}, bf16[256,512]{1,0:T(8,128)(2,1)S(1)}, u32[]{:S(2)}, u32[]{:S(2)}) %collective-permute-start.23) | collective-permute-done | bytes 262176 | tf_op jit(solution)/shard_map/ppermute | solution.py:669
  117.0 4.4 %collective-permute-done.24.refs_1_ = bf16[256,512]{1,0:T(8,128)(2,1)S(1)} collective-permute-done((bf16[256,512]{1,0:T(8,128)(2,1)S(1)}, bf16[256,512]{1,0:T(8,128)(2,1)S(1)}, u32[]{:S(2)}, u32[]{:S(2)}) %collective-permute-start.24) | collective-permute-done | bytes 262176 | tf_op jit(solution)/shard_map/ppermute | solution.py:669
  123.1 1.3 %finish.1 = bf16[128,3072]{1,0:T(8,128)(2,1)} custom-call(s32[1]{0:T(128)} %bitcast.unit, bf16[128,3072]{1,0:T(8,128)(2,1)S(1)} %copy-done.7, bf16[128,3072]{1,0:T(8,128)(2,1)S(1)} %get-tuple-element.109.mixed_ref, bf16[128,1536]{1,0:T(8,128)(2,1)S(1)} %collective-permute-done.12.low_ref, bf16[128,1536]{1,0:T(8,128)(2,1)S(1)} %collective-permute-done.13.high_ref, ...), custom_call_target="tpu_custom_call" | custom-call | tf_op jit(solution)/shard_map/finish/pallas_call | solution.py:508
  (99 shorter events, 29.6 us)
Async XLA Ops:
  4.2 30.4 %collective-permute-start.1 = (bf16[384,1536]{1,0:T(8,128)(2,1)S(1)}, bf16[384,1536]{1,0:T(8,128)(2,1)}, u32[]{:S(2)}, u32[]{:S(2)}) collective-permute-start(bf16[384,1536]{1,0:T(8,128)(2,1)S(1)} %stack_rows.3.refs_6_), channel_id=1, source_target_pairs={{0,8},{2,10},{4,12},{6,14},{8,24},{10,26},{12,28},{14,30},{24,16},... | collective-permute-start | bytes 3538952 | tf_op jit(solution)/shard_map/ppermute | solution.py:661
  10.1 41.4 %collective-permute-start.4 = (bf16[128,1536]{1,0:T(8,128)(2,1)}, bf16[128,1536]{1,0:T(8,128)(2,1)}, u32[]{:S(2)}, u32[]{:S(2)}) collective-permute-start(bf16[128,1536]{1,0:T(8,128)(2,1)} %get-tuple-element.99), channel_id=1, source_target_pairs={{0,2},{2,0},{4,6},{6,4},{8,10},{10,8},{12,14},{14,12},{16,18},{18,... | collective-permute-start | bytes 1179656 | tf_op jit(solution)/shard_map/ppermute | solution.py:669
  11.7 39.8 %collective-permute-start.5 = (bf16[128,1536]{1,0:T(8,128)(2,1)}, bf16[128,1536]{1,0:T(8,128)(2,1)}, u32[]{:S(2)}, u32[]{:S(2)}) collective-permute-start(bf16[128,1536]{1,0:T(8,128)(2,1)} %get-tuple-element.100), channel_id=1, source_target_pairs={{0,4},{2,6},{4,0},{6,2},{8,12},{10,14},{12,8},{14,10},{16,20},{18,... | collective-permute-start | bytes 1179656 | tf_op jit(solution)/shard_map/ppermute | solution.py:669
  13.2 38.3 %collective-permute-start.6 = (bf16[128,1536]{1,0:T(8,128)(2,1)}, bf16[128,1536]{1,0:T(8,128)(2,1)}, u32[]{:S(2)}, u32[]{:S(2)}) collective-permute-start(bf16[128,1536]{1,0:T(8,128)(2,1)} %get-tuple-element.101), channel_id=1, source_target_pairs={{0,6},{2,4},{4,2},{6,0},{8,14},{10,12},{12,10},{14,8},{16,22},{18,... | collective-permute-start | bytes 1179656 | tf_op jit(solution)/shard_map/ppermute | solution.py:669
  34.6 29.5 %collective-permute-start.9 = (bf16[384,1536]{1,0:T(8,128)(2,1)}, bf16[384,1536]{1,0:T(8,128)(2,1)S(1)}, u32[]{:S(2)}, u32[]{:S(2)}) collective-permute-start(bf16[384,1536]{1,0:T(8,128)(2,1)} %collective-permute-done.1.refs_7_), channel_id=1, source_target_pairs={{0,8},{2,10},{4,12},{6,14},{8,24},{10,26},{12,28},{14,30},{24,16},... | collective-permute-start | bytes 3538952 | tf_op jit(solution)/shard_map/ppermute | solution.py:661
  52.1 12.0 %collective-permute-start.2 = (bf16[7,128,512]{2,1,0:T(8,128)(2,1)S(1)}, bf16[7,128,512]{2,1,0:T(8,128)(2,1)S(1)}, u32[]{:S(2)}, u32[]{:S(2)}) collective-permute-start(bf16[7,128,512]{2,1,0:T(8,128)(2,1)S(1)} %copy-done.22), channel_id=1, source_target_pairs={{0,1},{1,0},{2,3},{3,2},{4,5},{5,4},{6,7},{7,6},{8,9},{9,8},{10,11... | collective-permute-start | bytes 2752520 | tf_op jit(solution)/shard_map/ppermute | solution.py:602
  54.4 9.7 %collective-permute-start.3 = (bf16[12,128,256]{2,1,0:T(8,128)(2,1)S(1)}, bf16[12,128,256]{2,1,0:T(8,128)(2,1)S(1)}, u32[]{:S(2)}, u32[]{:S(2)}) collective-permute-start(bf16[12,128,256]{2,1,0:T(8,128)(2,1)S(1)} %get-tuple-element.94), channel_id=1, source_target_pairs={{0,1},{1,0},{2,3},{3,2},{4,5},{5,4},{6,7},{7,6},{8,9},{9,8},{10,11... | collective-permute-start | bytes 2359304 | tf_op jit(solution)/shard_map/ppermute | solution.py:602
  54.9 9.2 %collective-permute-start.10 = (bf16[256,1536]{1,0:T(8,128)(2,1)S(1)}, bf16[256,1536]{1,0:T(8,128)(2,1)S(1)}, u32[]{:S(2)}, u32[]{:S(2)}) collective-permute-start(bf16[256,1536]{1,0:T(8,128)(2,1)S(1)} %stack_rows.4), channel_id=1, source_target_pairs={{0,1},{1,0},{2,3},{3,2},{4,5},{5,4},{6,7},{7,6},{8,9},{9,8},{10,11... | collective-permute-start | bytes 2359304 | tf_op jit(solution)/shard_map/ppermute | solution.py:602
  55.0 9.2 %collective-permute-start.11 = (bf16[256,1536]{1,0:T(8,128)(2,1)S(1)}, bf16[256,1536]{1,0:T(8,128)(2,1)S(1)}, u32[]{:S(2)}, u32[]{:S(2)}) collective-permute-start(bf16[256,1536]{1,0:T(8,128)(2,1)S(1)} %stack_rows.5), channel_id=1, source_target_pairs={{0,1},{1,0},{2,3},{3,2},{4,5},{5,4},{6,7},{7,6},{8,9},{9,8},{10,11... | collective-permute-start | bytes 2359304 | tf_op jit(solution)/shard_map/ppermute | solution.py:602
  64.2 15.8 %collective-permute-start.12 = (bf16[128,1536]{1,0:T(8,128)(2,1)S(1)}, bf16[128,1536]{1,0:T(8,128)(2,1)S(1)}, u32[]{:S(2)}, u32[]{:S(2)}) collective-permute-start(bf16[128,1536]{1,0:T(8,128)(2,1)S(1)} %get-tuple-element.115), channel_id=1, source_target_pairs={{0,1},{1,0},{2,3},{3,2},{4,5},{5,4},{6,7},{7,6},{8,9},{9,8},{10,11... | collective-permute-start | bytes 1179656 | tf_op jit(solution)/shard_map/ppermute | solution.py:602
  64.4 15.7 %collective-permute-start.13 = (bf16[128,1536]{1,0:T(8,128)(2,1)S(1)}, bf16[128,1536]{1,0:T(8,128)(2,1)S(1)}, u32[]{:S(2)}, u32[]{:S(2)}) collective-permute-start(bf16[128,1536]{1,0:T(8,128)(2,1)S(1)} %get-tuple-element.116), channel_id=1, source_target_pairs={{0,1},{1,0},{2,3},{3,2},{4,5},{5,4},{6,7},{7,6},{8,9},{9,8},{10,11... | collective-permute-start | bytes 1179656 | tf_op jit(solution)/shard_map/ppermute | solution.py:602
  65.6 14.4 %collective-permute-start.14 = (bf16[384,384]{1,0:T(8,128)(2,1)S(1)}, bf16[384,384]{1,0:T(8,128)(2,1)S(1)}, u32[]{:S(2)}, u32[]{:S(2)}) collective-permute-start(bf16[384,384]{1,0:T(8,128)(2,1)S(1)} %get-tuple-element.120), channel_id=1, source_target_pairs={{0,8},{2,10},{4,12},{6,14},{8,24},{10,26},{12,28},{14,30},{24,16},... | collective-permute-start | bytes 884744 | tf_op jit(solution)/shard_map/ppermute | solution.py:661
  69.1 17.9 %collective-permute-start.18 = (bf16[384,640]{1,0:T(8,128)(2,1)S(1)}, bf16[384,640]{1,0:T(8,128)(2,1)S(1)}, u32[]{:S(2)}, u32[]{:S(2)}) collective-permute-start(bf16[384,640]{1,0:T(8,128)(2,1)S(1)} %get-tuple-element.131), channel_id=1, source_target_pairs={{0,8},{2,10},{4,12},{6,14},{8,24},{10,26},{12,28},{14,30},{24,16},... | collective-permute-start | bytes 1474568 | tf_op jit(solution)/shard_map/ppermute | solution.py:661
  81.5 7.9 %collective-permute-start.15 = (bf16[256,384]{1,0:T(8,128)(2,1)S(1)}, bf16[256,384]{1,0:T(8,128)(2,1)S(1)}, u32[]{:S(2)}, u32[]{:S(2)}) collective-permute-start(bf16[256,384]{1,0:T(8,128)(2,1)S(1)} %get-tuple-element.123), channel_id=1, source_target_pairs={{0,2},{2,0},{4,6},{6,4},{8,10},{10,8},{12,14},{14,12},{16,18},{18,... | collective-permute-start | bytes 589832 | tf_op jit(solution)/shard_map/ppermute | solution.py:669
  83.1 10.6 %collective-permute-start.16 = (bf16[256,384]{1,0:T(8,128)(2,1)S(1)}, bf16[256,384]{1,0:T(8,128)(2,1)S(1)}, u32[]{:S(2)}, u32[]{:S(2)}) collective-permute-start(bf16[256,384]{1,0:T(8,128)(2,1)S(1)} %get-tuple-element.124), channel_id=1, source_target_pairs={{0,4},{2,6},{4,0},{6,2},{8,12},{10,14},{12,8},{14,10},{16,20},{18,... | collective-permute-start | bytes 589832 | tf_op jit(solution)/shard_map/ppermute | solution.py:669
  84.6 9.0 %collective-permute-start.17 = (bf16[256,384]{1,0:T(8,128)(2,1)S(1)}, bf16[256,384]{1,0:T(8,128)(2,1)S(1)}, u32[]{:S(2)}, u32[]{:S(2)}) collective-permute-start(bf16[256,384]{1,0:T(8,128)(2,1)S(1)} %get-tuple-element.125), channel_id=1, source_target_pairs={{0,6},{2,4},{4,2},{6,0},{8,14},{10,12},{12,10},{14,8},{16,22},{18,... | collective-permute-start | bytes 589832 | tf_op jit(solution)/shard_map/ppermute | solution.py:669
  85.1 12.2 %collective-permute-start.22 = (bf16[384,512]{1,0:T(8,128)(2,1)}, bf16[384,512]{1,0:T(8,128)(2,1)S(1)}, u32[]{:S(2)}, u32[]{:S(2)}) collective-permute-start(bf16[384,512]{1,0:T(8,128)(2,1)} %get-tuple-element.145), channel_id=1, source_target_pairs={{0,8},{2,10},{4,12},{6,14},{8,24},{10,26},{12,28},{14,30},{24,16},... | collective-permute-start | bytes 1179656 | tf_op jit(solution)/shard_map/ppermute | solution.py:661
  93.6 10.6 %collective-permute-start.19 = (bf16[256,640]{1,0:T(8,128)(2,1)S(1)}, bf16[256,640]{1,0:T(8,128)(2,1)S(1)}, u32[]{:S(2)}, u32[]{:S(2)}) collective-permute-start(bf16[256,640]{1,0:T(8,128)(2,1)S(1)} %get-tuple-element.137), channel_id=1, source_target_pairs={{0,2},{2,0},{4,6},{6,4},{8,10},{10,8},{12,14},{14,12},{16,18},{18,... | collective-permute-start | bytes 983048 | tf_op jit(solution)/shard_map/ppermute | solution.py:669
  94.9 18.0 %collective-permute-start.20 = (bf16[256,640]{1,0:T(8,128)(2,1)S(1)}, bf16[256,640]{1,0:T(8,128)(2,1)S(1)}, u32[]{:S(2)}, u32[]{:S(2)}) collective-permute-start(bf16[256,640]{1,0:T(8,128)(2,1)S(1)} %get-tuple-element.138), channel_id=1, source_target_pairs={{0,4},{2,6},{4,0},{6,2},{8,12},{10,14},{12,8},{14,10},{16,20},{18,... | collective-permute-start | bytes 983048 | tf_op jit(solution)/shard_map/ppermute | solution.py:669
  95.7 17.2 %collective-permute-start.21 = (bf16[256,640]{1,0:T(8,128)(2,1)S(1)}, bf16[256,640]{1,0:T(8,128)(2,1)S(1)}, u32[]{:S(2)}, u32[]{:S(2)}) collective-permute-start(bf16[256,640]{1,0:T(8,128)(2,1)S(1)} %get-tuple-element.139), channel_id=1, source_target_pairs={{0,6},{2,4},{4,2},{6,0},{8,14},{10,12},{12,10},{14,8},{16,22},{18,... | collective-permute-start | bytes 983048 | tf_op jit(solution)/shard_map/ppermute | solution.py:669
  104.3 12.7 %collective-permute-start.23 = (bf16[256,512]{1,0:T(8,128)(2,1)S(1)}, bf16[256,512]{1,0:T(8,128)(2,1)S(1)}, u32[]{:S(2)}, u32[]{:S(2)}) collective-permute-start(bf16[256,512]{1,0:T(8,128)(2,1)S(1)} %get-tuple-element.151), channel_id=1, source_target_pairs={{0,2},{2,0},{4,6},{6,4},{8,10},{10,8},{12,14},{14,12},{16,18},{18,... | collective-permute-start | bytes 786440 | tf_op jit(solution)/shard_map/ppermute | solution.py:669
  105.5 15.9 %collective-permute-start.24 = (bf16[256,512]{1,0:T(8,128)(2,1)S(1)}, bf16[256,512]{1,0:T(8,128)(2,1)S(1)}, u32[]{:S(2)}, u32[]{:S(2)}) collective-permute-start(bf16[256,512]{1,0:T(8,128)(2,1)S(1)} %get-tuple-element.152), channel_id=1, source_target_pairs={{0,4},{2,6},{4,0},{6,2},{8,12},{10,14},{12,8},{14,10},{16,20},{18,... | collective-permute-start | bytes 786440 | tf_op jit(solution)/shard_map/ppermute | solution.py:669
  106.3 15.1 %collective-permute-start.25 = (bf16[256,512]{1,0:T(8,128)(2,1)S(1)}, bf16[256,512]{1,0:T(8,128)(2,1)S(1)}, u32[]{:S(2)}, u32[]{:S(2)}) collective-permute-start(bf16[256,512]{1,0:T(8,128)(2,1)S(1)} %get-tuple-element.153), channel_id=1, source_target_pairs={{0,6},{2,4},{4,2},{6,0},{8,14},{10,12},{12,10},{14,8},{16,22},{18,... | collective-permute-start | bytes 786440 | tf_op jit(solution)/shard_map/ppermute | solution.py:669
  113.1 10.0 %collective-permute-start.27 = (bf16[128,640]{1,0:T(8,128)(2,1)S(1)}, bf16[128,640]{1,0:T(8,128)(2,1)S(1)}, u32[]{:S(2)}, u32[]{:S(2)}) collective-permute-start(bf16[128,640]{1,0:T(8,128)(2,1)S(1)} %get-tuple-element.159), channel_id=1, source_target_pairs={{0,1},{1,0},{2,3},{3,2},{4,5},{5,4},{6,7},{7,6},{8,9},{9,8},{10,11... | collective-permute-start | bytes 491528 | tf_op jit(solution)/shard_map/ppermute | solution.py:602
  (28 other events, 169.1 us)

commit v7 on v6

--- a/solution.py
+++ b/solution.py
@@ -381,50 +381,65 @@
     )(req, hidden)
 
 
-def place_rows(weight, pieces, unit):
-    block_rows = pieces[0].shape[0] // 2
+def place_rows(weight, pieces, unit, low=0):
+    block_rows, width = pieces[0].shape[0] // 2, weight.shape[1]
     for k, piece in enumerate(pieces):
         for which, place in ((0, unit), (1, 1 - unit)):
             at = pl.multiple_of((2 * k + place) * block_rows, 16)
-            weight[pl.ds(at, block_rows), :] = piece[which * block_rows : (which + 1) * block_rows, :]
-
-
-def begin_kernel(unit, *refs):
-    hidden, weight = refs[: PLANE + 2], refs[-1]
-    depth, width = weight.shape
-    count = depth // refs[PLANE + 2].shape[0]
-    pieces, (last_ref, *outs) = refs[PLANE + 2 : PLANE + 2 + count], refs[PLANE + 2 + count : -1]
-    place_rows(weight, pieces, unit[0])
-    rows = hidden[0].shape[0]
+            rows = slice(which * block_rows, (which + 1) * block_rows)
+            weight[pl.ds(at, block_rows), :] = piece[rows, low : low + width]
+
+
+def order_kernel(*refs):
+    hidden, (front_ref, last_ref) = refs[:-2], refs[-2:]
+    rows, done = hidden[0].shape[0], front_ref.shape[1]
     for d in range(PLANE):
         place = d % (PLANE // 2) * rows
-        other = hidden[PLANE + d // (PLANE // 2)][place : place + rows, :]
-        both = jnp.concatenate([hidden[d][...], other], axis=0)
-        span = slice(2 * d * rows, 2 * (d + 1) * rows)
-        last_ref[span, :] = both[:, depth:]
-        low = 0
-        for out in outs:
-            chunk = weight[:, low : low + out.shape[1]]
-            out[span, :] = jnp.dot(both[:, :depth], chunk, preferred_element_type=F32)
-            low += out.shape[1]
-
-
-def begin(unit, hidden, pieces, widths):
+        pair = hidden[PLANE + d // (PLANE // 2)]
+        for n, block in ((0, hidden[d][...]), (1, pair[place : place + rows, :])):
+            span = slice((2 * d + n) * rows, (2 * d + n + 1) * rows)
+            front_ref[span, :] = block[:, :done]
+            last_ref[span, :] = block[:, done:]
+
+
+def order_rows(hidden, done):
     rows, depth = hidden[0].shape
-    done = len(pieces) * pieces[0].shape[0]
     every = 2 * PLANE * rows
-    outs = pl.pallas_call(
-        begin_kernel,
-        out_shape=(jax.ShapeDtypeStruct((every, depth - done), BF16),)
-        + tuple(jax.ShapeDtypeStruct((every, w), F32) for w in widths),
-        in_specs=[SMEM] + [VMEM] * (PLANE + 2 + len(pieces)),
-        out_specs=(VMEM,) * (1 + len(widths)),
-        scratch_shapes=[pltpu.VMEM((done, pieces[0].shape[1]), BF16)],
-        compiler_params=PARAMS,
-        cost_estimate=cost(0, 12 << 20),
+    return pl.pallas_call(
+        order_kernel,
+        out_shape=(
+            jax.ShapeDtypeStruct((every, done), BF16),
+            jax.ShapeDtypeStruct((every, depth - done), BF16),
+        ),
+        in_specs=[VMEM] * len(hidden),
+        out_specs=(VMEM, VMEM),
+        compiler_params=PARAMS,
+        cost_estimate=cost(0, 6 << 20),
+        name="order_rows",
+    )(*hidden)
+
+
+def begin_kernel(low, unit, front, *refs):
+    pieces, (out, weight) = refs[:-2], refs[-2:]
+    place_rows(weight, pieces, unit[0], low)
+    rows = out.shape[0] // PLANE
+    for d in range(PLANE):
+        span = slice(d * rows, (d + 1) * rows)
+        out[span, :] = jnp.dot(front[span, :], weight[...], preferred_element_type=F32)
+
+
+def begin(unit, front, pieces, low, width):
+    every, done = front.shape
+    return pl.pallas_call(
+        functools.partial(begin_kernel, low),
+        out_shape=jax.ShapeDtypeStruct((every, width), F32),
+        in_specs=[SMEM] + [VMEM] * (1 + len(pieces)),
+        out_specs=VMEM,
+        scratch_shapes=[pltpu.VMEM((done, width), BF16)],
+        compiler_params=PARAMS,
+        cost_estimate=cost(0, 8 << 20),
         name="begin",
-    )(unit, *hidden, *pieces)
-    return outs[0], outs[1:]
+    )(unit, front, *pieces)
 
 
 def product_kernel(unit, hidden, partial, piece, own_ref, *refs):
@@ -704,14 +719,18 @@
     ]
     widths = chunk_widths(width // 2)
     ends = [pass_on(x) for x in split_columns(after(hops[-1], mixed), widths)]
-    decode_kv, decode_state, mixed = settle(
-        unit, pages_came, state_came, pages_held, state_held, mixed
-    )
-    last_hidden, partial = begin(unit, hidden, hops, widths)
-    sums, order, received = [], [mixed, *mixed_came], []
-    for n, (piece, end) in enumerate(zip(partial, ends)):
-        own, parts = product(unit, last_hidden, piece, after(end, *order))
-        order = list(parts) + [x[0] for x in sums]
+    done = len(hops) * hops[0].shape[0]
+    front, last_hidden = order_rows(hidden, done)
+    sums, order, received, low = [], mixed_came, [], 0
+    for n, end in enumerate(ends):
+        if n == 1:
+            decode_kv, decode_state, mixed = settle(
+                unit, pages_came, state_came, pages_held, state_held, after(mixed, *order)
+            )
+            order = order + [mixed]
+        piece = begin(unit, after(front, *order) if n else front, hops, low, widths[n])
+        own, parts = product(unit, last_hidden, piece, after(end, piece, *order))
+        order, low = list(parts) + [x[0] for x in sums], low + widths[n]
         if received:
             parts = after(parts, *(received if n < len(ends) - 1 else received[:1]))
         received = [plane_swap(x, d) for d, x in enumerate(parts, 1)]

time: 125 us -> 124 us (level)
  waiting for transfers between devices: 34.6 us -> 23.9 us
  local copies, waits for them, and re-layouts: 12.9 us -> 17.2 us
  Pallas kernels: 49.9 us -> 53.9 us
  starting transfers between devices: 25.4 us -> 27.1 us
    ppermute x12, waiting for transfers between devices: 25.3 us -> 15.1 us  [plane_swap(): lax.ppermute(x, 'req', [(r, r - r % PLANE + (r % PLANE ^ d)) for r in ran...]
    unnamed x47 -> x49, local copies, waits for them, and re-layouts: 12.9 us -> 17.2 us
    pallas_call x1 -> x4, Pallas kernels: 9.41 us -> 13.1 us  [the longest x3 10.2 us: begin(): pl.pallas_call(functools.partial(begin_kernel, low), out_shape=jax.ShapeD...]
    ppermute x5, starting transfers between devices: 7.96 us -> 9.74 us  [pass_on(): return lax.ppermute(x, 'req', ring_pairs)]
  transfers between devices with their start and end apart: 29 -> 29, of which waited for: 10 -> 9; matrix products, arithmetic and copies ran while one was open for 1% -> 1% of each run, Pallas kernels for 39% -> 42%
where the time goes in v7:
time: 124 us
  Pallas kernels  53.9 us (43%)
  starting transfers between devices  27.1 us (22%)
  waiting for transfers between devices  23.9 us (19%)
  local copies, waits for them, and re-layouts  17.2 us (14%)
  between operations  1.62 us (1%)
    unnamed x49, local copies, waits for them, and re-layouts  17.2 us
    ppermute x12, waiting for transfers between devices, plane_swap(): lax.ppermute(x, 'req', [(r, r - r % PLANE + (r % PLANE ^ d)) for r in ran...  15.1 us
    ppermute x12, starting transfers between devices, plane_swap(): lax.ppermute(x, 'req', [(r, r - r % PLANE + (r % PLANE ^ d)) for r in ran...  14 us
    pallas_call x1, Pallas kernels, attend(): pl.pallas_call(attend_kernel, out_shape=(jax.ShapeDtypeStruct(queries.sha...  11.4 us
    pallas_call x3, Pallas kernels, begin(): pl.pallas_call(functools.partial(begin_kernel, low), out_shape=jax.ShapeD...  10.2 us
    pallas_call x1, Pallas kernels, state_space(): pl.pallas_call(state_kernel, out_shape=(jax.ShapeDtypeStruct((length, hal...  10.1 us
    ppermute x5, starting transfers between devices, pass_on(): return lax.ppermute(x, 'req', ring_pairs)  9.74 us
    pallas_call x1, Pallas kernels, project(): pl.pallas_call(project_kernel, grid=(2 * half,), out_shape=(jax.ShapeDtyp...  8.71 us
  transfers between devices with their start and end apart: 29, of which 9 were waited for; matrix products, arithmetic and copies ran while one was open for 1% of the time, Pallas kernels for 42%

profile of v7, /device:TPU:0, one launch (start us, length us, event | category | flops | bytes accessed | tf_op | source)
XLA Modules:
  0.0 123.7 jit_solution(4831772314865402299)
XLA Ops:
  2.5 1.6 %collective-permute-done.refs_1_ = bf16[192,1536]{1,0:T(8,128)(2,1)S(1)} collective-permute-done((bf16[192,1536]{1,0:T(8,128)(2,1)S(1)}, bf16[192,1536]{1,0:T(8,128)(2,1)S(1)}, u32[]{:S(2)}, u32[]{:S(2)}) %collective-permute-start) | collective-permute-done | bytes 589856 | tf_op jit(solution)/shard_map/ppermute | solution.py:617
  4.2 3.0 %collective-permute-start.1 = (bf16[384,1536]{1,0:T(8,128)(2,1)S(1)}, bf16[384,1536]{1,0:T(8,128)(2,1)S(1)}, u32[]{:S(2)}, u32[]{:S(2)}) collective-permute-start(bf16[384,1536]{1,0:T(8,128)(2,1)S(1)} %stack_rows.3.refs_0_), channel_id=1, source_target_pairs={{0,8},{2,10},{4,12},{6,14},{8,24},{10,26},{12,28},{14,30},{24,16},... | collective-permute-start | bytes 3538952 | tf_op jit(solution)/shard_map/ppermute | solution.py:676
  10.8 1.5 %collective-permute-start.4 = (bf16[128,1536]{1,0:T(8,128)(2,1)}, bf16[128,1536]{1,0:T(8,128)(2,1)}, u32[]{:S(2)}, u32[]{:S(2)}) collective-permute-start(bf16[128,1536]{1,0:T(8,128)(2,1)} %get-tuple-element.100), channel_id=1, source_target_pairs={{0,2},{2,0},{4,6},{6,4},{8,10},{10,8},{12,14},{14,12},{16,18},{18,... | collective-permute-start | bytes 1179656 | tf_op jit(solution)/shard_map/ppermute | solution.py:684
  12.3 1.5 %collective-permute-start.5 = (bf16[128,1536]{1,0:T(8,128)(2,1)}, bf16[128,1536]{1,0:T(8,128)(2,1)}, u32[]{:S(2)}, u32[]{:S(2)}) collective-permute-start(bf16[128,1536]{1,0:T(8,128)(2,1)} %get-tuple-element.101), channel_id=1, source_target_pairs={{0,4},{2,6},{4,0},{6,2},{8,12},{10,14},{12,8},{14,10},{16,20},{18,... | collective-permute-start | bytes 1179656 | tf_op jit(solution)/shard_map/ppermute | solution.py:684
  16.5 11.4 %attend.1 = (bf16[128,1536]{1,0:T(8,128)(2,1)S(1)}, bf16[14,128,512]{2,1,0:T(8,128)(2,1)}, bf16[7,128,512]{2,1,0:T(8,128)(2,1)S(1)}) custom-call(s32[1,13]{1,0:T(1,128)S(1)} %copy-done.17, s32[1]{0:T(128)S(6)} %copy.29.ctx, s32[1,13]{1,0:T(1,128)S(1)} %bitcast.7, s32[1]{0:T(128)} %bitcast.unit, bf16[128,1536]{1,0:T(8,128)(2,1)S(1)} %copy-done.10, ...), custom_call_target="tpu_custom_call" | custom-call | tf_op jit(solution)/shard_map/attend/pallas_call | solution.py:128
  29.7 4.9 %collective-permute-done.1.refs_1_ = bf16[384,1536]{1,0:T(8,128)(2,1)S(1)} collective-permute-done((bf16[384,1536]{1,0:T(8,128)(2,1)S(1)}, bf16[384,1536]{1,0:T(8,128)(2,1)S(1)}, u32[]{:S(2)}, u32[]{:S(2)}) %collective-permute-start.1) | collective-permute-done | bytes 1179680 | tf_op jit(solution)/shard_map/ppermute | solution.py:676
  43.1 10.1 %state_space.1 = (bf16[128,2304]{1,0:T(8,128)(2,1)S(1)}, bf16[128,1152]{1,0:T(8,128)(2,1)S(1)}, bf16[128,1152]{1,0:T(8,128)(2,1)S(1)}, f32[2,12,128,256]{3,2,1,0:T(8,128)}, bf16[12,128,256]{2,1,0:T(8,128)(2,1)S(1)}) custom-call(s32[1]{0:T(128)} %bitcast.unit, f32[24]{0:T(128)S(1)} %copy-done.19, bf16[128,1536]{1,0:T(8,128)(2,1)S(1)} %copy-done.12, ...), custom_call_target="tpu_custom_call" | custom-call | tf_op jit(solution)/shard_map/state_space/pallas_call | solution.py:253
  57.1 8.7 %project.1 = (bf16[128,3072]{1,0:T(8,128)(2,1)S(1)}, bf16[128,1536]{1,0:T(8,128)(2,1)S(1)}, bf16[128,1536]{1,0:T(8,128)(2,1)S(1)}) custom-call(bf16[128,2304]{1,0:T(8,128)(2,1)S(1)} %get-tuple-element.93.stay_ref, bf16[128,1152]{1,0:T(8,128)(2,1)S(1)} %collective-permute-done.7.a_ref, bf16[128,1152]{1,0:T(8,128)(2,1)S(1)} %collective-permute-done.8.b_ref, ...), custom_call_target="tpu_custom_call" | custom-call | tf_op jit(solution)/shard_map/project/pallas_call | solution.py:557
  67.3 3.4 %collective-permute-start.12 = (bf16[384,384]{1,0:T(8,128)(2,1)S(1)}, bf16[384,384]{1,0:T(8,128)(2,1)S(1)}, u32[]{:S(2)}, u32[]{:S(2)}) collective-permute-start(bf16[384,384]{1,0:T(8,128)(2,1)S(1)} %get-tuple-element.116), channel_id=1, source_target_pairs={{0,8},{2,10},{4,12},{6,14},{8,24},{10,26},{12,28},{14,30},{24,16},... | collective-permute-start | bytes 884744 | tf_op jit(solution)/shard_map/ppermute | solution.py:676
  70.7 2.9 %order_rows.1 = (bf16[1024,1152]{1,0:T(8,128)(2,1)}, bf16[1024,384]{1,0:T(8,128)(2,1)S(1)}) custom-call(bf16[128,1536]{1,0:T(8,128)(2,1)S(1)} %copy-done.5, bf16[128,1536]{1,0:T(8,128)(2,1)} %collective-permute-done.4.refs_1_, bf16[128,1536]{1,0:T(8,128)(2,1)} %collective-permute-done.5.refs_0_.refs_2_, ...), custom_call_target="tpu_custom_call" | custom-call | tf_op jit(solution)/shard_map/order_rows/pallas_call | solution.py:408
  73.6 3.2 %begin.3.partial = f32[1024,384]{1,0:T(8,128)S(1)} custom-call(s32[1]{0:T(128)} %bitcast.unit, bf16[1024,1152]{1,0:T(8,128)(2,1)} %get-tuple-element.146.front, bf16[384,1536]{1,0:T(8,128)(2,1)S(1)} %stack_rows.3.refs_0_, bf16[384,1536]{1,0:T(8,128)(2,1)S(1)} %collective-permute-done.1.refs_1_, bf16[384,1536]{1,0:T(8,128)(2,1)S(1)} %collective-permute-done.11.refs_2_.x_ref), custom_call_target="tpu_custom_call" | custom-call | tf_op jit(solution)/shard_map/begin/pallas_call | solution.py:433
  80.7 1.5 %collective-permute-start.16 = (bf16[256,384]{1,0:T(8,128)(2,1)S(1)}, bf16[256,384]{1,0:T(8,128)(2,1)S(1)}, u32[]{:S(2)}, u32[]{:S(2)}) collective-permute-start(bf16[256,384]{1,0:T(8,128)(2,1)S(1)} %get-tuple-element.123), channel_id=1, source_target_pairs={{0,4},{2,6},{4,0},{6,2},{8,12},{10,14},{12,8},{14,10},{16,20},{18,... | collective-permute-start | bytes 589832 | tf_op jit(solution)/shard_map/ppermute | solution.py:684
  82.7 2.5 %collective-permute-start.22 = (bf16[384,512]{1,0:T(8,128)(2,1)}, bf16[384,512]{1,0:T(8,128)(2,1)S(1)}, u32[]{:S(2)}, u32[]{:S(2)}) collective-permute-start(bf16[384,512]{1,0:T(8,128)(2,1)} %get-tuple-element.147), channel_id=1, source_target_pairs={{0,8},{2,10},{4,12},{6,14},{8,24},{10,26},{12,28},{14,30},{24,16},... | collective-permute-start | bytes 1179656 | tf_op jit(solution)/shard_map/ppermute | solution.py:676
  87.8 3.8 %begin.4.partial = f32[1024,640]{1,0:T(8,128)} custom-call(s32[1]{0:T(128)} %bitcast.unit, bf16[1024,1152]{1,0:T(8,128)(2,1)S(1)} %copy-done, bf16[384,1536]{1,0:T(8,128)(2,1)S(1)} %stack_rows.3.refs_0_, bf16[384,1536]{1,0:T(8,128)(2,1)S(1)} %collective-permute-done.1.refs_1_, bf16[384,1536]{1,0:T(8,128)(2,1)S(1)} %collective-permute-done.11.refs_2_.x_ref), custom_call_target="tpu_custom_call" | custom-call | tf_op jit(solution)/shard_map/begin/pallas_call | solution.py:433
  91.5 1.7 %copy-done.1 = f32[1024,640]{1,0:T(8,128)S(1)} copy-done((f32[1024,640]{1,0:T(8,128)S(1)}, f32[1024,640]{1,0:T(8,128)}, u32[]{:S(2)}) %copy-start.1) | copy-done | bytes 2621464
  94.3 1.6 %collective-permute-start.19 = (bf16[256,640]{1,0:T(8,128)(2,1)S(1)}, bf16[256,640]{1,0:T(8,128)(2,1)S(1)}, u32[]{:S(2)}, u32[]{:S(2)}) collective-permute-start(bf16[256,640]{1,0:T(8,128)(2,1)S(1)} %get-tuple-element.139), channel_id=1, source_target_pairs={{0,2},{2,0},{4,6},{6,4},{8,10},{10,8},{12,14},{14,12},{16,18},{18,... | collective-permute-start | bytes 983048 | tf_op jit(solution)/shard_map/ppermute | solution.py:684
  95.9 1.5 %collective-permute-start.20 = (bf16[256,640]{1,0:T(8,128)(2,1)S(1)}, bf16[256,640]{1,0:T(8,128)(2,1)S(1)}, u32[]{:S(2)}, u32[]{:S(2)}) collective-permute-start(bf16[256,640]{1,0:T(8,128)(2,1)S(1)} %get-tuple-element.140), channel_id=1, source_target_pairs={{0,4},{2,6},{4,0},{6,2},{8,12},{10,14},{12,8},{14,10},{16,20},{18,... | collective-permute-start | bytes 983048 | tf_op jit(solution)/shard_map/ppermute | solution.py:684
  97.9 3.3 %begin.5.partial = f32[1024,512]{1,0:T(8,128)S(1)} custom-call(s32[1]{0:T(128)} %bitcast.unit, bf16[1024,1152]{1,0:T(8,128)(2,1)} %get-tuple-element.146.front, bf16[384,1536]{1,0:T(8,128)(2,1)S(1)} %stack_rows.3.refs_0_, bf16[384,1536]{1,0:T(8,128)(2,1)S(1)} %collective-permute-done.1.refs_1_, bf16[384,1536]{1,0:T(8,128)(2,1)S(1)} %collective-permute-done.11.refs_2_.x_ref), custom_call_target="tpu_custom_call" | custom-call | tf_op jit(solution)/shard_map/begin/pallas_call | solution.py:433
  102.0 3.0 %collective-permute-done.19.refs_0_ = bf16[256,640]{1,0:T(8,128)(2,1)S(1)} collective-permute-done((bf16[256,640]{1,0:T(8,128)(2,1)S(1)}, bf16[256,640]{1,0:T(8,128)(2,1)S(1)}, u32[]{:S(2)}, u32[]{:S(2)}) %collective-permute-start.19) | collective-permute-done | bytes 327712 | tf_op jit(solution)/shard_map/ppermute | solution.py:684
  105.0 1.5 %collective-permute-start.23 = (bf16[256,512]{1,0:T(8,128)(2,1)S(1)}, bf16[256,512]{1,0:T(8,128)(2,1)S(1)}, u32[]{:S(2)}, u32[]{:S(2)}) collective-permute-start(bf16[256,512]{1,0:T(8,128)(2,1)S(1)} %get-tuple-element.153), channel_id=1, source_target_pairs={{0,2},{2,0},{4,6},{6,4},{8,10},{10,8},{12,14},{14,12},{16,18},{18,... | collective-permute-start | bytes 786440 | tf_op jit(solution)/shard_map/ppermute | solution.py:684
  106.5 1.5 %collective-permute-start.24 = (bf16[256,512]{1,0:T(8,128)(2,1)S(1)}, bf16[256,512]{1,0:T(8,128)(2,1)S(1)}, u32[]{:S(2)}, u32[]{:S(2)}) collective-permute-start(bf16[256,512]{1,0:T(8,128)(2,1)S(1)} %get-tuple-element.154), channel_id=1, source_target_pairs={{0,4},{2,6},{4,0},{6,2},{8,12},{10,14},{12,8},{14,10},{16,20},{18,... | collective-permute-start | bytes 786440 | tf_op jit(solution)/shard_map/ppermute | solution.py:684
  108.5 3.9 %collective-permute-done.20.refs_1_ = bf16[256,640]{1,0:T(8,128)(2,1)S(1)} collective-permute-done((bf16[256,640]{1,0:T(8,128)(2,1)S(1)}, bf16[256,640]{1,0:T(8,128)(2,1)S(1)}, u32[]{:S(2)}, u32[]{:S(2)}) %collective-permute-start.20) | collective-permute-done | bytes 327712 | tf_op jit(solution)/shard_map/ppermute | solution.py:684
  113.3 3.5 %collective-permute-done.23.refs_0_ = bf16[256,512]{1,0:T(8,128)(2,1)S(1)} collective-permute-done((bf16[256,512]{1,0:T(8,128)(2,1)S(1)}, bf16[256,512]{1,0:T(8,128)(2,1)S(1)}, u32[]{:S(2)}, u32[]{:S(2)}) %collective-permute-start.23) | collective-permute-done | bytes 262176 | tf_op jit(solution)/shard_map/ppermute | solution.py:684
  116.8 4.0 %collective-permute-done.24.refs_1_ = bf16[256,512]{1,0:T(8,128)(2,1)S(1)} collective-permute-done((bf16[256,512]{1,0:T(8,128)(2,1)S(1)}, bf16[256,512]{1,0:T(8,128)(2,1)S(1)}, u32[]{:S(2)}, u32[]{:S(2)}) %collective-permute-start.24) | collective-permute-done | bytes 262176 | tf_op jit(solution)/shard_map/ppermute | solution.py:684
  (104 shorter events, 36.6 us)
Async XLA Ops:
  4.2 30.3 %collective-permute-start.1 = (bf16[384,1536]{1,0:T(8,128)(2,1)S(1)}, bf16[384,1536]{1,0:T(8,128)(2,1)S(1)}, u32[]{:S(2)}, u32[]{:S(2)}) collective-permute-start(bf16[384,1536]{1,0:T(8,128)(2,1)S(1)} %stack_rows.3.refs_0_), channel_id=1, source_target_pairs={{0,8},{2,10},{4,12},{6,14},{8,24},{10,26},{12,28},{14,30},{24,16},... | collective-permute-start | bytes 3538952 | tf_op jit(solution)/shard_map/ppermute | solution.py:676
  10.8 42.4 %collective-permute-start.4 = (bf16[128,1536]{1,0:T(8,128)(2,1)}, bf16[128,1536]{1,0:T(8,128)(2,1)}, u32[]{:S(2)}, u32[]{:S(2)}) collective-permute-start(bf16[128,1536]{1,0:T(8,128)(2,1)} %get-tuple-element.100), channel_id=1, source_target_pairs={{0,2},{2,0},{4,6},{6,4},{8,10},{10,8},{12,14},{14,12},{16,18},{18,... | collective-permute-start | bytes 1179656 | tf_op jit(solution)/shard_map/ppermute | solution.py:684
  12.3 40.9 %collective-permute-start.5 = (bf16[128,1536]{1,0:T(8,128)(2,1)}, bf16[128,1536]{1,0:T(8,128)(2,1)}, u32[]{:S(2)}, u32[]{:S(2)}) collective-permute-start(bf16[128,1536]{1,0:T(8,128)(2,1)} %get-tuple-element.101), channel_id=1, source_target_pairs={{0,4},{2,6},{4,0},{6,2},{8,12},{10,14},{12,8},{14,10},{16,20},{18,... | collective-permute-start | bytes 1179656 | tf_op jit(solution)/shard_map/ppermute | solution.py:684
  13.8 39.4 %collective-permute-start.6 = (bf16[128,1536]{1,0:T(8,128)(2,1)}, bf16[128,1536]{1,0:T(8,128)(2,1)}, u32[]{:S(2)}, u32[]{:S(2)}) collective-permute-start(bf16[128,1536]{1,0:T(8,128)(2,1)} %get-tuple-element.102), channel_id=1, source_target_pairs={{0,6},{2,4},{4,2},{6,0},{8,14},{10,12},{12,10},{14,8},{16,22},{18,... | collective-permute-start | bytes 1179656 | tf_op jit(solution)/shard_map/ppermute | solution.py:684
  34.5 31.4 %collective-permute-start.11 = (bf16[384,1536]{1,0:T(8,128)(2,1)S(1)}, bf16[384,1536]{1,0:T(8,128)(2,1)S(1)}, u32[]{:S(2)}, u32[]{:S(2)}) collective-permute-start(bf16[384,1536]{1,0:T(8,128)(2,1)S(1)} %collective-permute-done.1.refs_1_), channel_id=1, source_target_pairs={{0,8},{2,10},{4,12},{6,14},{8,24},{10,26},{12,28},{14,30},{24,16},... | collective-permute-start | bytes 3538952 | tf_op jit(solution)/shard_map/ppermute | solution.py:676
  53.8 12.0 %collective-permute-start.2 = (bf16[7,128,512]{2,1,0:T(8,128)(2,1)S(1)}, bf16[7,128,512]{2,1,0:T(8,128)(2,1)S(1)}, u32[]{:S(2)}, u32[]{:S(2)}) collective-permute-start(bf16[7,128,512]{2,1,0:T(8,128)(2,1)S(1)} %copy-done.23), channel_id=1, source_target_pairs={{0,1},{1,0},{2,3},{3,2},{4,5},{5,4},{6,7},{7,6},{8,9},{9,8},{10,11... | collective-permute-start | bytes 2752520 | tf_op jit(solution)/shard_map/ppermute | solution.py:617
  56.1 9.7 %collective-permute-start.3 = (bf16[12,128,256]{2,1,0:T(8,128)(2,1)S(1)}, bf16[12,128,256]{2,1,0:T(8,128)(2,1)S(1)}, u32[]{:S(2)}, u32[]{:S(2)}) collective-permute-start(bf16[12,128,256]{2,1,0:T(8,128)(2,1)S(1)} %get-tuple-element.95), channel_id=1, source_target_pairs={{0,1},{1,0},{2,3},{3,2},{4,5},{5,4},{6,7},{7,6},{8,9},{9,8},{10,11... | collective-permute-start | bytes 2359304 | tf_op jit(solution)/shard_map/ppermute | solution.py:617
  56.6 9.2 %collective-permute-start.10 = (bf16[256,1536]{1,0:T(8,128)(2,1)S(1)}, bf16[256,1536]{1,0:T(8,128)(2,1)S(1)}, u32[]{:S(2)}, u32[]{:S(2)}) collective-permute-start(bf16[256,1536]{1,0:T(8,128)(2,1)S(1)} %stack_rows.5), channel_id=1, source_target_pairs={{0,1},{1,0},{2,3},{3,2},{4,5},{5,4},{6,7},{7,6},{8,9},{9,8},{10,11... | collective-permute-start | bytes 2359304 | tf_op jit(solution)/shard_map/ppermute | solution.py:617
  56.7 9.2 %collective-permute-start.9 = (bf16[256,1536]{1,0:T(8,128)(2,1)S(1)}, bf16[256,1536]{1,0:T(8,128)(2,1)S(1)}, u32[]{:S(2)}, u32[]{:S(2)}) collective-permute-start(bf16[256,1536]{1,0:T(8,128)(2,1)S(1)} %stack_rows.4), channel_id=1, source_target_pairs={{0,1},{1,0},{2,3},{3,2},{4,5},{5,4},{6,7},{7,6},{8,9},{9,8},{10,11... | collective-permute-start | bytes 2359304 | tf_op jit(solution)/shard_map/ppermute | solution.py:617
  65.9 12.2 %collective-permute-start.13 = (bf16[128,1536]{1,0:T(8,128)(2,1)S(1)}, bf16[128,1536]{1,0:T(8,128)(2,1)S(1)}, u32[]{:S(2)}, u32[]{:S(2)}) collective-permute-start(bf16[128,1536]{1,0:T(8,128)(2,1)S(1)} %get-tuple-element.119), channel_id=1, source_target_pairs={{0,1},{1,0},{2,3},{3,2},{4,5},{5,4},{6,7},{7,6},{8,9},{9,8},{10,11... | collective-permute-start | bytes 1179656 | tf_op jit(solution)/shard_map/ppermute | solution.py:617
  66.1 12.0 %collective-permute-start.14 = (bf16[128,1536]{1,0:T(8,128)(2,1)S(1)}, bf16[128,1536]{1,0:T(8,128)(2,1)S(1)}, u32[]{:S(2)}, u32[]{:S(2)}) collective-permute-start(bf16[128,1536]{1,0:T(8,128)(2,1)S(1)} %get-tuple-element.120), channel_id=1, source_target_pairs={{0,1},{1,0},{2,3},{3,2},{4,5},{5,4},{6,7},{7,6},{8,9},{9,8},{10,11... | collective-permute-start | bytes 1179656 | tf_op jit(solution)/shard_map/ppermute | solution.py:617
  67.3 10.8 %collective-permute-start.12 = (bf16[384,384]{1,0:T(8,128)(2,1)S(1)}, bf16[384,384]{1,0:T(8,128)(2,1)S(1)}, u32[]{:S(2)}, u32[]{:S(2)}) collective-permute-start(bf16[384,384]{1,0:T(8,128)(2,1)S(1)} %get-tuple-element.116), channel_id=1, source_target_pairs={{0,8},{2,10},{4,12},{6,14},{8,24},{10,26},{12,28},{14,30},{24,16},... | collective-permute-start | bytes 884744 | tf_op jit(solution)/shard_map/ppermute | solution.py:676
  70.7 20.8 %collective-permute-start.18 = (bf16[384,640]{1,0:T(8,128)(2,1)S(1)}, bf16[384,640]{1,0:T(8,128)(2,1)S(1)}, u32[]{:S(2)}, u32[]{:S(2)}) collective-permute-start(bf16[384,640]{1,0:T(8,128)(2,1)S(1)} %get-tuple-element.133), channel_id=1, source_target_pairs={{0,8},{2,10},{4,12},{6,14},{8,24},{10,26},{12,28},{14,30},{24,16},... | collective-permute-start | bytes 1474568 | tf_op jit(solution)/shard_map/ppermute | solution.py:676
  79.2 15.0 %collective-permute-start.15 = (bf16[256,384]{1,0:T(8,128)(2,1)}, bf16[256,384]{1,0:T(8,128)(2,1)S(1)}, u32[]{:S(2)}, u32[]{:S(2)}) collective-permute-start(bf16[256,384]{1,0:T(8,128)(2,1)} %get-tuple-element.122), channel_id=1, source_target_pairs={{0,2},{2,0},{4,6},{6,4},{8,10},{10,8},{12,14},{14,12},{16,18},{18,... | collective-permute-start | bytes 589832 | tf_op jit(solution)/shard_map/ppermute | solution.py:684
  80.7 13.6 %collective-permute-start.16 = (bf16[256,384]{1,0:T(8,128)(2,1)S(1)}, bf16[256,384]{1,0:T(8,128)(2,1)S(1)}, u32[]{:S(2)}, u32[]{:S(2)}) collective-permute-start(bf16[256,384]{1,0:T(8,128)(2,1)S(1)} %get-tuple-element.123), channel_id=1, source_target_pairs={{0,4},{2,6},{4,0},{6,2},{8,12},{10,14},{12,8},{14,10},{16,20},{18,... | collective-permute-start | bytes 589832 | tf_op jit(solution)/shard_map/ppermute | solution.py:684
  82.3 12.0 %collective-permute-start.17 = (bf16[256,384]{1,0:T(8,128)(2,1)S(1)}, bf16[256,384]{1,0:T(8,128)(2,1)S(1)}, u32[]{:S(2)}, u32[]{:S(2)}) collective-permute-start(bf16[256,384]{1,0:T(8,128)(2,1)S(1)} %get-tuple-element.124), channel_id=1, source_target_pairs={{0,6},{2,4},{4,2},{6,0},{8,14},{10,12},{12,10},{14,8},{16,22},{18,... | collective-permute-start | bytes 589832 | tf_op jit(solution)/shard_map/ppermute | solution.py:684
  82.7 18.5 %collective-permute-start.22 = (bf16[384,512]{1,0:T(8,128)(2,1)}, bf16[384,512]{1,0:T(8,128)(2,1)S(1)}, u32[]{:S(2)}, u32[]{:S(2)}) collective-permute-start(bf16[384,512]{1,0:T(8,128)(2,1)} %get-tuple-element.147), channel_id=1, source_target_pairs={{0,8},{2,10},{4,12},{6,14},{8,24},{10,26},{12,28},{14,30},{24,16},... | collective-permute-start | bytes 1179656 | tf_op jit(solution)/shard_map/ppermute | solution.py:676
  94.3 10.7 %collective-permute-start.19 = (bf16[256,640]{1,0:T(8,128)(2,1)S(1)}, bf16[256,640]{1,0:T(8,128)(2,1)S(1)}, u32[]{:S(2)}, u32[]{:S(2)}) collective-permute-start(bf16[256,640]{1,0:T(8,128)(2,1)S(1)} %get-tuple-element.139), channel_id=1, source_target_pairs={{0,2},{2,0},{4,6},{6,4},{8,10},{10,8},{12,14},{14,12},{16,18},{18,... | collective-permute-start | bytes 983048 | tf_op jit(solution)/shard_map/ppermute | solution.py:684
  95.9 16.6 %collective-permute-start.20 = (bf16[256,640]{1,0:T(8,128)(2,1)S(1)}, bf16[256,640]{1,0:T(8,128)(2,1)S(1)}, u32[]{:S(2)}, u32[]{:S(2)}) collective-permute-start(bf16[256,640]{1,0:T(8,128)(2,1)S(1)} %get-tuple-element.140), channel_id=1, source_target_pairs={{0,4},{2,6},{4,0},{6,2},{8,12},{10,14},{12,8},{14,10},{16,20},{18,... | collective-permute-start | bytes 983048 | tf_op jit(solution)/shard_map/ppermute | solution.py:684
  97.4 15.7 %collective-permute-start.21 = (bf16[256,640]{1,0:T(8,128)(2,1)S(1)}, bf16[256,640]{1,0:T(8,128)(2,1)S(1)}, u32[]{:S(2)}, u32[]{:S(2)}) collective-permute-start(bf16[256,640]{1,0:T(8,128)(2,1)S(1)} %get-tuple-element.141), channel_id=1, source_target_pairs={{0,6},{2,4},{4,2},{6,0},{8,14},{10,12},{12,10},{14,8},{16,22},{18,... | collective-permute-start | bytes 983048 | tf_op jit(solution)/shard_map/ppermute | solution.py:684
  105.0 11.8 %collective-permute-start.23 = (bf16[256,512]{1,0:T(8,128)(2,1)S(1)}, bf16[256,512]{1,0:T(8,128)(2,1)S(1)}, u32[]{:S(2)}, u32[]{:S(2)}) collective-permute-start(bf16[256,512]{1,0:T(8,128)(2,1)S(1)} %get-tuple-element.153), channel_id=1, source_target_pairs={{0,2},{2,0},{4,6},{6,4},{8,10},{10,8},{12,14},{14,12},{16,18},{18,... | collective-permute-start | bytes 786440 | tf_op jit(solution)/shard_map/ppermute | solution.py:684
  106.5 14.2 %collective-permute-start.24 = (bf16[256,512]{1,0:T(8,128)(2,1)S(1)}, bf16[256,512]{1,0:T(8,128)(2,1)S(1)}, u32[]{:S(2)}, u32[]{:S(2)}) collective-permute-start(bf16[256,512]{1,0:T(8,128)(2,1)S(1)} %get-tuple-element.154), channel_id=1, source_target_pairs={{0,4},{2,6},{4,0},{6,2},{8,12},{10,14},{12,8},{14,10},{16,20},{18,... | collective-permute-start | bytes 786440 | tf_op jit(solution)/shard_map/ppermute | solution.py:684
  108.0 12.7 %collective-permute-start.25 = (bf16[256,512]{1,0:T(8,128)(2,1)S(1)}, bf16[256,512]{1,0:T(8,128)(2,1)S(1)}, u32[]{:S(2)}, u32[]{:S(2)}) collective-permute-start(bf16[256,512]{1,0:T(8,128)(2,1)S(1)} %get-tuple-element.155), channel_id=1, source_target_pairs={{0,6},{2,4},{4,2},{6,0},{8,14},{10,12},{12,10},{14,8},{16,22},{18,... | collective-permute-start | bytes 786440 | tf_op jit(solution)/shard_map/ppermute | solution.py:684
  113.2 9.2 %collective-permute-start.27 = (bf16[128,640]{1,0:T(8,128)(2,1)S(1)}, bf16[128,640]{1,0:T(8,128)(2,1)S(1)}, u32[]{:S(2)}, u32[]{:S(2)}) collective-permute-start(bf16[128,640]{1,0:T(8,128)(2,1)S(1)} %get-tuple-element.161), channel_id=1, source_target_pairs={{0,1},{1,0},{2,3},{3,2},{4,5},{5,4},{6,7},{7,6},{8,9},{9,8},{10,11... | collective-permute-start | bytes 491528 | tf_op jit(solution)/shard_map/ppermute | solution.py:617
  (29 other events, 170.7 us)

commit v8 on v7

--- a/solution.py
+++ b/solution.py
@@ -23,7 +23,7 @@
 VMEM = pl.BlockSpec(memory_space=pltpu.VMEM)
 SMEM = pl.BlockSpec(memory_space=pltpu.SMEM)
 ANY = pl.BlockSpec(memory_space=pl.ANY)
-PARAMS = pltpu.CompilerParams(vmem_limit_bytes=48 * 1024 * 1024)
+PARAMS = pltpu.CompilerParams(vmem_limit_bytes=24 * 1024 * 1024)
 
 
 def cost(flops, moved, exps=0):
@@ -531,12 +531,18 @@
     )(unit, resid, mixed, *mixed_came, *kept, *came)
 
 
-def project_kernel(stay_ref, a_ref, b_ref, weight_ref, keep_ref, low_ref, high_ref):
+def project_kernel(stay_ref, a_ref, b_ref, weight_ref, keep_ref, low_ref, high_ref, both):
     rows = stay_ref.shape[0]
     half = pl.num_programs(0) // 2
-    came = jnp.concatenate([a_ref[...], b_ref[...]], axis=1)
-    both = jnp.concatenate([stay_ref[...], came], axis=0)
-    result = jnp.dot(both, weight_ref[...], preferred_element_type=F32).astype(BF16)
+    cut_at = a_ref.shape[1]
+
+    @pl.when(pl.program_id(0) == 0)
+    def _():
+        both[:rows, :] = stay_ref[...]
+        both[rows:, :cut_at] = a_ref[...]
+        both[rows:, cut_at:] = b_ref[...]
+
+    result = jnp.dot(both[...], weight_ref[...], preferred_element_type=F32).astype(BF16)
     keep_ref[...] = result[:rows]
 
     @pl.when(pl.program_id(0) < half)
@@ -568,6 +574,7 @@
             pl.BlockSpec((rows, tile), lambda i: (0, jnp.minimum(i, half - 1))),
             pl.BlockSpec((rows, tile), lambda i: (0, jnp.maximum(i - half, 0))),
         ),
+        scratch_shapes=[pltpu.VMEM((2 * rows, depth), BF16)],
         compiler_params=PARAMS,
         cost_estimate=cost(0, 15 << 20),
         name="project",
@@ -723,19 +730,18 @@
     front, last_hidden = order_rows(hidden, done)
     sums, order, received, low = [], mixed_came, [], 0
     for n, end in enumerate(ends):
-        if n == 1:
-            decode_kv, decode_state, mixed = settle(
-                unit, pages_came, state_came, pages_held, state_held, after(mixed, *order)
-            )
-            order = order + [mixed]
         piece = begin(unit, after(front, *order) if n else front, hops, low, widths[n])
         own, parts = product(unit, last_hidden, piece, after(end, piece, *order))
         order, low = list(parts) + [x[0] for x in sums], low + widths[n]
+        if n == len(ends) - 1:
+            decode_kv, decode_state, mixed = settle(
+                unit, pages_came, state_came, pages_held, state_held, after(mixed, *parts)
+            )
         if received:
             parts = after(parts, *(received if n < len(ends) - 1 else received[:1]))
         received = [plane_swap(x, d) for d, x in enumerate(parts, 1)]
         token = sums[-1][0] if sums else own
-        sums.append(total(own, after(received, token)))
+        sums.append(total(own, after(received, token, *([mixed] if n == len(ends) - 1 else []))))
     kept, leave = zip(*sums)
     came = [swap_units(x) for x in leave]
     layer_out = finish(unit, resid, mixed, mixed_came, kept, came)

time: 124 us -> 123 us (level)
  Pallas kernels: 53.9 us -> 42.6 us
  waiting for transfers between devices: 23.9 us -> 29.7 us
  local copies, waits for them, and re-layouts: 17.2 us -> 21.3 us
    ppermute x5, waiting for transfers between devices: 6.15 us -> 11.8 us  [pass_on(): return lax.ppermute(x, 'req', ring_pairs)]
    pallas_call x3, Pallas kernels: 10.2 us -> 5.44 us  [begin(): pl.pallas_call(functools.partial(begin_kernel, low), out_shape=jax.ShapeD...]
    unnamed x49, local copies, waits for them, and re-layouts: 17.2 us -> 21.3 us
    pallas_call x1, Pallas kernels: 8.71 us -> 6.06 us  [project(): pl.pallas_call(project_kernel, grid=(2 * half,), out_shape=(jax.ShapeDtyp...]
    pallas_call x1, Pallas kernels: 2.86 us -> 1.47 us  [order_rows(): pl.pallas_call(order_kernel, out_shape=(jax.ShapeDtypeStruct((every, done...]
    pallas_call x1, Pallas kernels: 10.1 us -> 8.7 us  [state_space(): pl.pallas_call(state_kernel, out_shape=(jax.ShapeDtypeStruct((length, hal...]
  transfers between devices with their start and end apart: 29 -> 29, of which waited for: 9 -> 12; matrix products, arithmetic and copies ran while one was open for 1% -> 1% of each run, Pallas kernels for 42% -> 34%
where the time goes in v8:
time: 123 us; the launch traced here: 122 us
  Pallas kernels  42.6 us (35%)
  waiting for transfers between devices  29.7 us (24%)
  starting transfers between devices  27.2 us (22%)
  local copies, waits for them, and re-layouts  21.3 us (17%)
  between operations  1.61 us (1%)
    unnamed x49, local copies, waits for them, and re-layouts  21.3 us
    ppermute x12, waiting for transfers between devices, plane_swap(): lax.ppermute(x, 'req', [(r, r - r % PLANE + (r % PLANE ^ d)) for r in ran...  15.2 us
    ppermute x12, starting transfers between devices, plane_swap(): lax.ppermute(x, 'req', [(r, r - r % PLANE + (r % PLANE ^ d)) for r in ran...  14 us
    ppermute x5, waiting for transfers between devices, pass_on(): return lax.ppermute(x, 'req', ring_pairs)  11.8 us
    pallas_call x1, Pallas kernels, attend(): pl.pallas_call(attend_kernel, out_shape=(jax.ShapeDtypeStruct(queries.sha...  11.4 us
    ppermute x5, starting transfers between devices, pass_on(): return lax.ppermute(x, 'req', ring_pairs)  9.83 us
    pallas_call x1, Pallas kernels, state_space(): pl.pallas_call(state_kernel, out_shape=(jax.ShapeDtypeStruct((length, hal...  8.7 us
    pallas_call x1, Pallas kernels, project(): pl.pallas_call(project_kernel, grid=(2 * half,), out_shape=(jax.ShapeDtyp...  6.06 us
  transfers between devices with their start and end apart: 29, of which 12 were waited for; matrix products, arithmetic and copies ran while one was open for 1% of the time, Pallas kernels for 34%

profile of v8, /device:TPU:0, one launch (start us, length us, event | category | flops | bytes accessed | tf_op | source)
XLA Modules:
  0.0 122.4 jit_solution(10176807932568987740)
XLA Ops:
  2.5 1.6 %collective-permute-done.refs_1_ = bf16[192,1536]{1,0:T(8,128)(2,1)S(1)} collective-permute-done((bf16[192,1536]{1,0:T(8,128)(2,1)S(1)}, bf16[192,1536]{1,0:T(8,128)(2,1)S(1)}, u32[]{:S(2)}, u32[]{:S(2)}) %collective-permute-start) | collective-permute-done | bytes 589856 | tf_op jit(solution)/shard_map/ppermute | solution.py:624
  4.2 3.0 %collective-permute-start.1 = (bf16[384,1536]{1,0:T(8,128)(2,1)S(1)}, bf16[384,1536]{1,0:T(8,128)(2,1)S(1)}, u32[]{:S(2)}, u32[]{:S(2)}) collective-permute-start(bf16[384,1536]{1,0:T(8,128)(2,1)S(1)} %stack_rows.3.refs_0_), channel_id=1, source_target_pairs={{0,8},{2,10},{4,12},{6,14},{8,24},{10,26},{12,28},{14,30},{24,16},... | collective-permute-start | bytes 3538952 | tf_op jit(solution)/shard_map/ppermute | solution.py:683
  12.4 1.5 %collective-permute-start.5 = (bf16[128,1536]{1,0:T(8,128)(2,1)}, bf16[128,1536]{1,0:T(8,128)(2,1)}, u32[]{:S(2)}, u32[]{:S(2)}) collective-permute-start(bf16[128,1536]{1,0:T(8,128)(2,1)} %get-tuple-element.101), channel_id=1, source_target_pairs={{0,4},{2,6},{4,0},{6,2},{8,12},{10,14},{12,8},{14,10},{16,20},{18,... | collective-permute-start | bytes 1179656 | tf_op jit(solution)/shard_map/ppermute | solution.py:691
  16.5 11.4 %attend.1 = (bf16[128,1536]{1,0:T(8,128)(2,1)S(1)}, bf16[14,128,512]{2,1,0:T(8,128)(2,1)}, bf16[7,128,512]{2,1,0:T(8,128)(2,1)S(1)}) custom-call(s32[1,13]{1,0:T(1,128)S(1)} %copy-done.17, s32[1]{0:T(128)S(6)} %copy.29.ctx, s32[1,13]{1,0:T(1,128)S(1)} %bitcast.7, s32[1]{0:T(128)} %bitcast.unit, bf16[128,1536]{1,0:T(8,128)(2,1)S(1)} %copy-done.10, ...), custom_call_target="tpu_custom_call" | custom-call | tf_op jit(solution)/shard_map/attend/pallas_call | solution.py:128
  29.7 4.8 %collective-permute-done.1.refs_1_ = bf16[384,1536]{1,0:T(8,128)(2,1)S(1)} collective-permute-done((bf16[384,1536]{1,0:T(8,128)(2,1)S(1)}, bf16[384,1536]{1,0:T(8,128)(2,1)S(1)}, u32[]{:S(2)}, u32[]{:S(2)}) %collective-permute-start.1) | collective-permute-done | bytes 1179680 | tf_op jit(solution)/shard_map/ppermute | solution.py:683
  36.8 1.9 %copy-done.1 = f32[1,24,128,256]{3,2,1,0:T(8,128)S(1)} copy-done((f32[1,24,128,256]{3,2,1,0:T(8,128)S(1)}, f32[1,24,128,256]{3,2,1,0:T(8,128)}, u32[]{:S(2)}) %copy-start.1) | copy-done | bytes 3145752
  45.0 8.7 %state_space.1 = (bf16[128,2304]{1,0:T(8,128)(2,1)S(1)}, bf16[128,1152]{1,0:T(8,128)(2,1)S(1)}, bf16[128,1152]{1,0:T(8,128)(2,1)S(1)}, f32[2,12,128,256]{3,2,1,0:T(8,128)}, bf16[12,128,256]{2,1,0:T(8,128)(2,1)S(1)}) custom-call(s32[1]{0:T(128)} %bitcast.unit, f32[24]{0:T(128)S(1)} %copy-done.19, bf16[128,1536]{1,0:T(8,128)(2,1)S(1)} %copy-done.12, ...), custom_call_target="tpu_custom_call" | custom-call | tf_op jit(solution)/shard_map/state_space/pallas_call | solution.py:253
  57.6 5.0 %copy-done = bf16[2304,3072]{1,0:T(8,128)(2,1)S(1)} copy-done((bf16[2304,3072]{1,0:T(8,128)(2,1)S(1)}, bf16[2304,3072]{1,0:T(8,128)(2,1)}, u32[]{:S(2)}) %copy-start) | copy-done | bytes 14155800
  62.7 6.1 %project.1 = (bf16[128,3072]{1,0:T(8,128)(2,1)S(1)}, bf16[128,1536]{1,0:T(8,128)(2,1)S(1)}, bf16[128,1536]{1,0:T(8,128)(2,1)S(1)}) custom-call(bf16[128,2304]{1,0:T(8,128)(2,1)S(1)} %get-tuple-element.93.stay_ref, bf16[128,1152]{1,0:T(8,128)(2,1)S(1)} %collective-permute-done.7.a_ref, bf16[128,1152]{1,0:T(8,128)(2,1)S(1)} %collective-permute-done.8.b_ref, ...), custom_call_target="tpu_custom_call" | custom-call | tf_op jit(solution)/shard_map/project/pallas_call | solution.py:563
  69.5 3.4 %collective-permute-start.12 = (bf16[384,384]{1,0:T(8,128)(2,1)S(1)}, bf16[384,384]{1,0:T(8,128)(2,1)S(1)}, u32[]{:S(2)}, u32[]{:S(2)}) collective-permute-start(bf16[384,384]{1,0:T(8,128)(2,1)S(1)} %get-tuple-element.116), channel_id=1, source_target_pairs={{0,8},{2,10},{4,12},{6,14},{8,24},{10,26},{12,28},{14,30},{24,16},... | collective-permute-start | bytes 884744 | tf_op jit(solution)/shard_map/ppermute | solution.py:683
  74.4 1.6 %begin.3.partial = f32[1024,384]{1,0:T(8,128)S(1)} custom-call(s32[1]{0:T(128)} %bitcast.unit, bf16[1024,1152]{1,0:T(8,128)(2,1)S(1)} %get-tuple-element.136.front, bf16[384,1536]{1,0:T(8,128)(2,1)S(1)} %stack_rows.3.refs_0_, bf16[384,1536]{1,0:T(8,128)(2,1)S(1)} %collective-permute-done.1.refs_1_, bf16[384,1536]{1,0:T(8,128)(2,1)S(1)} %collective-permute-done.11.refs_2_.x_ref), custom_call_target="tpu_custom_call" | custom-call | tf_op jit(solution)/shard_map/begin/pallas_call | solution.py:433
  76.0 4.3 %collective-permute-done.12.piece = bf16[384,384]{1,0:T(8,128)(2,1)S(1)} collective-permute-done((bf16[384,384]{1,0:T(8,128)(2,1)S(1)}, bf16[384,384]{1,0:T(8,128)(2,1)S(1)}, u32[]{:S(2)}, u32[]{:S(2)}) %collective-permute-start.12) | collective-permute-done | bytes 294944 | tf_op jit(solution)/shard_map/ppermute | solution.py:683
  81.0 1.6 %collective-permute-start.16 = (bf16[256,384]{1,0:T(8,128)(2,1)S(1)}, bf16[256,384]{1,0:T(8,128)(2,1)S(1)}, u32[]{:S(2)}, u32[]{:S(2)}) collective-permute-start(bf16[256,384]{1,0:T(8,128)(2,1)S(1)} %get-tuple-element.122), channel_id=1, source_target_pairs={{0,2},{2,0},{4,6},{6,4},{8,10},{10,8},{12,14},{14,12},{16,18},{18,... | collective-permute-start | bytes 589832 | tf_op jit(solution)/shard_map/ppermute | solution.py:691
  82.5 1.5 %collective-permute-start.17 = (bf16[256,384]{1,0:T(8,128)(2,1)S(1)}, bf16[256,384]{1,0:T(8,128)(2,1)S(1)}, u32[]{:S(2)}, u32[]{:S(2)}) collective-permute-start(bf16[256,384]{1,0:T(8,128)(2,1)S(1)} %get-tuple-element.123), channel_id=1, source_target_pairs={{0,4},{2,6},{4,0},{6,2},{8,12},{10,14},{12,8},{14,10},{16,20},{18,... | collective-permute-start | bytes 589832 | tf_op jit(solution)/shard_map/ppermute | solution.py:691
  84.5 2.5 %collective-permute-start.19 = (bf16[384,512]{1,0:T(8,128)(2,1)S(1)}, bf16[384,512]{1,0:T(8,128)(2,1)S(1)}, u32[]{:S(2)}, u32[]{:S(2)}) collective-permute-start(bf16[384,512]{1,0:T(8,128)(2,1)S(1)} %get-tuple-element.137), channel_id=1, source_target_pairs={{0,8},{2,10},{4,12},{6,14},{8,24},{10,26},{12,28},{14,30},{24,16},... | collective-permute-start | bytes 1179656 | tf_op jit(solution)/shard_map/ppermute | solution.py:683
  87.0 2.3 %begin.4.partial = f32[1024,640]{1,0:T(8,128)S(1)} custom-call(s32[1]{0:T(128)} %bitcast.unit, bf16[1024,1152]{1,0:T(8,128)(2,1)S(1)} %get-tuple-element.136.front, bf16[384,1536]{1,0:T(8,128)(2,1)S(1)} %stack_rows.3.refs_0_, bf16[384,1536]{1,0:T(8,128)(2,1)S(1)} %collective-permute-done.1.refs_1_, bf16[384,1536]{1,0:T(8,128)(2,1)S(1)} %collective-permute-done.11.refs_2_.x_ref), custom_call_target="tpu_custom_call" | custom-call | tf_op jit(solution)/shard_map/begin/pallas_call | solution.py:433
  93.4 1.5 %collective-permute-start.21 = (bf16[256,640]{1,0:T(8,128)(2,1)S(1)}, bf16[256,640]{1,0:T(8,128)(2,1)S(1)}, u32[]{:S(2)}, u32[]{:S(2)}) collective-permute-start(bf16[256,640]{1,0:T(8,128)(2,1)S(1)} %get-tuple-element.146), channel_id=1, source_target_pairs={{0,4},{2,6},{4,0},{6,2},{8,12},{10,14},{12,8},{14,10},{16,20},{18,... | collective-permute-start | bytes 983048 | tf_op jit(solution)/shard_map/ppermute | solution.py:691
  95.6 1.6 %begin.5.partial = f32[1024,512]{1,0:T(8,128)S(1)} custom-call(s32[1]{0:T(128)} %bitcast.unit, bf16[1024,1152]{1,0:T(8,128)(2,1)S(1)} %get-tuple-element.136.front, bf16[384,1536]{1,0:T(8,128)(2,1)S(1)} %stack_rows.3.refs_0_, bf16[384,1536]{1,0:T(8,128)(2,1)S(1)} %collective-permute-done.1.refs_1_, bf16[384,1536]{1,0:T(8,128)(2,1)S(1)} %collective-permute-done.11.refs_2_.x_ref), custom_call_target="tpu_custom_call" | custom-call | tf_op jit(solution)/shard_map/begin/pallas_call | solution.py:433
  99.1 3.5 %collective-permute-done.20.refs_0_ = bf16[256,640]{1,0:T(8,128)(2,1)S(1)} collective-permute-done((bf16[256,640]{1,0:T(8,128)(2,1)S(1)}, bf16[256,640]{1,0:T(8,128)(2,1)S(1)}, u32[]{:S(2)}, u32[]{:S(2)}) %collective-permute-start.20) | collective-permute-done | bytes 327712 | tf_op jit(solution)/shard_map/ppermute | solution.py:691
  104.0 1.5 %collective-permute-start.24 = (bf16[256,512]{1,0:T(8,128)(2,1)S(1)}, bf16[256,512]{1,0:T(8,128)(2,1)S(1)}, u32[]{:S(2)}, u32[]{:S(2)}) collective-permute-start(bf16[256,512]{1,0:T(8,128)(2,1)S(1)} %get-tuple-element.154), channel_id=1, source_target_pairs={{0,4},{2,6},{4,0},{6,2},{8,12},{10,14},{12,8},{14,10},{16,20},{18,... | collective-permute-start | bytes 786440 | tf_op jit(solution)/shard_map/ppermute | solution.py:691
  106.1 1.8 %collective-permute-done.21.refs_1_ = bf16[256,640]{1,0:T(8,128)(2,1)S(1)} collective-permute-done((bf16[256,640]{1,0:T(8,128)(2,1)S(1)}, bf16[256,640]{1,0:T(8,128)(2,1)S(1)}, u32[]{:S(2)}, u32[]{:S(2)}) %collective-permute-start.21) | collective-permute-done | bytes 327712 | tf_op jit(solution)/shard_map/ppermute | solution.py:691
  107.9 2.6 %collective-permute-done.22.refs_2_ = bf16[256,640]{1,0:T(8,128)(2,1)S(1)} collective-permute-done((bf16[256,640]{1,0:T(8,128)(2,1)S(1)}, bf16[256,640]{1,0:T(8,128)(2,1)S(1)}, u32[]{:S(2)}, u32[]{:S(2)}) %collective-permute-start.22) | collective-permute-done | bytes 327712 | tf_op jit(solution)/shard_map/ppermute | solution.py:691
  112.3 3.0 %collective-permute-done.23.refs_0_ = bf16[256,512]{1,0:T(8,128)(2,1)S(1)} collective-permute-done((bf16[256,512]{1,0:T(8,128)(2,1)S(1)}, bf16[256,512]{1,0:T(8,128)(2,1)S(1)}, u32[]{:S(2)}, u32[]{:S(2)}) %collective-permute-start.23) | collective-permute-done | bytes 262176 | tf_op jit(solution)/shard_map/ppermute | solution.py:691
  115.3 4.1 %collective-permute-done.24.refs_1_ = bf16[256,512]{1,0:T(8,128)(2,1)S(1)} collective-permute-done((bf16[256,512]{1,0:T(8,128)(2,1)S(1)}, bf16[256,512]{1,0:T(8,128)(2,1)S(1)}, u32[]{:S(2)}, u32[]{:S(2)}) %collective-permute-start.24) | collective-permute-done | bytes 262176 | tf_op jit(solution)/shard_map/ppermute | solution.py:691
  (104 shorter events, 39.9 us)
Async XLA Ops:
  4.2 30.3 %collective-permute-start.1 = (bf16[384,1536]{1,0:T(8,128)(2,1)S(1)}, bf16[384,1536]{1,0:T(8,128)(2,1)S(1)}, u32[]{:S(2)}, u32[]{:S(2)}) collective-permute-start(bf16[384,1536]{1,0:T(8,128)(2,1)S(1)} %stack_rows.3.refs_0_), channel_id=1, source_target_pairs={{0,8},{2,10},{4,12},{6,14},{8,24},{10,26},{12,28},{14,30},{24,16},... | collective-permute-start | bytes 3538952 | tf_op jit(solution)/shard_map/ppermute | solution.py:683
  10.9 42.9 %collective-permute-start.4 = (bf16[128,1536]{1,0:T(8,128)(2,1)}, bf16[128,1536]{1,0:T(8,128)(2,1)}, u32[]{:S(2)}, u32[]{:S(2)}) collective-permute-start(bf16[128,1536]{1,0:T(8,128)(2,1)} %get-tuple-element.100), channel_id=1, source_target_pairs={{0,2},{2,0},{4,6},{6,4},{8,10},{10,8},{12,14},{14,12},{16,18},{18,... | collective-permute-start | bytes 1179656 | tf_op jit(solution)/shard_map/ppermute | solution.py:691
  12.4 41.4 %collective-permute-start.5 = (bf16[128,1536]{1,0:T(8,128)(2,1)}, bf16[128,1536]{1,0:T(8,128)(2,1)}, u32[]{:S(2)}, u32[]{:S(2)}) collective-permute-start(bf16[128,1536]{1,0:T(8,128)(2,1)} %get-tuple-element.101), channel_id=1, source_target_pairs={{0,4},{2,6},{4,0},{6,2},{8,12},{10,14},{12,8},{14,10},{16,20},{18,... | collective-permute-start | bytes 1179656 | tf_op jit(solution)/shard_map/ppermute | solution.py:691
  13.9 39.9 %collective-permute-start.6 = (bf16[128,1536]{1,0:T(8,128)(2,1)}, bf16[128,1536]{1,0:T(8,128)(2,1)}, u32[]{:S(2)}, u32[]{:S(2)}) collective-permute-start(bf16[128,1536]{1,0:T(8,128)(2,1)} %get-tuple-element.102), channel_id=1, source_target_pairs={{0,6},{2,4},{4,2},{6,0},{8,14},{10,12},{12,10},{14,8},{16,22},{18,... | collective-permute-start | bytes 1179656 | tf_op jit(solution)/shard_map/ppermute | solution.py:691
  34.5 34.3 %collective-permute-start.11 = (bf16[384,1536]{1,0:T(8,128)(2,1)S(1)}, bf16[384,1536]{1,0:T(8,128)(2,1)S(1)}, u32[]{:S(2)}, u32[]{:S(2)}) collective-permute-start(bf16[384,1536]{1,0:T(8,128)(2,1)S(1)} %collective-permute-done.1.refs_1_), channel_id=1, source_target_pairs={{0,8},{2,10},{4,12},{6,14},{8,24},{10,26},{12,28},{14,30},{24,16},... | collective-permute-start | bytes 3538952 | tf_op jit(solution)/shard_map/ppermute | solution.py:683
  54.3 14.4 %collective-permute-start.2 = (bf16[7,128,512]{2,1,0:T(8,128)(2,1)S(1)}, bf16[7,128,512]{2,1,0:T(8,128)(2,1)S(1)}, u32[]{:S(2)}, u32[]{:S(2)}) collective-permute-start(bf16[7,128,512]{2,1,0:T(8,128)(2,1)S(1)} %copy-done.23), channel_id=1, source_target_pairs={{0,1},{1,0},{2,3},{3,2},{4,5},{5,4},{6,7},{7,6},{8,9},{9,8},{10,11... | collective-permute-start | bytes 2752520 | tf_op jit(solution)/shard_map/ppermute | solution.py:624
  56.6 12.1 %collective-permute-start.3 = (bf16[12,128,256]{2,1,0:T(8,128)(2,1)S(1)}, bf16[12,128,256]{2,1,0:T(8,128)(2,1)S(1)}, u32[]{:S(2)}, u32[]{:S(2)}) collective-permute-start(bf16[12,128,256]{2,1,0:T(8,128)(2,1)S(1)} %get-tuple-element.95), channel_id=1, source_target_pairs={{0,1},{1,0},{2,3},{3,2},{4,5},{5,4},{6,7},{7,6},{8,9},{9,8},{10,11... | collective-permute-start | bytes 2359304 | tf_op jit(solution)/shard_map/ppermute | solution.py:624
  57.1 11.6 %collective-permute-start.10 = (bf16[256,1536]{1,0:T(8,128)(2,1)S(1)}, bf16[256,1536]{1,0:T(8,128)(2,1)S(1)}, u32[]{:S(2)}, u32[]{:S(2)}) collective-permute-start(bf16[256,1536]{1,0:T(8,128)(2,1)S(1)} %stack_rows.5), channel_id=1, source_target_pairs={{0,1},{1,0},{2,3},{3,2},{4,5},{5,4},{6,7},{7,6},{8,9},{9,8},{10,11... | collective-permute-start | bytes 2359304 | tf_op jit(solution)/shard_map/ppermute | solution.py:624
  57.2 11.5 %collective-permute-start.9 = (bf16[256,1536]{1,0:T(8,128)(2,1)S(1)}, bf16[256,1536]{1,0:T(8,128)(2,1)S(1)}, u32[]{:S(2)}, u32[]{:S(2)}) collective-permute-start(bf16[256,1536]{1,0:T(8,128)(2,1)S(1)} %stack_rows.4), channel_id=1, source_target_pairs={{0,1},{1,0},{2,3},{3,2},{4,5},{5,4},{6,7},{7,6},{8,9},{9,8},{10,11... | collective-permute-start | bytes 2359304 | tf_op jit(solution)/shard_map/ppermute | solution.py:624
  68.8 11.5 %collective-permute-start.13 = (bf16[128,1536]{1,0:T(8,128)(2,1)S(1)}, bf16[128,1536]{1,0:T(8,128)(2,1)S(1)}, u32[]{:S(2)}, u32[]{:S(2)}) collective-permute-start(bf16[128,1536]{1,0:T(8,128)(2,1)S(1)} %get-tuple-element.119), channel_id=1, source_target_pairs={{0,1},{1,0},{2,3},{3,2},{4,5},{5,4},{6,7},{7,6},{8,9},{9,8},{10,11... | collective-permute-start | bytes 1179656 | tf_op jit(solution)/shard_map/ppermute | solution.py:624
  69.0 11.3 %collective-permute-start.14 = (bf16[128,1536]{1,0:T(8,128)(2,1)S(1)}, bf16[128,1536]{1,0:T(8,128)(2,1)S(1)}, u32[]{:S(2)}, u32[]{:S(2)}) collective-permute-start(bf16[128,1536]{1,0:T(8,128)(2,1)S(1)} %get-tuple-element.120), channel_id=1, source_target_pairs={{0,1},{1,0},{2,3},{3,2},{4,5},{5,4},{6,7},{7,6},{8,9},{9,8},{10,11... | collective-permute-start | bytes 1179656 | tf_op jit(solution)/shard_map/ppermute | solution.py:624
  69.5 10.8 %collective-permute-start.12 = (bf16[384,384]{1,0:T(8,128)(2,1)S(1)}, bf16[384,384]{1,0:T(8,128)(2,1)S(1)}, u32[]{:S(2)}, u32[]{:S(2)}) collective-permute-start(bf16[384,384]{1,0:T(8,128)(2,1)S(1)} %get-tuple-element.116), channel_id=1, source_target_pairs={{0,8},{2,10},{4,12},{6,14},{8,24},{10,26},{12,28},{14,30},{24,16},... | collective-permute-start | bytes 884744 | tf_op jit(solution)/shard_map/ppermute | solution.py:683
  72.9 17.9 %collective-permute-start.15 = (bf16[384,640]{1,0:T(8,128)(2,1)S(1)}, bf16[384,640]{1,0:T(8,128)(2,1)S(1)}, u32[]{:S(2)}, u32[]{:S(2)}) collective-permute-start(bf16[384,640]{1,0:T(8,128)(2,1)S(1)} %get-tuple-element.126), channel_id=1, source_target_pairs={{0,8},{2,10},{4,12},{6,14},{8,24},{10,26},{12,28},{14,30},{24,16},... | collective-permute-start | bytes 1474568 | tf_op jit(solution)/shard_map/ppermute | solution.py:683
  81.0 10.8 %collective-permute-start.16 = (bf16[256,384]{1,0:T(8,128)(2,1)S(1)}, bf16[256,384]{1,0:T(8,128)(2,1)S(1)}, u32[]{:S(2)}, u32[]{:S(2)}) collective-permute-start(bf16[256,384]{1,0:T(8,128)(2,1)S(1)} %get-tuple-element.122), channel_id=1, source_target_pairs={{0,2},{2,0},{4,6},{6,4},{8,10},{10,8},{12,14},{14,12},{16,18},{18,... | collective-permute-start | bytes 589832 | tf_op jit(solution)/shard_map/ppermute | solution.py:691
  82.5 9.5 %collective-permute-start.17 = (bf16[256,384]{1,0:T(8,128)(2,1)S(1)}, bf16[256,384]{1,0:T(8,128)(2,1)S(1)}, u32[]{:S(2)}, u32[]{:S(2)}) collective-permute-start(bf16[256,384]{1,0:T(8,128)(2,1)S(1)} %get-tuple-element.123), channel_id=1, source_target_pairs={{0,4},{2,6},{4,0},{6,2},{8,12},{10,14},{12,8},{14,10},{16,20},{18,... | collective-permute-start | bytes 589832 | tf_op jit(solution)/shard_map/ppermute | solution.py:691
  84.0 7.9 %collective-permute-start.18 = (bf16[256,384]{1,0:T(8,128)(2,1)S(1)}, bf16[256,384]{1,0:T(8,128)(2,1)S(1)}, u32[]{:S(2)}, u32[]{:S(2)}) collective-permute-start(bf16[256,384]{1,0:T(8,128)(2,1)S(1)} %get-tuple-element.124), channel_id=1, source_target_pairs={{0,6},{2,4},{4,2},{6,0},{8,14},{10,12},{12,10},{14,8},{16,22},{18,... | collective-permute-start | bytes 589832 | tf_op jit(solution)/shard_map/ppermute | solution.py:691
  84.5 13.9 %collective-permute-start.19 = (bf16[384,512]{1,0:T(8,128)(2,1)S(1)}, bf16[384,512]{1,0:T(8,128)(2,1)S(1)}, u32[]{:S(2)}, u32[]{:S(2)}) collective-permute-start(bf16[384,512]{1,0:T(8,128)(2,1)S(1)} %get-tuple-element.137), channel_id=1, source_target_pairs={{0,8},{2,10},{4,12},{6,14},{8,24},{10,26},{12,28},{14,30},{24,16},... | collective-permute-start | bytes 1179656 | tf_op jit(solution)/shard_map/ppermute | solution.py:683
  92.0 10.7 %collective-permute-start.20 = (bf16[256,640]{1,0:T(8,128)(2,1)S(1)}, bf16[256,640]{1,0:T(8,128)(2,1)S(1)}, u32[]{:S(2)}, u32[]{:S(2)}) collective-permute-start(bf16[256,640]{1,0:T(8,128)(2,1)S(1)} %get-tuple-element.145), channel_id=1, source_target_pairs={{0,2},{2,0},{4,6},{6,4},{8,10},{10,8},{12,14},{14,12},{16,18},{18,... | collective-permute-start | bytes 983048 | tf_op jit(solution)/shard_map/ppermute | solution.py:691
  93.4 14.5 %collective-permute-start.21 = (bf16[256,640]{1,0:T(8,128)(2,1)S(1)}, bf16[256,640]{1,0:T(8,128)(2,1)S(1)}, u32[]{:S(2)}, u32[]{:S(2)}) collective-permute-start(bf16[256,640]{1,0:T(8,128)(2,1)S(1)} %get-tuple-element.146), channel_id=1, source_target_pairs={{0,4},{2,6},{4,0},{6,2},{8,12},{10,14},{12,8},{14,10},{16,20},{18,... | collective-permute-start | bytes 983048 | tf_op jit(solution)/shard_map/ppermute | solution.py:691
  94.9 15.7 %collective-permute-start.22 = (bf16[256,640]{1,0:T(8,128)(2,1)S(1)}, bf16[256,640]{1,0:T(8,128)(2,1)S(1)}, u32[]{:S(2)}, u32[]{:S(2)}) collective-permute-start(bf16[256,640]{1,0:T(8,128)(2,1)S(1)} %get-tuple-element.147), channel_id=1, source_target_pairs={{0,6},{2,4},{4,2},{6,0},{8,14},{10,12},{12,10},{14,8},{16,22},{18,... | collective-permute-start | bytes 983048 | tf_op jit(solution)/shard_map/ppermute | solution.py:691
  102.6 12.7 %collective-permute-start.23 = (bf16[256,512]{1,0:T(8,128)(2,1)S(1)}, bf16[256,512]{1,0:T(8,128)(2,1)S(1)}, u32[]{:S(2)}, u32[]{:S(2)}) collective-permute-start(bf16[256,512]{1,0:T(8,128)(2,1)S(1)} %get-tuple-element.153), channel_id=1, source_target_pairs={{0,2},{2,0},{4,6},{6,4},{8,10},{10,8},{12,14},{14,12},{16,18},{18,... | collective-permute-start | bytes 786440 | tf_op jit(solution)/shard_map/ppermute | solution.py:691
  104.0 15.4 %collective-permute-start.24 = (bf16[256,512]{1,0:T(8,128)(2,1)S(1)}, bf16[256,512]{1,0:T(8,128)(2,1)S(1)}, u32[]{:S(2)}, u32[]{:S(2)}) collective-permute-start(bf16[256,512]{1,0:T(8,128)(2,1)S(1)} %get-tuple-element.154), channel_id=1, source_target_pairs={{0,4},{2,6},{4,0},{6,2},{8,12},{10,14},{12,8},{14,10},{16,20},{18,... | collective-permute-start | bytes 786440 | tf_op jit(solution)/shard_map/ppermute | solution.py:691
  105.6 13.8 %collective-permute-start.25 = (bf16[256,512]{1,0:T(8,128)(2,1)S(1)}, bf16[256,512]{1,0:T(8,128)(2,1)S(1)}, u32[]{:S(2)}, u32[]{:S(2)}) collective-permute-start(bf16[256,512]{1,0:T(8,128)(2,1)S(1)} %get-tuple-element.155), channel_id=1, source_target_pairs={{0,6},{2,4},{4,2},{6,0},{8,14},{10,12},{12,10},{14,8},{16,22},{18,... | collective-permute-start | bytes 786440 | tf_op jit(solution)/shard_map/ppermute | solution.py:691
  110.7 10.4 %collective-permute-start.27 = (bf16[128,640]{1,0:T(8,128)(2,1)S(1)}, bf16[128,640]{1,0:T(8,128)(2,1)S(1)}, u32[]{:S(2)}, u32[]{:S(2)}) collective-permute-start(bf16[128,640]{1,0:T(8,128)(2,1)S(1)} %get-tuple-element.161), channel_id=1, source_target_pairs={{0,1},{1,0},{2,3},{3,2},{4,5},{5,4},{6,7},{7,6},{8,9},{9,8},{10,11... | collective-permute-start | bytes 491528 | tf_op jit(solution)/shard_map/ppermute | solution.py:624
  (29 other events, 159.1 us)

commit v9 on v8

--- a/solution.py
+++ b/solution.py
@@ -24,6 +24,7 @@
 SMEM = pl.BlockSpec(memory_space=pltpu.SMEM)
 ANY = pl.BlockSpec(memory_space=pl.ANY)
 PARAMS = pltpu.CompilerParams(vmem_limit_bytes=24 * 1024 * 1024)
+LARGE = pltpu.CompilerParams(vmem_limit_bytes=48 * 1024 * 1024)
 
 
 def cost(flops, moved, exps=0):
@@ -140,7 +141,7 @@
             pltpu.SemaphoreType.DMA((count,)),
             pltpu.SemaphoreType.DMA((count + 2 * slots,)),
         ],
-        compiler_params=PARAMS,
+        compiler_params=LARGE,
         cost_estimate=cost(4 * pairs * HEAD_WIDTH * 4, 6 << 20, pairs),
         name="attend",
     )(table, ctx, owner, unit, queries, kv_new, pool)
@@ -266,7 +267,7 @@
             pltpu.VMEM((share, PM, NS), F32),
             pltpu.SemaphoreType.DMA((share,)),
         ],
-        compiler_params=PARAMS,
+        compiler_params=LARGE,
         cost_estimate=cost(4 << 30, 10 << 20, MIXER_HEADS * length * length * 2),
         name="state_space",
     )(unit, skip, attn, x, z, bc, dt, bias, rate, gain, state)
@@ -575,7 +576,7 @@
             pl.BlockSpec((rows, tile), lambda i: (0, jnp.maximum(i - half, 0))),
         ),
         scratch_shapes=[pltpu.VMEM((2 * rows, depth), BF16)],
-        compiler_params=PARAMS,
+        compiler_params=LARGE,
         cost_estimate=cost(0, 15 << 20),
         name="project",
     )(stay, came_a, came_b, weight)

time: 123 us -> 120 us (0.976)
  local copies, waits for them, and re-layouts: 21.3 us -> 14.4 us
  Pallas kernels: 42.6 us -> 46.7 us
    unnamed x49 -> x45, local copies, waits for them, and re-layouts: 21.3 us -> 14.4 us
    pallas_call x1, Pallas kernels: 6.06 us -> 8.78 us  [project(): pl.pallas_call(project_kernel, grid=(2 * half,), out_shape=(jax.ShapeDtyp...]
    pallas_call x1, Pallas kernels: 8.7 us -> 10.1 us  [state_space(): pl.pallas_call(state_kernel, out_shape=(jax.ShapeDtypeStruct((length, hal...]
  transfers between devices with their start and end apart: 29 -> 29, of which waited for: 12 -> 12; matrix products, arithmetic and copies ran while one was open for 1% -> 1% of each run, Pallas kernels for 34% -> 38%
where the time goes in v9:
time: 120 us
  Pallas kernels  46.7 us (39%)
  waiting for transfers between devices  29.7 us (25%)
  starting transfers between devices  27.2 us (23%)
  local copies, waits for them, and re-layouts  14.4 us (12%)
  between operations  1.61 us (1%)
    ppermute x12, waiting for transfers between devices, plane_swap(): lax.ppermute(x, 'req', [(r, r - r % PLANE + (r % PLANE ^ d)) for r in ran...  15.2 us
    unnamed x45, local copies, waits for them, and re-layouts  14.4 us
    ppermute x12, starting transfers between devices, plane_swap(): lax.ppermute(x, 'req', [(r, r - r % PLANE + (r % PLANE ^ d)) for r in ran...  14 us
    ppermute x5, waiting for transfers between devices, pass_on(): return lax.ppermute(x, 'req', ring_pairs)  11.8 us
    pallas_call x1, Pallas kernels, attend(): pl.pallas_call(attend_kernel, out_shape=(jax.ShapeDtypeStruct(queries.sha...  11.4 us
    pallas_call x1, Pallas kernels, state_space(): pl.pallas_call(state_kernel, out_shape=(jax.ShapeDtypeStruct((length, hal...  10.1 us
    ppermute x5, starting transfers between devices, pass_on(): return lax.ppermute(x, 'req', ring_pairs)  9.83 us
    pallas_call x1, Pallas kernels, project(): pl.pallas_call(project_kernel, grid=(2 * half,), out_shape=(jax.ShapeDtyp...  8.78 us
  transfers between devices with their start and end apart: 29, of which 12 were waited for; matrix products, arithmetic and copies ran while one was open for 1% of the time, Pallas kernels for 38%

profile of v9, /device:TPU:0, one launch (start us, length us, event | category | flops | bytes accessed | tf_op | source)
XLA Modules:
  0.0 119.6 jit_solution(7727713317984062098)
XLA Ops:
  2.5 1.6 %collective-permute-done.refs_1_ = bf16[192,1536]{1,0:T(8,128)(2,1)S(1)} collective-permute-done((bf16[192,1536]{1,0:T(8,128)(2,1)S(1)}, bf16[192,1536]{1,0:T(8,128)(2,1)S(1)}, u32[]{:S(2)}, u32[]{:S(2)}) %collective-permute-start) | collective-permute-done | bytes 589856 | tf_op jit(solution)/shard_map/ppermute | solution.py:625
  4.2 3.0 %collective-permute-start.1 = (bf16[384,1536]{1,0:T(8,128)(2,1)S(1)}, bf16[384,1536]{1,0:T(8,128)(2,1)S(1)}, u32[]{:S(2)}, u32[]{:S(2)}) collective-permute-start(bf16[384,1536]{1,0:T(8,128)(2,1)S(1)} %stack_rows.3.refs_0_), channel_id=1, source_target_pairs={{0,8},{2,10},{4,12},{6,14},{8,24},{10,26},{12,28},{14,30},{24,16},... | collective-permute-start | bytes 3538952 | tf_op jit(solution)/shard_map/ppermute | solution.py:684
  10.9 1.5 %collective-permute-start.4 = (bf16[128,1536]{1,0:T(8,128)(2,1)}, bf16[128,1536]{1,0:T(8,128)(2,1)}, u32[]{:S(2)}, u32[]{:S(2)}) collective-permute-start(bf16[128,1536]{1,0:T(8,128)(2,1)} %get-tuple-element.100), channel_id=1, source_target_pairs={{0,2},{2,0},{4,6},{6,4},{8,10},{10,8},{12,14},{14,12},{16,18},{18,... | collective-permute-start | bytes 1179656 | tf_op jit(solution)/shard_map/ppermute | solution.py:692
  12.4 1.5 %collective-permute-start.5 = (bf16[128,1536]{1,0:T(8,128)(2,1)}, bf16[128,1536]{1,0:T(8,128)(2,1)}, u32[]{:S(2)}, u32[]{:S(2)}) collective-permute-start(bf16[128,1536]{1,0:T(8,128)(2,1)} %get-tuple-element.101), channel_id=1, source_target_pairs={{0,4},{2,6},{4,0},{6,2},{8,12},{10,14},{12,8},{14,10},{16,20},{18,... | collective-permute-start | bytes 1179656 | tf_op jit(solution)/shard_map/ppermute | solution.py:692
  16.5 11.4 %attend.1 = (bf16[128,1536]{1,0:T(8,128)(2,1)S(1)}, bf16[14,128,512]{2,1,0:T(8,128)(2,1)}, bf16[7,128,512]{2,1,0:T(8,128)(2,1)S(1)}) custom-call(s32[1,13]{1,0:T(1,128)S(1)} %copy-done.15, s32[1]{0:T(128)S(6)} %copy.29.ctx, s32[1,13]{1,0:T(1,128)S(1)} %bitcast.7, s32[1]{0:T(128)} %bitcast.unit, bf16[128,1536]{1,0:T(8,128)(2,1)S(1)} %copy-done.8, ...), custom_call_target="tpu_custom_call" | custom-call | tf_op jit(solution)/shard_map/attend/pallas_call | solution.py:129
  29.7 4.8 %collective-permute-done.1.refs_1_ = bf16[384,1536]{1,0:T(8,128)(2,1)S(1)} collective-permute-done((bf16[384,1536]{1,0:T(8,128)(2,1)S(1)}, bf16[384,1536]{1,0:T(8,128)(2,1)S(1)}, u32[]{:S(2)}, u32[]{:S(2)}) %collective-permute-start.1) | collective-permute-done | bytes 1179680 | tf_op jit(solution)/shard_map/ppermute | solution.py:684
  43.1 10.1 %state_space.1 = (bf16[128,2304]{1,0:T(8,128)(2,1)S(1)}, bf16[128,1152]{1,0:T(8,128)(2,1)S(1)}, bf16[128,1152]{1,0:T(8,128)(2,1)S(1)}, f32[2,12,128,256]{3,2,1,0:T(8,128)}, bf16[12,128,256]{2,1,0:T(8,128)(2,1)S(1)}) custom-call(s32[1]{0:T(128)} %bitcast.unit, f32[24]{0:T(128)S(1)} %copy-done.17, bf16[128,1536]{1,0:T(8,128)(2,1)S(1)} %copy-done.10, ...), custom_call_target="tpu_custom_call" | custom-call | tf_op jit(solution)/shard_map/state_space/pallas_call | solution.py:254
  57.1 8.8 %project.1 = (bf16[128,3072]{1,0:T(8,128)(2,1)S(1)}, bf16[128,1536]{1,0:T(8,128)(2,1)S(1)}, bf16[128,1536]{1,0:T(8,128)(2,1)S(1)}) custom-call(bf16[128,2304]{1,0:T(8,128)(2,1)S(1)} %get-tuple-element.93.stay_ref, bf16[128,1152]{1,0:T(8,128)(2,1)S(1)} %collective-permute-done.7.a_ref, bf16[128,1152]{1,0:T(8,128)(2,1)S(1)} %collective-permute-done.8.b_ref, ...), custom_call_target="tpu_custom_call" | custom-call | tf_op jit(solution)/shard_map/project/pallas_call | solution.py:564
  66.7 3.4 %collective-permute-start.12 = (bf16[384,384]{1,0:T(8,128)(2,1)S(1)}, bf16[384,384]{1,0:T(8,128)(2,1)S(1)}, u32[]{:S(2)}, u32[]{:S(2)}) collective-permute-start(bf16[384,384]{1,0:T(8,128)(2,1)S(1)} %get-tuple-element.116), channel_id=1, source_target_pairs={{0,8},{2,10},{4,12},{6,14},{8,24},{10,26},{12,28},{14,30},{24,16},... | collective-permute-start | bytes 884744 | tf_op jit(solution)/shard_map/ppermute | solution.py:684
  71.6 1.5 %begin.3.partial = f32[1024,384]{1,0:T(8,128)S(1)} custom-call(s32[1]{0:T(128)} %bitcast.unit, bf16[1024,1152]{1,0:T(8,128)(2,1)S(1)} %get-tuple-element.136.front, bf16[384,1536]{1,0:T(8,128)(2,1)S(1)} %stack_rows.3.refs_0_, bf16[384,1536]{1,0:T(8,128)(2,1)S(1)} %collective-permute-done.1.refs_1_, bf16[384,1536]{1,0:T(8,128)(2,1)S(1)} %collective-permute-done.11.refs_2_.x_ref), custom_call_target="tpu_custom_call" | custom-call | tf_op jit(solution)/shard_map/begin/pallas_call | solution.py:434
  73.2 4.3 %collective-permute-done.12.piece = bf16[384,384]{1,0:T(8,128)(2,1)S(1)} collective-permute-done((bf16[384,384]{1,0:T(8,128)(2,1)S(1)}, bf16[384,384]{1,0:T(8,128)(2,1)S(1)}, u32[]{:S(2)}, u32[]{:S(2)}) %collective-permute-start.12) | collective-permute-done | bytes 294944 | tf_op jit(solution)/shard_map/ppermute | solution.py:684
  78.2 1.6 %collective-permute-start.16 = (bf16[256,384]{1,0:T(8,128)(2,1)S(1)}, bf16[256,384]{1,0:T(8,128)(2,1)S(1)}, u32[]{:S(2)}, u32[]{:S(2)}) collective-permute-start(bf16[256,384]{1,0:T(8,128)(2,1)S(1)} %get-tuple-element.122), channel_id=1, source_target_pairs={{0,2},{2,0},{4,6},{6,4},{8,10},{10,8},{12,14},{14,12},{16,18},{18,... | collective-permute-start | bytes 589832 | tf_op jit(solution)/shard_map/ppermute | solution.py:692
  79.7 1.5 %collective-permute-start.17 = (bf16[256,384]{1,0:T(8,128)(2,1)S(1)}, bf16[256,384]{1,0:T(8,128)(2,1)S(1)}, u32[]{:S(2)}, u32[]{:S(2)}) collective-permute-start(bf16[256,384]{1,0:T(8,128)(2,1)S(1)} %get-tuple-element.123), channel_id=1, source_target_pairs={{0,4},{2,6},{4,0},{6,2},{8,12},{10,14},{12,8},{14,10},{16,20},{18,... | collective-permute-start | bytes 589832 | tf_op jit(solution)/shard_map/ppermute | solution.py:692
  81.7 2.5 %collective-permute-start.19 = (bf16[384,512]{1,0:T(8,128)(2,1)S(1)}, bf16[384,512]{1,0:T(8,128)(2,1)S(1)}, u32[]{:S(2)}, u32[]{:S(2)}) collective-permute-start(bf16[384,512]{1,0:T(8,128)(2,1)S(1)} %get-tuple-element.137), channel_id=1, source_target_pairs={{0,8},{2,10},{4,12},{6,14},{8,24},{10,26},{12,28},{14,30},{24,16},... | collective-permute-start | bytes 1179656 | tf_op jit(solution)/shard_map/ppermute | solution.py:684
  84.2 2.3 %begin.4.partial = f32[1024,640]{1,0:T(8,128)S(1)} custom-call(s32[1]{0:T(128)} %bitcast.unit, bf16[1024,1152]{1,0:T(8,128)(2,1)S(1)} %get-tuple-element.136.front, bf16[384,1536]{1,0:T(8,128)(2,1)S(1)} %stack_rows.3.refs_0_, bf16[384,1536]{1,0:T(8,128)(2,1)S(1)} %collective-permute-done.1.refs_1_, bf16[384,1536]{1,0:T(8,128)(2,1)S(1)} %collective-permute-done.11.refs_2_.x_ref), custom_call_target="tpu_custom_call" | custom-call | tf_op jit(solution)/shard_map/begin/pallas_call | solution.py:434
  86.5 1.5 %collective-permute-done.15.piece = bf16[384,640]{1,0:T(8,128)(2,1)S(1)} collective-permute-done((bf16[384,640]{1,0:T(8,128)(2,1)S(1)}, bf16[384,640]{1,0:T(8,128)(2,1)S(1)}, u32[]{:S(2)}, u32[]{:S(2)}) %collective-permute-start.15) | collective-permute-done | bytes 491552 | tf_op jit(solution)/shard_map/ppermute | solution.py:684
  90.6 1.5 %collective-permute-start.21 = (bf16[256,640]{1,0:T(8,128)(2,1)S(1)}, bf16[256,640]{1,0:T(8,128)(2,1)S(1)}, u32[]{:S(2)}, u32[]{:S(2)}) collective-permute-start(bf16[256,640]{1,0:T(8,128)(2,1)S(1)} %get-tuple-element.146), channel_id=1, source_target_pairs={{0,4},{2,6},{4,0},{6,2},{8,12},{10,14},{12,8},{14,10},{16,20},{18,... | collective-permute-start | bytes 983048 | tf_op jit(solution)/shard_map/ppermute | solution.py:692
  92.8 1.6 %begin.5.partial = f32[1024,512]{1,0:T(8,128)S(1)} custom-call(s32[1]{0:T(128)} %bitcast.unit, bf16[1024,1152]{1,0:T(8,128)(2,1)S(1)} %get-tuple-element.136.front, bf16[384,1536]{1,0:T(8,128)(2,1)S(1)} %stack_rows.3.refs_0_, bf16[384,1536]{1,0:T(8,128)(2,1)S(1)} %collective-permute-done.1.refs_1_, bf16[384,1536]{1,0:T(8,128)(2,1)S(1)} %collective-permute-done.11.refs_2_.x_ref), custom_call_target="tpu_custom_call" | custom-call | tf_op jit(solution)/shard_map/begin/pallas_call | solution.py:434
  96.3 3.5 %collective-permute-done.20.refs_0_ = bf16[256,640]{1,0:T(8,128)(2,1)S(1)} collective-permute-done((bf16[256,640]{1,0:T(8,128)(2,1)S(1)}, bf16[256,640]{1,0:T(8,128)(2,1)S(1)}, u32[]{:S(2)}, u32[]{:S(2)}) %collective-permute-start.20) | collective-permute-done | bytes 327712 | tf_op jit(solution)/shard_map/ppermute | solution.py:692
  101.2 1.5 %collective-permute-start.24 = (bf16[256,512]{1,0:T(8,128)(2,1)S(1)}, bf16[256,512]{1,0:T(8,128)(2,1)S(1)}, u32[]{:S(2)}, u32[]{:S(2)}) collective-permute-start(bf16[256,512]{1,0:T(8,128)(2,1)S(1)} %get-tuple-element.154), channel_id=1, source_target_pairs={{0,4},{2,6},{4,0},{6,2},{8,12},{10,14},{12,8},{14,10},{16,20},{18,... | collective-permute-start | bytes 786440 | tf_op jit(solution)/shard_map/ppermute | solution.py:692
  103.3 1.8 %collective-permute-done.21.refs_1_ = bf16[256,640]{1,0:T(8,128)(2,1)S(1)} collective-permute-done((bf16[256,640]{1,0:T(8,128)(2,1)S(1)}, bf16[256,640]{1,0:T(8,128)(2,1)S(1)}, u32[]{:S(2)}, u32[]{:S(2)}) %collective-permute-start.21) | collective-permute-done | bytes 327712 | tf_op jit(solution)/shard_map/ppermute | solution.py:692
  105.1 2.7 %collective-permute-done.22.refs_2_ = bf16[256,640]{1,0:T(8,128)(2,1)S(1)} collective-permute-done((bf16[256,640]{1,0:T(8,128)(2,1)S(1)}, bf16[256,640]{1,0:T(8,128)(2,1)S(1)}, u32[]{:S(2)}, u32[]{:S(2)}) %collective-permute-start.22) | collective-permute-done | bytes 327712 | tf_op jit(solution)/shard_map/ppermute | solution.py:692
  109.5 3.0 %collective-permute-done.23.refs_0_ = bf16[256,512]{1,0:T(8,128)(2,1)S(1)} collective-permute-done((bf16[256,512]{1,0:T(8,128)(2,1)S(1)}, bf16[256,512]{1,0:T(8,128)(2,1)S(1)}, u32[]{:S(2)}, u32[]{:S(2)}) %collective-permute-start.23) | collective-permute-done | bytes 262176 | tf_op jit(solution)/shard_map/ppermute | solution.py:692
  112.5 4.1 %collective-permute-done.24.refs_1_ = bf16[256,512]{1,0:T(8,128)(2,1)S(1)} collective-permute-done((bf16[256,512]{1,0:T(8,128)(2,1)S(1)}, bf16[256,512]{1,0:T(8,128)(2,1)S(1)}, u32[]{:S(2)}, u32[]{:S(2)}) %collective-permute-start.24) | collective-permute-done | bytes 262176 | tf_op jit(solution)/shard_map/ppermute | solution.py:692
  (100 shorter events, 36.9 us)
Async XLA Ops:
  4.2 30.3 %collective-permute-start.1 = (bf16[384,1536]{1,0:T(8,128)(2,1)S(1)}, bf16[384,1536]{1,0:T(8,128)(2,1)S(1)}, u32[]{:S(2)}, u32[]{:S(2)}) collective-permute-start(bf16[384,1536]{1,0:T(8,128)(2,1)S(1)} %stack_rows.3.refs_0_), channel_id=1, source_target_pairs={{0,8},{2,10},{4,12},{6,14},{8,24},{10,26},{12,28},{14,30},{24,16},... | collective-permute-start | bytes 3538952 | tf_op jit(solution)/shard_map/ppermute | solution.py:684
  10.9 42.3 %collective-permute-start.4 = (bf16[128,1536]{1,0:T(8,128)(2,1)}, bf16[128,1536]{1,0:T(8,128)(2,1)}, u32[]{:S(2)}, u32[]{:S(2)}) collective-permute-start(bf16[128,1536]{1,0:T(8,128)(2,1)} %get-tuple-element.100), channel_id=1, source_target_pairs={{0,2},{2,0},{4,6},{6,4},{8,10},{10,8},{12,14},{14,12},{16,18},{18,... | collective-permute-start | bytes 1179656 | tf_op jit(solution)/shard_map/ppermute | solution.py:692
  12.4 40.8 %collective-permute-start.5 = (bf16[128,1536]{1,0:T(8,128)(2,1)}, bf16[128,1536]{1,0:T(8,128)(2,1)}, u32[]{:S(2)}, u32[]{:S(2)}) collective-permute-start(bf16[128,1536]{1,0:T(8,128)(2,1)} %get-tuple-element.101), channel_id=1, source_target_pairs={{0,4},{2,6},{4,0},{6,2},{8,12},{10,14},{12,8},{14,10},{16,20},{18,... | collective-permute-start | bytes 1179656 | tf_op jit(solution)/shard_map/ppermute | solution.py:692
  13.9 39.3 %collective-permute-start.6 = (bf16[128,1536]{1,0:T(8,128)(2,1)}, bf16[128,1536]{1,0:T(8,128)(2,1)}, u32[]{:S(2)}, u32[]{:S(2)}) collective-permute-start(bf16[128,1536]{1,0:T(8,128)(2,1)} %get-tuple-element.102), channel_id=1, source_target_pairs={{0,6},{2,4},{4,2},{6,0},{8,14},{10,12},{12,10},{14,8},{16,22},{18,... | collective-permute-start | bytes 1179656 | tf_op jit(solution)/shard_map/ppermute | solution.py:692
  34.5 31.5 %collective-permute-start.11 = (bf16[384,1536]{1,0:T(8,128)(2,1)S(1)}, bf16[384,1536]{1,0:T(8,128)(2,1)S(1)}, u32[]{:S(2)}, u32[]{:S(2)}) collective-permute-start(bf16[384,1536]{1,0:T(8,128)(2,1)S(1)} %collective-permute-done.1.refs_1_), channel_id=1, source_target_pairs={{0,8},{2,10},{4,12},{6,14},{8,24},{10,26},{12,28},{14,30},{24,16},... | collective-permute-start | bytes 3538952 | tf_op jit(solution)/shard_map/ppermute | solution.py:684
  53.8 12.1 %collective-permute-start.2 = (bf16[7,128,512]{2,1,0:T(8,128)(2,1)S(1)}, bf16[7,128,512]{2,1,0:T(8,128)(2,1)S(1)}, u32[]{:S(2)}, u32[]{:S(2)}) collective-permute-start(bf16[7,128,512]{2,1,0:T(8,128)(2,1)S(1)} %copy-done.21), channel_id=1, source_target_pairs={{0,1},{1,0},{2,3},{3,2},{4,5},{5,4},{6,7},{7,6},{8,9},{9,8},{10,11... | collective-permute-start | bytes 2752520 | tf_op jit(solution)/shard_map/ppermute | solution.py:625
  56.1 9.8 %collective-permute-start.3 = (bf16[12,128,256]{2,1,0:T(8,128)(2,1)S(1)}, bf16[12,128,256]{2,1,0:T(8,128)(2,1)S(1)}, u32[]{:S(2)}, u32[]{:S(2)}) collective-permute-start(bf16[12,128,256]{2,1,0:T(8,128)(2,1)S(1)} %get-tuple-element.95), channel_id=1, source_target_pairs={{0,1},{1,0},{2,3},{3,2},{4,5},{5,4},{6,7},{7,6},{8,9},{9,8},{10,11... | collective-permute-start | bytes 2359304 | tf_op jit(solution)/shard_map/ppermute | solution.py:625
  56.6 9.3 %collective-permute-start.10 = (bf16[256,1536]{1,0:T(8,128)(2,1)S(1)}, bf16[256,1536]{1,0:T(8,128)(2,1)S(1)}, u32[]{:S(2)}, u32[]{:S(2)}) collective-permute-start(bf16[256,1536]{1,0:T(8,128)(2,1)S(1)} %stack_rows.5), channel_id=1, source_target_pairs={{0,1},{1,0},{2,3},{3,2},{4,5},{5,4},{6,7},{7,6},{8,9},{9,8},{10,11... | collective-permute-start | bytes 2359304 | tf_op jit(solution)/shard_map/ppermute | solution.py:625
  56.7 9.2 %collective-permute-start.9 = (bf16[256,1536]{1,0:T(8,128)(2,1)S(1)}, bf16[256,1536]{1,0:T(8,128)(2,1)S(1)}, u32[]{:S(2)}, u32[]{:S(2)}) collective-permute-start(bf16[256,1536]{1,0:T(8,128)(2,1)S(1)} %stack_rows.4), channel_id=1, source_target_pairs={{0,1},{1,0},{2,3},{3,2},{4,5},{5,4},{6,7},{7,6},{8,9},{9,8},{10,11... | collective-permute-start | bytes 2359304 | tf_op jit(solution)/shard_map/ppermute | solution.py:625
  66.0 11.5 %collective-permute-start.13 = (bf16[128,1536]{1,0:T(8,128)(2,1)S(1)}, bf16[128,1536]{1,0:T(8,128)(2,1)S(1)}, u32[]{:S(2)}, u32[]{:S(2)}) collective-permute-start(bf16[128,1536]{1,0:T(8,128)(2,1)S(1)} %get-tuple-element.119), channel_id=1, source_target_pairs={{0,1},{1,0},{2,3},{3,2},{4,5},{5,4},{6,7},{7,6},{8,9},{9,8},{10,11... | collective-permute-start | bytes 1179656 | tf_op jit(solution)/shard_map/ppermute | solution.py:625
  66.2 11.3 %collective-permute-start.14 = (bf16[128,1536]{1,0:T(8,128)(2,1)S(1)}, bf16[128,1536]{1,0:T(8,128)(2,1)S(1)}, u32[]{:S(2)}, u32[]{:S(2)}) collective-permute-start(bf16[128,1536]{1,0:T(8,128)(2,1)S(1)} %get-tuple-element.120), channel_id=1, source_target_pairs={{0,1},{1,0},{2,3},{3,2},{4,5},{5,4},{6,7},{7,6},{8,9},{9,8},{10,11... | collective-permute-start | bytes 1179656 | tf_op jit(solution)/shard_map/ppermute | solution.py:625
  66.7 10.8 %collective-permute-start.12 = (bf16[384,384]{1,0:T(8,128)(2,1)S(1)}, bf16[384,384]{1,0:T(8,128)(2,1)S(1)}, u32[]{:S(2)}, u32[]{:S(2)}) collective-permute-start(bf16[384,384]{1,0:T(8,128)(2,1)S(1)} %get-tuple-element.116), channel_id=1, source_target_pairs={{0,8},{2,10},{4,12},{6,14},{8,24},{10,26},{12,28},{14,30},{24,16},... | collective-permute-start | bytes 884744 | tf_op jit(solution)/shard_map/ppermute | solution.py:684
  70.1 17.9 %collective-permute-start.15 = (bf16[384,640]{1,0:T(8,128)(2,1)S(1)}, bf16[384,640]{1,0:T(8,128)(2,1)S(1)}, u32[]{:S(2)}, u32[]{:S(2)}) collective-permute-start(bf16[384,640]{1,0:T(8,128)(2,1)S(1)} %get-tuple-element.126), channel_id=1, source_target_pairs={{0,8},{2,10},{4,12},{6,14},{8,24},{10,26},{12,28},{14,30},{24,16},... | collective-permute-start | bytes 1474568 | tf_op jit(solution)/shard_map/ppermute | solution.py:684
  78.2 10.8 %collective-permute-start.16 = (bf16[256,384]{1,0:T(8,128)(2,1)S(1)}, bf16[256,384]{1,0:T(8,128)(2,1)S(1)}, u32[]{:S(2)}, u32[]{:S(2)}) collective-permute-start(bf16[256,384]{1,0:T(8,128)(2,1)S(1)} %get-tuple-element.122), channel_id=1, source_target_pairs={{0,2},{2,0},{4,6},{6,4},{8,10},{10,8},{12,14},{14,12},{16,18},{18,... | collective-permute-start | bytes 589832 | tf_op jit(solution)/shard_map/ppermute | solution.py:692
  79.7 9.5 %collective-permute-start.17 = (bf16[256,384]{1,0:T(8,128)(2,1)S(1)}, bf16[256,384]{1,0:T(8,128)(2,1)S(1)}, u32[]{:S(2)}, u32[]{:S(2)}) collective-permute-start(bf16[256,384]{1,0:T(8,128)(2,1)S(1)} %get-tuple-element.123), channel_id=1, source_target_pairs={{0,4},{2,6},{4,0},{6,2},{8,12},{10,14},{12,8},{14,10},{16,20},{18,... | collective-permute-start | bytes 589832 | tf_op jit(solution)/shard_map/ppermute | solution.py:692
  81.2 7.9 %collective-permute-start.18 = (bf16[256,384]{1,0:T(8,128)(2,1)S(1)}, bf16[256,384]{1,0:T(8,128)(2,1)S(1)}, u32[]{:S(2)}, u32[]{:S(2)}) collective-permute-start(bf16[256,384]{1,0:T(8,128)(2,1)S(1)} %get-tuple-element.124), channel_id=1, source_target_pairs={{0,6},{2,4},{4,2},{6,0},{8,14},{10,12},{12,10},{14,8},{16,22},{18,... | collective-permute-start | bytes 589832 | tf_op jit(solution)/shard_map/ppermute | solution.py:692
  81.7 13.9 %collective-permute-start.19 = (bf16[384,512]{1,0:T(8,128)(2,1)S(1)}, bf16[384,512]{1,0:T(8,128)(2,1)S(1)}, u32[]{:S(2)}, u32[]{:S(2)}) collective-permute-start(bf16[384,512]{1,0:T(8,128)(2,1)S(1)} %get-tuple-element.137), channel_id=1, source_target_pairs={{0,8},{2,10},{4,12},{6,14},{8,24},{10,26},{12,28},{14,30},{24,16},... | collective-permute-start | bytes 1179656 | tf_op jit(solution)/shard_map/ppermute | solution.py:684
  89.2 10.6 %collective-permute-start.20 = (bf16[256,640]{1,0:T(8,128)(2,1)S(1)}, bf16[256,640]{1,0:T(8,128)(2,1)S(1)}, u32[]{:S(2)}, u32[]{:S(2)}) collective-permute-start(bf16[256,640]{1,0:T(8,128)(2,1)S(1)} %get-tuple-element.145), channel_id=1, source_target_pairs={{0,2},{2,0},{4,6},{6,4},{8,10},{10,8},{12,14},{14,12},{16,18},{18,... | collective-permute-start | bytes 983048 | tf_op jit(solution)/shard_map/ppermute | solution.py:692
  90.6 14.5 %collective-permute-start.21 = (bf16[256,640]{1,0:T(8,128)(2,1)S(1)}, bf16[256,640]{1,0:T(8,128)(2,1)S(1)}, u32[]{:S(2)}, u32[]{:S(2)}) collective-permute-start(bf16[256,640]{1,0:T(8,128)(2,1)S(1)} %get-tuple-element.146), channel_id=1, source_target_pairs={{0,4},{2,6},{4,0},{6,2},{8,12},{10,14},{12,8},{14,10},{16,20},{18,... | collective-permute-start | bytes 983048 | tf_op jit(solution)/shard_map/ppermute | solution.py:692
  92.1 15.7 %collective-permute-start.22 = (bf16[256,640]{1,0:T(8,128)(2,1)S(1)}, bf16[256,640]{1,0:T(8,128)(2,1)S(1)}, u32[]{:S(2)}, u32[]{:S(2)}) collective-permute-start(bf16[256,640]{1,0:T(8,128)(2,1)S(1)} %get-tuple-element.147), channel_id=1, source_target_pairs={{0,6},{2,4},{4,2},{6,0},{8,14},{10,12},{12,10},{14,8},{16,22},{18,... | collective-permute-start | bytes 983048 | tf_op jit(solution)/shard_map/ppermute | solution.py:692
  99.8 12.7 %collective-permute-start.23 = (bf16[256,512]{1,0:T(8,128)(2,1)S(1)}, bf16[256,512]{1,0:T(8,128)(2,1)S(1)}, u32[]{:S(2)}, u32[]{:S(2)}) collective-permute-start(bf16[256,512]{1,0:T(8,128)(2,1)S(1)} %get-tuple-element.153), channel_id=1, source_target_pairs={{0,2},{2,0},{4,6},{6,4},{8,10},{10,8},{12,14},{14,12},{16,18},{18,... | collective-permute-start | bytes 786440 | tf_op jit(solution)/shard_map/ppermute | solution.py:692
  101.2 15.4 %collective-permute-start.24 = (bf16[256,512]{1,0:T(8,128)(2,1)S(1)}, bf16[256,512]{1,0:T(8,128)(2,1)S(1)}, u32[]{:S(2)}, u32[]{:S(2)}) collective-permute-start(bf16[256,512]{1,0:T(8,128)(2,1)S(1)} %get-tuple-element.154), channel_id=1, source_target_pairs={{0,4},{2,6},{4,0},{6,2},{8,12},{10,14},{12,8},{14,10},{16,20},{18,... | collective-permute-start | bytes 786440 | tf_op jit(solution)/shard_map/ppermute | solution.py:692
  102.8 13.8 %collective-permute-start.25 = (bf16[256,512]{1,0:T(8,128)(2,1)S(1)}, bf16[256,512]{1,0:T(8,128)(2,1)S(1)}, u32[]{:S(2)}, u32[]{:S(2)}) collective-permute-start(bf16[256,512]{1,0:T(8,128)(2,1)S(1)} %get-tuple-element.155), channel_id=1, source_target_pairs={{0,6},{2,4},{4,2},{6,0},{8,14},{10,12},{12,10},{14,8},{16,22},{18,... | collective-permute-start | bytes 786440 | tf_op jit(solution)/shard_map/ppermute | solution.py:692
  107.9 10.4 %collective-permute-start.27 = (bf16[128,640]{1,0:T(8,128)(2,1)S(1)}, bf16[128,640]{1,0:T(8,128)(2,1)S(1)}, u32[]{:S(2)}, u32[]{:S(2)}) collective-permute-start(bf16[128,640]{1,0:T(8,128)(2,1)S(1)} %get-tuple-element.161), channel_id=1, source_target_pairs={{0,1},{1,0},{2,3},{3,2},{4,5},{5,4},{6,7},{7,6},{8,9},{9,8},{10,11... | collective-permute-start | bytes 491528 | tf_op jit(solution)/shard_map/ppermute | solution.py:625
  (27 other events, 155.0 us)

commit v10 on v9

--- a/solution.py
+++ b/solution.py
@@ -558,7 +558,7 @@
 def project(stay, came_a, came_b, weight):
     rows, depth = stay.shape
     width = weight.shape[1]
-    tile = 512 if width % 1024 == 0 else width // 2
+    tile = 768 if width % 1536 == 0 else width // 2
     half = width // tile // 2
     fixed = [pl.BlockSpec(x.shape, lambda i: (0, 0)) for x in (stay, came_a, came_b)]
     return pl.pallas_call(

time: 120 us -> 119 us (level)
  transfers between devices with their start and end apart: 29 -> 29, of which waited for: 12 -> 12; matrix products, arithmetic and copies ran while one was open for 1% -> 1% of each run, Pallas kernels for 38% -> 37%
where the time goes in v10:
time: 119 us
  Pallas kernels  45.7 us (38%)
  waiting for transfers between devices  29.7 us (25%)
  starting transfers between devices  27.2 us (23%)
  local copies, waits for them, and re-layouts  14.4 us (12%)
  between operations  1.61 us (1%)
    ppermute x12, waiting for transfers between devices, plane_swap(): lax.ppermute(x, 'req', [(r, r - r % PLANE + (r % PLANE ^ d)) for r in ran...  15.2 us
    unnamed x45, local copies, waits for them, and re-layouts  14.4 us
    ppermute x12, starting transfers between devices, plane_swap(): lax.ppermute(x, 'req', [(r, r - r % PLANE + (r % PLANE ^ d)) for r in ran...  14 us
    ppermute x5, waiting for transfers between devices, pass_on(): return lax.ppermute(x, 'req', ring_pairs)  11.8 us
    pallas_call x1, Pallas kernels, attend(): pl.pallas_call(attend_kernel, out_shape=(jax.ShapeDtypeStruct(queries.sha...  11.4 us
    pallas_call x1, Pallas kernels, state_space(): pl.pallas_call(state_kernel, out_shape=(jax.ShapeDtypeStruct((length, hal...  10.1 us
    ppermute x5, starting transfers between devices, pass_on(): return lax.ppermute(x, 'req', ring_pairs)  9.83 us
    pallas_call x1, Pallas kernels, project(): pl.pallas_call(project_kernel, grid=(2 * half,), out_shape=(jax.ShapeDtyp...  7.79 us
  transfers between devices with their start and end apart: 29, of which 12 were waited for; matrix products, arithmetic and copies ran while one was open for 1% of the time, Pallas kernels for 37%

profile of v10, /device:TPU:0, one launch (start us, length us, event | category | flops | bytes accessed | tf_op | source)
XLA Modules:
  0.0 118.6 jit_solution(12137240177765281238)
XLA Ops:
  2.5 1.6 %collective-permute-done.refs_1_ = bf16[192,1536]{1,0:T(8,128)(2,1)S(1)} collective-permute-done((bf16[192,1536]{1,0:T(8,128)(2,1)S(1)}, bf16[192,1536]{1,0:T(8,128)(2,1)S(1)}, u32[]{:S(2)}, u32[]{:S(2)}) %collective-permute-start) | collective-permute-done | bytes 589856 | tf_op jit(solution)/shard_map/ppermute | solution.py:625
  4.2 3.0 %collective-permute-start.1 = (bf16[384,1536]{1,0:T(8,128)(2,1)S(1)}, bf16[384,1536]{1,0:T(8,128)(2,1)S(1)}, u32[]{:S(2)}, u32[]{:S(2)}) collective-permute-start(bf16[384,1536]{1,0:T(8,128)(2,1)S(1)} %stack_rows.3.refs_0_), channel_id=1, source_target_pairs={{0,8},{2,10},{4,12},{6,14},{8,24},{10,26},{12,28},{14,30},{24,16},... | collective-permute-start | bytes 3538952 | tf_op jit(solution)/shard_map/ppermute | solution.py:684
  10.9 1.5 %collective-permute-start.4 = (bf16[128,1536]{1,0:T(8,128)(2,1)}, bf16[128,1536]{1,0:T(8,128)(2,1)}, u32[]{:S(2)}, u32[]{:S(2)}) collective-permute-start(bf16[128,1536]{1,0:T(8,128)(2,1)} %get-tuple-element.100), channel_id=1, source_target_pairs={{0,2},{2,0},{4,6},{6,4},{8,10},{10,8},{12,14},{14,12},{16,18},{18,... | collective-permute-start | bytes 1179656 | tf_op jit(solution)/shard_map/ppermute | solution.py:692
  12.4 1.5 %collective-permute-start.5 = (bf16[128,1536]{1,0:T(8,128)(2,1)}, bf16[128,1536]{1,0:T(8,128)(2,1)}, u32[]{:S(2)}, u32[]{:S(2)}) collective-permute-start(bf16[128,1536]{1,0:T(8,128)(2,1)} %get-tuple-element.101), channel_id=1, source_target_pairs={{0,4},{2,6},{4,0},{6,2},{8,12},{10,14},{12,8},{14,10},{16,20},{18,... | collective-permute-start | bytes 1179656 | tf_op jit(solution)/shard_map/ppermute | solution.py:692
  16.5 11.4 %attend.1 = (bf16[128,1536]{1,0:T(8,128)(2,1)S(1)}, bf16[14,128,512]{2,1,0:T(8,128)(2,1)}, bf16[7,128,512]{2,1,0:T(8,128)(2,1)S(1)}) custom-call(s32[1,13]{1,0:T(1,128)S(1)} %copy-done.15, s32[1]{0:T(128)S(6)} %copy.29.ctx, s32[1,13]{1,0:T(1,128)S(1)} %bitcast.7, s32[1]{0:T(128)} %bitcast.unit, bf16[128,1536]{1,0:T(8,128)(2,1)S(1)} %copy-done.8, ...), custom_call_target="tpu_custom_call" | custom-call | tf_op jit(solution)/shard_map/attend/pallas_call | solution.py:129
  29.7 4.8 %collective-permute-done.1.refs_1_ = bf16[384,1536]{1,0:T(8,128)(2,1)S(1)} collective-permute-done((bf16[384,1536]{1,0:T(8,128)(2,1)S(1)}, bf16[384,1536]{1,0:T(8,128)(2,1)S(1)}, u32[]{:S(2)}, u32[]{:S(2)}) %collective-permute-start.1) | collective-permute-done | bytes 1179680 | tf_op jit(solution)/shard_map/ppermute | solution.py:684
  43.1 10.1 %state_space.1 = (bf16[128,2304]{1,0:T(8,128)(2,1)S(1)}, bf16[128,1152]{1,0:T(8,128)(2,1)S(1)}, bf16[128,1152]{1,0:T(8,128)(2,1)S(1)}, f32[2,12,128,256]{3,2,1,0:T(8,128)}, bf16[12,128,256]{2,1,0:T(8,128)(2,1)S(1)}) custom-call(s32[1]{0:T(128)} %bitcast.unit, f32[24]{0:T(128)S(1)} %copy-done.17, bf16[128,1536]{1,0:T(8,128)(2,1)S(1)} %copy-done.10, ...), custom_call_target="tpu_custom_call" | custom-call | tf_op jit(solution)/shard_map/state_space/pallas_call | solution.py:254
  57.1 7.8 %project.1 = (bf16[128,3072]{1,0:T(8,128)(2,1)S(1)}, bf16[128,1536]{1,0:T(8,128)(2,1)S(1)}, bf16[128,1536]{1,0:T(8,128)(2,1)S(1)}) custom-call(bf16[128,2304]{1,0:T(8,128)(2,1)S(1)} %get-tuple-element.93.stay_ref, bf16[128,1152]{1,0:T(8,128)(2,1)S(1)} %collective-permute-done.7.a_ref, bf16[128,1152]{1,0:T(8,128)(2,1)S(1)} %collective-permute-done.8.b_ref, ...), custom_call_target="tpu_custom_call" | custom-call | tf_op jit(solution)/shard_map/project/pallas_call | solution.py:564
  65.7 3.4 %collective-permute-start.12 = (bf16[384,384]{1,0:T(8,128)(2,1)S(1)}, bf16[384,384]{1,0:T(8,128)(2,1)S(1)}, u32[]{:S(2)}, u32[]{:S(2)}) collective-permute-start(bf16[384,384]{1,0:T(8,128)(2,1)S(1)} %get-tuple-element.116), channel_id=1, source_target_pairs={{0,8},{2,10},{4,12},{6,14},{8,24},{10,26},{12,28},{14,30},{24,16},... | collective-permute-start | bytes 884744 | tf_op jit(solution)/shard_map/ppermute | solution.py:684
  70.6 1.6 %begin.3.partial = f32[1024,384]{1,0:T(8,128)S(1)} custom-call(s32[1]{0:T(128)} %bitcast.unit, bf16[1024,1152]{1,0:T(8,128)(2,1)S(1)} %get-tuple-element.136.front, bf16[384,1536]{1,0:T(8,128)(2,1)S(1)} %stack_rows.3.refs_0_, bf16[384,1536]{1,0:T(8,128)(2,1)S(1)} %collective-permute-done.1.refs_1_, bf16[384,1536]{1,0:T(8,128)(2,1)S(1)} %collective-permute-done.11.refs_2_.x_ref), custom_call_target="tpu_custom_call" | custom-call | tf_op jit(solution)/shard_map/begin/pallas_call | solution.py:434
  72.2 4.3 %collective-permute-done.12.piece = bf16[384,384]{1,0:T(8,128)(2,1)S(1)} collective-permute-done((bf16[384,384]{1,0:T(8,128)(2,1)S(1)}, bf16[384,384]{1,0:T(8,128)(2,1)S(1)}, u32[]{:S(2)}, u32[]{:S(2)}) %collective-permute-start.12) | collective-permute-done | bytes 294944 | tf_op jit(solution)/shard_map/ppermute | solution.py:684
  77.2 1.6 %collective-permute-start.16 = (bf16[256,384]{1,0:T(8,128)(2,1)S(1)}, bf16[256,384]{1,0:T(8,128)(2,1)S(1)}, u32[]{:S(2)}, u32[]{:S(2)}) collective-permute-start(bf16[256,384]{1,0:T(8,128)(2,1)S(1)} %get-tuple-element.122), channel_id=1, source_target_pairs={{0,2},{2,0},{4,6},{6,4},{8,10},{10,8},{12,14},{14,12},{16,18},{18,... | collective-permute-start | bytes 589832 | tf_op jit(solution)/shard_map/ppermute | solution.py:692
  78.7 1.5 %collective-permute-start.17 = (bf16[256,384]{1,0:T(8,128)(2,1)S(1)}, bf16[256,384]{1,0:T(8,128)(2,1)S(1)}, u32[]{:S(2)}, u32[]{:S(2)}) collective-permute-start(bf16[256,384]{1,0:T(8,128)(2,1)S(1)} %get-tuple-element.123), channel_id=1, source_target_pairs={{0,4},{2,6},{4,0},{6,2},{8,12},{10,14},{12,8},{14,10},{16,20},{18,... | collective-permute-start | bytes 589832 | tf_op jit(solution)/shard_map/ppermute | solution.py:692
  80.7 2.5 %collective-permute-start.19 = (bf16[384,512]{1,0:T(8,128)(2,1)S(1)}, bf16[384,512]{1,0:T(8,128)(2,1)S(1)}, u32[]{:S(2)}, u32[]{:S(2)}) collective-permute-start(bf16[384,512]{1,0:T(8,128)(2,1)S(1)} %get-tuple-element.137), channel_id=1, source_target_pairs={{0,8},{2,10},{4,12},{6,14},{8,24},{10,26},{12,28},{14,30},{24,16},... | collective-permute-start | bytes 1179656 | tf_op jit(solution)/shard_map/ppermute | solution.py:684
  83.2 2.3 %begin.4.partial = f32[1024,640]{1,0:T(8,128)S(1)} custom-call(s32[1]{0:T(128)} %bitcast.unit, bf16[1024,1152]{1,0:T(8,128)(2,1)S(1)} %get-tuple-element.136.front, bf16[384,1536]{1,0:T(8,128)(2,1)S(1)} %stack_rows.3.refs_0_, bf16[384,1536]{1,0:T(8,128)(2,1)S(1)} %collective-permute-done.1.refs_1_, bf16[384,1536]{1,0:T(8,128)(2,1)S(1)} %collective-permute-done.11.refs_2_.x_ref), custom_call_target="tpu_custom_call" | custom-call | tf_op jit(solution)/shard_map/begin/pallas_call | solution.py:434
  85.5 1.5 %collective-permute-done.15.piece = bf16[384,640]{1,0:T(8,128)(2,1)S(1)} collective-permute-done((bf16[384,640]{1,0:T(8,128)(2,1)S(1)}, bf16[384,640]{1,0:T(8,128)(2,1)S(1)}, u32[]{:S(2)}, u32[]{:S(2)}) %collective-permute-start.15) | collective-permute-done | bytes 491552 | tf_op jit(solution)/shard_map/ppermute | solution.py:684
  89.6 1.5 %collective-permute-start.21 = (bf16[256,640]{1,0:T(8,128)(2,1)S(1)}, bf16[256,640]{1,0:T(8,128)(2,1)S(1)}, u32[]{:S(2)}, u32[]{:S(2)}) collective-permute-start(bf16[256,640]{1,0:T(8,128)(2,1)S(1)} %get-tuple-element.146), channel_id=1, source_target_pairs={{0,4},{2,6},{4,0},{6,2},{8,12},{10,14},{12,8},{14,10},{16,20},{18,... | collective-permute-start | bytes 983048 | tf_op jit(solution)/shard_map/ppermute | solution.py:692
  91.8 1.6 %begin.5.partial = f32[1024,512]{1,0:T(8,128)S(1)} custom-call(s32[1]{0:T(128)} %bitcast.unit, bf16[1024,1152]{1,0:T(8,128)(2,1)S(1)} %get-tuple-element.136.front, bf16[384,1536]{1,0:T(8,128)(2,1)S(1)} %stack_rows.3.refs_0_, bf16[384,1536]{1,0:T(8,128)(2,1)S(1)} %collective-permute-done.1.refs_1_, bf16[384,1536]{1,0:T(8,128)(2,1)S(1)} %collective-permute-done.11.refs_2_.x_ref), custom_call_target="tpu_custom_call" | custom-call | tf_op jit(solution)/shard_map/begin/pallas_call | solution.py:434
  95.4 3.5 %collective-permute-done.20.refs_0_ = bf16[256,640]{1,0:T(8,128)(2,1)S(1)} collective-permute-done((bf16[256,640]{1,0:T(8,128)(2,1)S(1)}, bf16[256,640]{1,0:T(8,128)(2,1)S(1)}, u32[]{:S(2)}, u32[]{:S(2)}) %collective-permute-start.20) | collective-permute-done | bytes 327712 | tf_op jit(solution)/shard_map/ppermute | solution.py:692
  100.2 1.5 %collective-permute-start.24 = (bf16[256,512]{1,0:T(8,128)(2,1)S(1)}, bf16[256,512]{1,0:T(8,128)(2,1)S(1)}, u32[]{:S(2)}, u32[]{:S(2)}) collective-permute-start(bf16[256,512]{1,0:T(8,128)(2,1)S(1)} %get-tuple-element.154), channel_id=1, source_target_pairs={{0,4},{2,6},{4,0},{6,2},{8,12},{10,14},{12,8},{14,10},{16,20},{18,... | collective-permute-start | bytes 786440 | tf_op jit(solution)/shard_map/ppermute | solution.py:692
  102.3 1.8 %collective-permute-done.21.refs_1_ = bf16[256,640]{1,0:T(8,128)(2,1)S(1)} collective-permute-done((bf16[256,640]{1,0:T(8,128)(2,1)S(1)}, bf16[256,640]{1,0:T(8,128)(2,1)S(1)}, u32[]{:S(2)}, u32[]{:S(2)}) %collective-permute-start.21) | collective-permute-done | bytes 327712 | tf_op jit(solution)/shard_map/ppermute | solution.py:692
  104.1 2.7 %collective-permute-done.22.refs_2_ = bf16[256,640]{1,0:T(8,128)(2,1)S(1)} collective-permute-done((bf16[256,640]{1,0:T(8,128)(2,1)S(1)}, bf16[256,640]{1,0:T(8,128)(2,1)S(1)}, u32[]{:S(2)}, u32[]{:S(2)}) %collective-permute-start.22) | collective-permute-done | bytes 327712 | tf_op jit(solution)/shard_map/ppermute | solution.py:692
  108.5 3.0 %collective-permute-done.23.refs_0_ = bf16[256,512]{1,0:T(8,128)(2,1)S(1)} collective-permute-done((bf16[256,512]{1,0:T(8,128)(2,1)S(1)}, bf16[256,512]{1,0:T(8,128)(2,1)S(1)}, u32[]{:S(2)}, u32[]{:S(2)}) %collective-permute-start.23) | collective-permute-done | bytes 262176 | tf_op jit(solution)/shard_map/ppermute | solution.py:692
  111.5 4.1 %collective-permute-done.24.refs_1_ = bf16[256,512]{1,0:T(8,128)(2,1)S(1)} collective-permute-done((bf16[256,512]{1,0:T(8,128)(2,1)S(1)}, bf16[256,512]{1,0:T(8,128)(2,1)S(1)}, u32[]{:S(2)}, u32[]{:S(2)}) %collective-permute-start.24) | collective-permute-done | bytes 262176 | tf_op jit(solution)/shard_map/ppermute | solution.py:692
  (100 shorter events, 36.9 us)
Async XLA Ops:
  4.2 30.3 %collective-permute-start.1 = (bf16[384,1536]{1,0:T(8,128)(2,1)S(1)}, bf16[384,1536]{1,0:T(8,128)(2,1)S(1)}, u32[]{:S(2)}, u32[]{:S(2)}) collective-permute-start(bf16[384,1536]{1,0:T(8,128)(2,1)S(1)} %stack_rows.3.refs_0_), channel_id=1, source_target_pairs={{0,8},{2,10},{4,12},{6,14},{8,24},{10,26},{12,28},{14,30},{24,16},... | collective-permute-start | bytes 3538952 | tf_op jit(solution)/shard_map/ppermute | solution.py:684
  10.9 42.3 %collective-permute-start.4 = (bf16[128,1536]{1,0:T(8,128)(2,1)}, bf16[128,1536]{1,0:T(8,128)(2,1)}, u32[]{:S(2)}, u32[]{:S(2)}) collective-permute-start(bf16[128,1536]{1,0:T(8,128)(2,1)} %get-tuple-element.100), channel_id=1, source_target_pairs={{0,2},{2,0},{4,6},{6,4},{8,10},{10,8},{12,14},{14,12},{16,18},{18,... | collective-permute-start | bytes 1179656 | tf_op jit(solution)/shard_map/ppermute | solution.py:692
  12.4 40.8 %collective-permute-start.5 = (bf16[128,1536]{1,0:T(8,128)(2,1)}, bf16[128,1536]{1,0:T(8,128)(2,1)}, u32[]{:S(2)}, u32[]{:S(2)}) collective-permute-start(bf16[128,1536]{1,0:T(8,128)(2,1)} %get-tuple-element.101), channel_id=1, source_target_pairs={{0,4},{2,6},{4,0},{6,2},{8,12},{10,14},{12,8},{14,10},{16,20},{18,... | collective-permute-start | bytes 1179656 | tf_op jit(solution)/shard_map/ppermute | solution.py:692
  13.9 39.3 %collective-permute-start.6 = (bf16[128,1536]{1,0:T(8,128)(2,1)}, bf16[128,1536]{1,0:T(8,128)(2,1)}, u32[]{:S(2)}, u32[]{:S(2)}) collective-permute-start(bf16[128,1536]{1,0:T(8,128)(2,1)} %get-tuple-element.102), channel_id=1, source_target_pairs={{0,6},{2,4},{4,2},{6,0},{8,14},{10,12},{12,10},{14,8},{16,22},{18,... | collective-permute-start | bytes 1179656 | tf_op jit(solution)/shard_map/ppermute | solution.py:692
  34.5 30.5 %collective-permute-start.11 = (bf16[384,1536]{1,0:T(8,128)(2,1)S(1)}, bf16[384,1536]{1,0:T(8,128)(2,1)S(1)}, u32[]{:S(2)}, u32[]{:S(2)}) collective-permute-start(bf16[384,1536]{1,0:T(8,128)(2,1)S(1)} %collective-permute-done.1.refs_1_), channel_id=1, source_target_pairs={{0,8},{2,10},{4,12},{6,14},{8,24},{10,26},{12,28},{14,30},{24,16},... | collective-permute-start | bytes 3538952 | tf_op jit(solution)/shard_map/ppermute | solution.py:684
  53.8 11.1 %collective-permute-start.2 = (bf16[7,128,512]{2,1,0:T(8,128)(2,1)S(1)}, bf16[7,128,512]{2,1,0:T(8,128)(2,1)S(1)}, u32[]{:S(2)}, u32[]{:S(2)}) collective-permute-start(bf16[7,128,512]{2,1,0:T(8,128)(2,1)S(1)} %copy-done.21), channel_id=1, source_target_pairs={{0,1},{1,0},{2,3},{3,2},{4,5},{5,4},{6,7},{7,6},{8,9},{9,8},{10,11... | collective-permute-start | bytes 2752520 | tf_op jit(solution)/shard_map/ppermute | solution.py:625
  56.1 8.8 %collective-permute-start.3 = (bf16[12,128,256]{2,1,0:T(8,128)(2,1)S(1)}, bf16[12,128,256]{2,1,0:T(8,128)(2,1)S(1)}, u32[]{:S(2)}, u32[]{:S(2)}) collective-permute-start(bf16[12,128,256]{2,1,0:T(8,128)(2,1)S(1)} %get-tuple-element.95), channel_id=1, source_target_pairs={{0,1},{1,0},{2,3},{3,2},{4,5},{5,4},{6,7},{7,6},{8,9},{9,8},{10,11... | collective-permute-start | bytes 2359304 | tf_op jit(solution)/shard_map/ppermute | solution.py:625
  56.6 8.3 %collective-permute-start.10 = (bf16[256,1536]{1,0:T(8,128)(2,1)S(1)}, bf16[256,1536]{1,0:T(8,128)(2,1)S(1)}, u32[]{:S(2)}, u32[]{:S(2)}) collective-permute-start(bf16[256,1536]{1,0:T(8,128)(2,1)S(1)} %stack_rows.5), channel_id=1, source_target_pairs={{0,1},{1,0},{2,3},{3,2},{4,5},{5,4},{6,7},{7,6},{8,9},{9,8},{10,11... | collective-permute-start | bytes 2359304 | tf_op jit(solution)/shard_map/ppermute | solution.py:625
  56.7 8.2 %collective-permute-start.9 = (bf16[256,1536]{1,0:T(8,128)(2,1)S(1)}, bf16[256,1536]{1,0:T(8,128)(2,1)S(1)}, u32[]{:S(2)}, u32[]{:S(2)}) collective-permute-start(bf16[256,1536]{1,0:T(8,128)(2,1)S(1)} %stack_rows.4), channel_id=1, source_target_pairs={{0,1},{1,0},{2,3},{3,2},{4,5},{5,4},{6,7},{7,6},{8,9},{9,8},{10,11... | collective-permute-start | bytes 2359304 | tf_op jit(solution)/shard_map/ppermute | solution.py:625
  65.0 11.5 %collective-permute-start.13 = (bf16[128,1536]{1,0:T(8,128)(2,1)S(1)}, bf16[128,1536]{1,0:T(8,128)(2,1)S(1)}, u32[]{:S(2)}, u32[]{:S(2)}) collective-permute-start(bf16[128,1536]{1,0:T(8,128)(2,1)S(1)} %get-tuple-element.119), channel_id=1, source_target_pairs={{0,1},{1,0},{2,3},{3,2},{4,5},{5,4},{6,7},{7,6},{8,9},{9,8},{10,11... | collective-permute-start | bytes 1179656 | tf_op jit(solution)/shard_map/ppermute | solution.py:625
  65.2 11.3 %collective-permute-start.14 = (bf16[128,1536]{1,0:T(8,128)(2,1)S(1)}, bf16[128,1536]{1,0:T(8,128)(2,1)S(1)}, u32[]{:S(2)}, u32[]{:S(2)}) collective-permute-start(bf16[128,1536]{1,0:T(8,128)(2,1)S(1)} %get-tuple-element.120), channel_id=1, source_target_pairs={{0,1},{1,0},{2,3},{3,2},{4,5},{5,4},{6,7},{7,6},{8,9},{9,8},{10,11... | collective-permute-start | bytes 1179656 | tf_op jit(solution)/shard_map/ppermute | solution.py:625
  65.7 10.8 %collective-permute-start.12 = (bf16[384,384]{1,0:T(8,128)(2,1)S(1)}, bf16[384,384]{1,0:T(8,128)(2,1)S(1)}, u32[]{:S(2)}, u32[]{:S(2)}) collective-permute-start(bf16[384,384]{1,0:T(8,128)(2,1)S(1)} %get-tuple-element.116), channel_id=1, source_target_pairs={{0,8},{2,10},{4,12},{6,14},{8,24},{10,26},{12,28},{14,30},{24,16},... | collective-permute-start | bytes 884744 | tf_op jit(solution)/shard_map/ppermute | solution.py:684
  69.1 17.9 %collective-permute-start.15 = (bf16[384,640]{1,0:T(8,128)(2,1)S(1)}, bf16[384,640]{1,0:T(8,128)(2,1)S(1)}, u32[]{:S(2)}, u32[]{:S(2)}) collective-permute-start(bf16[384,640]{1,0:T(8,128)(2,1)S(1)} %get-tuple-element.126), channel_id=1, source_target_pairs={{0,8},{2,10},{4,12},{6,14},{8,24},{10,26},{12,28},{14,30},{24,16},... | collective-permute-start | bytes 1474568 | tf_op jit(solution)/shard_map/ppermute | solution.py:684
  77.2 10.8 %collective-permute-start.16 = (bf16[256,384]{1,0:T(8,128)(2,1)S(1)}, bf16[256,384]{1,0:T(8,128)(2,1)S(1)}, u32[]{:S(2)}, u32[]{:S(2)}) collective-permute-start(bf16[256,384]{1,0:T(8,128)(2,1)S(1)} %get-tuple-element.122), channel_id=1, source_target_pairs={{0,2},{2,0},{4,6},{6,4},{8,10},{10,8},{12,14},{14,12},{16,18},{18,... | collective-permute-start | bytes 589832 | tf_op jit(solution)/shard_map/ppermute | solution.py:692
  78.7 9.5 %collective-permute-start.17 = (bf16[256,384]{1,0:T(8,128)(2,1)S(1)}, bf16[256,384]{1,0:T(8,128)(2,1)S(1)}, u32[]{:S(2)}, u32[]{:S(2)}) collective-permute-start(bf16[256,384]{1,0:T(8,128)(2,1)S(1)} %get-tuple-element.123), channel_id=1, source_target_pairs={{0,4},{2,6},{4,0},{6,2},{8,12},{10,14},{12,8},{14,10},{16,20},{18,... | collective-permute-start | bytes 589832 | tf_op jit(solution)/shard_map/ppermute | solution.py:692
  80.2 7.9 %collective-permute-start.18 = (bf16[256,384]{1,0:T(8,128)(2,1)S(1)}, bf16[256,384]{1,0:T(8,128)(2,1)S(1)}, u32[]{:S(2)}, u32[]{:S(2)}) collective-permute-start(bf16[256,384]{1,0:T(8,128)(2,1)S(1)} %get-tuple-element.124), channel_id=1, source_target_pairs={{0,6},{2,4},{4,2},{6,0},{8,14},{10,12},{12,10},{14,8},{16,22},{18,... | collective-permute-start | bytes 589832 | tf_op jit(solution)/shard_map/ppermute | solution.py:692
  80.7 13.9 %collective-permute-start.19 = (bf16[384,512]{1,0:T(8,128)(2,1)S(1)}, bf16[384,512]{1,0:T(8,128)(2,1)S(1)}, u32[]{:S(2)}, u32[]{:S(2)}) collective-permute-start(bf16[384,512]{1,0:T(8,128)(2,1)S(1)} %get-tuple-element.137), channel_id=1, source_target_pairs={{0,8},{2,10},{4,12},{6,14},{8,24},{10,26},{12,28},{14,30},{24,16},... | collective-permute-start | bytes 1179656 | tf_op jit(solution)/shard_map/ppermute | solution.py:684
  88.2 10.7 %collective-permute-start.20 = (bf16[256,640]{1,0:T(8,128)(2,1)S(1)}, bf16[256,640]{1,0:T(8,128)(2,1)S(1)}, u32[]{:S(2)}, u32[]{:S(2)}) collective-permute-start(bf16[256,640]{1,0:T(8,128)(2,1)S(1)} %get-tuple-element.145), channel_id=1, source_target_pairs={{0,2},{2,0},{4,6},{6,4},{8,10},{10,8},{12,14},{14,12},{16,18},{18,... | collective-permute-start | bytes 983048 | tf_op jit(solution)/shard_map/ppermute | solution.py:692
  89.6 14.5 %collective-permute-start.21 = (bf16[256,640]{1,0:T(8,128)(2,1)S(1)}, bf16[256,640]{1,0:T(8,128)(2,1)S(1)}, u32[]{:S(2)}, u32[]{:S(2)}) collective-permute-start(bf16[256,640]{1,0:T(8,128)(2,1)S(1)} %get-tuple-element.146), channel_id=1, source_target_pairs={{0,4},{2,6},{4,0},{6,2},{8,12},{10,14},{12,8},{14,10},{16,20},{18,... | collective-permute-start | bytes 983048 | tf_op jit(solution)/shard_map/ppermute | solution.py:692
  91.1 15.6 %collective-permute-start.22 = (bf16[256,640]{1,0:T(8,128)(2,1)S(1)}, bf16[256,640]{1,0:T(8,128)(2,1)S(1)}, u32[]{:S(2)}, u32[]{:S(2)}) collective-permute-start(bf16[256,640]{1,0:T(8,128)(2,1)S(1)} %get-tuple-element.147), channel_id=1, source_target_pairs={{0,6},{2,4},{4,2},{6,0},{8,14},{10,12},{12,10},{14,8},{16,22},{18,... | collective-permute-start | bytes 983048 | tf_op jit(solution)/shard_map/ppermute | solution.py:692
  98.8 12.7 %collective-permute-start.23 = (bf16[256,512]{1,0:T(8,128)(2,1)S(1)}, bf16[256,512]{1,0:T(8,128)(2,1)S(1)}, u32[]{:S(2)}, u32[]{:S(2)}) collective-permute-start(bf16[256,512]{1,0:T(8,128)(2,1)S(1)} %get-tuple-element.153), channel_id=1, source_target_pairs={{0,2},{2,0},{4,6},{6,4},{8,10},{10,8},{12,14},{14,12},{16,18},{18,... | collective-permute-start | bytes 786440 | tf_op jit(solution)/shard_map/ppermute | solution.py:692
  100.2 15.4 %collective-permute-start.24 = (bf16[256,512]{1,0:T(8,128)(2,1)S(1)}, bf16[256,512]{1,0:T(8,128)(2,1)S(1)}, u32[]{:S(2)}, u32[]{:S(2)}) collective-permute-start(bf16[256,512]{1,0:T(8,128)(2,1)S(1)} %get-tuple-element.154), channel_id=1, source_target_pairs={{0,4},{2,6},{4,0},{6,2},{8,12},{10,14},{12,8},{14,10},{16,20},{18,... | collective-permute-start | bytes 786440 | tf_op jit(solution)/shard_map/ppermute | solution.py:692
  101.8 13.8 %collective-permute-start.25 = (bf16[256,512]{1,0:T(8,128)(2,1)S(1)}, bf16[256,512]{1,0:T(8,128)(2,1)S(1)}, u32[]{:S(2)}, u32[]{:S(2)}) collective-permute-start(bf16[256,512]{1,0:T(8,128)(2,1)S(1)} %get-tuple-element.155), channel_id=1, source_target_pairs={{0,6},{2,4},{4,2},{6,0},{8,14},{10,12},{12,10},{14,8},{16,22},{18,... | collective-permute-start | bytes 786440 | tf_op jit(solution)/shard_map/ppermute | solution.py:692
  106.9 10.4 %collective-permute-start.27 = (bf16[128,640]{1,0:T(8,128)(2,1)S(1)}, bf16[128,640]{1,0:T(8,128)(2,1)S(1)}, u32[]{:S(2)}, u32[]{:S(2)}) collective-permute-start(bf16[128,640]{1,0:T(8,128)(2,1)S(1)} %get-tuple-element.161), channel_id=1, source_target_pairs={{0,1},{1,0},{2,3},{3,2},{4,5},{5,4},{6,7},{7,6},{8,9},{9,8},{10,11... | collective-permute-start | bytes 491528 | tf_op jit(solution)/shard_map/ppermute | solution.py:625
  (27 other events, 155.1 us)
